TPU v7x, 32 devices: a whole 2x2x4 slice. The times are simulated.
32 devices in a mesh: groups: 2 (over y), ctx: 4 (over z), head: 2 (over x), sec: 2 (over core).
Axes of the slice: x: 2, y: 2, z: 4, core: 2. Of those that a mesh axis runs over, the one named last changes fastest.
Arguments:
- queries: bfloat16 [256, 8192], P(('groups', 'ctx'), ('head', 'sec')), parts along dimension 0, may hold values from -128 to 128
- key_cache: bfloat16 [16384, 1024], P(('groups', 'ctx'), ('head', 'sec')), parts along dimension 0, may hold values from -4.5 to 4.5
- value_cache: bfloat16 [16384, 1024], P(('groups', 'ctx'), ('head', 'sec')), parts along dimension 0, may hold values from -6 to 6
- block_index: int32 [2, 8], P('groups'), parts along dimension 0, may hold values from 0 to 63, as said below
- stream: bfloat16 [256, 8192], P(('groups', 'head', 'sec'), 'ctx'), parts along dimension 0, may hold values from -6 to 6
- out_weight: bfloat16 [8192, 8192], P(('head', 'sec'), 'ctx'), may hold values from -0.0625 to 0.0625
- norm_gain: float32 [8192], replicated, may hold values from 0.5 to 1.5
- gate_weight: bfloat16 [8192, 14336], P(('head', 'sec'), 'ctx'), may hold values from -0.0625 to 0.0625
- up_weight: bfloat16 [8192, 14336], P(('head', 'sec'), 'ctx'), may hold values from -0.0625 to 0.0625
- down_weight: bfloat16 [14336, 8192], P('ctx', ('head', 'sec')), may hold values from -0.046875 to 0.046875
Outputs:
- layer_out: bfloat16 [256, 8192], P(('groups', 'ctx'), ('head', 'sec')), parts along dimension 0
There are 2 independent parts, one for each index of `groups`. A program takes and returns all parts, laid end to end along the dimension named above; an argument that names none is the same for every part. Nothing has to cross between parts.
Inputs may be any that keep to these rules, and one draw needn't show every extreme that they name: `block_index`: row b lists 8 distinct key blocks in increasing order, none after the block 63 + b, and includes that block and block 0. Of the aligned runs of 16 key blocks (k * 16 to (k + 1) * 16 - 1), each holds at least one of a row's blocks and at most 4, and in every row some run holds exactly 4.
All inputs are finite; a program needn't handle non-finite values.
Results may differ from a plain program's by a relative error of at most 0.014.
Values may be sent and summed in bfloat16 or wider, within the bound.
No kernel may reach another device: no remote copies, remote signals or barrier semaphores. Data moves between devices by JAX's collectives and lax.ppermute only.
A program may use at most 128 MiB of HBM per device.

v0:
```python
import functools
import math

import jax
import jax.numpy as jnp
from jax import lax
from jax.experimental import pallas as pl
from jax.experimental.pallas import tpu as pltpu
from jax.sharding import PartitionSpec as P


HQ = 64
KVH = 8
DH = 128
KB = 128
MOST = 4
LANES = 128
EPS = 1e-05
ALL = ("ctx", "head", "sec")


VM = pl.BlockSpec(memory_space=pltpu.VMEM)
SM = pl.BlockSpec(memory_space=pltpu.SMEM)
ANY = pl.BlockSpec(memory_space=pl.ANY)
F32 = jnp.float32
BF16 = jnp.bfloat16


def struct(shape, dtype):
    return jax.ShapeDtypeStruct(shape, dtype)


def call(kernel, out, in_specs, args, cost=3, scratch=(), vmem=8):
    outs = out if isinstance(out, (tuple, list)) else (out,)
    nbytes = sum(math.prod(a.shape) * a.dtype.itemsize for a in args)
    nbytes += sum(math.prod(o.shape) * o.dtype.itemsize for o in outs)
    return pl.pallas_call(
        kernel,
        out_shape=out,
        in_specs=in_specs,
        out_specs=jax.tree.map(lambda _: VM, out),
        scratch_shapes=scratch,
        compiler_params=pltpu.CompilerParams(vmem_limit_bytes=vmem << 20),
        cost_estimate=pl.CostEstimate(flops=cost * 10**9, bytes_accessed=nbytes, transcendentals=0),
    )(*args)


def in_vmem(x):
    return pltpu.with_memory_space_constraint(x, pltpu.VMEM)


def in_hbm(x):
    return pltpu.with_memory_space_constraint(x, pltpu.HBM)


def slots(index_ref, blocks):
    entries = index_ref.shape[1]
    base = lax.axis_index("ctx") * blocks
    first = jnp.int32(0)
    end = jnp.int32(0)
    for n in range(entries):
        block = index_ref[0, n]
        first += (block < base).astype(jnp.int32)
        end += (block < base + blocks).astype(jnp.int32)
    found = []
    for slot in range(MOST):
        entry = jnp.minimum(first + slot, entries - 1)
        local = jnp.clip(index_ref[0, entry] - base, 0, blocks - 1)
        found.append((local, first + slot < end))
    return found


def attend(offset, first_token, start_ref, q_ref, key_ref, value_ref, out_ref, score_ref, weight_ref):
    rows = q_ref.shape[0]
    heads = q_ref.shape[1] // DH
    kv_dev = key_ref.shape[1] // DH
    group = heads // kv_dev
    scale = 1.0 / math.sqrt(DH)
    token0 = first_token + (lax.axis_index("ctx") ^ offset) * rows
    ahead = (
        lax.broadcasted_iota(jnp.int32, (rows, KB), 1)
        - lax.broadcasted_iota(jnp.int32, (rows, KB), 0)
        - token0
    )
    allowed = [ahead + start_ref[slot : slot + 1, :] <= 0 for slot in range(MOST)]
    head_lane = lax.broadcasted_iota(jnp.int32, (rows, LANES), 1)
    peak_tile = jnp.zeros((rows, LANES), F32)
    total_tile = jnp.ones((rows, LANES), F32)
    for kv in range(kv_dev):
        stacked = jnp.concatenate(
            [q_ref[:, (kv * group + h) * DH : (kv * group + h + 1) * DH] for h in range(group)], axis=0
        )
        score_ref[kv] = lax.dot_general(
            stacked,
            key_ref[:, kv * DH : (kv + 1) * DH],
            (((1,), (1,)), ((), ())),
            preferred_element_type=F32,
        )
    for kv in range(kv_dev):
        for h in range(group):
            head = kv * group + h
            span = slice(h * rows, (h + 1) * rows)
            parts = [
                jnp.where(allowed[slot], score_ref[kv, span, slot * KB : (slot + 1) * KB], -1e30)
                for slot in range(MOST)
            ]
            peak = jnp.max(functools.reduce(jnp.maximum, parts), axis=1, keepdims=True)
            parts = [jnp.exp((p - peak) * scale) for p in parts]
            row_total = jnp.sum(functools.reduce(jnp.add, parts), axis=1, keepdims=True)
            for slot, p in enumerate(parts):
                weight_ref[kv, span, slot * KB : (slot + 1) * KB] = p.astype(BF16)
            peak_tile = jnp.where(head_lane == head, peak, peak_tile)
            total_tile = jnp.where(head_lane == head, row_total, total_tile)
    inverse = 1.0 / total_tile
    for kv in range(kv_dev):
        mixture = jnp.dot(
            weight_ref[kv], value_ref[:, kv * DH : (kv + 1) * DH], preferred_element_type=F32
        )
        for h in range(group):
            head = kv * group + h
            out_ref[:, head * DH : (head + 1) * DH] = (
                mixture[h * rows : (h + 1) * rows] * inverse[:, head : head + 1]
            ).astype(BF16)
    lse_tile = peak_tile * scale + jnp.log(total_tile)
    high = lse_tile.astype(BF16).astype(F32)
    rest = lse_tile - high
    mid = rest.astype(BF16).astype(F32)
    low = rest - mid
    tile = high + pltpu.roll(mid, heads, 1) + pltpu.roll(low, 2 * heads, 1)
    out_ref[:, heads * DH :] = tile.astype(BF16)


def first_attend_kernel(
    blocks, first_token, index_ref, q_hbm, key_hbm, value_hbm,
    key_ref, value_ref, start_ref, out_ref, q_ref, score_ref, weight_ref, sems, q_sem,
):
    copies = [pltpu.make_async_copy(q_hbm, q_ref, q_sem)]
    found = slots(index_ref, blocks)
    for slot, (local, _) in enumerate(found):
        rows = pl.ds(pl.multiple_of(local * KB, KB), KB)
        for n, (src, dst) in enumerate(((key_hbm, key_ref), (value_hbm, value_ref))):
            copies.append(
                pltpu.make_async_copy(
                    src.at[rows, :], dst.at[slot * KB : (slot + 1) * KB, :], sems.at[n, slot]
                )
            )
    for copy in copies:
        copy.start()
    row = lax.broadcasted_iota(jnp.int32, start_ref.shape, 0)
    starts = jnp.zeros(start_ref.shape, jnp.int32)
    base = lax.axis_index("ctx") * blocks
    for slot, (local, valid) in enumerate(found):
        starts = jnp.where(row == slot, jnp.where(valid, (base + local) * KB, jnp.int32(1 << 29)), starts)
    start_ref[...] = starts
    for copy in copies:
        copy.wait()
    attend(0, first_token, start_ref, q_ref, key_ref, value_ref, out_ref, score_ref, weight_ref)


def blend_kernel(*refs):
    out_ref = refs[-1]
    parts = refs[:-1]
    heads = out_ref.shape[1] // DH
    logs = []
    for part in parts:
        tile = part[:, heads * DH :].astype(F32)
        logs.append(
            tile + pltpu.roll(tile, LANES - heads, 1) + pltpu.roll(tile, LANES - 2 * heads, 1)
        )
    peak = functools.reduce(jnp.maximum, logs)
    shares = [jnp.exp(log - peak) for log in logs]
    total = functools.reduce(jnp.add, shares)
    shares = [share / total for share in shares]
    for head in range(heads):
        span = slice(head * DH, (head + 1) * DH)
        out_ref[:, span] = functools.reduce(
            jnp.add,
            [share[:, head : head + 1] * part[:, span].astype(F32) for share, part in zip(shares, parts)],
        ).astype(BF16)


def place():
    return lax.axis_index("head") * lax.axis_size("sec") + lax.axis_index("sec")


def place_of(n, rows, count):
    n_sec = lax.axis_size("sec")
    owner = lax.axis_index("ctx") ^ n
    other = ((owner % n_sec) != lax.axis_index("sec")).astype(jnp.int32)
    return pl.multiple_of(other * (count // n_sec * rows) + owner // n_sec * rows, rows)


def product(rows_ref, weight_ref, source, keep_ref, send_ref, target, width, tile):
    half = rows_ref.shape[0] // 2
    for at in range(0, width, tile):
        size = min(tile, width - at)
        part = jnp.dot(
            rows_ref[...],
            weight_ref[:, source + at : source + at + size],
            preferred_element_type=F32,
        )
        keep_ref[:, target + at : target + at + size] = part[:half]
        send_ref[:, target + at : target + at + size] = part[half:].astype(BF16)


def project_kernel(tile, *refs):
    pieces, (weight_ref, keep_ref, send_ref, rows_ref) = refs[:-4], refs[-4:]
    rows = pieces[0].shape[0]
    for n, piece in enumerate(pieces):
        rows_ref[pl.ds(place_of(n, rows, len(pieces)), rows), :] = piece[...]
    product(rows_ref, weight_ref, 0, keep_ref, send_ref, 0, weight_ref.shape[1], tile)


def fold_kernel(width, keep_ref, got_ref, keep_out, send_out):
    rows = keep_out.shape[0]
    head = lax.axis_index("head")
    mine = pl.ds(pl.multiple_of(head * rows, rows), rows)
    other = pl.ds(pl.multiple_of((1 - head) * rows, rows), rows)
    keep_out[:, :width] = keep_ref[mine, :width] + got_ref[mine, :width].astype(F32)
    send_out[:, :width] = (keep_ref[other, :width] + got_ref[other, :width].astype(F32)).astype(BF16)
    if keep_ref.shape[1] > width:
        keep_out[:, width:] = keep_ref[mine, width:] + take_exact(got_ref[mine, width:])
        put_exact(send_out, slice(None), width, keep_ref[other, width:] + take_exact(got_ref[other, width:]))


def middle_kernel(stream_ref, keep_ref, got_ref, out_ref):
    out_ref[...] = (
        stream_ref[...].astype(F32) + (keep_ref[...] + got_ref[...].astype(F32))
    ).astype(BF16)


def put_exact(ref, rows, at, value):
    high = value.astype(BF16)
    ref[rows, at : at + LANES] = high
    ref[rows, at + LANES : at + 2 * LANES] = (value - high.astype(F32)).astype(BF16)


def take_exact(tile):
    return tile[:, :LANES].astype(F32) + tile[:, LANES:].astype(F32)


def prepare_kernel(piece_ref, gain_ref, row_ref, square_ref):
    model = piece_ref.shape[1]
    gain = gain_ref[:, pl.ds(pl.multiple_of(place() * model, model), model)]
    wide = piece_ref[...].astype(F32)
    row_ref[...] = (wide * gain).astype(BF16)
    square_ref[...] = jnp.broadcast_to(jnp.sum(wide * wide, axis=1, keepdims=True), square_ref.shape)


def first_gate_kernel(width, tile, *refs):
    pieces, squares = refs[:4], refs[4:8]
    gate_ref, up_ref, keep_ref, send_ref, rows_ref = refs[8:]
    rows = pieces[0].shape[0]
    half = rows_ref.shape[0] // 2
    for n, (piece, square) in enumerate(zip(pieces, squares)):
        at = place_of(n, rows, len(pieces))
        rows_ref[pl.ds(at, rows), :] = piece[...]

        @pl.when(at < half)
        def _():
            keep_ref[pl.ds(at, rows), 2 * width :] = square[...]

        @pl.when(at >= half)
        def _():
            put_exact(send_ref, pl.ds(pl.multiple_of(at - half, rows), rows), 2 * width, square[...])

    product(rows_ref, gate_ref, 0, keep_ref, send_ref, 0, width, tile)
    product(rows_ref, up_ref, 0, keep_ref, send_ref, width, width, tile)


def gate_kernel(start, width, tile, rows_ref, gate_ref, up_ref, keep_ref, send_ref):
    product(rows_ref, gate_ref, start, keep_ref, send_ref, 0, width, tile)
    product(rows_ref, up_ref, start, keep_ref, send_ref, width, width, tile)


def scale_kernel(model, keep_ref, got_ref, out_ref):
    at = keep_ref.shape[1] - LANES
    square = keep_ref[:, at:] + take_exact(got_ref[:, at:])
    out_ref[...] = lax.rsqrt(square / model + EPS)


def hidden_kernel(scale_ref, keep_ref, got_ref, out_ref):
    width = out_ref.shape[1]
    scale = scale_ref[...]
    for at in range(0, width, LANES):
        gate = keep_ref[:, at : at + LANES] + got_ref[:, at : at + LANES].astype(F32)
        up = keep_ref[:, width + at : width + at + LANES] + got_ref[
            :, width + at : width + at + LANES
        ].astype(F32)
        gate = gate * scale
        out_ref[:, at : at + LANES] = (
            gate / (1.0 + jnp.exp(-gate)) * (up * scale)
        ).astype(BF16)


def first_hidden_kernel(model, keep_ref, got_ref, out_ref, scale_ref):
    scale_kernel(model, keep_ref, got_ref, scale_ref)
    hidden_kernel(scale_ref, keep_ref, got_ref, out_ref)


def gather_rows(pieces, rows_ref):
    rows = pieces[0].shape[0]
    for n, piece in enumerate(pieces):
        at = pl.ds(pl.multiple_of((lax.axis_index("ctx") ^ place() ^ n) * rows, rows), rows)
        rows_ref[at, :] = piece[...]


def first_down_kernel(tile, *refs):
    pieces, (weight_ref, out_ref, rows_ref) = refs[:4], refs[4:]
    gather_rows(pieces, rows_ref)
    depth = rows_ref.shape[1]
    for at in range(0, weight_ref.shape[1], tile):
        out_ref[:, at : at + tile] = jnp.dot(
            rows_ref[...], weight_ref[:depth, at : at + tile], preferred_element_type=F32
        )


def down_kernel(tile, *refs):
    pieces, (weight_ref, so_far_ref, own_ref) = refs[:4], refs[4:7]
    sends, rows_ref = refs[7:-1], refs[-1]
    gather_rows(pieces, rows_ref)
    rows = pieces[0].shape[0]
    depth = rows_ref.shape[1]
    start = weight_ref.shape[0] - depth
    for at in range(0, weight_ref.shape[1], tile):
        columns = slice(at, at + tile)
        part = so_far_ref[:, columns] + jnp.dot(
            rows_ref[...], weight_ref[start:, columns], preferred_element_type=F32
        )
        own_ref[:, columns] = part[:rows]
        for n, send in enumerate(sends):
            send[:, columns] = part[(n + 1) * rows : (n + 2) * rows].astype(BF16)


def final_kernel(middle_ref, own_ref, *refs):
    parts, out_ref = refs[:-1], refs[-1]
    total = own_ref[...]
    for part in parts:
        total = total + part[...].astype(F32)
    out_ref[...] = (middle_ref[...].astype(F32) + total).astype(BF16)


def swap(x, axis):
    return lax.ppermute(x, axis, [(0, 1), (1, 0)])


def turn(x, axis, n, offset):
    return lax.ppermute(x, axis, [(i, i ^ offset) for i in range(n)])


def direct_body(
    queries,
    key_cache,
    value_cache,
    block_index,
    stream,
    out_weight,
    norm_gain,
    gate_weight,
    up_weight,
    down_weight,
):
    n_context, n_head, _ = (lax.axis_size(a) for a in ALL)
    rows, heads_width = queries.shape
    context_len = key_cache.shape[0] * n_context
    model = norm_gain.shape[0]
    total = rows * n_context
    blocks = key_cache.shape[0] // KB
    kv_width = key_cache.shape[1]
    order = (3, 2, 1)

    got_q = {m: turn(queries, "ctx", n_context, m) for m in (2, 1)}
    got_q[3] = turn(got_q[2], "ctx", n_context, 1)
    picked = struct((MOST * KB, kv_width), BF16)
    partial_out = struct((rows, heads_width + LANES), BF16)
    kv_dev = kv_width // DH
    tall = heads_width // kv_width * rows
    scratch = [
        pltpu.VMEM((kv_dev, tall, MOST * KB), F32),
        pltpu.VMEM((kv_dev, tall, MOST * KB), BF16),
    ]
    keys, values, starts, own_partial = call(
        functools.partial(first_attend_kernel, blocks, context_len - total),
        (picked, picked, struct((8, LANES), jnp.int32), partial_out),
        [SM, ANY, ANY, ANY],
        (block_index, in_hbm(queries), in_hbm(key_cache), in_hbm(value_cache)),
        scratch=[pltpu.VMEM((rows, heads_width), BF16)]
        + scratch
        + [pltpu.SemaphoreType.DMA((2, MOST)), pltpu.SemaphoreType.DMA],
    )
    partial = {0: own_partial}
    for m in order:
        partial[m] = call(
            functools.partial(attend, m, context_len - total),
            partial_out,
            [VM] * 4,
            (starts, got_q[m], keys, values),
            scratch=scratch,
        )
    back = {m: turn(partial[m], "ctx", n_context, m) for m in order}
    back[0] = partial[0]
    blended = call(
        blend_kernel, struct((rows, heads_width), BF16), [VM] * 4, tuple(back[m] for m in range(4))
    )

    attention = {m: turn(blended, "ctx", n_context, m) for m in order}
    attention[0] = blended
    width = out_weight.shape[1]
    keep, away = call(
        functools.partial(project_kernel, 512),
        (struct((n_head * rows, width), F32), struct((n_head * rows, width), BF16)),
        [VM] * 5,
        tuple(attention[m] for m in range(4)) + (in_vmem(out_weight),),
        scratch=[pltpu.VMEM((total, heads_width), BF16)],
        cost=6,
    )
    got = swap(away, "sec")
    keep, away = call(
        functools.partial(fold_kernel, width),
        (struct((rows, width), F32), struct((rows, width), BF16)),
        [VM, VM],
        (keep, got),
        cost=6,
    )
    got = swap(away, "head")
    middle = call(middle_kernel, struct((rows, width), BF16), [VM] * 3, (stream, keep, got), cost=6)

    all_middle = {
        m: lax.ppermute(
            middle,
            ALL,
            [
                (a * n_context + b, (b ^ m) * n_context + a)
                for a in range(n_context)
                for b in range(n_context)
            ],
        )
        for m in (3, 0, 1, 2)
    }
    hidden_width = gate_weight.shape[1]
    first = hidden_width // 2 // LANES * LANES
    chunks = ((0, first), (first, hidden_width - first))
    hidden = []
    gate_vmem, up_vmem = in_vmem(gate_weight), in_vmem(up_weight)
    prepared = [
        call(
            prepare_kernel,
            (struct((rows, width), BF16), struct((rows, LANES), F32)),
            [VM, VM],
            (all_middle[m], norm_gain[None]),
            cost=0,
        )
        for m in range(4)
    ]
    scale = None
    for c, (start, chunk) in enumerate(chunks):
        extra = LANES if c == 0 else 0
        out = (
            struct((n_head * rows, 2 * chunk + extra), F32),
            struct((n_head * rows, 2 * chunk + 2 * extra), BF16),
        )
        if c == 0:
            keep, away, all_rows = call(
                functools.partial(first_gate_kernel, chunk, 512),
                out + (struct((total, width), BF16),),
                [VM] * 10,
                tuple(p[0] for p in prepared)
                + tuple(p[1] for p in prepared)
                + (gate_vmem, up_vmem),
            )
        else:
            keep, away = call(
                functools.partial(gate_kernel, start, chunk, 512),
                out,
                [VM] * 3,
                (all_rows, gate_vmem, up_vmem),
            )
        keep, away = call(
            functools.partial(fold_kernel, 2 * chunk),
            (
                struct((rows, 2 * chunk + extra), F32),
                struct((rows, 2 * chunk + 2 * extra), BF16),
            ),
            [VM, VM],
            (keep, swap(away, "sec")),
        )
        got = swap(away, "head")
        if c == 0:
            own, scale = call(
                functools.partial(first_hidden_kernel, model),
                (struct((rows, chunk), BF16), struct((rows, LANES), F32)),
                [VM] * 2,
                (keep, got),
            )
        else:
            own = call(hidden_kernel, struct((rows, chunk), BF16), [VM] * 3, (scale, keep, got))
        across = swap(own, "head")
        beside = swap(own, "sec")
        hidden.append((own, beside, across, swap(across, "sec")))
    out_width = down_weight.shape[1]
    down_vmem = in_vmem(down_weight)
    so_far = call(
        functools.partial(first_down_kernel, 512),
        struct((total, out_width), F32),
        [VM] * 5,
        hidden[0] + (down_vmem,),
        scratch=[pltpu.VMEM((total, chunks[0][1]), BF16)],
    )
    res = call(
        functools.partial(down_kernel, 512),
        (struct((rows, out_width), F32),) + (struct((rows, out_width), BF16),) * 3,
        [VM] * 6,
        hidden[1] + (down_vmem, so_far),
        scratch=[pltpu.VMEM((total, chunks[1][1]), BF16)],
    )
    parts = [turn(res[m], "ctx", n_context, m) for m in order]
    return call(
        final_kernel, struct((rows, out_width), BF16), [VM] * 5, (all_middle[0], res[0]) + tuple(parts)
    )


def local_attention(gathered, key_cache, value_cache, block_index, context_index, context_len):
    group_size = HQ // KVH
    kv_dev = key_cache.shape[1] // DH
    blocks_dev = key_cache.shape[0] // KB
    total_tokens = gathered.shape[0]
    key_blocks = key_cache.reshape(blocks_dev, KB, kv_dev, DH)
    value_blocks = value_cache.reshape(blocks_dev, KB, kv_dev, DH)
    local_ids = context_index * blocks_dev + jnp.arange(blocks_dev, dtype=jnp.int32)
    member = jnp.any(block_index[:, :, None] == local_ids[None, None, :], axis=1)
    member_rank = jnp.cumsum(member.astype(jnp.int32), axis=1) - 1
    slot_hit = member[:, None, :] & (
        member_rank[:, None, :] == jnp.arange(MOST, dtype=jnp.int32)[None, :, None]
    )
    slot_block = jnp.sum(
        jnp.where(slot_hit, jnp.arange(blocks_dev, dtype=jnp.int32)[None, None, :], 0), axis=2
    )
    slot_valid = jnp.any(slot_hit, axis=2)
    picked_keys = jnp.take(key_blocks, slot_block[0], axis=0).reshape(MOST * KB, kv_dev, DH)
    picked_values = jnp.take(value_blocks, slot_block[0], axis=0).reshape(MOST * KB, kv_dev, DH)
    key_pos = (
        (local_ids[0] + slot_block[0])[:, None] * KB + jnp.arange(KB, dtype=jnp.int32)[None, :]
    ).reshape(-1)
    live_keys = jnp.broadcast_to(slot_valid[0][:, None], (MOST, KB)).reshape(-1)
    query_pos = context_len - total_tokens + jnp.arange(KB, dtype=jnp.int32)
    allowed = live_keys[None, :] & (key_pos[None, :] <= query_pos[:, None])
    query_block = gathered.reshape(KB, kv_dev, group_size, DH)
    scores = jnp.einsum(
        "qhgd,phd->hgqp", query_block, picked_keys, preferred_element_type=jnp.float32
    ) / math.sqrt(DH)
    scores = jnp.where(allowed[None, None], scores, -jnp.inf)
    peak_score = jnp.max(scores, axis=-1, keepdims=True)
    unnormed = jnp.exp(scores - peak_score)
    row_total = jnp.sum(unnormed, axis=-1)
    mixture = jnp.einsum(
        "hgqp,phd->qhgd",
        unnormed.astype(jnp.bfloat16),
        picked_values,
        preferred_element_type=jnp.float32,
    )
    result = mixture / jnp.transpose(row_total, (2, 0, 1))[..., None]
    log_total = jnp.transpose(peak_score[..., 0] + jnp.log(row_total), (2, 0, 1))
    out_list = result.reshape(KB, -1)
    lse_list = log_total.reshape(KB, -1)
    return (out_list, lse_list)


def general_body(
    queries,
    key_cache,
    value_cache,
    block_index,
    stream,
    out_weight,
    norm_gain,
    gate_weight,
    up_weight,
    down_weight,
):
    n_context = lax.axis_size("ctx")
    context_index = lax.axis_index("ctx")
    context_len = key_cache.shape[0] * n_context
    gathered = lax.all_gather(queries, "ctx", axis=0, tiled=True)
    part_out, part_lse = local_attention(
        gathered, key_cache, value_cache, block_index, context_index, context_len
    )
    spread_out, spread_lse = (
        lax.all_to_all(part_out[:, None, :], "ctx", split_axis=0, concat_axis=1, tiled=True),
        lax.all_to_all(part_lse[:, None, :], "ctx", split_axis=0, concat_axis=1, tiled=True),
    )
    share_rows = spread_out.shape[0]
    head_count = spread_lse.shape[2]
    peak_value = jnp.max(spread_lse, axis=1, keepdims=True)
    share_weight = jnp.exp(spread_lse - peak_value)
    blended = jnp.sum(
        spread_out.reshape(share_rows, n_context, head_count, -1) * share_weight[..., None], axis=1
    )
    blended = blended / jnp.sum(share_weight, axis=1)[..., None]
    attention = lax.all_gather(
        blended.reshape(share_rows, -1).astype(jnp.bfloat16), "ctx", axis=0, tiled=True
    )
    row_piece = attention
    projected = lax.psum_scatter(
        jnp.dot(row_piece, out_weight, preferred_element_type=jnp.float32),
        ("head", "sec"),
        scatter_dimension=0,
        tiled=True,
    )
    middle = (stream.astype(jnp.float32) + projected).astype(jnp.bfloat16)
    full_middle = lax.all_gather(middle, "ctx", axis=1, tiled=True)
    middle_wide = full_middle.astype(jnp.float32)
    mean_square = jnp.mean(middle_wide * middle_wide, axis=-1, keepdims=True)
    normed = (middle_wide * lax.rsqrt(mean_square + 1e-05) * norm_gain).astype(jnp.bfloat16)
    normed_cols, middle_cols = (
        lax.all_to_all(normed, ("head", "sec"), split_axis=1, concat_axis=0, tiled=True),
        lax.all_to_all(full_middle, ("head", "sec"), split_axis=1, concat_axis=0, tiled=True),
    )
    row_piece = normed_cols
    gate_up = lax.psum_scatter(
        jnp.concatenate(
            [
                jnp.dot(row_piece, gate_weight, preferred_element_type=jnp.float32),
                jnp.dot(row_piece, up_weight, preferred_element_type=jnp.float32),
            ],
            axis=1,
        ),
        ("head", "sec"),
        scatter_dimension=0,
        tiled=True,
    )
    hidden_width = gate_weight.shape[1]
    hidden = (jax.nn.silu(gate_up[:, :hidden_width]) * gate_up[:, hidden_width:]).astype(
        jnp.bfloat16
    )
    all_hidden = lax.all_gather(hidden, ("head", "sec"), axis=0, tiled=True)
    row_piece = all_hidden
    down_part = lax.psum_scatter(
        jnp.dot(row_piece, down_weight, preferred_element_type=jnp.float32),
        "ctx",
        scatter_dimension=0,
        tiled=True,
    )
    own_middle = lax.dynamic_slice_in_dim(
        middle_cols, context_index * down_part.shape[0], down_part.shape[0], 0
    )
    return (own_middle.astype(jnp.float32) + down_part).astype(jnp.bfloat16)


def solution(mesh):
    size = dict(mesh.shape)
    direct = size["ctx"] == 4 and size["head"] == 2 and size["sec"] == 2
    return jax.shard_map(
        direct_body if direct else general_body,
        mesh=mesh,
        in_specs=(
            P(("groups", "ctx"), ("head", "sec")),
            P(("groups", "ctx"), ("head", "sec")),
            P(("groups", "ctx"), ("head", "sec")),
            P("groups", None),
            P(("groups", "head", "sec"), "ctx"),
            P(("head", "sec"), "ctx"),
            P(),
            P(("head", "sec"), "ctx"),
            P(("head", "sec"), "ctx"),
            P("ctx", ("head", "sec")),
        ),
        out_specs=P(("groups", "ctx"), ("head", "sec")),
        check_vma=False,
    )
```

profile of v0, /device:TPU:0, one launch (start us, length us, event | category | flops | bytes accessed | tf_op | source)
XLA Modules:
  0.0 109.5 jit_solution(18224218386044646595)
XLA Ops:
  0.0 3.1 %collective-permute-start = (bf16[32,2048]{1,0:T(8,128)(2,1)}, bf16[32,2048]{1,0:T(8,128)(2,1)S(1)}, u32[]{:S(2)}, u32[]{:S(2)}) collective-permute-start(bf16[32,2048]{1,0:T(8,128)(2,1)} %q_hbm.1), channel_id=1, source_target_pairs={{0,4},{4,0},{8,12},{12,8},{1,5},{5,1},{9,13},{13,9},{2,6},{6,2},{1... | collective-permute-start | bytes 393224 | tf_op jit(solution)/shard_map/ppermute | solution.py:348
  3.1 2.6 %collective-permute-start.2 = (bf16[32,2048]{1,0:T(8,128)(2,1)}, bf16[32,2048]{1,0:T(8,128)(2,1)S(1)}, u32[]{:S(2)}, u32[]{:S(2)}) collective-permute-start(bf16[32,2048]{1,0:T(8,128)(2,1)} %q_hbm.1), channel_id=1, source_target_pairs={{0,8},{4,12},{8,0},{12,4},{1,9},{5,13},{9,1},{13,5},{2,10},{6,14},... | collective-permute-start | bytes 393224 | tf_op jit(solution)/shard_map/ppermute | solution.py:348
  5.6 0.7 copy-done.2
  6.3 2.6 %shard_map.100 = (bf16[512,256]{1,0:T(8,128)(2,1)S(1)}, bf16[512,256]{1,0:T(8,128)(2,1)S(1)}, s32[8,128]{1,0:T(8,128)S(1)}, bf16[32,2176]{1,0:T(8,128)(2,1)S(1)}) custom-call(s32[1,8]{1,0:T(1,128)S(1)} %copy-done.2, bf16[32,2048]{1,0:T(8,128)(2,1)} %q_hbm.1, bf16[2048,256]{1,0:T(8,128)(2,1)} %key_hbm.1, bf16[2048,256]{1,0:T(8,128)(2,1)} %value_hbm.1), custom_call_target="tpu_custom_call" | custom-call | flops 3000000000 | bytes 2895904 | tf_op jit(solution)/shard_map/pallas_call | solution.py:37
  8.9 0.8 shard_map.101
  9.7 0.5 collective-permute-start.1
  10.3 1.8 %collective-permute-done.2.q_ref = bf16[32,2048]{1,0:T(8,128)(2,1)S(1)} collective-permute-done((bf16[32,2048]{1,0:T(8,128)(2,1)}, bf16[32,2048]{1,0:T(8,128)(2,1)S(1)}, u32[]{:S(2)}, u32[]{:S(2)}) %collective-permute-start.2) | collective-permute-done | bytes 131104 | tf_op jit(solution)/shard_map/ppermute | solution.py:348
  12.1 0.3 collective-permute-start.4
  12.4 0.8 shard_map.102
  13.3 2.7 %collective-permute-start.3 = (bf16[32,2176]{1,0:T(8,128)(2,1)S(1)}, bf16[32,2176]{1,0:T(8,128)(2,1)S(1)}, u32[]{:S(2)}, u32[]{:S(2)}) collective-permute-start(bf16[32,2176]{1,0:T(8,128)(2,1)S(1)} %shard_map.102), channel_id=1, source_target_pairs={{0,8},{4,12},{8,0},{12,4},{1,9},{5,13},{9,1},{13,5},{2,10},{6,14},... | collective-permute-start | bytes 417800 | tf_op jit(solution)/shard_map/ppermute | solution.py:348
  15.9 4.4 %collective-permute-done.4.q_ref = bf16[32,2048]{1,0:T(8,128)(2,1)S(1)} collective-permute-done((bf16[32,2048]{1,0:T(8,128)(2,1)S(1)}, bf16[32,2048]{1,0:T(8,128)(2,1)S(1)}, u32[]{:S(2)}, u32[]{:S(2)}) %collective-permute-start.4) | collective-permute-done | bytes 131104 | tf_op jit(solution)/shard_map/ppermute | solution.py:348
  20.3 0.8 shard_map.103
  21.1 2.0 %collective-permute-start.5 = (bf16[32,2176]{1,0:T(8,128)(2,1)S(1)}, bf16[32,2176]{1,0:T(8,128)(2,1)S(1)}, u32[]{:S(2)}, u32[]{:S(2)}) collective-permute-start(bf16[32,2176]{1,0:T(8,128)(2,1)S(1)} %shard_map.103), channel_id=1, source_target_pairs={{0,12},{4,8},{8,4},{12,0},{1,13},{5,9},{9,5},{13,1},{2,14},{6,10},... | collective-permute-start | bytes 417800 | tf_op jit(solution)/shard_map/ppermute | solution.py:348
  23.1 5.0 %collective-permute-done.5.refs_3_ = bf16[32,2176]{1,0:T(8,128)(2,1)S(1)} collective-permute-done((bf16[32,2176]{1,0:T(8,128)(2,1)S(1)}, bf16[32,2176]{1,0:T(8,128)(2,1)S(1)}, u32[]{:S(2)}, u32[]{:S(2)}) %collective-permute-start.5) | collective-permute-done | bytes 139296 | tf_op jit(solution)/shard_map/ppermute | solution.py:348
  28.1 0.5 shard_map.104.refs_0_
  28.7 2.5 %collective-permute-start.7 = (bf16[32,2048]{1,0:T(8,128)(2,1)S(1)}, bf16[32,2048]{1,0:T(8,128)(2,1)S(1)}, u32[]{:S(2)}, u32[]{:S(2)}) collective-permute-start(bf16[32,2048]{1,0:T(8,128)(2,1)S(1)} %shard_map.104.refs_0_), channel_id=1, source_target_pairs={{0,8},{4,12},{8,0},{12,4},{1,9},{5,13},{9,1},{13,5},{2,10},{6,14},... | collective-permute-start | bytes 393224 | tf_op jit(solution)/shard_map/ppermute | solution.py:348
  31.2 1.9 %collective-permute-start.8 = (bf16[32,2048]{1,0:T(8,128)(2,1)S(1)}, bf16[32,2048]{1,0:T(8,128)(2,1)S(1)}, u32[]{:S(2)}, u32[]{:S(2)}) collective-permute-start(bf16[32,2048]{1,0:T(8,128)(2,1)S(1)} %shard_map.104.refs_0_), channel_id=1, source_target_pairs={{0,12},{4,8},{8,4},{12,0},{1,13},{5,9},{9,5},{13,1},{2,14},{6,10},... | collective-permute-start | bytes 393224 | tf_op jit(solution)/shard_map/ppermute | solution.py:348
  33.0 2.8 %collective-permute-done.6.refs_1_ = bf16[32,2048]{1,0:T(8,128)(2,1)S(1)} collective-permute-done((bf16[32,2048]{1,0:T(8,128)(2,1)S(1)}, bf16[32,2048]{1,0:T(8,128)(2,1)S(1)}, u32[]{:S(2)}, u32[]{:S(2)}) %collective-permute-start.6) | collective-permute-done | bytes 131104 | tf_op jit(solution)/shard_map/ppermute | solution.py:348
  35.8 3.4 %collective-permute-done.7.refs_2_ = bf16[32,2048]{1,0:T(8,128)(2,1)S(1)} collective-permute-done((bf16[32,2048]{1,0:T(8,128)(2,1)S(1)}, bf16[32,2048]{1,0:T(8,128)(2,1)S(1)}, u32[]{:S(2)}, u32[]{:S(2)}) %collective-permute-start.7) | collective-permute-done | bytes 131104 | tf_op jit(solution)/shard_map/ppermute | solution.py:348
  39.3 1.3 %shard_map.105 = (f32[64,2048]{1,0:T(8,128)S(1)}, bf16[64,2048]{1,0:T(8,128)(2,1)S(1)}) custom-call(bf16[32,2048]{1,0:T(8,128)(2,1)S(1)} %shard_map.104.refs_0_, bf16[32,2048]{1,0:T(8,128)(2,1)S(1)} %collective-permute-done.6.refs_1_, bf16[32,2048]{1,0:T(8,128)(2,1)S(1)} %collective-permute-done.7.refs_2_, ...), custom_call_target="tpu_custom_call" | custom-call | flops 6000000000 | bytes 9699328 | tf_op jit(solution)/shard_map/pallas_call | solution.py:37
  40.7 1.5 %collective-permute-done.9.got_ref = bf16[64,2048]{1,0:T(8,128)(2,1)S(1)} collective-permute-done((bf16[64,2048]{1,0:T(8,128)(2,1)S(1)}, bf16[64,2048]{1,0:T(8,128)(2,1)S(1)}, u32[]{:S(2)}, u32[]{:S(2)}) %collective-permute-start.9) | collective-permute-done | bytes 262176 | tf_op jit(solution)/shard_map/ppermute | solution.py:344
  42.3 1.6 %collective-permute-start.10 = (bf16[32,2048]{1,0:T(8,128)(2,1)S(1)}, bf16[32,2048]{1,0:T(8,128)(2,1)S(1)}, u32[]{:S(2)}, u32[]{:S(2)}) collective-permute-start(bf16[32,2048]{1,0:T(8,128)(2,1)S(1)} %get-tuple-element.43), channel_id=1, source_target_pairs={{0,2},{2,0},{1,3},{3,1},{4,6},{6,4},{5,7},{7,5},{8,10},{10,8},{9,1... | collective-permute-start | bytes 393224 | tf_op jit(solution)/shard_map/ppermute | solution.py:344
  43.9 4.0 %collective-permute-done.10.got_ref = bf16[32,2048]{1,0:T(8,128)(2,1)S(1)} collective-permute-done((bf16[32,2048]{1,0:T(8,128)(2,1)S(1)}, bf16[32,2048]{1,0:T(8,128)(2,1)S(1)}, u32[]{:S(2)}, u32[]{:S(2)}) %collective-permute-start.10) | collective-permute-done | bytes 131104 | tf_op jit(solution)/shard_map/ppermute | solution.py:344
  48.0 0.8 collective-permute-start.11
  48.8 3.6 %collective-permute-start.12 = (bf16[32,2048]{1,0:T(8,128)(2,1)S(1)}, bf16[32,2048]{1,0:T(8,128)(2,1)S(1)}, u32[]{:S(2)}, u32[]{:S(2)}) collective-permute-start(bf16[32,2048]{1,0:T(8,128)(2,1)S(1)} %shard_map.107), channel_id=1, source_target_pairs={{0,4},{1,0},{2,12},{3,8},{4,5},{5,1},{6,13},{7,9},{8,6},{9,2},{10,... | collective-permute-start | bytes 393224 | tf_op jit(solution)/shard_map/ppermute | solution.py:429
  52.4 2.6 %collective-permute-start.13 = (bf16[32,2048]{1,0:T(8,128)(2,1)S(1)}, bf16[32,2048]{1,0:T(8,128)(2,1)S(1)}, u32[]{:S(2)}, u32[]{:S(2)}) collective-permute-start(bf16[32,2048]{1,0:T(8,128)(2,1)S(1)} %shard_map.107), channel_id=1, source_target_pairs={{0,8},{1,12},{2,0},{3,4},{4,9},{5,13},{6,1},{7,5},{8,10},{9,14},{1... | collective-permute-start | bytes 393224 | tf_op jit(solution)/shard_map/ppermute | solution.py:429
  55.1 0.2 collective-permute-start.14
  55.3 0.1 shard_map.108
  55.6 6.7 %collective-permute-done.13.piece_ref = bf16[32,2048]{1,0:T(8,128)(2,1)S(1)} collective-permute-done((bf16[32,2048]{1,0:T(8,128)(2,1)S(1)}, bf16[32,2048]{1,0:T(8,128)(2,1)S(1)}, u32[]{:S(2)}, u32[]{:S(2)}) %collective-permute-start.13) | collective-permute-done | bytes 131104 | tf_op jit(solution)/shard_map/ppermute | solution.py:429
  62.5 0.2 collective-permute-done.14.piece_ref
  62.8 2.4 %shard_map.112 = (f32[64,3712]{1,0:T(8,128)S(1)}, bf16[64,3840]{1,0:T(8,128)(2,1)S(1)}, bf16[128,2048]{1,0:T(8,128)(2,1)S(1)}) custom-call(bf16[32,2048]{1,0:T(8,128)(2,1)S(1)} %get-tuple-element.44.refs_0_, bf16[32,2048]{1,0:T(8,128)(2,1)S(1)} %get-tuple-element.45.refs_1_, bf16[32,2048]{1,0:T(8,128)(2,1)S(1)} %get-tuple-element.46.refs_2_, ...), custom_call_target="tpu_custom_call" | custom-call | flops 3000000000 | bytes 31916032 | tf_op jit(solution)/shard_map/pallas_call | solution.py:37
  65.3 2.1 %shard_map.115 = (f32[64,3584]{1,0:T(8,128)S(1)}, bf16[64,3584]{1,0:T(8,128)(2,1)S(1)}) custom-call(bf16[128,2048]{1,0:T(8,128)(2,1)S(1)} %get-tuple-element.57.rows_ref, bf16[2048,3584]{1,0:T(8,128)(2,1)S(1)} %bitcast.2, bf16[2048,3584]{1,0:T(8,128)(2,1)S(1)} %bitcast.4), custom_call_target="tpu_custom_call" | custom-call | flops 3000000000 | bytes 31260672 | tf_op jit(solution)/shard_map/pallas_call | solution.py:37
  67.4 0.6 collective-permute-start.17
  68.0 6.2 %collective-permute-start.16 = (bf16[32,3840]{1,0:T(8,128)(2,1)S(1)}, bf16[32,3840]{1,0:T(8,128)(2,1)S(1)}, u32[]{:S(2)}, u32[]{:S(2)}) collective-permute-start(bf16[32,3840]{1,0:T(8,128)(2,1)S(1)} %get-tuple-element.55), channel_id=1, source_target_pairs={{0,2},{2,0},{1,3},{3,1},{4,6},{6,4},{5,7},{7,5},{8,10},{10,8},{9,1... | collective-permute-start | bytes 737288 | tf_op jit(solution)/shard_map/ppermute | solution.py:344
  74.3 1.3 %collective-permute-start.18 = (bf16[32,3584]{1,0:T(8,128)(2,1)S(1)}, bf16[32,3584]{1,0:T(8,128)(2,1)S(1)}, u32[]{:S(2)}, u32[]{:S(2)}) collective-permute-start(bf16[32,3584]{1,0:T(8,128)(2,1)S(1)} %get-tuple-element.61), channel_id=1, source_target_pairs={{0,2},{2,0},{1,3},{3,1},{4,6},{6,4},{5,7},{7,5},{8,10},{10,8},{9,1... | collective-permute-start | bytes 688136 | tf_op jit(solution)/shard_map/ppermute | solution.py:344
  75.7 5.4 %collective-permute-done.16.got_ref = bf16[32,3840]{1,0:T(8,128)(2,1)S(1)} collective-permute-done((bf16[32,3840]{1,0:T(8,128)(2,1)S(1)}, bf16[32,3840]{1,0:T(8,128)(2,1)S(1)}, u32[]{:S(2)}, u32[]{:S(2)}) %collective-permute-start.16) | collective-permute-done | bytes 245792 | tf_op jit(solution)/shard_map/ppermute | solution.py:344
  81.2 2.1 %collective-permute-start.23 = (bf16[32,1792]{1,0:T(8,128)(2,1)S(1)}, bf16[32,1792]{1,0:T(8,128)(2,1)S(1)}, u32[]{:S(2)}, u32[]{:S(2)}) collective-permute-start(bf16[32,1792]{1,0:T(8,128)(2,1)S(1)} %get-tuple-element.62.refs_0_), channel_id=1, source_target_pairs={{0,2},{2,0},{1,3},{3,1},{4,6},{6,4},{5,7},{7,5},{8,10},{10,8},{9,1... | collective-permute-start | bytes 344072 | tf_op jit(solution)/shard_map/ppermute | solution.py:344
  83.3 2.7 %collective-permute-done.18.got_ref = bf16[32,3584]{1,0:T(8,128)(2,1)S(1)} collective-permute-done((bf16[32,3584]{1,0:T(8,128)(2,1)S(1)}, bf16[32,3584]{1,0:T(8,128)(2,1)S(1)}, u32[]{:S(2)}, u32[]{:S(2)}) %collective-permute-start.18) | collective-permute-done | bytes 229408 | tf_op jit(solution)/shard_map/ppermute | solution.py:344
  86.1 2.1 %collective-permute-start.20 = (bf16[32,1792]{1,0:T(8,128)(2,1)S(1)}, bf16[32,1792]{1,0:T(8,128)(2,1)S(1)}, u32[]{:S(2)}, u32[]{:S(2)}) collective-permute-start(bf16[32,1792]{1,0:T(8,128)(2,1)S(1)} %shard_map.117.refs_0_), channel_id=1, source_target_pairs={{0,2},{2,0},{1,3},{3,1},{4,6},{6,4},{5,7},{7,5},{8,10},{10,8},{9,1... | collective-permute-start | bytes 344072 | tf_op jit(solution)/shard_map/ppermute | solution.py:344
  88.2 0.5 collective-permute-start.24
  88.7 2.3 %collective-permute-done.20.refs_2_ = bf16[32,1792]{1,0:T(8,128)(2,1)S(1)} collective-permute-done((bf16[32,1792]{1,0:T(8,128)(2,1)S(1)}, bf16[32,1792]{1,0:T(8,128)(2,1)S(1)}, u32[]{:S(2)}, u32[]{:S(2)}) %collective-permute-start.20) | collective-permute-done | bytes 114720 | tf_op jit(solution)/shard_map/ppermute | solution.py:344
  91.0 1.1 %shard_map.118.refs_5_ = f32[128,2048]{1,0:T(8,128)S(1)} custom-call(bf16[32,1792]{1,0:T(8,128)(2,1)S(1)} %get-tuple-element.62.refs_0_, bf16[32,1792]{1,0:T(8,128)(2,1)S(1)} %collective-permute-done.22.refs_1_, bf16[32,1792]{1,0:T(8,128)(2,1)S(1)} %collective-permute-done.23.refs_2_, bf16[32,1792]{1,0:T(8,128)(2,1)S(1)} %collective-permute-done.24.refs_3_, ...), custom_call_target="tpu_custom_call" | custom-call | flops 3000000000 | bytes 16187392 | tf_op jit(solution)/shard_map/pallas_call | solution.py:37
  92.3 1.1 %shard_map.119 = (f32[32,2048]{1,0:T(8,128)S(1)}, bf16[32,2048]{1,0:T(8,128)(2,1)S(1)}, bf16[32,2048]{1,0:T(8,128)(2,1)S(1)}, bf16[32,2048]{1,0:T(8,128)(2,1)S(1)}) custom-call(bf16[32,1792]{1,0:T(8,128)(2,1)S(1)} %shard_map.117.refs_0_, bf16[32,1792]{1,0:T(8,128)(2,1)S(1)} %collective-permute-done.19.refs_1_, ...), custom_call_target="tpu_custom_call" | custom-call | flops 3000000000 | bytes 16842752 | tf_op jit(solution)/shard_map/pallas_call | solution.py:37
  93.4 3.7 %collective-permute-start.25 = (bf16[32,2048]{1,0:T(8,128)(2,1)S(1)}, bf16[32,2048]{1,0:T(8,128)(2,1)S(1)}, u32[]{:S(2)}, u32[]{:S(2)}) collective-permute-start(bf16[32,2048]{1,0:T(8,128)(2,1)S(1)} %get-tuple-element.64), channel_id=1, source_target_pairs={{0,12},{4,8},{8,4},{12,0},{1,13},{5,9},{9,5},{13,1},{2,14},{6,10},... | collective-permute-start | bytes 393224 | tf_op jit(solution)/shard_map/ppermute | solution.py:348
  97.1 0.8 collective-permute-start.27
  97.9 3.9 %collective-permute-done.25.refs_0_ = bf16[32,2048]{1,0:T(8,128)(2,1)S(1)} collective-permute-done((bf16[32,2048]{1,0:T(8,128)(2,1)S(1)}, bf16[32,2048]{1,0:T(8,128)(2,1)S(1)}, u32[]{:S(2)}, u32[]{:S(2)}) %collective-permute-start.25) | collective-permute-done | bytes 131104 | tf_op jit(solution)/shard_map/ppermute | solution.py:348
  101.8 7.0 %collective-permute-done.26.refs_1_ = bf16[32,2048]{1,0:T(8,128)(2,1)S(1)} collective-permute-done((bf16[32,2048]{1,0:T(8,128)(2,1)S(1)}, bf16[32,2048]{1,0:T(8,128)(2,1)S(1)}, u32[]{:S(2)}, u32[]{:S(2)}) %collective-permute-start.26) | collective-permute-done | bytes 131104 | tf_op jit(solution)/shard_map/ppermute | solution.py:348
  108.8 0.7 shard_map.120
  (67 shorter events, 1.4 us)
Async XLA Ops:
  0.0 8.9 %collective-permute-start = (bf16[32,2048]{1,0:T(8,128)(2,1)}, bf16[32,2048]{1,0:T(8,128)(2,1)S(1)}, u32[]{:S(2)}, u32[]{:S(2)}) collective-permute-start(bf16[32,2048]{1,0:T(8,128)(2,1)} %q_hbm.1), channel_id=1, source_target_pairs={{0,4},{4,0},{8,12},{12,8},{1,5},{5,1},{9,13},{13,9},{2,6},{6,2},{1... | collective-permute-start | bytes 393224 | tf_op jit(solution)/shard_map/ppermute | solution.py:348
  3.1 9.0 %collective-permute-start.2 = (bf16[32,2048]{1,0:T(8,128)(2,1)}, bf16[32,2048]{1,0:T(8,128)(2,1)S(1)}, u32[]{:S(2)}, u32[]{:S(2)}) collective-permute-start(bf16[32,2048]{1,0:T(8,128)(2,1)} %q_hbm.1), channel_id=1, source_target_pairs={{0,8},{4,12},{8,0},{12,4},{1,9},{5,13},{9,1},{13,5},{2,10},{6,14},... | collective-permute-start | bytes 393224 | tf_op jit(solution)/shard_map/ppermute | solution.py:348
  5.6 0.7 copy-start.2
  9.7 29.6 %slice-start.12 = ((s8[8388608]{0:T(1024)(128)(4,1)}), s8[4194304]{0:T(1024)(128)(4,1)S(1)}, s32[]{:S(2)}) async-start(s8[8388608]{0:T(1024)(128)(4,1)} %bitcast.11), calls=%async_computation.12 | async-start | bytes 8388608
  9.7 13.4 %collective-permute-start.1 = (bf16[32,2176]{1,0:T(8,128)(2,1)S(1)}, bf16[32,2176]{1,0:T(8,128)(2,1)S(1)}, u32[]{:S(2)}, u32[]{:S(2)}) collective-permute-start(bf16[32,2176]{1,0:T(8,128)(2,1)S(1)} %shard_map.101), channel_id=1, source_target_pairs={{0,4},{4,0},{8,12},{12,8},{1,5},{5,1},{9,13},{13,9},{2,6},{6,2},{1... | collective-permute-start | bytes 417800 | tf_op jit(solution)/shard_map/ppermute | solution.py:348
  12.1 8.2 %collective-permute-start.4 = (bf16[32,2048]{1,0:T(8,128)(2,1)S(1)}, bf16[32,2048]{1,0:T(8,128)(2,1)S(1)}, u32[]{:S(2)}, u32[]{:S(2)}) collective-permute-start(bf16[32,2048]{1,0:T(8,128)(2,1)S(1)} %collective-permute-done.2.q_ref), channel_id=1, source_target_pairs={{0,4},{4,0},{8,12},{12,8},{1,5},{5,1},{9,13},{13,9},{2,6},{6,2},{1... | collective-permute-start | bytes 393224 | tf_op jit(solution)/shard_map/ppermute | solution.py:348
  13.2 26.0 %slice-start.13 = ((s8[8388608]{0:T(1024)(128)(4,1)}), s8[4194304]{0:T(1024)(128)(4,1)S(1)}, s32[]{:S(2)}) async-start(s8[8388608]{0:T(1024)(128)(4,1)} %bitcast.11), calls=%async_computation.13 | async-start | bytes 8388608
  13.3 9.9 %collective-permute-start.3 = (bf16[32,2176]{1,0:T(8,128)(2,1)S(1)}, bf16[32,2176]{1,0:T(8,128)(2,1)S(1)}, u32[]{:S(2)}, u32[]{:S(2)}) collective-permute-start(bf16[32,2176]{1,0:T(8,128)(2,1)S(1)} %shard_map.102), channel_id=1, source_target_pairs={{0,8},{4,12},{8,0},{12,4},{1,9},{5,13},{9,1},{13,5},{2,10},{6,14},... | collective-permute-start | bytes 417800 | tf_op jit(solution)/shard_map/ppermute | solution.py:348
  21.1 7.0 %collective-permute-start.5 = (bf16[32,2176]{1,0:T(8,128)(2,1)S(1)}, bf16[32,2176]{1,0:T(8,128)(2,1)S(1)}, u32[]{:S(2)}, u32[]{:S(2)}) collective-permute-start(bf16[32,2176]{1,0:T(8,128)(2,1)S(1)} %shard_map.103), channel_id=1, source_target_pairs={{0,12},{4,8},{8,4},{12,0},{1,13},{5,9},{9,5},{13,1},{2,14},{6,10},... | collective-permute-start | bytes 417800 | tf_op jit(solution)/shard_map/ppermute | solution.py:348
  28.6 7.2 %collective-permute-start.6 = (bf16[32,2048]{1,0:T(8,128)(2,1)S(1)}, bf16[32,2048]{1,0:T(8,128)(2,1)S(1)}, u32[]{:S(2)}, u32[]{:S(2)}) collective-permute-start(bf16[32,2048]{1,0:T(8,128)(2,1)S(1)} %shard_map.104.refs_0_), channel_id=1, source_target_pairs={{0,4},{4,0},{8,12},{12,8},{1,5},{5,1},{9,13},{13,9},{2,6},{6,2},{1... | collective-permute-start | bytes 393224 | tf_op jit(solution)/shard_map/ppermute | solution.py:348
  28.7 10.6 %collective-permute-start.7 = (bf16[32,2048]{1,0:T(8,128)(2,1)S(1)}, bf16[32,2048]{1,0:T(8,128)(2,1)S(1)}, u32[]{:S(2)}, u32[]{:S(2)}) collective-permute-start(bf16[32,2048]{1,0:T(8,128)(2,1)S(1)} %shard_map.104.refs_0_), channel_id=1, source_target_pairs={{0,8},{4,12},{8,0},{12,4},{1,9},{5,13},{9,1},{13,5},{2,10},{6,14},... | collective-permute-start | bytes 393224 | tf_op jit(solution)/shard_map/ppermute | solution.py:348
  31.2 8.1 %collective-permute-start.8 = (bf16[32,2048]{1,0:T(8,128)(2,1)S(1)}, bf16[32,2048]{1,0:T(8,128)(2,1)S(1)}, u32[]{:S(2)}, u32[]{:S(2)}) collective-permute-start(bf16[32,2048]{1,0:T(8,128)(2,1)S(1)} %shard_map.104.refs_0_), channel_id=1, source_target_pairs={{0,12},{4,8},{8,4},{12,0},{1,13},{5,9},{9,5},{13,1},{2,14},{6,10},... | collective-permute-start | bytes 393224 | tf_op jit(solution)/shard_map/ppermute | solution.py:348
  40.6 7.3 %copy-start.1 = (bf16[32,2048]{1,0:T(8,128)(2,1)S(1)}, bf16[32,2048]{1,0:T(8,128)(2,1)}, u32[]{:S(2)}) copy-start(bf16[32,2048]{1,0:T(8,128)(2,1)} %stream_ref.1) | copy-start | bytes 393220
  40.6 1.6 %collective-permute-start.9 = (bf16[64,2048]{1,0:T(8,128)(2,1)S(1)}, bf16[64,2048]{1,0:T(8,128)(2,1)S(1)}, u32[]{:S(2)}, u32[]{:S(2)}) collective-permute-start(bf16[64,2048]{1,0:T(8,128)(2,1)S(1)} %get-tuple-element.41), channel_id=1, source_target_pairs={{0,1},{1,0},{2,3},{3,2},{4,5},{5,4},{6,7},{7,6},{8,9},{9,8},{10,11... | collective-permute-start | bytes 786440 | tf_op jit(solution)/shard_map/ppermute | solution.py:344
  42.2 20.5 %slice-start = ((s8[14680064]{0:T(1024)(128)(4,1)}), s8[4194304]{0:T(1024)(128)(4,1)S(1)}, s32[]{:S(2)}) async-start(s8[14680064]{0:T(1024)(128)(4,1)} %bitcast.1), calls=%async_computation | async-start | bytes 8388608
  42.2 20.5 %slice-start.1 = ((s8[14680064]{0:T(1024)(128)(4,1)}), s8[4194304]{0:T(1024)(128)(4,1)S(1)}, s32[]{:S(2)}) async-start(s8[14680064]{0:T(1024)(128)(4,1)} %bitcast.1), calls=%async_computation.1 | async-start | bytes 8388608
  42.2 20.5 %slice-start.4 = ((s8[14680064]{0:T(1024)(128)(4,1)}), s8[2097152]{0:T(1024)(128)(4,1)S(1)}, s32[]{:S(2)}) async-start(s8[14680064]{0:T(1024)(128)(4,1)} %bitcast.3), calls=%async_computation.4 | async-start | bytes 4194304
  42.2 20.5 %slice-start.5 = ((s8[14680064]{0:T(1024)(128)(4,1)}), s8[4194304]{0:T(1024)(128)(4,1)S(1)}, s32[]{:S(2)}) async-start(s8[14680064]{0:T(1024)(128)(4,1)} %bitcast.3), calls=%async_computation.5 | async-start | bytes 8388608
  42.3 13.0 %copy-start = (f32[8192]{0:T(1024)S(1)}, f32[8192]{0:T(1024)}, u32[]{:S(2)}) copy-start(f32[8192]{0:T(1024)} %param.16) | copy-start | bytes 98308
  42.3 5.6 %collective-permute-start.10 = (bf16[32,2048]{1,0:T(8,128)(2,1)S(1)}, bf16[32,2048]{1,0:T(8,128)(2,1)S(1)}, u32[]{:S(2)}, u32[]{:S(2)}) collective-permute-start(bf16[32,2048]{1,0:T(8,128)(2,1)S(1)} %get-tuple-element.43), channel_id=1, source_target_pairs={{0,2},{2,0},{1,3},{3,1},{4,6},{6,4},{5,7},{7,5},{8,10},{10,8},{9,1... | collective-permute-start | bytes 393224 | tf_op jit(solution)/shard_map/ppermute | solution.py:344
  47.9 14.9 %slice-start.2 = ((s8[14680064]{0:T(1024)(128)(4,1)}), s8[4194304]{0:T(1024)(128)(4,1)S(1)}, s32[]{:S(2)}) async-start(s8[14680064]{0:T(1024)(128)(4,1)} %bitcast.1), calls=%async_computation.2 | async-start | bytes 8388608
  47.9 14.9 %slice-start.3 = ((s8[14680064]{0:T(1024)(128)(4,1)}), s8[2097152]{0:T(1024)(128)(4,1)S(1)}, s32[]{:S(2)}) async-start(s8[14680064]{0:T(1024)(128)(4,1)} %bitcast.1), calls=%async_computation.3 | async-start | bytes 4194304
  47.9 14.9 %slice-start.6 = ((s8[14680064]{0:T(1024)(128)(4,1)}), s8[4194304]{0:T(1024)(128)(4,1)S(1)}, s32[]{:S(2)}) async-start(s8[14680064]{0:T(1024)(128)(4,1)} %bitcast.3), calls=%async_computation.6 | async-start | bytes 8388608
  47.9 14.9 %slice-start.7 = ((s8[14680064]{0:T(1024)(128)(4,1)}), s8[4194304]{0:T(1024)(128)(4,1)S(1)}, s32[]{:S(2)}) async-start(s8[14680064]{0:T(1024)(128)(4,1)} %bitcast.3), calls=%async_computation.7 | async-start | bytes 8388608
  48.0 7.3 %collective-permute-start.11 = (bf16[32,2048]{1,0:T(8,128)(2,1)S(1)}, bf16[32,2048]{1,0:T(8,128)(2,1)S(1)}, u32[]{:S(2)}, u32[]{:S(2)}) collective-permute-start(bf16[32,2048]{1,0:T(8,128)(2,1)S(1)} %shard_map.107), channel_id=1, source_target_pairs={{0,0},{1,4},{2,8},{3,12},{4,1},{5,5},{6,9},{7,13},{8,2},{9,6},{10,... | collective-permute-start | bytes 393224 | tf_op jit(solution)/shard_map/ppermute | solution.py:429
  48.8 6.7 %collective-permute-start.12 = (bf16[32,2048]{1,0:T(8,128)(2,1)S(1)}, bf16[32,2048]{1,0:T(8,128)(2,1)S(1)}, u32[]{:S(2)}, u32[]{:S(2)}) collective-permute-start(bf16[32,2048]{1,0:T(8,128)(2,1)S(1)} %shard_map.107), channel_id=1, source_target_pairs={{0,4},{1,0},{2,12},{3,8},{4,5},{5,1},{6,13},{7,9},{8,6},{9,2},{10,... | collective-permute-start | bytes 393224 | tf_op jit(solution)/shard_map/ppermute | solution.py:429
  52.4 9.9 %collective-permute-start.13 = (bf16[32,2048]{1,0:T(8,128)(2,1)S(1)}, bf16[32,2048]{1,0:T(8,128)(2,1)S(1)}, u32[]{:S(2)}, u32[]{:S(2)}) collective-permute-start(bf16[32,2048]{1,0:T(8,128)(2,1)S(1)} %shard_map.107), channel_id=1, source_target_pairs={{0,8},{1,12},{2,0},{3,4},{4,9},{5,13},{6,1},{7,5},{8,10},{9,14},{1... | collective-permute-start | bytes 393224 | tf_op jit(solution)/shard_map/ppermute | solution.py:429
  55.1 7.5 %collective-permute-start.14 = (bf16[32,2048]{1,0:T(8,128)(2,1)S(1)}, bf16[32,2048]{1,0:T(8,128)(2,1)S(1)}, u32[]{:S(2)}, u32[]{:S(2)}) collective-permute-start(bf16[32,2048]{1,0:T(8,128)(2,1)S(1)} %shard_map.107), channel_id=1, source_target_pairs={{0,12},{1,8},{2,4},{3,0},{4,13},{5,9},{6,5},{7,1},{8,14},{9,10},{1... | collective-permute-start | bytes 393224 | tf_op jit(solution)/shard_map/ppermute | solution.py:429
  65.2 2.7 %collective-permute-start.15 = (bf16[64,3840]{1,0:T(8,128)(2,1)S(1)}, bf16[64,3840]{1,0:T(8,128)(2,1)S(1)}, u32[]{:S(2)}, u32[]{:S(2)}) collective-permute-start(bf16[64,3840]{1,0:T(8,128)(2,1)S(1)} %get-tuple-element.53), channel_id=1, source_target_pairs={{0,1},{1,0},{2,3},{3,2},{4,5},{5,4},{6,7},{7,6},{8,9},{9,8},{10,11... | collective-permute-start | bytes 1474568 | tf_op jit(solution)/shard_map/ppermute | solution.py:344
  67.4 6.9 %collective-permute-start.17 = (bf16[64,3584]{1,0:T(8,128)(2,1)S(1)}, bf16[64,3584]{1,0:T(8,128)(2,1)S(1)}, u32[]{:S(2)}, u32[]{:S(2)}) collective-permute-start(bf16[64,3584]{1,0:T(8,128)(2,1)S(1)} %get-tuple-element.59), channel_id=1, source_target_pairs={{0,1},{1,0},{2,3},{3,2},{4,5},{5,4},{6,7},{7,6},{8,9},{9,8},{10,11... | collective-permute-start | bytes 1376264 | tf_op jit(solution)/shard_map/ppermute | solution.py:344
  68.0 13.0 %collective-permute-start.16 = (bf16[32,3840]{1,0:T(8,128)(2,1)S(1)}, bf16[32,3840]{1,0:T(8,128)(2,1)S(1)}, u32[]{:S(2)}, u32[]{:S(2)}) collective-permute-start(bf16[32,3840]{1,0:T(8,128)(2,1)S(1)} %get-tuple-element.55), channel_id=1, source_target_pairs={{0,2},{2,0},{1,3},{3,1},{4,6},{6,4},{5,7},{7,5},{8,10},{10,8},{9,1... | collective-permute-start | bytes 737288 | tf_op jit(solution)/shard_map/ppermute | solution.py:344
  74.2 16.7 %slice-start.8 = ((s8[14680064]{0:T(1024)(128)(4,1)}), s8[4194304]{0:T(1024)(128)(4,1)S(1)}, s32[]{:S(2)}) async-start(s8[14680064]{0:T(1024)(128)(4,1)} %bitcast.5), calls=%async_computation.8 | async-start | bytes 8388608
  74.3 16.7 %slice-start.9 = ((s8[14680064]{0:T(1024)(128)(4,1)}), s8[4194304]{0:T(1024)(128)(4,1)S(1)}, s32[]{:S(2)}) async-start(s8[14680064]{0:T(1024)(128)(4,1)} %bitcast.5), calls=%async_computation.9 | async-start | bytes 8388608
  74.3 11.6 %collective-permute-start.18 = (bf16[32,3584]{1,0:T(8,128)(2,1)S(1)}, bf16[32,3584]{1,0:T(8,128)(2,1)S(1)}, u32[]{:S(2)}, u32[]{:S(2)}) collective-permute-start(bf16[32,3584]{1,0:T(8,128)(2,1)S(1)} %get-tuple-element.61), channel_id=1, source_target_pairs={{0,2},{2,0},{1,3},{3,1},{4,6},{6,4},{5,7},{7,5},{8,10},{10,8},{9,1... | collective-permute-start | bytes 688136 | tf_op jit(solution)/shard_map/ppermute | solution.py:344
  81.1 9.9 %slice-start.10 = ((s8[14680064]{0:T(1024)(128)(4,1)}), s8[4194304]{0:T(1024)(128)(4,1)S(1)}, s32[]{:S(2)}) async-start(s8[14680064]{0:T(1024)(128)(4,1)} %bitcast.5), calls=%async_computation.10 | async-start | bytes 8388608
  81.2 7.0 %collective-permute-start.23 = (bf16[32,1792]{1,0:T(8,128)(2,1)S(1)}, bf16[32,1792]{1,0:T(8,128)(2,1)S(1)}, u32[]{:S(2)}, u32[]{:S(2)}) collective-permute-start(bf16[32,1792]{1,0:T(8,128)(2,1)S(1)} %get-tuple-element.62.refs_0_), channel_id=1, source_target_pairs={{0,2},{2,0},{1,3},{3,1},{4,6},{6,4},{5,7},{7,5},{8,10},{10,8},{9,1... | collective-permute-start | bytes 344072 | tf_op jit(solution)/shard_map/ppermute | solution.py:344
  86.0 5.0 %slice-start.11 = ((s8[14680064]{0:T(1024)(128)(4,1)}), s8[2097152]{0:T(1024)(128)(4,1)S(1)}, s32[]{:S(2)}) async-start(s8[14680064]{0:T(1024)(128)(4,1)} %bitcast.5), calls=%async_computation.11 | async-start | bytes 4194304
  86.1 4.9 %collective-permute-start.20 = (bf16[32,1792]{1,0:T(8,128)(2,1)S(1)}, bf16[32,1792]{1,0:T(8,128)(2,1)S(1)}, u32[]{:S(2)}, u32[]{:S(2)}) collective-permute-start(bf16[32,1792]{1,0:T(8,128)(2,1)S(1)} %shard_map.117.refs_0_), channel_id=1, source_target_pairs={{0,2},{2,0},{1,3},{3,1},{4,6},{6,4},{5,7},{7,5},{8,10},{10,8},{9,1... | collective-permute-start | bytes 344072 | tf_op jit(solution)/shard_map/ppermute | solution.py:344
  88.2 2.8 %collective-permute-start.22 = (bf16[32,1792]{1,0:T(8,128)(2,1)S(1)}, bf16[32,1792]{1,0:T(8,128)(2,1)S(1)}, u32[]{:S(2)}, u32[]{:S(2)}) collective-permute-start(bf16[32,1792]{1,0:T(8,128)(2,1)S(1)} %get-tuple-element.62.refs_0_), channel_id=1, source_target_pairs={{0,1},{1,0},{2,3},{3,2},{4,5},{5,4},{6,7},{7,6},{8,9},{9,8},{10,11... | collective-permute-start | bytes 344072 | tf_op jit(solution)/shard_map/ppermute | solution.py:344
  88.2 2.8 %collective-permute-start.24 = (bf16[32,1792]{1,0:T(8,128)(2,1)S(1)}, bf16[32,1792]{1,0:T(8,128)(2,1)S(1)}, u32[]{:S(2)}, u32[]{:S(2)}) collective-permute-start(bf16[32,1792]{1,0:T(8,128)(2,1)S(1)} %collective-permute-done.23.refs_2_), channel_id=1, source_target_pairs={{0,1},{1,0},{2,3},{3,2},{4,5},{5,4},{6,7},{7,6},{8,9},{9,8},{10,11... | collective-permute-start | bytes 344072 | tf_op jit(solution)/shard_map/ppermute | solution.py:344
  88.7 3.5 %collective-permute-start.19 = (bf16[32,1792]{1,0:T(8,128)(2,1)S(1)}, bf16[32,1792]{1,0:T(8,128)(2,1)S(1)}, u32[]{:S(2)}, u32[]{:S(2)}) collective-permute-start(bf16[32,1792]{1,0:T(8,128)(2,1)S(1)} %shard_map.117.refs_0_), channel_id=1, source_target_pairs={{0,1},{1,0},{2,3},{3,2},{4,5},{5,4},{6,7},{7,6},{8,9},{9,8},{10,11... | collective-permute-start | bytes 344072 | tf_op jit(solution)/shard_map/ppermute | solution.py:344
  91.0 1.3 %collective-permute-start.21 = (bf16[32,1792]{1,0:T(8,128)(2,1)S(1)}, bf16[32,1792]{1,0:T(8,128)(2,1)S(1)}, u32[]{:S(2)}, u32[]{:S(2)}) collective-permute-start(bf16[32,1792]{1,0:T(8,128)(2,1)S(1)} %collective-permute-done.20.refs_2_), channel_id=1, source_target_pairs={{0,1},{1,0},{2,3},{3,2},{4,5},{5,4},{6,7},{7,6},{8,9},{9,8},{10,11... | collective-permute-start | bytes 344072 | tf_op jit(solution)/shard_map/ppermute | solution.py:344
  93.4 8.3 %collective-permute-start.25 = (bf16[32,2048]{1,0:T(8,128)(2,1)S(1)}, bf16[32,2048]{1,0:T(8,128)(2,1)S(1)}, u32[]{:S(2)}, u32[]{:S(2)}) collective-permute-start(bf16[32,2048]{1,0:T(8,128)(2,1)S(1)} %get-tuple-element.64), channel_id=1, source_target_pairs={{0,12},{4,8},{8,4},{12,0},{1,13},{5,9},{9,5},{13,1},{2,14},{6,10},... | collective-permute-start | bytes 393224 | tf_op jit(solution)/shard_map/ppermute | solution.py:348
  97.1 11.7 %collective-permute-start.26 = (bf16[32,2048]{1,0:T(8,128)(2,1)S(1)}, bf16[32,2048]{1,0:T(8,128)(2,1)S(1)}, u32[]{:S(2)}, u32[]{:S(2)}) collective-permute-start(bf16[32,2048]{1,0:T(8,128)(2,1)S(1)} %get-tuple-element.65), channel_id=1, source_target_pairs={{0,8},{4,12},{8,0},{12,4},{1,9},{5,13},{9,1},{13,5},{2,10},{6,14},... | collective-permute-start | bytes 393224 | tf_op jit(solution)/shard_map/ppermute | solution.py:348
  97.1 11.7 %collective-permute-start.27 = (bf16[32,2048]{1,0:T(8,128)(2,1)S(1)}, bf16[32,2048]{1,0:T(8,128)(2,1)S(1)}, u32[]{:S(2)}, u32[]{:S(2)}) collective-permute-start(bf16[32,2048]{1,0:T(8,128)(2,1)S(1)} %get-tuple-element.66), channel_id=1, source_target_pairs={{0,4},{4,0},{8,12},{12,8},{1,5},{5,1},{9,13},{13,9},{2,6},{6,2},{1... | collective-permute-start | bytes 393224 | tf_op jit(solution)/shard_map/ppermute | solution.py:348
where the time goes:
time: 110 us
  waiting for transfers between devices  51.4 us (47%)
  starting transfers between devices  41.9 us (38%)
  Pallas kernels  15.3 us (14%)
    ppermute x12, waiting for transfers between devices, turn(): return lax.ppermute(x, axis, [(i, i ^ offset) for i in range(n)])  28.4 us
    ppermute x12, starting transfers between devices, turn(): return lax.ppermute(x, axis, [(i, i ^ offset) for i in range(n)])  20 us
    ppermute x12, waiting for transfers between devices, swap(): return lax.ppermute(x, axis, [(0, 1), (1, 0)])  16 us
    pallas_call x21, Pallas kernels, call(): pl.pallas_call(kernel, out_shape=out, in_specs=in_specs, out_specs=jax.tr...  15.3 us
    ppermute x12, starting transfers between devices, swap(): return lax.ppermute(x, axis, [(0, 1), (1, 0)])  14.6 us
    ppermute x4, starting transfers between devices, direct_body(): lax.ppermute(middle, ALL, [(a * n_context + b, (b ^ m) * n_context + a) f...  7.3 us
    ppermute x4, waiting for transfers between devices, direct_body(): lax.ppermute(middle, ALL, [(a * n_context + b, (b ^ m) * n_context + a) f...  6.94 us
  transfers between devices with their start and end apart: 28, of which 16 were waited for; matrix products, arithmetic and copies ran while one was open for 0% of the time, Pallas kernels for 8%

commit v1 on v0

--- a/solution.py
+++ b/solution.py
@@ -305,14 +305,19 @@
         rows_ref[at, :] = piece[...]
 
 
-def first_down_kernel(tile, *refs):
-    pieces, (weight_ref, out_ref, rows_ref) = refs[:4], refs[4:]
+def part_down_kernel(tile, start, *refs):
+    pieces, weight_ref, so_far = refs[:4], refs[4], refs[5:-2]
+    out_ref, rows_ref = refs[-2:]
     gather_rows(pieces, rows_ref)
     depth = rows_ref.shape[1]
     for at in range(0, weight_ref.shape[1], tile):
-        out_ref[:, at : at + tile] = jnp.dot(
-            rows_ref[...], weight_ref[:depth, at : at + tile], preferred_element_type=F32
-        )
+        columns = slice(at, at + tile)
+        part = jnp.dot(
+            rows_ref[...], weight_ref[start : start + depth, columns], preferred_element_type=F32
+        )
+        for ref in so_far:
+            part = part + ref[:, columns]
+        out_ref[:, columns] = part
 
 
 def down_kernel(tile, *refs):
@@ -438,8 +443,10 @@
         for m in (3, 0, 1, 2)
     }
     hidden_width = gate_weight.shape[1]
-    first = hidden_width // 2 // LANES * LANES
-    chunks = ((0, first), (first, hidden_width - first))
+    first = hidden_width * 2 // 7 // (2 * LANES) * 2 * LANES
+    second = (hidden_width - first) // 2 // LANES * LANES
+    widths = (first, second, hidden_width - first - second)
+    chunks = tuple((sum(widths[:c]), widths[c]) for c in range(len(widths)))
     hidden = []
     gate_vmem, up_vmem = in_vmem(gate_weight), in_vmem(up_weight)
     prepared = [
@@ -499,19 +506,23 @@
         hidden.append((own, beside, across, swap(across, "sec")))
     out_width = down_weight.shape[1]
     down_vmem = in_vmem(down_weight)
-    so_far = call(
-        functools.partial(first_down_kernel, 512),
-        struct((total, out_width), F32),
-        [VM] * 5,
-        hidden[0] + (down_vmem,),
-        scratch=[pltpu.VMEM((total, chunks[0][1]), BF16)],
-    )
+    so_far = ()
+    for c, (start, chunk) in enumerate(chunks[:-1]):
+        so_far = (
+            call(
+                functools.partial(part_down_kernel, 512, start),
+                struct((total, out_width), F32),
+                [VM] * (5 + len(so_far)),
+                hidden[c] + (down_vmem,) + so_far,
+                scratch=[pltpu.VMEM((total, chunk), BF16)],
+            ),
+        )
     res = call(
         functools.partial(down_kernel, 512),
         (struct((rows, out_width), F32),) + (struct((rows, out_width), BF16),) * 3,
         [VM] * 6,
-        hidden[1] + (down_vmem, so_far),
-        scratch=[pltpu.VMEM((total, chunks[1][1]), BF16)],
+        hidden[-1] + (down_vmem,) + so_far,
+        scratch=[pltpu.VMEM((total, chunks[-1][1]), BF16)],
     )
     parts = [turn(res[m], "ctx", n_context, m) for m in order]
     return call(

time: 110 us -> 110 us (level)
  waiting for transfers between devices: 51.4 us -> 47.7 us
  starting transfers between devices: 41.9 us -> 45.5 us
    ppermute x12 -> x17, starting transfers between devices: 14.6 us -> 18 us  [swap(): return lax.ppermute(x, axis, [(0, 1), (1, 0)])]
    ppermute x12 -> x17, waiting for transfers between devices: 16 us -> 12.6 us  [swap(): return lax.ppermute(x, axis, [(0, 1), (1, 0)])]
    pallas_call x21 -> x25, Pallas kernels: 15.3 us -> 15.7 us  [call(): pl.pallas_call(kernel, out_shape=out, in_specs=in_specs, out_specs=jax.tr...]
  transfers between devices with their start and end apart: 28 -> 33, of which waited for: 16 -> 18; matrix products, arithmetic and copies ran while one was open for 0% -> 0% of each run, Pallas kernels for 8% -> 10%
where the time goes in v1:
time: 110 us
  waiting for transfers between devices  47.7 us (43%)
  starting transfers between devices  45.5 us (41%)
  Pallas kernels  15.7 us (14%)
    ppermute x12, waiting for transfers between devices, turn(): return lax.ppermute(x, axis, [(i, i ^ offset) for i in range(n)])  28.1 us
    ppermute x12, starting transfers between devices, turn(): return lax.ppermute(x, axis, [(i, i ^ offset) for i in range(n)])  20.2 us
    ppermute x17, starting transfers between devices, swap(): return lax.ppermute(x, axis, [(0, 1), (1, 0)])  18 us
    pallas_call x25, Pallas kernels, call(): pl.pallas_call(kernel, out_shape=out, in_specs=in_specs, out_specs=jax.tr...  15.7 us
    ppermute x17, waiting for transfers between devices, swap(): return lax.ppermute(x, axis, [(0, 1), (1, 0)])  12.6 us
    ppermute x4, starting transfers between devices, direct_body(): lax.ppermute(middle, ALL, [(a * n_context + b, (b ^ m) * n_context + a) f...  7.3 us
    ppermute x4, waiting for transfers between devices, direct_body(): lax.ppermute(middle, ALL, [(a * n_context + b, (b ^ m) * n_context + a) f...  6.94 us
  transfers between devices with their start and end apart: 33, of which 18 were waited for; matrix products, arithmetic and copies ran while one was open for 0% of the time, Pallas kernels for 10%

profile of v1, /device:TPU:0, one launch (start us, length us, event | category | flops | bytes accessed | tf_op | source)
XLA Modules:
  0.0 110.0 jit_solution(6176026682719477355)
XLA Ops:
  0.0 3.1 %collective-permute-start = (bf16[32,2048]{1,0:T(8,128)(2,1)}, bf16[32,2048]{1,0:T(8,128)(2,1)S(1)}, u32[]{:S(2)}, u32[]{:S(2)}) collective-permute-start(bf16[32,2048]{1,0:T(8,128)(2,1)} %q_hbm.1), channel_id=1, source_target_pairs={{0,4},{4,0},{8,12},{12,8},{1,5},{5,1},{9,13},{13,9},{2,6},{6,2},{1... | collective-permute-start | bytes 393224 | tf_op jit(solution)/shard_map/ppermute | solution.py:353
  3.1 2.6 %collective-permute-start.2 = (bf16[32,2048]{1,0:T(8,128)(2,1)}, bf16[32,2048]{1,0:T(8,128)(2,1)S(1)}, u32[]{:S(2)}, u32[]{:S(2)}) collective-permute-start(bf16[32,2048]{1,0:T(8,128)(2,1)} %q_hbm.1), channel_id=1, source_target_pairs={{0,8},{4,12},{8,0},{12,4},{1,9},{5,13},{9,1},{13,5},{2,10},{6,14},... | collective-permute-start | bytes 393224 | tf_op jit(solution)/shard_map/ppermute | solution.py:353
  5.6 0.7 copy-done.2
  6.3 2.6 %shard_map.100 = (bf16[512,256]{1,0:T(8,128)(2,1)S(1)}, bf16[512,256]{1,0:T(8,128)(2,1)S(1)}, s32[8,128]{1,0:T(8,128)S(1)}, bf16[32,2176]{1,0:T(8,128)(2,1)S(1)}) custom-call(s32[1,8]{1,0:T(1,128)S(1)} %copy-done.2, bf16[32,2048]{1,0:T(8,128)(2,1)} %q_hbm.1, bf16[2048,256]{1,0:T(8,128)(2,1)} %key_hbm.1, bf16[2048,256]{1,0:T(8,128)(2,1)} %value_hbm.1), custom_call_target="tpu_custom_call" | custom-call | flops 3000000000 | bytes 2895904 | tf_op jit(solution)/shard_map/pallas_call | solution.py:37
  8.9 0.8 shard_map.101
  9.7 0.5 collective-permute-start.1
  10.3 1.8 %collective-permute-done.2.q_ref = bf16[32,2048]{1,0:T(8,128)(2,1)S(1)} collective-permute-done((bf16[32,2048]{1,0:T(8,128)(2,1)}, bf16[32,2048]{1,0:T(8,128)(2,1)S(1)}, u32[]{:S(2)}, u32[]{:S(2)}) %collective-permute-start.2) | collective-permute-done | bytes 131104 | tf_op jit(solution)/shard_map/ppermute | solution.py:353
  12.4 0.8 shard_map.102
  13.3 2.7 %collective-permute-start.3 = (bf16[32,2176]{1,0:T(8,128)(2,1)S(1)}, bf16[32,2176]{1,0:T(8,128)(2,1)S(1)}, u32[]{:S(2)}, u32[]{:S(2)}) collective-permute-start(bf16[32,2176]{1,0:T(8,128)(2,1)S(1)} %shard_map.102), channel_id=1, source_target_pairs={{0,8},{4,12},{8,0},{12,4},{1,9},{5,13},{9,1},{13,5},{2,10},{6,14},... | collective-permute-start | bytes 417800 | tf_op jit(solution)/shard_map/ppermute | solution.py:353
  15.9 4.4 %collective-permute-done.4.q_ref = bf16[32,2048]{1,0:T(8,128)(2,1)S(1)} collective-permute-done((bf16[32,2048]{1,0:T(8,128)(2,1)S(1)}, bf16[32,2048]{1,0:T(8,128)(2,1)S(1)}, u32[]{:S(2)}, u32[]{:S(2)}) %collective-permute-start.4) | collective-permute-done | bytes 131104 | tf_op jit(solution)/shard_map/ppermute | solution.py:353
  20.3 0.8 shard_map.103
  21.1 2.0 %collective-permute-start.5 = (bf16[32,2176]{1,0:T(8,128)(2,1)S(1)}, bf16[32,2176]{1,0:T(8,128)(2,1)S(1)}, u32[]{:S(2)}, u32[]{:S(2)}) collective-permute-start(bf16[32,2176]{1,0:T(8,128)(2,1)S(1)} %shard_map.103), channel_id=1, source_target_pairs={{0,12},{4,8},{8,4},{12,0},{1,13},{5,9},{9,5},{13,1},{2,14},{6,10},... | collective-permute-start | bytes 417800 | tf_op jit(solution)/shard_map/ppermute | solution.py:353
  23.1 5.0 %collective-permute-done.5.refs_3_ = bf16[32,2176]{1,0:T(8,128)(2,1)S(1)} collective-permute-done((bf16[32,2176]{1,0:T(8,128)(2,1)S(1)}, bf16[32,2176]{1,0:T(8,128)(2,1)S(1)}, u32[]{:S(2)}, u32[]{:S(2)}) %collective-permute-start.5) | collective-permute-done | bytes 139296 | tf_op jit(solution)/shard_map/ppermute | solution.py:353
  28.7 2.5 %collective-permute-start.7 = (bf16[32,2048]{1,0:T(8,128)(2,1)S(1)}, bf16[32,2048]{1,0:T(8,128)(2,1)S(1)}, u32[]{:S(2)}, u32[]{:S(2)}) collective-permute-start(bf16[32,2048]{1,0:T(8,128)(2,1)S(1)} %shard_map.104.refs_0_), channel_id=1, source_target_pairs={{0,8},{4,12},{8,0},{12,4},{1,9},{5,13},{9,1},{13,5},{2,10},{6,14},... | collective-permute-start | bytes 393224 | tf_op jit(solution)/shard_map/ppermute | solution.py:353
  31.2 1.9 %collective-permute-start.8 = (bf16[32,2048]{1,0:T(8,128)(2,1)S(1)}, bf16[32,2048]{1,0:T(8,128)(2,1)S(1)}, u32[]{:S(2)}, u32[]{:S(2)}) collective-permute-start(bf16[32,2048]{1,0:T(8,128)(2,1)S(1)} %shard_map.104.refs_0_), channel_id=1, source_target_pairs={{0,12},{4,8},{8,4},{12,0},{1,13},{5,9},{9,5},{13,1},{2,14},{6,10},... | collective-permute-start | bytes 393224 | tf_op jit(solution)/shard_map/ppermute | solution.py:353
  33.0 2.8 %collective-permute-done.6.refs_1_ = bf16[32,2048]{1,0:T(8,128)(2,1)S(1)} collective-permute-done((bf16[32,2048]{1,0:T(8,128)(2,1)S(1)}, bf16[32,2048]{1,0:T(8,128)(2,1)S(1)}, u32[]{:S(2)}, u32[]{:S(2)}) %collective-permute-start.6) | collective-permute-done | bytes 131104 | tf_op jit(solution)/shard_map/ppermute | solution.py:353
  35.8 3.4 %collective-permute-done.7.refs_2_ = bf16[32,2048]{1,0:T(8,128)(2,1)S(1)} collective-permute-done((bf16[32,2048]{1,0:T(8,128)(2,1)S(1)}, bf16[32,2048]{1,0:T(8,128)(2,1)S(1)}, u32[]{:S(2)}, u32[]{:S(2)}) %collective-permute-start.7) | collective-permute-done | bytes 131104 | tf_op jit(solution)/shard_map/ppermute | solution.py:353
  39.3 1.3 %shard_map.105 = (f32[64,2048]{1,0:T(8,128)S(1)}, bf16[64,2048]{1,0:T(8,128)(2,1)S(1)}) custom-call(bf16[32,2048]{1,0:T(8,128)(2,1)S(1)} %shard_map.104.refs_0_, bf16[32,2048]{1,0:T(8,128)(2,1)S(1)} %collective-permute-done.6.refs_1_, bf16[32,2048]{1,0:T(8,128)(2,1)S(1)} %collective-permute-done.7.refs_2_, ...), custom_call_target="tpu_custom_call" | custom-call | flops 6000000000 | bytes 9699328 | tf_op jit(solution)/shard_map/pallas_call | solution.py:37
  40.7 1.5 %collective-permute-done.9.got_ref = bf16[64,2048]{1,0:T(8,128)(2,1)S(1)} collective-permute-done((bf16[64,2048]{1,0:T(8,128)(2,1)S(1)}, bf16[64,2048]{1,0:T(8,128)(2,1)S(1)}, u32[]{:S(2)}, u32[]{:S(2)}) %collective-permute-start.9) | collective-permute-done | bytes 262176 | tf_op jit(solution)/shard_map/ppermute | solution.py:349
  42.3 1.6 %collective-permute-start.10 = (bf16[32,2048]{1,0:T(8,128)(2,1)S(1)}, bf16[32,2048]{1,0:T(8,128)(2,1)S(1)}, u32[]{:S(2)}, u32[]{:S(2)}) collective-permute-start(bf16[32,2048]{1,0:T(8,128)(2,1)S(1)} %get-tuple-element.47), channel_id=1, source_target_pairs={{0,2},{2,0},{1,3},{3,1},{4,6},{6,4},{5,7},{7,5},{8,10},{10,8},{9,1... | collective-permute-start | bytes 393224 | tf_op jit(solution)/shard_map/ppermute | solution.py:349
  43.9 4.0 %collective-permute-done.10.got_ref = bf16[32,2048]{1,0:T(8,128)(2,1)S(1)} collective-permute-done((bf16[32,2048]{1,0:T(8,128)(2,1)S(1)}, bf16[32,2048]{1,0:T(8,128)(2,1)S(1)}, u32[]{:S(2)}, u32[]{:S(2)}) %collective-permute-start.10) | collective-permute-done | bytes 131104 | tf_op jit(solution)/shard_map/ppermute | solution.py:349
  48.0 0.8 collective-permute-start.11
  48.8 3.6 %collective-permute-start.12 = (bf16[32,2048]{1,0:T(8,128)(2,1)S(1)}, bf16[32,2048]{1,0:T(8,128)(2,1)S(1)}, u32[]{:S(2)}, u32[]{:S(2)}) collective-permute-start(bf16[32,2048]{1,0:T(8,128)(2,1)S(1)} %shard_map.107), channel_id=1, source_target_pairs={{0,4},{1,0},{2,12},{3,8},{4,5},{5,1},{6,13},{7,9},{8,6},{9,2},{10,... | collective-permute-start | bytes 393224 | tf_op jit(solution)/shard_map/ppermute | solution.py:434
  52.4 2.6 %collective-permute-start.13 = (bf16[32,2048]{1,0:T(8,128)(2,1)S(1)}, bf16[32,2048]{1,0:T(8,128)(2,1)S(1)}, u32[]{:S(2)}, u32[]{:S(2)}) collective-permute-start(bf16[32,2048]{1,0:T(8,128)(2,1)S(1)} %shard_map.107), channel_id=1, source_target_pairs={{0,8},{1,12},{2,0},{3,4},{4,9},{5,13},{6,1},{7,5},{8,10},{9,14},{1... | collective-permute-start | bytes 393224 | tf_op jit(solution)/shard_map/ppermute | solution.py:434
  55.6 6.7 %collective-permute-done.13.piece_ref = bf16[32,2048]{1,0:T(8,128)(2,1)S(1)} collective-permute-done((bf16[32,2048]{1,0:T(8,128)(2,1)S(1)}, bf16[32,2048]{1,0:T(8,128)(2,1)S(1)}, u32[]{:S(2)}, u32[]{:S(2)}) %collective-permute-start.13) | collective-permute-done | bytes 131104 | tf_op jit(solution)/shard_map/ppermute | solution.py:434
  62.8 1.6 %shard_map.112 = (f32[64,2176]{1,0:T(8,128)S(1)}, bf16[64,2304]{1,0:T(8,128)(2,1)S(1)}, bf16[128,2048]{1,0:T(8,128)(2,1)S(1)}) custom-call(bf16[32,2048]{1,0:T(8,128)(2,1)S(1)} %get-tuple-element.48.refs_0_, bf16[32,2048]{1,0:T(8,128)(2,1)S(1)} %get-tuple-element.49.refs_1_, bf16[32,2048]{1,0:T(8,128)(2,1)S(1)} %get-tuple-element.50.refs_2_, ...), custom_call_target="tpu_custom_call" | custom-call | flops 3000000000 | bytes 31326208 | tf_op jit(solution)/shard_map/pallas_call | solution.py:37
  64.5 1.5 %shard_map.115 = (f32[64,2560]{1,0:T(8,128)S(1)}, bf16[64,2560]{1,0:T(8,128)(2,1)S(1)}) custom-call(bf16[128,2048]{1,0:T(8,128)(2,1)S(1)} %get-tuple-element.61.rows_ref, bf16[2048,3584]{1,0:T(8,128)(2,1)S(1)} %bitcast.2, bf16[2048,3584]{1,0:T(8,128)(2,1)S(1)} %bitcast.4), custom_call_target="tpu_custom_call" | custom-call | flops 3000000000 | bytes 30867456 | tf_op jit(solution)/shard_map/pallas_call | solution.py:37
  66.0 0.6 collective-permute-start.17
  66.6 1.5 %shard_map.118 = (f32[64,2560]{1,0:T(8,128)S(1)}, bf16[64,2560]{1,0:T(8,128)(2,1)S(1)}) custom-call(bf16[128,2048]{1,0:T(8,128)(2,1)S(1)} %get-tuple-element.61.rows_ref, bf16[2048,3584]{1,0:T(8,128)(2,1)S(1)} %bitcast.2, bf16[2048,3584]{1,0:T(8,128)(2,1)S(1)} %bitcast.4), custom_call_target="tpu_custom_call" | custom-call | flops 3000000000 | bytes 30867456 | tf_op jit(solution)/shard_map/pallas_call | solution.py:37
  68.3 6.2 %collective-permute-start.16 = (bf16[32,2304]{1,0:T(8,128)(2,1)S(1)}, bf16[32,2304]{1,0:T(8,128)(2,1)S(1)}, u32[]{:S(2)}, u32[]{:S(2)}) collective-permute-start(bf16[32,2304]{1,0:T(8,128)(2,1)S(1)} %get-tuple-element.59), channel_id=1, source_target_pairs={{0,2},{2,0},{1,3},{3,1},{4,6},{6,4},{5,7},{7,5},{8,10},{10,8},{9,1... | collective-permute-start | bytes 442376 | tf_op jit(solution)/shard_map/ppermute | solution.py:349
  74.7 2.1 %collective-permute-start.23 = (bf16[32,2560]{1,0:T(8,128)(2,1)S(1)}, bf16[32,2560]{1,0:T(8,128)(2,1)S(1)}, u32[]{:S(2)}, u32[]{:S(2)}) collective-permute-start(bf16[32,2560]{1,0:T(8,128)(2,1)S(1)} %get-tuple-element.69), channel_id=1, source_target_pairs={{0,2},{2,0},{1,3},{3,1},{4,6},{6,4},{5,7},{7,5},{8,10},{10,8},{9,1... | collective-permute-start | bytes 491528 | tf_op jit(solution)/shard_map/ppermute | solution.py:349
  76.8 2.4 %collective-permute-done.16.got_ref = bf16[32,2304]{1,0:T(8,128)(2,1)S(1)} collective-permute-done((bf16[32,2304]{1,0:T(8,128)(2,1)S(1)}, bf16[32,2304]{1,0:T(8,128)(2,1)S(1)}, u32[]{:S(2)}, u32[]{:S(2)}) %collective-permute-start.16) | collective-permute-done | bytes 147488 | tf_op jit(solution)/shard_map/ppermute | solution.py:349
  79.3 2.1 %collective-permute-start.28 = (bf16[32,1024]{1,0:T(8,128)(2,1)S(1)}, bf16[32,1024]{1,0:T(8,128)(2,1)S(1)}, u32[]{:S(2)}, u32[]{:S(2)}) collective-permute-start(bf16[32,1024]{1,0:T(8,128)(2,1)S(1)} %get-tuple-element.70.refs_0_), channel_id=1, source_target_pairs={{0,2},{2,0},{1,3},{3,1},{4,6},{6,4},{5,7},{7,5},{8,10},{10,8},{9,1... | collective-permute-start | bytes 196616 | tf_op jit(solution)/shard_map/ppermute | solution.py:349
  81.4 1.3 %collective-permute-done.18.got_ref = bf16[32,2560]{1,0:T(8,128)(2,1)S(1)} collective-permute-done((bf16[32,2560]{1,0:T(8,128)(2,1)S(1)}, bf16[32,2560]{1,0:T(8,128)(2,1)S(1)}, u32[]{:S(2)}, u32[]{:S(2)}) %collective-permute-start.18) | collective-permute-done | bytes 163872 | tf_op jit(solution)/shard_map/ppermute | solution.py:349
  82.8 2.1 %collective-permute-start.20 = (bf16[32,1280]{1,0:T(8,128)(2,1)S(1)}, bf16[32,1280]{1,0:T(8,128)(2,1)S(1)}, u32[]{:S(2)}, u32[]{:S(2)}) collective-permute-start(bf16[32,1280]{1,0:T(8,128)(2,1)S(1)} %shard_map.117.refs_0_), channel_id=1, source_target_pairs={{0,2},{2,0},{1,3},{3,1},{4,6},{6,4},{5,7},{7,5},{8,10},{10,8},{9,1... | collective-permute-start | bytes 245768 | tf_op jit(solution)/shard_map/ppermute | solution.py:349
  84.9 1.3 %collective-permute-done.23.got_ref = bf16[32,2560]{1,0:T(8,128)(2,1)S(1)} collective-permute-done((bf16[32,2560]{1,0:T(8,128)(2,1)S(1)}, bf16[32,2560]{1,0:T(8,128)(2,1)S(1)}, u32[]{:S(2)}, u32[]{:S(2)}) %collective-permute-start.23) | collective-permute-done | bytes 163872 | tf_op jit(solution)/shard_map/ppermute | solution.py:349
  86.3 2.1 %collective-permute-start.25 = (bf16[32,1280]{1,0:T(8,128)(2,1)S(1)}, bf16[32,1280]{1,0:T(8,128)(2,1)S(1)}, u32[]{:S(2)}, u32[]{:S(2)}) collective-permute-start(bf16[32,1280]{1,0:T(8,128)(2,1)S(1)} %shard_map.120.refs_0_), channel_id=1, source_target_pairs={{0,2},{2,0},{1,3},{3,1},{4,6},{6,4},{5,7},{7,5},{8,10},{10,8},{9,1... | collective-permute-start | bytes 245768 | tf_op jit(solution)/shard_map/ppermute | solution.py:349
  88.4 0.5 collective-permute-start.29
  88.9 0.7 collective-permute-done.27.refs_1_
  90.2 0.8 collective-permute-done.25.refs_2_
  91.0 0.7 shard_map.121.refs_5_
  92.2 0.9 shard_map.122.refs_5_
  93.1 0.9 shard_map.123
  94.0 4.0 %collective-permute-start.30 = (bf16[32,2048]{1,0:T(8,128)(2,1)S(1)}, bf16[32,2048]{1,0:T(8,128)(2,1)S(1)}, u32[]{:S(2)}, u32[]{:S(2)}) collective-permute-start(bf16[32,2048]{1,0:T(8,128)(2,1)S(1)} %get-tuple-element.72), channel_id=1, source_target_pairs={{0,12},{4,8},{8,4},{12,0},{1,13},{5,9},{9,5},{13,1},{2,14},{6,10},... | collective-permute-start | bytes 393224 | tf_op jit(solution)/shard_map/ppermute | solution.py:353
  98.0 0.6 collective-permute-start.32
  98.6 3.8 %collective-permute-done.30.refs_0_ = bf16[32,2048]{1,0:T(8,128)(2,1)S(1)} collective-permute-done((bf16[32,2048]{1,0:T(8,128)(2,1)S(1)}, bf16[32,2048]{1,0:T(8,128)(2,1)S(1)}, u32[]{:S(2)}, u32[]{:S(2)}) %collective-permute-start.30) | collective-permute-done | bytes 131104 | tf_op jit(solution)/shard_map/ppermute | solution.py:353
  102.4 6.8 %collective-permute-done.31.refs_1_ = bf16[32,2048]{1,0:T(8,128)(2,1)S(1)} collective-permute-done((bf16[32,2048]{1,0:T(8,128)(2,1)S(1)}, bf16[32,2048]{1,0:T(8,128)(2,1)S(1)}, u32[]{:S(2)}, u32[]{:S(2)}) %collective-permute-start.31) | collective-permute-done | bytes 131104 | tf_op jit(solution)/shard_map/ppermute | solution.py:353
  109.3 0.7 shard_map.124
  (81 shorter events, 3.8 us)
Async XLA Ops:
  0.0 8.9 %collective-permute-start = (bf16[32,2048]{1,0:T(8,128)(2,1)}, bf16[32,2048]{1,0:T(8,128)(2,1)S(1)}, u32[]{:S(2)}, u32[]{:S(2)}) collective-permute-start(bf16[32,2048]{1,0:T(8,128)(2,1)} %q_hbm.1), channel_id=1, source_target_pairs={{0,4},{4,0},{8,12},{12,8},{1,5},{5,1},{9,13},{13,9},{2,6},{6,2},{1... | collective-permute-start | bytes 393224 | tf_op jit(solution)/shard_map/ppermute | solution.py:353
  3.1 9.0 %collective-permute-start.2 = (bf16[32,2048]{1,0:T(8,128)(2,1)}, bf16[32,2048]{1,0:T(8,128)(2,1)S(1)}, u32[]{:S(2)}, u32[]{:S(2)}) collective-permute-start(bf16[32,2048]{1,0:T(8,128)(2,1)} %q_hbm.1), channel_id=1, source_target_pairs={{0,8},{4,12},{8,0},{12,4},{1,9},{5,13},{9,1},{13,5},{2,10},{6,14},... | collective-permute-start | bytes 393224 | tf_op jit(solution)/shard_map/ppermute | solution.py:353
  9.7 29.6 %slice-start.12 = ((s8[8388608]{0:T(1024)(128)(4,1)}), s8[4194304]{0:T(1024)(128)(4,1)S(1)}, s32[]{:S(2)}) async-start(s8[8388608]{0:T(1024)(128)(4,1)} %bitcast.11), calls=%async_computation.12 | async-start | bytes 8388608
  9.7 13.4 %collective-permute-start.1 = (bf16[32,2176]{1,0:T(8,128)(2,1)S(1)}, bf16[32,2176]{1,0:T(8,128)(2,1)S(1)}, u32[]{:S(2)}, u32[]{:S(2)}) collective-permute-start(bf16[32,2176]{1,0:T(8,128)(2,1)S(1)} %shard_map.101), channel_id=1, source_target_pairs={{0,4},{4,0},{8,12},{12,8},{1,5},{5,1},{9,13},{13,9},{2,6},{6,2},{1... | collective-permute-start | bytes 417800 | tf_op jit(solution)/shard_map/ppermute | solution.py:353
  12.1 8.2 %collective-permute-start.4 = (bf16[32,2048]{1,0:T(8,128)(2,1)S(1)}, bf16[32,2048]{1,0:T(8,128)(2,1)S(1)}, u32[]{:S(2)}, u32[]{:S(2)}) collective-permute-start(bf16[32,2048]{1,0:T(8,128)(2,1)S(1)} %collective-permute-done.2.q_ref), channel_id=1, source_target_pairs={{0,4},{4,0},{8,12},{12,8},{1,5},{5,1},{9,13},{13,9},{2,6},{6,2},{1... | collective-permute-start | bytes 393224 | tf_op jit(solution)/shard_map/ppermute | solution.py:353
  13.2 26.0 %slice-start.13 = ((s8[8388608]{0:T(1024)(128)(4,1)}), s8[4194304]{0:T(1024)(128)(4,1)S(1)}, s32[]{:S(2)}) async-start(s8[8388608]{0:T(1024)(128)(4,1)} %bitcast.11), calls=%async_computation.13 | async-start | bytes 8388608
  13.3 9.9 %collective-permute-start.3 = (bf16[32,2176]{1,0:T(8,128)(2,1)S(1)}, bf16[32,2176]{1,0:T(8,128)(2,1)S(1)}, u32[]{:S(2)}, u32[]{:S(2)}) collective-permute-start(bf16[32,2176]{1,0:T(8,128)(2,1)S(1)} %shard_map.102), channel_id=1, source_target_pairs={{0,8},{4,12},{8,0},{12,4},{1,9},{5,13},{9,1},{13,5},{2,10},{6,14},... | collective-permute-start | bytes 417800 | tf_op jit(solution)/shard_map/ppermute | solution.py:353
  21.1 7.0 %collective-permute-start.5 = (bf16[32,2176]{1,0:T(8,128)(2,1)S(1)}, bf16[32,2176]{1,0:T(8,128)(2,1)S(1)}, u32[]{:S(2)}, u32[]{:S(2)}) collective-permute-start(bf16[32,2176]{1,0:T(8,128)(2,1)S(1)} %shard_map.103), channel_id=1, source_target_pairs={{0,12},{4,8},{8,4},{12,0},{1,13},{5,9},{9,5},{13,1},{2,14},{6,10},... | collective-permute-start | bytes 417800 | tf_op jit(solution)/shard_map/ppermute | solution.py:353
  28.6 7.2 %collective-permute-start.6 = (bf16[32,2048]{1,0:T(8,128)(2,1)S(1)}, bf16[32,2048]{1,0:T(8,128)(2,1)S(1)}, u32[]{:S(2)}, u32[]{:S(2)}) collective-permute-start(bf16[32,2048]{1,0:T(8,128)(2,1)S(1)} %shard_map.104.refs_0_), channel_id=1, source_target_pairs={{0,4},{4,0},{8,12},{12,8},{1,5},{5,1},{9,13},{13,9},{2,6},{6,2},{1... | collective-permute-start | bytes 393224 | tf_op jit(solution)/shard_map/ppermute | solution.py:353
  28.7 10.6 %collective-permute-start.7 = (bf16[32,2048]{1,0:T(8,128)(2,1)S(1)}, bf16[32,2048]{1,0:T(8,128)(2,1)S(1)}, u32[]{:S(2)}, u32[]{:S(2)}) collective-permute-start(bf16[32,2048]{1,0:T(8,128)(2,1)S(1)} %shard_map.104.refs_0_), channel_id=1, source_target_pairs={{0,8},{4,12},{8,0},{12,4},{1,9},{5,13},{9,1},{13,5},{2,10},{6,14},... | collective-permute-start | bytes 393224 | tf_op jit(solution)/shard_map/ppermute | solution.py:353
  31.2 8.1 %collective-permute-start.8 = (bf16[32,2048]{1,0:T(8,128)(2,1)S(1)}, bf16[32,2048]{1,0:T(8,128)(2,1)S(1)}, u32[]{:S(2)}, u32[]{:S(2)}) collective-permute-start(bf16[32,2048]{1,0:T(8,128)(2,1)S(1)} %shard_map.104.refs_0_), channel_id=1, source_target_pairs={{0,12},{4,8},{8,4},{12,0},{1,13},{5,9},{9,5},{13,1},{2,14},{6,10},... | collective-permute-start | bytes 393224 | tf_op jit(solution)/shard_map/ppermute | solution.py:353
  40.6 7.3 %copy-start.1 = (bf16[32,2048]{1,0:T(8,128)(2,1)S(1)}, bf16[32,2048]{1,0:T(8,128)(2,1)}, u32[]{:S(2)}) copy-start(bf16[32,2048]{1,0:T(8,128)(2,1)} %stream_ref.1) | copy-start | bytes 393220
  40.6 1.6 %collective-permute-start.9 = (bf16[64,2048]{1,0:T(8,128)(2,1)S(1)}, bf16[64,2048]{1,0:T(8,128)(2,1)S(1)}, u32[]{:S(2)}, u32[]{:S(2)}) collective-permute-start(bf16[64,2048]{1,0:T(8,128)(2,1)S(1)} %get-tuple-element.45), channel_id=1, source_target_pairs={{0,1},{1,0},{2,3},{3,2},{4,5},{5,4},{6,7},{7,6},{8,9},{9,8},{10,11... | collective-permute-start | bytes 786440 | tf_op jit(solution)/shard_map/ppermute | solution.py:349
  42.2 20.5 %slice-start = ((s8[14680064]{0:T(1024)(128)(4,1)}), s8[4194304]{0:T(1024)(128)(4,1)S(1)}, s32[]{:S(2)}) async-start(s8[14680064]{0:T(1024)(128)(4,1)} %bitcast.1), calls=%async_computation | async-start | bytes 8388608
  42.2 20.5 %slice-start.1 = ((s8[14680064]{0:T(1024)(128)(4,1)}), s8[4194304]{0:T(1024)(128)(4,1)S(1)}, s32[]{:S(2)}) async-start(s8[14680064]{0:T(1024)(128)(4,1)} %bitcast.1), calls=%async_computation.1 | async-start | bytes 8388608
  42.2 20.5 %slice-start.4 = ((s8[14680064]{0:T(1024)(128)(4,1)}), s8[2097152]{0:T(1024)(128)(4,1)S(1)}, s32[]{:S(2)}) async-start(s8[14680064]{0:T(1024)(128)(4,1)} %bitcast.3), calls=%async_computation.4 | async-start | bytes 4194304
  42.2 20.5 %slice-start.5 = ((s8[14680064]{0:T(1024)(128)(4,1)}), s8[4194304]{0:T(1024)(128)(4,1)S(1)}, s32[]{:S(2)}) async-start(s8[14680064]{0:T(1024)(128)(4,1)} %bitcast.3), calls=%async_computation.5 | async-start | bytes 8388608
  42.3 13.0 %copy-start = (f32[8192]{0:T(1024)S(1)}, f32[8192]{0:T(1024)}, u32[]{:S(2)}) copy-start(f32[8192]{0:T(1024)} %param.16) | copy-start | bytes 98308
  42.3 5.6 %collective-permute-start.10 = (bf16[32,2048]{1,0:T(8,128)(2,1)S(1)}, bf16[32,2048]{1,0:T(8,128)(2,1)S(1)}, u32[]{:S(2)}, u32[]{:S(2)}) collective-permute-start(bf16[32,2048]{1,0:T(8,128)(2,1)S(1)} %get-tuple-element.47), channel_id=1, source_target_pairs={{0,2},{2,0},{1,3},{3,1},{4,6},{6,4},{5,7},{7,5},{8,10},{10,8},{9,1... | collective-permute-start | bytes 393224 | tf_op jit(solution)/shard_map/ppermute | solution.py:349
  47.9 14.9 %slice-start.2 = ((s8[14680064]{0:T(1024)(128)(4,1)}), s8[4194304]{0:T(1024)(128)(4,1)S(1)}, s32[]{:S(2)}) async-start(s8[14680064]{0:T(1024)(128)(4,1)} %bitcast.1), calls=%async_computation.2 | async-start | bytes 8388608
  47.9 14.9 %slice-start.3 = ((s8[14680064]{0:T(1024)(128)(4,1)}), s8[2097152]{0:T(1024)(128)(4,1)S(1)}, s32[]{:S(2)}) async-start(s8[14680064]{0:T(1024)(128)(4,1)} %bitcast.1), calls=%async_computation.3 | async-start | bytes 4194304
  47.9 14.9 %slice-start.6 = ((s8[14680064]{0:T(1024)(128)(4,1)}), s8[4194304]{0:T(1024)(128)(4,1)S(1)}, s32[]{:S(2)}) async-start(s8[14680064]{0:T(1024)(128)(4,1)} %bitcast.3), calls=%async_computation.6 | async-start | bytes 8388608
  47.9 14.9 %slice-start.7 = ((s8[14680064]{0:T(1024)(128)(4,1)}), s8[4194304]{0:T(1024)(128)(4,1)S(1)}, s32[]{:S(2)}) async-start(s8[14680064]{0:T(1024)(128)(4,1)} %bitcast.3), calls=%async_computation.7 | async-start | bytes 8388608
  48.0 7.3 %collective-permute-start.11 = (bf16[32,2048]{1,0:T(8,128)(2,1)S(1)}, bf16[32,2048]{1,0:T(8,128)(2,1)S(1)}, u32[]{:S(2)}, u32[]{:S(2)}) collective-permute-start(bf16[32,2048]{1,0:T(8,128)(2,1)S(1)} %shard_map.107), channel_id=1, source_target_pairs={{0,0},{1,4},{2,8},{3,12},{4,1},{5,5},{6,9},{7,13},{8,2},{9,6},{10,... | collective-permute-start | bytes 393224 | tf_op jit(solution)/shard_map/ppermute | solution.py:434
  48.8 6.7 %collective-permute-start.12 = (bf16[32,2048]{1,0:T(8,128)(2,1)S(1)}, bf16[32,2048]{1,0:T(8,128)(2,1)S(1)}, u32[]{:S(2)}, u32[]{:S(2)}) collective-permute-start(bf16[32,2048]{1,0:T(8,128)(2,1)S(1)} %shard_map.107), channel_id=1, source_target_pairs={{0,4},{1,0},{2,12},{3,8},{4,5},{5,1},{6,13},{7,9},{8,6},{9,2},{10,... | collective-permute-start | bytes 393224 | tf_op jit(solution)/shard_map/ppermute | solution.py:434
  52.4 9.9 %collective-permute-start.13 = (bf16[32,2048]{1,0:T(8,128)(2,1)S(1)}, bf16[32,2048]{1,0:T(8,128)(2,1)S(1)}, u32[]{:S(2)}, u32[]{:S(2)}) collective-permute-start(bf16[32,2048]{1,0:T(8,128)(2,1)S(1)} %shard_map.107), channel_id=1, source_target_pairs={{0,8},{1,12},{2,0},{3,4},{4,9},{5,13},{6,1},{7,5},{8,10},{9,14},{1... | collective-permute-start | bytes 393224 | tf_op jit(solution)/shard_map/ppermute | solution.py:434
  55.1 7.5 %collective-permute-start.14 = (bf16[32,2048]{1,0:T(8,128)(2,1)S(1)}, bf16[32,2048]{1,0:T(8,128)(2,1)S(1)}, u32[]{:S(2)}, u32[]{:S(2)}) collective-permute-start(bf16[32,2048]{1,0:T(8,128)(2,1)S(1)} %shard_map.107), channel_id=1, source_target_pairs={{0,12},{1,8},{2,4},{3,0},{4,13},{5,9},{6,5},{7,1},{8,14},{9,10},{1... | collective-permute-start | bytes 393224 | tf_op jit(solution)/shard_map/ppermute | solution.py:434
  64.4 3.8 %collective-permute-start.15 = (bf16[64,2304]{1,0:T(8,128)(2,1)S(1)}, bf16[64,2304]{1,0:T(8,128)(2,1)S(1)}, u32[]{:S(2)}, u32[]{:S(2)}) collective-permute-start(bf16[64,2304]{1,0:T(8,128)(2,1)S(1)} %get-tuple-element.57), channel_id=1, source_target_pairs={{0,1},{1,0},{2,3},{3,2},{4,5},{5,4},{6,7},{7,6},{8,9},{9,8},{10,11... | collective-permute-start | bytes 884744 | tf_op jit(solution)/shard_map/ppermute | solution.py:349
  66.0 8.5 %collective-permute-start.17 = (bf16[64,2560]{1,0:T(8,128)(2,1)S(1)}, bf16[64,2560]{1,0:T(8,128)(2,1)S(1)}, u32[]{:S(2)}, u32[]{:S(2)}) collective-permute-start(bf16[64,2560]{1,0:T(8,128)(2,1)S(1)} %get-tuple-element.63), channel_id=1, source_target_pairs={{0,1},{1,0},{2,3},{3,2},{4,5},{5,4},{6,7},{7,6},{8,9},{9,8},{10,11... | collective-permute-start | bytes 983048 | tf_op jit(solution)/shard_map/ppermute | solution.py:349
  68.1 6.6 %collective-permute-start.22 = (bf16[64,2560]{1,0:T(8,128)(2,1)S(1)}, bf16[64,2560]{1,0:T(8,128)(2,1)S(1)}, u32[]{:S(2)}, u32[]{:S(2)}) collective-permute-start(bf16[64,2560]{1,0:T(8,128)(2,1)S(1)} %get-tuple-element.67), channel_id=1, source_target_pairs={{0,1},{1,0},{2,3},{3,2},{4,5},{5,4},{6,7},{7,6},{8,9},{9,8},{10,11... | collective-permute-start | bytes 983048 | tf_op jit(solution)/shard_map/ppermute | solution.py:349
  68.3 10.9 %collective-permute-start.16 = (bf16[32,2304]{1,0:T(8,128)(2,1)S(1)}, bf16[32,2304]{1,0:T(8,128)(2,1)S(1)}, u32[]{:S(2)}, u32[]{:S(2)}) collective-permute-start(bf16[32,2304]{1,0:T(8,128)(2,1)S(1)} %get-tuple-element.59), channel_id=1, source_target_pairs={{0,2},{2,0},{1,3},{3,1},{4,6},{6,4},{5,7},{7,5},{8,10},{10,8},{9,1... | collective-permute-start | bytes 442376 | tf_op jit(solution)/shard_map/ppermute | solution.py:349
  74.6 8.1 %collective-permute-start.18 = (bf16[32,2560]{1,0:T(8,128)(2,1)S(1)}, bf16[32,2560]{1,0:T(8,128)(2,1)S(1)}, u32[]{:S(2)}, u32[]{:S(2)}) collective-permute-start(bf16[32,2560]{1,0:T(8,128)(2,1)S(1)} %get-tuple-element.65), channel_id=1, source_target_pairs={{0,2},{2,0},{1,3},{3,1},{4,6},{6,4},{5,7},{7,5},{8,10},{10,8},{9,1... | collective-permute-start | bytes 491528 | tf_op jit(solution)/shard_map/ppermute | solution.py:349
  74.7 11.5 %collective-permute-start.23 = (bf16[32,2560]{1,0:T(8,128)(2,1)S(1)}, bf16[32,2560]{1,0:T(8,128)(2,1)S(1)}, u32[]{:S(2)}, u32[]{:S(2)}) collective-permute-start(bf16[32,2560]{1,0:T(8,128)(2,1)S(1)} %get-tuple-element.69), channel_id=1, source_target_pairs={{0,2},{2,0},{1,3},{3,1},{4,6},{6,4},{5,7},{7,5},{8,10},{10,8},{9,1... | collective-permute-start | bytes 491528 | tf_op jit(solution)/shard_map/ppermute | solution.py:349
  79.2 11.7 %slice-start.8 = ((s8[14680064]{0:T(1024)(128)(4,1)}), s8[4194304]{0:T(1024)(128)(4,1)S(1)}, s32[]{:S(2)}) async-start(s8[14680064]{0:T(1024)(128)(4,1)} %bitcast.5), calls=%async_computation.8 | async-start | bytes 8388608
  79.2 11.7 %slice-start.9 = ((s8[14680064]{0:T(1024)(128)(4,1)}), s8[4194304]{0:T(1024)(128)(4,1)S(1)}, s32[]{:S(2)}) async-start(s8[14680064]{0:T(1024)(128)(4,1)} %bitcast.5), calls=%async_computation.9 | async-start | bytes 8388608
  79.3 9.1 %collective-permute-start.28 = (bf16[32,1024]{1,0:T(8,128)(2,1)S(1)}, bf16[32,1024]{1,0:T(8,128)(2,1)S(1)}, u32[]{:S(2)}, u32[]{:S(2)}) collective-permute-start(bf16[32,1024]{1,0:T(8,128)(2,1)S(1)} %get-tuple-element.70.refs_0_), channel_id=1, source_target_pairs={{0,2},{2,0},{1,3},{3,1},{4,6},{6,4},{5,7},{7,5},{8,10},{10,8},{9,1... | collective-permute-start | bytes 196616 | tf_op jit(solution)/shard_map/ppermute | solution.py:349
  82.7 8.2 %slice-start.10 = ((s8[14680064]{0:T(1024)(128)(4,1)}), s8[4194304]{0:T(1024)(128)(4,1)S(1)}, s32[]{:S(2)}) async-start(s8[14680064]{0:T(1024)(128)(4,1)} %bitcast.5), calls=%async_computation.10 | async-start | bytes 8388608
  82.8 7.0 %collective-permute-start.20 = (bf16[32,1280]{1,0:T(8,128)(2,1)S(1)}, bf16[32,1280]{1,0:T(8,128)(2,1)S(1)}, u32[]{:S(2)}, u32[]{:S(2)}) collective-permute-start(bf16[32,1280]{1,0:T(8,128)(2,1)S(1)} %shard_map.117.refs_0_), channel_id=1, source_target_pairs={{0,2},{2,0},{1,3},{3,1},{4,6},{6,4},{5,7},{7,5},{8,10},{10,8},{9,1... | collective-permute-start | bytes 245768 | tf_op jit(solution)/shard_map/ppermute | solution.py:349
  86.3 4.6 %collective-permute-start.25 = (bf16[32,1280]{1,0:T(8,128)(2,1)S(1)}, bf16[32,1280]{1,0:T(8,128)(2,1)S(1)}, u32[]{:S(2)}, u32[]{:S(2)}) collective-permute-start(bf16[32,1280]{1,0:T(8,128)(2,1)S(1)} %shard_map.120.refs_0_), channel_id=1, source_target_pairs={{0,2},{2,0},{1,3},{3,1},{4,6},{6,4},{5,7},{7,5},{8,10},{10,8},{9,1... | collective-permute-start | bytes 245768 | tf_op jit(solution)/shard_map/ppermute | solution.py:349
  88.4 1.3 %collective-permute-start.27 = (bf16[32,1024]{1,0:T(8,128)(2,1)S(1)}, bf16[32,1024]{1,0:T(8,128)(2,1)S(1)}, u32[]{:S(2)}, u32[]{:S(2)}) collective-permute-start(bf16[32,1024]{1,0:T(8,128)(2,1)S(1)} %get-tuple-element.70.refs_0_), channel_id=1, source_target_pairs={{0,1},{1,0},{2,3},{3,2},{4,5},{5,4},{6,7},{7,6},{8,9},{9,8},{10,11... | collective-permute-start | bytes 196616 | tf_op jit(solution)/shard_map/ppermute | solution.py:349
  88.4 2.5 %collective-permute-start.29 = (bf16[32,1024]{1,0:T(8,128)(2,1)S(1)}, bf16[32,1024]{1,0:T(8,128)(2,1)S(1)}, u32[]{:S(2)}, u32[]{:S(2)}) collective-permute-start(bf16[32,1024]{1,0:T(8,128)(2,1)S(1)} %collective-permute-done.28.refs_2_), channel_id=1, source_target_pairs={{0,1},{1,0},{2,3},{3,2},{4,5},{5,4},{6,7},{7,6},{8,9},{9,8},{10,11... | collective-permute-start | bytes 196616 | tf_op jit(solution)/shard_map/ppermute | solution.py:349
  88.9 4.2 %collective-permute-start.19 = (bf16[32,1280]{1,0:T(8,128)(2,1)S(1)}, bf16[32,1280]{1,0:T(8,128)(2,1)S(1)}, u32[]{:S(2)}, u32[]{:S(2)}) collective-permute-start(bf16[32,1280]{1,0:T(8,128)(2,1)S(1)} %shard_map.117.refs_0_), channel_id=1, source_target_pairs={{0,1},{1,0},{2,3},{3,2},{4,5},{5,4},{6,7},{7,6},{8,9},{9,8},{10,11... | collective-permute-start | bytes 245768 | tf_op jit(solution)/shard_map/ppermute | solution.py:349
  89.7 2.1 %collective-permute-start.24 = (bf16[32,1280]{1,0:T(8,128)(2,1)S(1)}, bf16[32,1280]{1,0:T(8,128)(2,1)S(1)}, u32[]{:S(2)}, u32[]{:S(2)}) collective-permute-start(bf16[32,1280]{1,0:T(8,128)(2,1)S(1)} %shard_map.120.refs_0_), channel_id=1, source_target_pairs={{0,1},{1,0},{2,3},{3,2},{4,5},{5,4},{6,7},{7,6},{8,9},{9,8},{10,11... | collective-permute-start | bytes 245768 | tf_op jit(solution)/shard_map/ppermute | solution.py:349
  89.8 3.3 %collective-permute-start.21 = (bf16[32,1280]{1,0:T(8,128)(2,1)S(1)}, bf16[32,1280]{1,0:T(8,128)(2,1)S(1)}, u32[]{:S(2)}, u32[]{:S(2)}) collective-permute-start(bf16[32,1280]{1,0:T(8,128)(2,1)S(1)} %collective-permute-done.20.refs_2_), channel_id=1, source_target_pairs={{0,1},{1,0},{2,3},{3,2},{4,5},{5,4},{6,7},{7,6},{8,9},{9,8},{10,11... | collective-permute-start | bytes 245768 | tf_op jit(solution)/shard_map/ppermute | solution.py:349
  90.9 1.3 %collective-permute-start.26 = (bf16[32,1280]{1,0:T(8,128)(2,1)S(1)}, bf16[32,1280]{1,0:T(8,128)(2,1)S(1)}, u32[]{:S(2)}, u32[]{:S(2)}) collective-permute-start(bf16[32,1280]{1,0:T(8,128)(2,1)S(1)} %collective-permute-done.25.refs_2_), channel_id=1, source_target_pairs={{0,1},{1,0},{2,3},{3,2},{4,5},{5,4},{6,7},{7,6},{8,9},{9,8},{10,11... | collective-permute-start | bytes 245768 | tf_op jit(solution)/shard_map/ppermute | solution.py:349
  94.0 8.5 %collective-permute-start.30 = (bf16[32,2048]{1,0:T(8,128)(2,1)S(1)}, bf16[32,2048]{1,0:T(8,128)(2,1)S(1)}, u32[]{:S(2)}, u32[]{:S(2)}) collective-permute-start(bf16[32,2048]{1,0:T(8,128)(2,1)S(1)} %get-tuple-element.72), channel_id=1, source_target_pairs={{0,12},{4,8},{8,4},{12,0},{1,13},{5,9},{9,5},{13,1},{2,14},{6,10},... | collective-permute-start | bytes 393224 | tf_op jit(solution)/shard_map/ppermute | solution.py:353
  98.0 11.3 %collective-permute-start.31 = (bf16[32,2048]{1,0:T(8,128)(2,1)S(1)}, bf16[32,2048]{1,0:T(8,128)(2,1)S(1)}, u32[]{:S(2)}, u32[]{:S(2)}) collective-permute-start(bf16[32,2048]{1,0:T(8,128)(2,1)S(1)} %get-tuple-element.73), channel_id=1, source_target_pairs={{0,8},{4,12},{8,0},{12,4},{1,9},{5,13},{9,1},{13,5},{2,10},{6,14},... | collective-permute-start | bytes 393224 | tf_op jit(solution)/shard_map/ppermute | solution.py:353
  98.0 11.3 %collective-permute-start.32 = (bf16[32,2048]{1,0:T(8,128)(2,1)S(1)}, bf16[32,2048]{1,0:T(8,128)(2,1)S(1)}, u32[]{:S(2)}, u32[]{:S(2)}) collective-permute-start(bf16[32,2048]{1,0:T(8,128)(2,1)S(1)} %get-tuple-element.74), channel_id=1, source_target_pairs={{0,4},{4,0},{8,12},{12,8},{1,5},{5,1},{9,13},{13,9},{2,6},{6,2},{1... | collective-permute-start | bytes 393224 | tf_op jit(solution)/shard_map/ppermute | solution.py:353
  (2 other events, 5.4 us)

commit v2 on v1

--- a/solution.py
+++ b/solution.py
@@ -16,7 +16,10 @@
 MOST = 4
 LANES = 128
 EPS = 1e-05
-ALL = ("ctx", "head", "sec")
+CTX, HEAD, SEC = "ctx", "head", "sec"
+ALL = (CTX, HEAD, SEC)
+HS = (HEAD, SEC)
+ROWS = ("groups", CTX)
 
 
 VM = pl.BlockSpec(memory_space=pltpu.VMEM)
@@ -55,7 +58,7 @@
 
 def slots(index_ref, blocks):
     entries = index_ref.shape[1]
-    base = lax.axis_index("ctx") * blocks
+    base = lax.axis_index(CTX) * blocks
     first = jnp.int32(0)
     end = jnp.int32(0)
     for n in range(entries):
@@ -76,7 +79,7 @@
     kv_dev = key_ref.shape[1] // DH
     group = heads // kv_dev
     scale = 1.0 / math.sqrt(DH)
-    token0 = first_token + (lax.axis_index("ctx") ^ offset) * rows
+    token0 = first_token + (lax.axis_index(CTX) ^ offset) * rows
     ahead = (
         lax.broadcasted_iota(jnp.int32, (rows, KB), 1)
         - lax.broadcasted_iota(jnp.int32, (rows, KB), 0)
@@ -148,7 +151,7 @@
         copy.start()
     row = lax.broadcasted_iota(jnp.int32, start_ref.shape, 0)
     starts = jnp.zeros(start_ref.shape, jnp.int32)
-    base = lax.axis_index("ctx") * blocks
+    base = lax.axis_index(CTX) * blocks
     for slot, (local, valid) in enumerate(found):
         starts = jnp.where(row == slot, jnp.where(valid, (base + local) * KB, jnp.int32(1 << 29)), starts)
     start_ref[...] = starts
@@ -180,13 +183,13 @@
 
 
 def place():
-    return lax.axis_index("head") * lax.axis_size("sec") + lax.axis_index("sec")
+    return lax.axis_index(HEAD) * lax.axis_size(SEC) + lax.axis_index(SEC)
 
 
 def place_of(n, rows, count):
-    n_sec = lax.axis_size("sec")
-    owner = lax.axis_index("ctx") ^ n
-    other = ((owner % n_sec) != lax.axis_index("sec")).astype(jnp.int32)
+    n_sec = lax.axis_size(SEC)
+    owner = lax.axis_index(CTX) ^ n
+    other = ((owner % n_sec) != lax.axis_index(SEC)).astype(jnp.int32)
     return pl.multiple_of(other * (count // n_sec * rows) + owner // n_sec * rows, rows)
 
 
@@ -213,7 +216,7 @@
 
 def fold_kernel(width, keep_ref, got_ref, keep_out, send_out):
     rows = keep_out.shape[0]
-    head = lax.axis_index("head")
+    head = lax.axis_index(HEAD)
     mine = pl.ds(pl.multiple_of(head * rows, rows), rows)
     other = pl.ds(pl.multiple_of((1 - head) * rows, rows), rows)
     keep_out[:, :width] = keep_ref[mine, :width] + got_ref[mine, :width].astype(F32)
@@ -301,7 +304,7 @@
 def gather_rows(pieces, rows_ref):
     rows = pieces[0].shape[0]
     for n, piece in enumerate(pieces):
-        at = pl.ds(pl.multiple_of((lax.axis_index("ctx") ^ place() ^ n) * rows, rows), rows)
+        at = pl.ds(pl.multiple_of((lax.axis_index(CTX) ^ place() ^ n) * rows, rows), rows)
         rows_ref[at, :] = piece[...]
 
 
@@ -374,8 +377,8 @@
     kv_width = key_cache.shape[1]
     order = (3, 2, 1)
 
-    got_q = {m: turn(queries, "ctx", n_context, m) for m in (2, 1)}
-    got_q[3] = turn(got_q[2], "ctx", n_context, 1)
+    got_q = {m: turn(queries, CTX, n_context, m) for m in (2, 1)}
+    got_q[3] = turn(got_q[2], CTX, n_context, 1)
     picked = struct((MOST * KB, kv_width), BF16)
     partial_out = struct((rows, heads_width + LANES), BF16)
     kv_dev = kv_width // DH
@@ -402,13 +405,14 @@
             (starts, got_q[m], keys, values),
             scratch=scratch,
         )
-    back = {m: turn(partial[m], "ctx", n_context, m) for m in order}
+    back = {m: turn(partial[m], CTX, n_context, m) for m in order}
     back[0] = partial[0]
     blended = call(
         blend_kernel, struct((rows, heads_width), BF16), [VM] * 4, tuple(back[m] for m in range(4))
     )
 
-    attention = {m: turn(blended, "ctx", n_context, m) for m in order}
+    attention = {m: turn(blended, CTX, n_context, m) for m in (2, 1)}
+    attention[3] = turn(attention[2], CTX, n_context, 1)
     attention[0] = blended
     width = out_weight.shape[1]
     keep, away = call(
@@ -419,7 +423,7 @@
         scratch=[pltpu.VMEM((total, heads_width), BF16)],
         cost=6,
     )
-    got = swap(away, "sec")
+    got = swap(away, SEC)
     keep, away = call(
         functools.partial(fold_kernel, width),
         (struct((rows, width), F32), struct((rows, width), BF16)),
@@ -427,7 +431,7 @@
         (keep, got),
         cost=6,
     )
-    got = swap(away, "head")
+    got = swap(away, HEAD)
     middle = call(middle_kernel, struct((rows, width), BF16), [VM] * 3, (stream, keep, got), cost=6)
 
     all_middle = {
@@ -489,9 +493,9 @@
                 struct((rows, 2 * chunk + 2 * extra), BF16),
             ),
             [VM, VM],
-            (keep, swap(away, "sec")),
-        )
-        got = swap(away, "head")
+            (keep, swap(away, SEC)),
+        )
+        got = swap(away, HEAD)
         if c == 0:
             own, scale = call(
                 functools.partial(first_hidden_kernel, model),
@@ -501,9 +505,9 @@
             )
         else:
             own = call(hidden_kernel, struct((rows, chunk), BF16), [VM] * 3, (scale, keep, got))
-        across = swap(own, "head")
-        beside = swap(own, "sec")
-        hidden.append((own, beside, across, swap(across, "sec")))
+        across = swap(own, HEAD)
+        beside = swap(own, SEC)
+        hidden.append((own, beside, across, swap(across, SEC)))
     out_width = down_weight.shape[1]
     down_vmem = in_vmem(down_weight)
     so_far = ()
@@ -524,7 +528,7 @@
         hidden[-1] + (down_vmem,) + so_far,
         scratch=[pltpu.VMEM((total, chunks[-1][1]), BF16)],
     )
-    parts = [turn(res[m], "ctx", n_context, m) for m in order]
+    parts = [turn(res[m], CTX, n_context, m) for m in order]
     return call(
         final_kernel, struct((rows, out_width), BF16), [VM] * 5, (all_middle[0], res[0]) + tuple(parts)
     )
@@ -588,16 +592,16 @@
     up_weight,
     down_weight,
 ):
-    n_context = lax.axis_size("ctx")
-    context_index = lax.axis_index("ctx")
+    n_context = lax.axis_size(CTX)
+    context_index = lax.axis_index(CTX)
     context_len = key_cache.shape[0] * n_context
-    gathered = lax.all_gather(queries, "ctx", axis=0, tiled=True)
+    gathered = lax.all_gather(queries, CTX, axis=0, tiled=True)
     part_out, part_lse = local_attention(
         gathered, key_cache, value_cache, block_index, context_index, context_len
     )
     spread_out, spread_lse = (
-        lax.all_to_all(part_out[:, None, :], "ctx", split_axis=0, concat_axis=1, tiled=True),
-        lax.all_to_all(part_lse[:, None, :], "ctx", split_axis=0, concat_axis=1, tiled=True),
+        lax.all_to_all(part_out[:, None, :], CTX, split_axis=0, concat_axis=1, tiled=True),
+        lax.all_to_all(part_lse[:, None, :], CTX, split_axis=0, concat_axis=1, tiled=True),
     )
     share_rows = spread_out.shape[0]
     head_count = spread_lse.shape[2]
@@ -608,23 +612,23 @@
     )
     blended = blended / jnp.sum(share_weight, axis=1)[..., None]
     attention = lax.all_gather(
-        blended.reshape(share_rows, -1).astype(jnp.bfloat16), "ctx", axis=0, tiled=True
+        blended.reshape(share_rows, -1).astype(jnp.bfloat16), CTX, axis=0, tiled=True
     )
     row_piece = attention
     projected = lax.psum_scatter(
         jnp.dot(row_piece, out_weight, preferred_element_type=jnp.float32),
-        ("head", "sec"),
+        HS,
         scatter_dimension=0,
         tiled=True,
     )
     middle = (stream.astype(jnp.float32) + projected).astype(jnp.bfloat16)
-    full_middle = lax.all_gather(middle, "ctx", axis=1, tiled=True)
+    full_middle = lax.all_gather(middle, CTX, axis=1, tiled=True)
     middle_wide = full_middle.astype(jnp.float32)
     mean_square = jnp.mean(middle_wide * middle_wide, axis=-1, keepdims=True)
     normed = (middle_wide * lax.rsqrt(mean_square + 1e-05) * norm_gain).astype(jnp.bfloat16)
     normed_cols, middle_cols = (
-        lax.all_to_all(normed, ("head", "sec"), split_axis=1, concat_axis=0, tiled=True),
-        lax.all_to_all(full_middle, ("head", "sec"), split_axis=1, concat_axis=0, tiled=True),
+        lax.all_to_all(normed, HS, split_axis=1, concat_axis=0, tiled=True),
+        lax.all_to_all(full_middle, HS, split_axis=1, concat_axis=0, tiled=True),
     )
     row_piece = normed_cols
     gate_up = lax.psum_scatter(
@@ -635,7 +639,7 @@
             ],
             axis=1,
         ),
-        ("head", "sec"),
+        HS,
         scatter_dimension=0,
         tiled=True,
     )
@@ -643,11 +647,11 @@
     hidden = (jax.nn.silu(gate_up[:, :hidden_width]) * gate_up[:, hidden_width:]).astype(
         jnp.bfloat16
     )
-    all_hidden = lax.all_gather(hidden, ("head", "sec"), axis=0, tiled=True)
+    all_hidden = lax.all_gather(hidden, HS, axis=0, tiled=True)
     row_piece = all_hidden
     down_part = lax.psum_scatter(
         jnp.dot(row_piece, down_weight, preferred_element_type=jnp.float32),
-        "ctx",
+        CTX,
         scatter_dimension=0,
         tiled=True,
     )
@@ -659,22 +663,22 @@
 
 def solution(mesh):
     size = dict(mesh.shape)
-    direct = size["ctx"] == 4 and size["head"] == 2 and size["sec"] == 2
+    direct = size[CTX] == 4 and size[HEAD] == 2 and size[SEC] == 2
     return jax.shard_map(
         direct_body if direct else general_body,
         mesh=mesh,
         in_specs=(
-            P(("groups", "ctx"), ("head", "sec")),
-            P(("groups", "ctx"), ("head", "sec")),
-            P(("groups", "ctx"), ("head", "sec")),
+            P(ROWS, HS),
+            P(ROWS, HS),
+            P(ROWS, HS),
             P("groups", None),
-            P(("groups", "head", "sec"), "ctx"),
-            P(("head", "sec"), "ctx"),
+            P(("groups",) + HS, CTX),
+            P(HS, CTX),
             P(),
-            P(("head", "sec"), "ctx"),
-            P(("head", "sec"), "ctx"),
-            P("ctx", ("head", "sec")),
+            P(HS, CTX),
+            P(HS, CTX),
+            P(CTX, HS),
         ),
-        out_specs=P(("groups", "ctx"), ("head", "sec")),
+        out_specs=P(ROWS, HS),
         check_vma=False,
     )

time: 110 us -> 111 us (level)
    ppermute x12, waiting for transfers between devices: 28.1 us -> 30.8 us  [turn(): return lax.ppermute(x, axis, [(i, i ^ offset) for i in range(n)])]
    ppermute x4, waiting for transfers between devices: 6.94 us -> 4.38 us  [direct_body(): lax.ppermute(middle, ALL, [(a * n_context + b, (b ^ m) * n_context + a) f...]
  transfers between devices with their start and end apart: 33 -> 33, of which waited for: 18 -> 18; matrix products, arithmetic and copies ran while one was open for 0% -> 0% of each run, Pallas kernels for 10% -> 9%
where the time goes in v2:
time: 111 us
  waiting for transfers between devices  47.8 us (43%)
  starting transfers between devices  46.1 us (42%)
  Pallas kernels  15.6 us (14%)
    ppermute x12, waiting for transfers between devices, turn(): return lax.ppermute(x, axis, [(i, i ^ offset) for i in range(n)])  30.8 us
    ppermute x12, starting transfers between devices, turn(): return lax.ppermute(x, axis, [(i, i ^ offset) for i in range(n)])  19.3 us
    ppermute x17, starting transfers between devices, swap(): return lax.ppermute(x, axis, [(0, 1), (1, 0)])  18.9 us
    pallas_call x25, Pallas kernels, call(): pl.pallas_call(kernel, out_shape=out, in_specs=in_specs, out_specs=jax.tr...  15.6 us
    ppermute x17, waiting for transfers between devices, swap(): return lax.ppermute(x, axis, [(0, 1), (1, 0)])  12.6 us
    ppermute x4, starting transfers between devices, direct_body(): lax.ppermute(middle, ALL, [(a * n_context + b, (b ^ m) * n_context + a) f...  7.87 us
    ppermute x4, waiting for transfers between devices, direct_body(): lax.ppermute(middle, ALL, [(a * n_context + b, (b ^ m) * n_context + a) f...  4.38 us
  transfers between devices with their start and end apart: 33, of which 18 were waited for; matrix products, arithmetic and copies ran while one was open for 0% of the time, Pallas kernels for 9%

profile of v2, /device:TPU:0, one launch (start us, length us, event | category | flops | bytes accessed | tf_op | source)
XLA Modules:
  0.0 110.6 jit_solution(13591591585220321190)
XLA Ops:
  0.0 3.1 %collective-permute-start = (bf16[32,2048]{1,0:T(8,128)(2,1)}, bf16[32,2048]{1,0:T(8,128)(2,1)S(1)}, u32[]{:S(2)}, u32[]{:S(2)}) collective-permute-start(bf16[32,2048]{1,0:T(8,128)(2,1)} %q_hbm.1), channel_id=1, source_target_pairs={{0,4},{4,0},{8,12},{12,8},{1,5},{5,1},{9,13},{13,9},{2,6},{6,2},{1... | collective-permute-start | bytes 393224 | tf_op jit(solution)/shard_map/ppermute | solution.py:356
  3.1 2.6 %collective-permute-start.2 = (bf16[32,2048]{1,0:T(8,128)(2,1)}, bf16[32,2048]{1,0:T(8,128)(2,1)S(1)}, u32[]{:S(2)}, u32[]{:S(2)}) collective-permute-start(bf16[32,2048]{1,0:T(8,128)(2,1)} %q_hbm.1), channel_id=1, source_target_pairs={{0,8},{4,12},{8,0},{12,4},{1,9},{5,13},{9,1},{13,5},{2,10},{6,14},... | collective-permute-start | bytes 393224 | tf_op jit(solution)/shard_map/ppermute | solution.py:356
  5.6 0.7 copy-done.2
  6.3 2.6 %shard_map.100 = (bf16[512,256]{1,0:T(8,128)(2,1)S(1)}, bf16[512,256]{1,0:T(8,128)(2,1)S(1)}, s32[8,128]{1,0:T(8,128)S(1)}, bf16[32,2176]{1,0:T(8,128)(2,1)S(1)}) custom-call(s32[1,8]{1,0:T(1,128)S(1)} %copy-done.2, bf16[32,2048]{1,0:T(8,128)(2,1)} %q_hbm.1, bf16[2048,256]{1,0:T(8,128)(2,1)} %key_hbm.1, bf16[2048,256]{1,0:T(8,128)(2,1)} %value_hbm.1), custom_call_target="tpu_custom_call" | custom-call | flops 3000000000 | bytes 2895904 | tf_op jit(solution)/shard_map/pallas_call | solution.py:40
  8.9 0.8 shard_map.101
  10.3 1.8 %collective-permute-done.2.q_ref = bf16[32,2048]{1,0:T(8,128)(2,1)S(1)} collective-permute-done((bf16[32,2048]{1,0:T(8,128)(2,1)}, bf16[32,2048]{1,0:T(8,128)(2,1)S(1)}, u32[]{:S(2)}, u32[]{:S(2)}) %collective-permute-start.2) | collective-permute-done | bytes 131104 | tf_op jit(solution)/shard_map/ppermute | solution.py:356
  12.4 0.8 shard_map.102
  13.3 2.7 %collective-permute-start.3 = (bf16[32,2176]{1,0:T(8,128)(2,1)S(1)}, bf16[32,2176]{1,0:T(8,128)(2,1)S(1)}, u32[]{:S(2)}, u32[]{:S(2)}) collective-permute-start(bf16[32,2176]{1,0:T(8,128)(2,1)S(1)} %shard_map.102), channel_id=1, source_target_pairs={{0,8},{4,12},{8,0},{12,4},{1,9},{5,13},{9,1},{13,5},{2,10},{6,14},... | collective-permute-start | bytes 417800 | tf_op jit(solution)/shard_map/ppermute | solution.py:356
  15.9 4.4 %collective-permute-done.4.q_ref = bf16[32,2048]{1,0:T(8,128)(2,1)S(1)} collective-permute-done((bf16[32,2048]{1,0:T(8,128)(2,1)S(1)}, bf16[32,2048]{1,0:T(8,128)(2,1)S(1)}, u32[]{:S(2)}, u32[]{:S(2)}) %collective-permute-start.4) | collective-permute-done | bytes 131104 | tf_op jit(solution)/shard_map/ppermute | solution.py:356
  20.3 0.8 shard_map.103
  21.1 2.0 %collective-permute-start.5 = (bf16[32,2176]{1,0:T(8,128)(2,1)S(1)}, bf16[32,2176]{1,0:T(8,128)(2,1)S(1)}, u32[]{:S(2)}, u32[]{:S(2)}) collective-permute-start(bf16[32,2176]{1,0:T(8,128)(2,1)S(1)} %shard_map.103), channel_id=1, source_target_pairs={{0,12},{4,8},{8,4},{12,0},{1,13},{5,9},{9,5},{13,1},{2,14},{6,10},... | collective-permute-start | bytes 417800 | tf_op jit(solution)/shard_map/ppermute | solution.py:356
  23.1 5.0 %collective-permute-done.5.refs_3_ = bf16[32,2176]{1,0:T(8,128)(2,1)S(1)} collective-permute-done((bf16[32,2176]{1,0:T(8,128)(2,1)S(1)}, bf16[32,2176]{1,0:T(8,128)(2,1)S(1)}, u32[]{:S(2)}, u32[]{:S(2)}) %collective-permute-start.5) | collective-permute-done | bytes 139296 | tf_op jit(solution)/shard_map/ppermute | solution.py:356
  28.5 1.2 %collective-permute-start.7 = (bf16[32,2048]{1,0:T(8,128)(2,1)S(1)}, bf16[32,2048]{1,0:T(8,128)(2,1)S(1)}, u32[]{:S(2)}, u32[]{:S(2)}) collective-permute-start(bf16[32,2048]{1,0:T(8,128)(2,1)S(1)} %shard_map.104.refs_0_), channel_id=1, source_target_pairs={{0,8},{4,12},{8,0},{12,4},{1,9},{5,13},{9,1},{13,5},{2,10},{6,14},... | collective-permute-start | bytes 393224 | tf_op jit(solution)/shard_map/ppermute | solution.py:356
  29.8 1.4 %collective-permute-start.6 = (bf16[32,2048]{1,0:T(8,128)(2,1)S(1)}, bf16[32,2048]{1,0:T(8,128)(2,1)S(1)}, u32[]{:S(2)}, u32[]{:S(2)}) collective-permute-start(bf16[32,2048]{1,0:T(8,128)(2,1)S(1)} %shard_map.104.refs_0_), channel_id=1, source_target_pairs={{0,4},{4,0},{8,12},{12,8},{1,5},{5,1},{9,13},{13,9},{2,6},{6,2},{1... | collective-permute-start | bytes 393224 | tf_op jit(solution)/shard_map/ppermute | solution.py:356
  31.2 3.9 %collective-permute-done.7.refs_2_ = bf16[32,2048]{1,0:T(8,128)(2,1)S(1)} collective-permute-done((bf16[32,2048]{1,0:T(8,128)(2,1)S(1)}, bf16[32,2048]{1,0:T(8,128)(2,1)S(1)}, u32[]{:S(2)}, u32[]{:S(2)}) %collective-permute-start.7) | collective-permute-done | bytes 131104 | tf_op jit(solution)/shard_map/ppermute | solution.py:356
  35.1 2.1 %collective-permute-done.6.refs_1_ = bf16[32,2048]{1,0:T(8,128)(2,1)S(1)} collective-permute-done((bf16[32,2048]{1,0:T(8,128)(2,1)S(1)}, bf16[32,2048]{1,0:T(8,128)(2,1)S(1)}, u32[]{:S(2)}, u32[]{:S(2)}) %collective-permute-start.6) | collective-permute-done | bytes 131104 | tf_op jit(solution)/shard_map/ppermute | solution.py:356
  37.2 2.8 %collective-permute-done.8.refs_3_ = bf16[32,2048]{1,0:T(8,128)(2,1)S(1)} collective-permute-done((bf16[32,2048]{1,0:T(8,128)(2,1)S(1)}, bf16[32,2048]{1,0:T(8,128)(2,1)S(1)}, u32[]{:S(2)}, u32[]{:S(2)}) %collective-permute-start.8) | collective-permute-done | bytes 131104 | tf_op jit(solution)/shard_map/ppermute | solution.py:356
  40.0 1.3 %shard_map.105 = (f32[64,2048]{1,0:T(8,128)S(1)}, bf16[64,2048]{1,0:T(8,128)(2,1)S(1)}) custom-call(bf16[32,2048]{1,0:T(8,128)(2,1)S(1)} %shard_map.104.refs_0_, bf16[32,2048]{1,0:T(8,128)(2,1)S(1)} %collective-permute-done.6.refs_1_, bf16[32,2048]{1,0:T(8,128)(2,1)S(1)} %collective-permute-done.7.refs_2_, ...), custom_call_target="tpu_custom_call" | custom-call | flops 6000000000 | bytes 9699328 | tf_op jit(solution)/shard_map/pallas_call | solution.py:40
  41.4 1.5 %collective-permute-done.9.got_ref = bf16[64,2048]{1,0:T(8,128)(2,1)S(1)} collective-permute-done((bf16[64,2048]{1,0:T(8,128)(2,1)S(1)}, bf16[64,2048]{1,0:T(8,128)(2,1)S(1)}, u32[]{:S(2)}, u32[]{:S(2)}) %collective-permute-start.9) | collective-permute-done | bytes 262176 | tf_op jit(solution)/shard_map/ppermute | solution.py:352
  43.0 1.6 %collective-permute-start.10 = (bf16[32,2048]{1,0:T(8,128)(2,1)S(1)}, bf16[32,2048]{1,0:T(8,128)(2,1)S(1)}, u32[]{:S(2)}, u32[]{:S(2)}) collective-permute-start(bf16[32,2048]{1,0:T(8,128)(2,1)S(1)} %get-tuple-element.47), channel_id=1, source_target_pairs={{0,2},{2,0},{1,3},{3,1},{4,6},{6,4},{5,7},{7,5},{8,10},{10,8},{9,1... | collective-permute-start | bytes 393224 | tf_op jit(solution)/shard_map/ppermute | solution.py:352
  44.6 4.0 %collective-permute-done.10.got_ref = bf16[32,2048]{1,0:T(8,128)(2,1)S(1)} collective-permute-done((bf16[32,2048]{1,0:T(8,128)(2,1)S(1)}, bf16[32,2048]{1,0:T(8,128)(2,1)S(1)}, u32[]{:S(2)}, u32[]{:S(2)}) %collective-permute-start.10) | collective-permute-done | bytes 131104 | tf_op jit(solution)/shard_map/ppermute | solution.py:352
  48.7 0.8 collective-permute-start.11
  49.5 2.5 %collective-permute-start.12 = (bf16[32,2048]{1,0:T(8,128)(2,1)S(1)}, bf16[32,2048]{1,0:T(8,128)(2,1)S(1)}, u32[]{:S(2)}, u32[]{:S(2)}) collective-permute-start(bf16[32,2048]{1,0:T(8,128)(2,1)S(1)} %shard_map.107), channel_id=1, source_target_pairs={{0,4},{1,0},{2,12},{3,8},{4,5},{5,1},{6,13},{7,9},{8,6},{9,2},{10,... | collective-permute-start | bytes 393224 | tf_op jit(solution)/shard_map/ppermute | solution.py:438
  52.0 3.0 %collective-permute-start.13 = (bf16[32,2048]{1,0:T(8,128)(2,1)S(1)}, bf16[32,2048]{1,0:T(8,128)(2,1)S(1)}, u32[]{:S(2)}, u32[]{:S(2)}) collective-permute-start(bf16[32,2048]{1,0:T(8,128)(2,1)S(1)} %shard_map.107), channel_id=1, source_target_pairs={{0,8},{1,12},{2,0},{3,4},{4,9},{5,13},{6,1},{7,5},{8,10},{9,14},{1... | collective-permute-start | bytes 393224 | tf_op jit(solution)/shard_map/ppermute | solution.py:438
  55.0 1.6 %collective-permute-start.14 = (bf16[32,2048]{1,0:T(8,128)(2,1)S(1)}, bf16[32,2048]{1,0:T(8,128)(2,1)S(1)}, u32[]{:S(2)}, u32[]{:S(2)}) collective-permute-start(bf16[32,2048]{1,0:T(8,128)(2,1)S(1)} %shard_map.107), channel_id=1, source_target_pairs={{0,12},{1,8},{2,4},{3,0},{4,13},{5,9},{6,5},{7,1},{8,14},{9,10},{1... | collective-permute-start | bytes 393224 | tf_op jit(solution)/shard_map/ppermute | solution.py:438
  56.8 4.2 %collective-permute-done.13.piece_ref = bf16[32,2048]{1,0:T(8,128)(2,1)S(1)} collective-permute-done((bf16[32,2048]{1,0:T(8,128)(2,1)S(1)}, bf16[32,2048]{1,0:T(8,128)(2,1)S(1)}, u32[]{:S(2)}, u32[]{:S(2)}) %collective-permute-start.13) | collective-permute-done | bytes 131104 | tf_op jit(solution)/shard_map/ppermute | solution.py:438
  61.6 1.6 %shard_map.112 = (f32[64,2176]{1,0:T(8,128)S(1)}, bf16[64,2304]{1,0:T(8,128)(2,1)S(1)}, bf16[128,2048]{1,0:T(8,128)(2,1)S(1)}) custom-call(bf16[32,2048]{1,0:T(8,128)(2,1)S(1)} %get-tuple-element.48.refs_0_, bf16[32,2048]{1,0:T(8,128)(2,1)S(1)} %get-tuple-element.49.refs_1_, bf16[32,2048]{1,0:T(8,128)(2,1)S(1)} %get-tuple-element.50.refs_2_, ...), custom_call_target="tpu_custom_call" | custom-call | flops 3000000000 | bytes 31326208 | tf_op jit(solution)/shard_map/pallas_call | solution.py:40
  63.1 2.7 %collective-permute-start.15 = (bf16[64,2304]{1,0:T(8,128)(2,1)S(1)}, bf16[64,2304]{1,0:T(8,128)(2,1)S(1)}, u32[]{:S(2)}, u32[]{:S(2)}) collective-permute-start(bf16[64,2304]{1,0:T(8,128)(2,1)S(1)} %get-tuple-element.57), channel_id=1, source_target_pairs={{0,1},{1,0},{2,3},{3,2},{4,5},{5,4},{6,7},{7,6},{8,9},{9,8},{10,11... | collective-permute-start | bytes 884744 | tf_op jit(solution)/shard_map/ppermute | solution.py:352
  65.8 1.5 %shard_map.115 = (f32[64,2560]{1,0:T(8,128)S(1)}, bf16[64,2560]{1,0:T(8,128)(2,1)S(1)}) custom-call(bf16[128,2048]{1,0:T(8,128)(2,1)S(1)} %get-tuple-element.61.rows_ref, bf16[2048,3584]{1,0:T(8,128)(2,1)S(1)} %bitcast.2, bf16[2048,3584]{1,0:T(8,128)(2,1)S(1)} %bitcast.4), custom_call_target="tpu_custom_call" | custom-call | flops 3000000000 | bytes 30867456 | tf_op jit(solution)/shard_map/pallas_call | solution.py:40
  67.4 1.5 %shard_map.118 = (f32[64,2560]{1,0:T(8,128)S(1)}, bf16[64,2560]{1,0:T(8,128)(2,1)S(1)}) custom-call(bf16[128,2048]{1,0:T(8,128)(2,1)S(1)} %get-tuple-element.61.rows_ref, bf16[2048,3584]{1,0:T(8,128)(2,1)S(1)} %bitcast.2, bf16[2048,3584]{1,0:T(8,128)(2,1)S(1)} %bitcast.4), custom_call_target="tpu_custom_call" | custom-call | flops 3000000000 | bytes 30867456 | tf_op jit(solution)/shard_map/pallas_call | solution.py:40
  69.6 4.5 %collective-permute-start.16 = (bf16[32,2304]{1,0:T(8,128)(2,1)S(1)}, bf16[32,2304]{1,0:T(8,128)(2,1)S(1)}, u32[]{:S(2)}, u32[]{:S(2)}) collective-permute-start(bf16[32,2304]{1,0:T(8,128)(2,1)S(1)} %get-tuple-element.59), channel_id=1, source_target_pairs={{0,2},{2,0},{1,3},{3,1},{4,6},{6,4},{5,7},{7,5},{8,10},{10,8},{9,1... | collective-permute-start | bytes 442376 | tf_op jit(solution)/shard_map/ppermute | solution.py:352
  74.3 2.1 %collective-permute-start.23 = (bf16[32,2560]{1,0:T(8,128)(2,1)S(1)}, bf16[32,2560]{1,0:T(8,128)(2,1)S(1)}, u32[]{:S(2)}, u32[]{:S(2)}) collective-permute-start(bf16[32,2560]{1,0:T(8,128)(2,1)S(1)} %get-tuple-element.69), channel_id=1, source_target_pairs={{0,2},{2,0},{1,3},{3,1},{4,6},{6,4},{5,7},{7,5},{8,10},{10,8},{9,1... | collective-permute-start | bytes 491528 | tf_op jit(solution)/shard_map/ppermute | solution.py:352
  76.3 2.4 %collective-permute-done.16.got_ref = bf16[32,2304]{1,0:T(8,128)(2,1)S(1)} collective-permute-done((bf16[32,2304]{1,0:T(8,128)(2,1)S(1)}, bf16[32,2304]{1,0:T(8,128)(2,1)S(1)}, u32[]{:S(2)}, u32[]{:S(2)}) %collective-permute-start.16) | collective-permute-done | bytes 147488 | tf_op jit(solution)/shard_map/ppermute | solution.py:352
  78.8 2.1 %collective-permute-start.28 = (bf16[32,1024]{1,0:T(8,128)(2,1)S(1)}, bf16[32,1024]{1,0:T(8,128)(2,1)S(1)}, u32[]{:S(2)}, u32[]{:S(2)}) collective-permute-start(bf16[32,1024]{1,0:T(8,128)(2,1)S(1)} %get-tuple-element.70.refs_0_), channel_id=1, source_target_pairs={{0,2},{2,0},{1,3},{3,1},{4,6},{6,4},{5,7},{7,5},{8,10},{10,8},{9,1... | collective-permute-start | bytes 196616 | tf_op jit(solution)/shard_map/ppermute | solution.py:352
  80.9 1.3 %collective-permute-done.18.got_ref = bf16[32,2560]{1,0:T(8,128)(2,1)S(1)} collective-permute-done((bf16[32,2560]{1,0:T(8,128)(2,1)S(1)}, bf16[32,2560]{1,0:T(8,128)(2,1)S(1)}, u32[]{:S(2)}, u32[]{:S(2)}) %collective-permute-start.18) | collective-permute-done | bytes 163872 | tf_op jit(solution)/shard_map/ppermute | solution.py:352
  82.4 2.1 %collective-permute-start.20 = (bf16[32,1280]{1,0:T(8,128)(2,1)S(1)}, bf16[32,1280]{1,0:T(8,128)(2,1)S(1)}, u32[]{:S(2)}, u32[]{:S(2)}) collective-permute-start(bf16[32,1280]{1,0:T(8,128)(2,1)S(1)} %shard_map.117.refs_0_), channel_id=1, source_target_pairs={{0,2},{2,0},{1,3},{3,1},{4,6},{6,4},{5,7},{7,5},{8,10},{10,8},{9,1... | collective-permute-start | bytes 245768 | tf_op jit(solution)/shard_map/ppermute | solution.py:352
  84.4 1.3 %collective-permute-done.23.got_ref = bf16[32,2560]{1,0:T(8,128)(2,1)S(1)} collective-permute-done((bf16[32,2560]{1,0:T(8,128)(2,1)S(1)}, bf16[32,2560]{1,0:T(8,128)(2,1)S(1)}, u32[]{:S(2)}, u32[]{:S(2)}) %collective-permute-start.23) | collective-permute-done | bytes 163872 | tf_op jit(solution)/shard_map/ppermute | solution.py:352
  85.9 2.1 %collective-permute-start.25 = (bf16[32,1280]{1,0:T(8,128)(2,1)S(1)}, bf16[32,1280]{1,0:T(8,128)(2,1)S(1)}, u32[]{:S(2)}, u32[]{:S(2)}) collective-permute-start(bf16[32,1280]{1,0:T(8,128)(2,1)S(1)} %shard_map.120.refs_0_), channel_id=1, source_target_pairs={{0,2},{2,0},{1,3},{3,1},{4,6},{6,4},{5,7},{7,5},{8,10},{10,8},{9,1... | collective-permute-start | bytes 245768 | tf_op jit(solution)/shard_map/ppermute | solution.py:352
  88.5 0.7 collective-permute-done.27.refs_1_
  89.7 0.8 collective-permute-done.25.refs_2_
  90.5 0.7 shard_map.121.refs_5_
  91.8 0.9 shard_map.122.refs_5_
  92.7 0.9 shard_map.123
  93.5 4.9 %collective-permute-start.30 = (bf16[32,2048]{1,0:T(8,128)(2,1)S(1)}, bf16[32,2048]{1,0:T(8,128)(2,1)S(1)}, u32[]{:S(2)}, u32[]{:S(2)}) collective-permute-start(bf16[32,2048]{1,0:T(8,128)(2,1)S(1)} %get-tuple-element.72), channel_id=1, source_target_pairs={{0,12},{4,8},{8,4},{12,0},{1,13},{5,9},{9,5},{13,1},{2,14},{6,10},... | collective-permute-start | bytes 393224 | tf_op jit(solution)/shard_map/ppermute | solution.py:356
  98.5 0.6 collective-permute-start.32
  99.1 3.8 %collective-permute-done.30.refs_0_ = bf16[32,2048]{1,0:T(8,128)(2,1)S(1)} collective-permute-done((bf16[32,2048]{1,0:T(8,128)(2,1)S(1)}, bf16[32,2048]{1,0:T(8,128)(2,1)S(1)}, u32[]{:S(2)}, u32[]{:S(2)}) %collective-permute-start.30) | collective-permute-done | bytes 131104 | tf_op jit(solution)/shard_map/ppermute | solution.py:356
  102.9 7.0 %collective-permute-done.31.refs_1_ = bf16[32,2048]{1,0:T(8,128)(2,1)S(1)} collective-permute-done((bf16[32,2048]{1,0:T(8,128)(2,1)S(1)}, bf16[32,2048]{1,0:T(8,128)(2,1)S(1)}, u32[]{:S(2)}, u32[]{:S(2)}) %collective-permute-start.31) | collective-permute-done | bytes 131104 | tf_op jit(solution)/shard_map/ppermute | solution.py:356
  109.9 0.7 shard_map.124
  (81 shorter events, 5.0 us)
Async XLA Ops:
  0.0 8.9 %collective-permute-start = (bf16[32,2048]{1,0:T(8,128)(2,1)}, bf16[32,2048]{1,0:T(8,128)(2,1)S(1)}, u32[]{:S(2)}, u32[]{:S(2)}) collective-permute-start(bf16[32,2048]{1,0:T(8,128)(2,1)} %q_hbm.1), channel_id=1, source_target_pairs={{0,4},{4,0},{8,12},{12,8},{1,5},{5,1},{9,13},{13,9},{2,6},{6,2},{1... | collective-permute-start | bytes 393224 | tf_op jit(solution)/shard_map/ppermute | solution.py:356
  3.1 9.0 %collective-permute-start.2 = (bf16[32,2048]{1,0:T(8,128)(2,1)}, bf16[32,2048]{1,0:T(8,128)(2,1)S(1)}, u32[]{:S(2)}, u32[]{:S(2)}) collective-permute-start(bf16[32,2048]{1,0:T(8,128)(2,1)} %q_hbm.1), channel_id=1, source_target_pairs={{0,8},{4,12},{8,0},{12,4},{1,9},{5,13},{9,1},{13,5},{2,10},{6,14},... | collective-permute-start | bytes 393224 | tf_op jit(solution)/shard_map/ppermute | solution.py:356
  9.7 30.3 %slice-start.12 = ((s8[8388608]{0:T(1024)(128)(4,1)}), s8[4194304]{0:T(1024)(128)(4,1)S(1)}, s32[]{:S(2)}) async-start(s8[8388608]{0:T(1024)(128)(4,1)} %bitcast.11), calls=%async_computation.12 | async-start | bytes 8388608
  9.7 13.4 %collective-permute-start.1 = (bf16[32,2176]{1,0:T(8,128)(2,1)S(1)}, bf16[32,2176]{1,0:T(8,128)(2,1)S(1)}, u32[]{:S(2)}, u32[]{:S(2)}) collective-permute-start(bf16[32,2176]{1,0:T(8,128)(2,1)S(1)} %shard_map.101), channel_id=1, source_target_pairs={{0,4},{4,0},{8,12},{12,8},{1,5},{5,1},{9,13},{13,9},{2,6},{6,2},{1... | collective-permute-start | bytes 417800 | tf_op jit(solution)/shard_map/ppermute | solution.py:356
  12.1 8.2 %collective-permute-start.4 = (bf16[32,2048]{1,0:T(8,128)(2,1)S(1)}, bf16[32,2048]{1,0:T(8,128)(2,1)S(1)}, u32[]{:S(2)}, u32[]{:S(2)}) collective-permute-start(bf16[32,2048]{1,0:T(8,128)(2,1)S(1)} %collective-permute-done.2.q_ref), channel_id=1, source_target_pairs={{0,4},{4,0},{8,12},{12,8},{1,5},{5,1},{9,13},{13,9},{2,6},{6,2},{1... | collective-permute-start | bytes 393224 | tf_op jit(solution)/shard_map/ppermute | solution.py:356
  13.2 26.8 %slice-start.13 = ((s8[8388608]{0:T(1024)(128)(4,1)}), s8[4194304]{0:T(1024)(128)(4,1)S(1)}, s32[]{:S(2)}) async-start(s8[8388608]{0:T(1024)(128)(4,1)} %bitcast.11), calls=%async_computation.13 | async-start | bytes 8388608
  13.3 9.9 %collective-permute-start.3 = (bf16[32,2176]{1,0:T(8,128)(2,1)S(1)}, bf16[32,2176]{1,0:T(8,128)(2,1)S(1)}, u32[]{:S(2)}, u32[]{:S(2)}) collective-permute-start(bf16[32,2176]{1,0:T(8,128)(2,1)S(1)} %shard_map.102), channel_id=1, source_target_pairs={{0,8},{4,12},{8,0},{12,4},{1,9},{5,13},{9,1},{13,5},{2,10},{6,14},... | collective-permute-start | bytes 417800 | tf_op jit(solution)/shard_map/ppermute | solution.py:356
  21.1 6.9 %collective-permute-start.5 = (bf16[32,2176]{1,0:T(8,128)(2,1)S(1)}, bf16[32,2176]{1,0:T(8,128)(2,1)S(1)}, u32[]{:S(2)}, u32[]{:S(2)}) collective-permute-start(bf16[32,2176]{1,0:T(8,128)(2,1)S(1)} %shard_map.103), channel_id=1, source_target_pairs={{0,12},{4,8},{8,4},{12,0},{1,13},{5,9},{9,5},{13,1},{2,14},{6,10},... | collective-permute-start | bytes 417800 | tf_op jit(solution)/shard_map/ppermute | solution.py:356
  28.5 6.5 %collective-permute-start.7 = (bf16[32,2048]{1,0:T(8,128)(2,1)S(1)}, bf16[32,2048]{1,0:T(8,128)(2,1)S(1)}, u32[]{:S(2)}, u32[]{:S(2)}) collective-permute-start(bf16[32,2048]{1,0:T(8,128)(2,1)S(1)} %shard_map.104.refs_0_), channel_id=1, source_target_pairs={{0,8},{4,12},{8,0},{12,4},{1,9},{5,13},{9,1},{13,5},{2,10},{6,14},... | collective-permute-start | bytes 393224 | tf_op jit(solution)/shard_map/ppermute | solution.py:356
  29.8 7.5 %collective-permute-start.6 = (bf16[32,2048]{1,0:T(8,128)(2,1)S(1)}, bf16[32,2048]{1,0:T(8,128)(2,1)S(1)}, u32[]{:S(2)}, u32[]{:S(2)}) collective-permute-start(bf16[32,2048]{1,0:T(8,128)(2,1)S(1)} %shard_map.104.refs_0_), channel_id=1, source_target_pairs={{0,4},{4,0},{8,12},{12,8},{1,5},{5,1},{9,13},{13,9},{2,6},{6,2},{1... | collective-permute-start | bytes 393224 | tf_op jit(solution)/shard_map/ppermute | solution.py:356
  35.0 5.0 %collective-permute-start.8 = (bf16[32,2048]{1,0:T(8,128)(2,1)S(1)}, bf16[32,2048]{1,0:T(8,128)(2,1)S(1)}, u32[]{:S(2)}, u32[]{:S(2)}) collective-permute-start(bf16[32,2048]{1,0:T(8,128)(2,1)S(1)} %collective-permute-done.7.refs_2_), channel_id=1, source_target_pairs={{0,4},{4,0},{8,12},{12,8},{1,5},{5,1},{9,13},{13,9},{2,6},{6,2},{1... | collective-permute-start | bytes 393224 | tf_op jit(solution)/shard_map/ppermute | solution.py:356
  41.3 7.3 %copy-start.1 = (bf16[32,2048]{1,0:T(8,128)(2,1)S(1)}, bf16[32,2048]{1,0:T(8,128)(2,1)}, u32[]{:S(2)}) copy-start(bf16[32,2048]{1,0:T(8,128)(2,1)} %stream_ref.1) | copy-start | bytes 393220
  41.3 1.6 %collective-permute-start.9 = (bf16[64,2048]{1,0:T(8,128)(2,1)S(1)}, bf16[64,2048]{1,0:T(8,128)(2,1)S(1)}, u32[]{:S(2)}, u32[]{:S(2)}) collective-permute-start(bf16[64,2048]{1,0:T(8,128)(2,1)S(1)} %get-tuple-element.45), channel_id=1, source_target_pairs={{0,1},{1,0},{2,3},{3,2},{4,5},{5,4},{6,7},{7,6},{8,9},{9,8},{10,11... | collective-permute-start | bytes 786440 | tf_op jit(solution)/shard_map/ppermute | solution.py:352
  42.9 18.5 %slice-start = ((s8[14680064]{0:T(1024)(128)(4,1)}), s8[4194304]{0:T(1024)(128)(4,1)S(1)}, s32[]{:S(2)}) async-start(s8[14680064]{0:T(1024)(128)(4,1)} %bitcast.1), calls=%async_computation | async-start | bytes 8388608
  42.9 18.5 %slice-start.1 = ((s8[14680064]{0:T(1024)(128)(4,1)}), s8[4194304]{0:T(1024)(128)(4,1)S(1)}, s32[]{:S(2)}) async-start(s8[14680064]{0:T(1024)(128)(4,1)} %bitcast.1), calls=%async_computation.1 | async-start | bytes 8388608
  42.9 18.5 %slice-start.4 = ((s8[14680064]{0:T(1024)(128)(4,1)}), s8[2097152]{0:T(1024)(128)(4,1)S(1)}, s32[]{:S(2)}) async-start(s8[14680064]{0:T(1024)(128)(4,1)} %bitcast.3), calls=%async_computation.4 | async-start | bytes 4194304
  42.9 18.5 %slice-start.5 = ((s8[14680064]{0:T(1024)(128)(4,1)}), s8[4194304]{0:T(1024)(128)(4,1)S(1)}, s32[]{:S(2)}) async-start(s8[14680064]{0:T(1024)(128)(4,1)} %bitcast.3), calls=%async_computation.5 | async-start | bytes 8388608
  43.0 13.6 %copy-start = (f32[8192]{0:T(1024)S(1)}, f32[8192]{0:T(1024)}, u32[]{:S(2)}) copy-start(f32[8192]{0:T(1024)} %param.16) | copy-start | bytes 98308
  43.0 5.6 %collective-permute-start.10 = (bf16[32,2048]{1,0:T(8,128)(2,1)S(1)}, bf16[32,2048]{1,0:T(8,128)(2,1)S(1)}, u32[]{:S(2)}, u32[]{:S(2)}) collective-permute-start(bf16[32,2048]{1,0:T(8,128)(2,1)S(1)} %get-tuple-element.47), channel_id=1, source_target_pairs={{0,2},{2,0},{1,3},{3,1},{4,6},{6,4},{5,7},{7,5},{8,10},{10,8},{9,1... | collective-permute-start | bytes 393224 | tf_op jit(solution)/shard_map/ppermute | solution.py:352
  48.6 12.9 %slice-start.2 = ((s8[14680064]{0:T(1024)(128)(4,1)}), s8[4194304]{0:T(1024)(128)(4,1)S(1)}, s32[]{:S(2)}) async-start(s8[14680064]{0:T(1024)(128)(4,1)} %bitcast.1), calls=%async_computation.2 | async-start | bytes 8388608
  48.6 12.9 %slice-start.3 = ((s8[14680064]{0:T(1024)(128)(4,1)}), s8[2097152]{0:T(1024)(128)(4,1)S(1)}, s32[]{:S(2)}) async-start(s8[14680064]{0:T(1024)(128)(4,1)} %bitcast.1), calls=%async_computation.3 | async-start | bytes 4194304
  48.6 12.9 %slice-start.6 = ((s8[14680064]{0:T(1024)(128)(4,1)}), s8[4194304]{0:T(1024)(128)(4,1)S(1)}, s32[]{:S(2)}) async-start(s8[14680064]{0:T(1024)(128)(4,1)} %bitcast.3), calls=%async_computation.6 | async-start | bytes 8388608
  48.6 12.9 %slice-start.7 = ((s8[14680064]{0:T(1024)(128)(4,1)}), s8[4194304]{0:T(1024)(128)(4,1)S(1)}, s32[]{:S(2)}) async-start(s8[14680064]{0:T(1024)(128)(4,1)} %bitcast.3), calls=%async_computation.7 | async-start | bytes 8388608
  48.7 7.9 %collective-permute-start.11 = (bf16[32,2048]{1,0:T(8,128)(2,1)S(1)}, bf16[32,2048]{1,0:T(8,128)(2,1)S(1)}, u32[]{:S(2)}, u32[]{:S(2)}) collective-permute-start(bf16[32,2048]{1,0:T(8,128)(2,1)S(1)} %shard_map.107), channel_id=1, source_target_pairs={{0,0},{1,4},{2,8},{3,12},{4,1},{5,5},{6,9},{7,13},{8,2},{9,6},{10,... | collective-permute-start | bytes 393224 | tf_op jit(solution)/shard_map/ppermute | solution.py:438
  49.5 7.2 %collective-permute-start.12 = (bf16[32,2048]{1,0:T(8,128)(2,1)S(1)}, bf16[32,2048]{1,0:T(8,128)(2,1)S(1)}, u32[]{:S(2)}, u32[]{:S(2)}) collective-permute-start(bf16[32,2048]{1,0:T(8,128)(2,1)S(1)} %shard_map.107), channel_id=1, source_target_pairs={{0,4},{1,0},{2,12},{3,8},{4,5},{5,1},{6,13},{7,9},{8,6},{9,2},{10,... | collective-permute-start | bytes 393224 | tf_op jit(solution)/shard_map/ppermute | solution.py:438
  52.0 9.1 %collective-permute-start.13 = (bf16[32,2048]{1,0:T(8,128)(2,1)S(1)}, bf16[32,2048]{1,0:T(8,128)(2,1)S(1)}, u32[]{:S(2)}, u32[]{:S(2)}) collective-permute-start(bf16[32,2048]{1,0:T(8,128)(2,1)S(1)} %shard_map.107), channel_id=1, source_target_pairs={{0,8},{1,12},{2,0},{3,4},{4,9},{5,13},{6,1},{7,5},{8,10},{9,14},{1... | collective-permute-start | bytes 393224 | tf_op jit(solution)/shard_map/ppermute | solution.py:438
  55.0 6.4 %collective-permute-start.14 = (bf16[32,2048]{1,0:T(8,128)(2,1)S(1)}, bf16[32,2048]{1,0:T(8,128)(2,1)S(1)}, u32[]{:S(2)}, u32[]{:S(2)}) collective-permute-start(bf16[32,2048]{1,0:T(8,128)(2,1)S(1)} %shard_map.107), channel_id=1, source_target_pairs={{0,12},{1,8},{2,4},{3,0},{4,13},{5,9},{6,5},{7,1},{8,14},{9,10},{1... | collective-permute-start | bytes 393224 | tf_op jit(solution)/shard_map/ppermute | solution.py:438
  63.1 6.4 %collective-permute-start.15 = (bf16[64,2304]{1,0:T(8,128)(2,1)S(1)}, bf16[64,2304]{1,0:T(8,128)(2,1)S(1)}, u32[]{:S(2)}, u32[]{:S(2)}) collective-permute-start(bf16[64,2304]{1,0:T(8,128)(2,1)S(1)} %get-tuple-element.57), channel_id=1, source_target_pairs={{0,1},{1,0},{2,3},{3,2},{4,5},{5,4},{6,7},{7,6},{8,9},{9,8},{10,11... | collective-permute-start | bytes 884744 | tf_op jit(solution)/shard_map/ppermute | solution.py:352
  67.3 6.7 %collective-permute-start.17 = (bf16[64,2560]{1,0:T(8,128)(2,1)S(1)}, bf16[64,2560]{1,0:T(8,128)(2,1)S(1)}, u32[]{:S(2)}, u32[]{:S(2)}) collective-permute-start(bf16[64,2560]{1,0:T(8,128)(2,1)S(1)} %get-tuple-element.63), channel_id=1, source_target_pairs={{0,1},{1,0},{2,3},{3,2},{4,5},{5,4},{6,7},{7,6},{8,9},{9,8},{10,11... | collective-permute-start | bytes 983048 | tf_op jit(solution)/shard_map/ppermute | solution.py:352
  69.0 5.2 %collective-permute-start.22 = (bf16[64,2560]{1,0:T(8,128)(2,1)S(1)}, bf16[64,2560]{1,0:T(8,128)(2,1)S(1)}, u32[]{:S(2)}, u32[]{:S(2)}) collective-permute-start(bf16[64,2560]{1,0:T(8,128)(2,1)S(1)} %get-tuple-element.67), channel_id=1, source_target_pairs={{0,1},{1,0},{2,3},{3,2},{4,5},{5,4},{6,7},{7,6},{8,9},{9,8},{10,11... | collective-permute-start | bytes 983048 | tf_op jit(solution)/shard_map/ppermute | solution.py:352
  69.6 9.2 %collective-permute-start.16 = (bf16[32,2304]{1,0:T(8,128)(2,1)S(1)}, bf16[32,2304]{1,0:T(8,128)(2,1)S(1)}, u32[]{:S(2)}, u32[]{:S(2)}) collective-permute-start(bf16[32,2304]{1,0:T(8,128)(2,1)S(1)} %get-tuple-element.59), channel_id=1, source_target_pairs={{0,2},{2,0},{1,3},{3,1},{4,6},{6,4},{5,7},{7,5},{8,10},{10,8},{9,1... | collective-permute-start | bytes 442376 | tf_op jit(solution)/shard_map/ppermute | solution.py:352
  74.1 8.1 %collective-permute-start.18 = (bf16[32,2560]{1,0:T(8,128)(2,1)S(1)}, bf16[32,2560]{1,0:T(8,128)(2,1)S(1)}, u32[]{:S(2)}, u32[]{:S(2)}) collective-permute-start(bf16[32,2560]{1,0:T(8,128)(2,1)S(1)} %get-tuple-element.65), channel_id=1, source_target_pairs={{0,2},{2,0},{1,3},{3,1},{4,6},{6,4},{5,7},{7,5},{8,10},{10,8},{9,1... | collective-permute-start | bytes 491528 | tf_op jit(solution)/shard_map/ppermute | solution.py:352
  74.3 11.5 %collective-permute-start.23 = (bf16[32,2560]{1,0:T(8,128)(2,1)S(1)}, bf16[32,2560]{1,0:T(8,128)(2,1)S(1)}, u32[]{:S(2)}, u32[]{:S(2)}) collective-permute-start(bf16[32,2560]{1,0:T(8,128)(2,1)S(1)} %get-tuple-element.69), channel_id=1, source_target_pairs={{0,2},{2,0},{1,3},{3,1},{4,6},{6,4},{5,7},{7,5},{8,10},{10,8},{9,1... | collective-permute-start | bytes 491528 | tf_op jit(solution)/shard_map/ppermute | solution.py:352
  78.7 11.7 %slice-start.8 = ((s8[14680064]{0:T(1024)(128)(4,1)}), s8[4194304]{0:T(1024)(128)(4,1)S(1)}, s32[]{:S(2)}) async-start(s8[14680064]{0:T(1024)(128)(4,1)} %bitcast.5), calls=%async_computation.8 | async-start | bytes 8388608
  78.8 11.7 %slice-start.9 = ((s8[14680064]{0:T(1024)(128)(4,1)}), s8[4194304]{0:T(1024)(128)(4,1)S(1)}, s32[]{:S(2)}) async-start(s8[14680064]{0:T(1024)(128)(4,1)} %bitcast.5), calls=%async_computation.9 | async-start | bytes 8388608
  78.8 9.1 %collective-permute-start.28 = (bf16[32,1024]{1,0:T(8,128)(2,1)S(1)}, bf16[32,1024]{1,0:T(8,128)(2,1)S(1)}, u32[]{:S(2)}, u32[]{:S(2)}) collective-permute-start(bf16[32,1024]{1,0:T(8,128)(2,1)S(1)} %get-tuple-element.70.refs_0_), channel_id=1, source_target_pairs={{0,2},{2,0},{1,3},{3,1},{4,6},{6,4},{5,7},{7,5},{8,10},{10,8},{9,1... | collective-permute-start | bytes 196616 | tf_op jit(solution)/shard_map/ppermute | solution.py:352
  82.3 8.2 %slice-start.10 = ((s8[14680064]{0:T(1024)(128)(4,1)}), s8[4194304]{0:T(1024)(128)(4,1)S(1)}, s32[]{:S(2)}) async-start(s8[14680064]{0:T(1024)(128)(4,1)} %bitcast.5), calls=%async_computation.10 | async-start | bytes 8388608
  82.4 7.0 %collective-permute-start.20 = (bf16[32,1280]{1,0:T(8,128)(2,1)S(1)}, bf16[32,1280]{1,0:T(8,128)(2,1)S(1)}, u32[]{:S(2)}, u32[]{:S(2)}) collective-permute-start(bf16[32,1280]{1,0:T(8,128)(2,1)S(1)} %shard_map.117.refs_0_), channel_id=1, source_target_pairs={{0,2},{2,0},{1,3},{3,1},{4,6},{6,4},{5,7},{7,5},{8,10},{10,8},{9,1... | collective-permute-start | bytes 245768 | tf_op jit(solution)/shard_map/ppermute | solution.py:352
  85.9 4.6 %collective-permute-start.25 = (bf16[32,1280]{1,0:T(8,128)(2,1)S(1)}, bf16[32,1280]{1,0:T(8,128)(2,1)S(1)}, u32[]{:S(2)}, u32[]{:S(2)}) collective-permute-start(bf16[32,1280]{1,0:T(8,128)(2,1)S(1)} %shard_map.120.refs_0_), channel_id=1, source_target_pairs={{0,2},{2,0},{1,3},{3,1},{4,6},{6,4},{5,7},{7,5},{8,10},{10,8},{9,1... | collective-permute-start | bytes 245768 | tf_op jit(solution)/shard_map/ppermute | solution.py:352
  88.0 1.3 %collective-permute-start.27 = (bf16[32,1024]{1,0:T(8,128)(2,1)S(1)}, bf16[32,1024]{1,0:T(8,128)(2,1)S(1)}, u32[]{:S(2)}, u32[]{:S(2)}) collective-permute-start(bf16[32,1024]{1,0:T(8,128)(2,1)S(1)} %get-tuple-element.70.refs_0_), channel_id=1, source_target_pairs={{0,1},{1,0},{2,3},{3,2},{4,5},{5,4},{6,7},{7,6},{8,9},{9,8},{10,11... | collective-permute-start | bytes 196616 | tf_op jit(solution)/shard_map/ppermute | solution.py:352
  88.0 2.5 %collective-permute-start.29 = (bf16[32,1024]{1,0:T(8,128)(2,1)S(1)}, bf16[32,1024]{1,0:T(8,128)(2,1)S(1)}, u32[]{:S(2)}, u32[]{:S(2)}) collective-permute-start(bf16[32,1024]{1,0:T(8,128)(2,1)S(1)} %collective-permute-done.28.refs_2_), channel_id=1, source_target_pairs={{0,1},{1,0},{2,3},{3,2},{4,5},{5,4},{6,7},{7,6},{8,9},{9,8},{10,11... | collective-permute-start | bytes 196616 | tf_op jit(solution)/shard_map/ppermute | solution.py:352
  88.5 4.2 %collective-permute-start.19 = (bf16[32,1280]{1,0:T(8,128)(2,1)S(1)}, bf16[32,1280]{1,0:T(8,128)(2,1)S(1)}, u32[]{:S(2)}, u32[]{:S(2)}) collective-permute-start(bf16[32,1280]{1,0:T(8,128)(2,1)S(1)} %shard_map.117.refs_0_), channel_id=1, source_target_pairs={{0,1},{1,0},{2,3},{3,2},{4,5},{5,4},{6,7},{7,6},{8,9},{9,8},{10,11... | collective-permute-start | bytes 245768 | tf_op jit(solution)/shard_map/ppermute | solution.py:352
  89.2 2.1 %collective-permute-start.24 = (bf16[32,1280]{1,0:T(8,128)(2,1)S(1)}, bf16[32,1280]{1,0:T(8,128)(2,1)S(1)}, u32[]{:S(2)}, u32[]{:S(2)}) collective-permute-start(bf16[32,1280]{1,0:T(8,128)(2,1)S(1)} %shard_map.120.refs_0_), channel_id=1, source_target_pairs={{0,1},{1,0},{2,3},{3,2},{4,5},{5,4},{6,7},{7,6},{8,9},{9,8},{10,11... | collective-permute-start | bytes 245768 | tf_op jit(solution)/shard_map/ppermute | solution.py:352
  89.4 3.3 %collective-permute-start.21 = (bf16[32,1280]{1,0:T(8,128)(2,1)S(1)}, bf16[32,1280]{1,0:T(8,128)(2,1)S(1)}, u32[]{:S(2)}, u32[]{:S(2)}) collective-permute-start(bf16[32,1280]{1,0:T(8,128)(2,1)S(1)} %collective-permute-done.20.refs_2_), channel_id=1, source_target_pairs={{0,1},{1,0},{2,3},{3,2},{4,5},{5,4},{6,7},{7,6},{8,9},{9,8},{10,11... | collective-permute-start | bytes 245768 | tf_op jit(solution)/shard_map/ppermute | solution.py:352
  90.5 1.3 %collective-permute-start.26 = (bf16[32,1280]{1,0:T(8,128)(2,1)S(1)}, bf16[32,1280]{1,0:T(8,128)(2,1)S(1)}, u32[]{:S(2)}, u32[]{:S(2)}) collective-permute-start(bf16[32,1280]{1,0:T(8,128)(2,1)S(1)} %collective-permute-done.25.refs_2_), channel_id=1, source_target_pairs={{0,1},{1,0},{2,3},{3,2},{4,5},{5,4},{6,7},{7,6},{8,9},{9,8},{10,11... | collective-permute-start | bytes 245768 | tf_op jit(solution)/shard_map/ppermute | solution.py:352
  93.5 9.4 %collective-permute-start.30 = (bf16[32,2048]{1,0:T(8,128)(2,1)S(1)}, bf16[32,2048]{1,0:T(8,128)(2,1)S(1)}, u32[]{:S(2)}, u32[]{:S(2)}) collective-permute-start(bf16[32,2048]{1,0:T(8,128)(2,1)S(1)} %get-tuple-element.72), channel_id=1, source_target_pairs={{0,12},{4,8},{8,4},{12,0},{1,13},{5,9},{9,5},{13,1},{2,14},{6,10},... | collective-permute-start | bytes 393224 | tf_op jit(solution)/shard_map/ppermute | solution.py:356
  98.5 11.4 %collective-permute-start.31 = (bf16[32,2048]{1,0:T(8,128)(2,1)S(1)}, bf16[32,2048]{1,0:T(8,128)(2,1)S(1)}, u32[]{:S(2)}, u32[]{:S(2)}) collective-permute-start(bf16[32,2048]{1,0:T(8,128)(2,1)S(1)} %get-tuple-element.73), channel_id=1, source_target_pairs={{0,8},{4,12},{8,0},{12,4},{1,9},{5,13},{9,1},{13,5},{2,10},{6,14},... | collective-permute-start | bytes 393224 | tf_op jit(solution)/shard_map/ppermute | solution.py:356
  98.5 11.4 %collective-permute-start.32 = (bf16[32,2048]{1,0:T(8,128)(2,1)S(1)}, bf16[32,2048]{1,0:T(8,128)(2,1)S(1)}, u32[]{:S(2)}, u32[]{:S(2)}) collective-permute-start(bf16[32,2048]{1,0:T(8,128)(2,1)S(1)} %get-tuple-element.74), channel_id=1, source_target_pairs={{0,4},{4,0},{8,12},{12,8},{1,5},{5,1},{9,13},{13,9},{2,6},{6,2},{1... | collective-permute-start | bytes 393224 | tf_op jit(solution)/shard_map/ppermute | solution.py:356
  (2 other events, 5.4 us)

commit v3 on v2

--- a/solution.py
+++ b/solution.py
@@ -337,7 +337,11 @@
         )
         own_ref[:, columns] = part[:rows]
         for n, send in enumerate(sends):
-            send[:, columns] = part[(n + 1) * rows : (n + 2) * rows].astype(BF16)
+            send[:, columns] = part[(n + 1) * rows : (n + 2) * rows].astype(send.dtype)
+
+
+def add_kernel(own_ref, got_ref, out_ref):
+    out_ref[...] = (own_ref[...] + got_ref[...].astype(F32)).astype(BF16)
 
 
 def final_kernel(middle_ref, own_ref, *refs):
@@ -523,14 +527,17 @@
         )
     res = call(
         functools.partial(down_kernel, 512),
-        (struct((rows, out_width), F32),) + (struct((rows, out_width), BF16),) * 3,
+        tuple(struct((rows, out_width), t) for t in (F32, BF16, F32, BF16)),
         [VM] * 6,
         hidden[-1] + (down_vmem,) + so_far,
         scratch=[pltpu.VMEM((total, chunks[-1][1]), BF16)],
     )
-    parts = [turn(res[m], CTX, n_context, m) for m in order]
+    beside = turn(res[3], CTX, n_context, 1)
+    near = turn(res[1], CTX, n_context, 1)
+    pair = call(add_kernel, struct((rows, out_width), BF16), [VM] * 2, (res[2], beside))
+    far = turn(pair, CTX, n_context, 2)
     return call(
-        final_kernel, struct((rows, out_width), BF16), [VM] * 5, (all_middle[0], res[0]) + tuple(parts)
+        final_kernel, struct((rows, out_width), BF16), [VM] * 4, (all_middle[0], res[0], near, far)
     )
 
 

time: 111 us -> 110 us (level)
  waiting for transfers between devices: 47.8 us -> 46.6 us
    ppermute x12, waiting for transfers between devices: 30.8 us -> 29.5 us  [turn(): return lax.ppermute(x, axis, [(i, i ^ offset) for i in range(n)])]
    pallas_call x25 -> x26, Pallas kernels: 15.6 us -> 15.7 us  [call(): pl.pallas_call(kernel, out_shape=out, in_specs=in_specs, out_specs=jax.tr...]
  transfers between devices with their start and end apart: 33 -> 33, of which waited for: 18 -> 18; matrix products, arithmetic and copies ran while one was open for 0% -> 0% of each run, Pallas kernels for 9% -> 10%
where the time goes in v3:
time: 110 us
  starting transfers between devices  46.8 us (43%)
  waiting for transfers between devices  46.6 us (42%)
  Pallas kernels  15.7 us (14%)
    ppermute x12, waiting for transfers between devices, turn(): return lax.ppermute(x, axis, [(i, i ^ offset) for i in range(n)])  29.5 us
    ppermute x12, starting transfers between devices, turn(): return lax.ppermute(x, axis, [(i, i ^ offset) for i in range(n)])  20 us
    ppermute x17, starting transfers between devices, swap(): return lax.ppermute(x, axis, [(0, 1), (1, 0)])  18.9 us
    pallas_call x26, Pallas kernels, call(): pl.pallas_call(kernel, out_shape=out, in_specs=in_specs, out_specs=jax.tr...  15.7 us
    ppermute x17, waiting for transfers between devices, swap(): return lax.ppermute(x, axis, [(0, 1), (1, 0)])  12.6 us
    ppermute x4, starting transfers between devices, direct_body(): lax.ppermute(middle, ALL, [(a * n_context + b, (b ^ m) * n_context + a) f...  7.87 us
    ppermute x4, waiting for transfers between devices, direct_body(): lax.ppermute(middle, ALL, [(a * n_context + b, (b ^ m) * n_context + a) f...  4.38 us
  transfers between devices with their start and end apart: 33, of which 18 were waited for; matrix products, arithmetic and copies ran while one was open for 0% of the time, Pallas kernels for 10%

profile of v3, /device:TPU:0, one launch (start us, length us, event | category | flops | bytes accessed | tf_op | source)
XLA Modules:
  0.0 110.1 jit_solution(214646634208675705)
XLA Ops:
  0.0 3.1 %collective-permute-start = (bf16[32,2048]{1,0:T(8,128)(2,1)}, bf16[32,2048]{1,0:T(8,128)(2,1)S(1)}, u32[]{:S(2)}, u32[]{:S(2)}) collective-permute-start(bf16[32,2048]{1,0:T(8,128)(2,1)} %q_hbm.1), channel_id=1, source_target_pairs={{0,4},{4,0},{8,12},{12,8},{1,5},{5,1},{9,13},{13,9},{2,6},{6,2},{1... | collective-permute-start | bytes 393224 | tf_op jit(solution)/shard_map/ppermute | solution.py:360
  3.1 2.6 %collective-permute-start.2 = (bf16[32,2048]{1,0:T(8,128)(2,1)}, bf16[32,2048]{1,0:T(8,128)(2,1)S(1)}, u32[]{:S(2)}, u32[]{:S(2)}) collective-permute-start(bf16[32,2048]{1,0:T(8,128)(2,1)} %q_hbm.1), channel_id=1, source_target_pairs={{0,8},{4,12},{8,0},{12,4},{1,9},{5,13},{9,1},{13,5},{2,10},{6,14},... | collective-permute-start | bytes 393224 | tf_op jit(solution)/shard_map/ppermute | solution.py:360
  5.6 0.7 copy-done.2
  6.3 2.6 %shard_map.100 = (bf16[512,256]{1,0:T(8,128)(2,1)S(1)}, bf16[512,256]{1,0:T(8,128)(2,1)S(1)}, s32[8,128]{1,0:T(8,128)S(1)}, bf16[32,2176]{1,0:T(8,128)(2,1)S(1)}) custom-call(s32[1,8]{1,0:T(1,128)S(1)} %copy-done.2, bf16[32,2048]{1,0:T(8,128)(2,1)} %q_hbm.1, bf16[2048,256]{1,0:T(8,128)(2,1)} %key_hbm.1, bf16[2048,256]{1,0:T(8,128)(2,1)} %value_hbm.1), custom_call_target="tpu_custom_call" | custom-call | flops 3000000000 | bytes 2895904 | tf_op jit(solution)/shard_map/pallas_call | solution.py:40
  8.9 0.8 shard_map.101
  10.3 1.8 %collective-permute-done.2.q_ref = bf16[32,2048]{1,0:T(8,128)(2,1)S(1)} collective-permute-done((bf16[32,2048]{1,0:T(8,128)(2,1)}, bf16[32,2048]{1,0:T(8,128)(2,1)S(1)}, u32[]{:S(2)}, u32[]{:S(2)}) %collective-permute-start.2) | collective-permute-done | bytes 131104 | tf_op jit(solution)/shard_map/ppermute | solution.py:360
  12.4 0.8 shard_map.102
  13.3 2.7 %collective-permute-start.3 = (bf16[32,2176]{1,0:T(8,128)(2,1)S(1)}, bf16[32,2176]{1,0:T(8,128)(2,1)S(1)}, u32[]{:S(2)}, u32[]{:S(2)}) collective-permute-start(bf16[32,2176]{1,0:T(8,128)(2,1)S(1)} %shard_map.102), channel_id=1, source_target_pairs={{0,8},{4,12},{8,0},{12,4},{1,9},{5,13},{9,1},{13,5},{2,10},{6,14},... | collective-permute-start | bytes 417800 | tf_op jit(solution)/shard_map/ppermute | solution.py:360
  15.9 4.4 %collective-permute-done.4.q_ref = bf16[32,2048]{1,0:T(8,128)(2,1)S(1)} collective-permute-done((bf16[32,2048]{1,0:T(8,128)(2,1)S(1)}, bf16[32,2048]{1,0:T(8,128)(2,1)S(1)}, u32[]{:S(2)}, u32[]{:S(2)}) %collective-permute-start.4) | collective-permute-done | bytes 131104 | tf_op jit(solution)/shard_map/ppermute | solution.py:360
  20.3 0.8 shard_map.103
  21.1 2.0 %collective-permute-start.5 = (bf16[32,2176]{1,0:T(8,128)(2,1)S(1)}, bf16[32,2176]{1,0:T(8,128)(2,1)S(1)}, u32[]{:S(2)}, u32[]{:S(2)}) collective-permute-start(bf16[32,2176]{1,0:T(8,128)(2,1)S(1)} %shard_map.103), channel_id=1, source_target_pairs={{0,12},{4,8},{8,4},{12,0},{1,13},{5,9},{9,5},{13,1},{2,14},{6,10},... | collective-permute-start | bytes 417800 | tf_op jit(solution)/shard_map/ppermute | solution.py:360
  23.1 5.0 %collective-permute-done.5.refs_3_ = bf16[32,2176]{1,0:T(8,128)(2,1)S(1)} collective-permute-done((bf16[32,2176]{1,0:T(8,128)(2,1)S(1)}, bf16[32,2176]{1,0:T(8,128)(2,1)S(1)}, u32[]{:S(2)}, u32[]{:S(2)}) %collective-permute-start.5) | collective-permute-done | bytes 139296 | tf_op jit(solution)/shard_map/ppermute | solution.py:360
  28.5 1.2 %collective-permute-start.7 = (bf16[32,2048]{1,0:T(8,128)(2,1)S(1)}, bf16[32,2048]{1,0:T(8,128)(2,1)S(1)}, u32[]{:S(2)}, u32[]{:S(2)}) collective-permute-start(bf16[32,2048]{1,0:T(8,128)(2,1)S(1)} %shard_map.104.refs_0_), channel_id=1, source_target_pairs={{0,8},{4,12},{8,0},{12,4},{1,9},{5,13},{9,1},{13,5},{2,10},{6,14},... | collective-permute-start | bytes 393224 | tf_op jit(solution)/shard_map/ppermute | solution.py:360
  29.8 1.4 %collective-permute-start.6 = (bf16[32,2048]{1,0:T(8,128)(2,1)S(1)}, bf16[32,2048]{1,0:T(8,128)(2,1)S(1)}, u32[]{:S(2)}, u32[]{:S(2)}) collective-permute-start(bf16[32,2048]{1,0:T(8,128)(2,1)S(1)} %shard_map.104.refs_0_), channel_id=1, source_target_pairs={{0,4},{4,0},{8,12},{12,8},{1,5},{5,1},{9,13},{13,9},{2,6},{6,2},{1... | collective-permute-start | bytes 393224 | tf_op jit(solution)/shard_map/ppermute | solution.py:360
  31.2 3.9 %collective-permute-done.7.refs_2_ = bf16[32,2048]{1,0:T(8,128)(2,1)S(1)} collective-permute-done((bf16[32,2048]{1,0:T(8,128)(2,1)S(1)}, bf16[32,2048]{1,0:T(8,128)(2,1)S(1)}, u32[]{:S(2)}, u32[]{:S(2)}) %collective-permute-start.7) | collective-permute-done | bytes 131104 | tf_op jit(solution)/shard_map/ppermute | solution.py:360
  35.1 2.1 %collective-permute-done.6.refs_1_ = bf16[32,2048]{1,0:T(8,128)(2,1)S(1)} collective-permute-done((bf16[32,2048]{1,0:T(8,128)(2,1)S(1)}, bf16[32,2048]{1,0:T(8,128)(2,1)S(1)}, u32[]{:S(2)}, u32[]{:S(2)}) %collective-permute-start.6) | collective-permute-done | bytes 131104 | tf_op jit(solution)/shard_map/ppermute | solution.py:360
  37.2 2.8 %collective-permute-done.8.refs_3_ = bf16[32,2048]{1,0:T(8,128)(2,1)S(1)} collective-permute-done((bf16[32,2048]{1,0:T(8,128)(2,1)S(1)}, bf16[32,2048]{1,0:T(8,128)(2,1)S(1)}, u32[]{:S(2)}, u32[]{:S(2)}) %collective-permute-start.8) | collective-permute-done | bytes 131104 | tf_op jit(solution)/shard_map/ppermute | solution.py:360
  40.0 1.3 %shard_map.105 = (f32[64,2048]{1,0:T(8,128)S(1)}, bf16[64,2048]{1,0:T(8,128)(2,1)S(1)}) custom-call(bf16[32,2048]{1,0:T(8,128)(2,1)S(1)} %shard_map.104.refs_0_, bf16[32,2048]{1,0:T(8,128)(2,1)S(1)} %collective-permute-done.6.refs_1_, bf16[32,2048]{1,0:T(8,128)(2,1)S(1)} %collective-permute-done.7.refs_2_, ...), custom_call_target="tpu_custom_call" | custom-call | flops 6000000000 | bytes 9699328 | tf_op jit(solution)/shard_map/pallas_call | solution.py:40
  41.4 1.5 %collective-permute-done.9.got_ref = bf16[64,2048]{1,0:T(8,128)(2,1)S(1)} collective-permute-done((bf16[64,2048]{1,0:T(8,128)(2,1)S(1)}, bf16[64,2048]{1,0:T(8,128)(2,1)S(1)}, u32[]{:S(2)}, u32[]{:S(2)}) %collective-permute-start.9) | collective-permute-done | bytes 262176 | tf_op jit(solution)/shard_map/ppermute | solution.py:356
  43.0 1.6 %collective-permute-start.10 = (bf16[32,2048]{1,0:T(8,128)(2,1)S(1)}, bf16[32,2048]{1,0:T(8,128)(2,1)S(1)}, u32[]{:S(2)}, u32[]{:S(2)}) collective-permute-start(bf16[32,2048]{1,0:T(8,128)(2,1)S(1)} %get-tuple-element.47), channel_id=1, source_target_pairs={{0,2},{2,0},{1,3},{3,1},{4,6},{6,4},{5,7},{7,5},{8,10},{10,8},{9,1... | collective-permute-start | bytes 393224 | tf_op jit(solution)/shard_map/ppermute | solution.py:356
  44.6 4.0 %collective-permute-done.10.got_ref = bf16[32,2048]{1,0:T(8,128)(2,1)S(1)} collective-permute-done((bf16[32,2048]{1,0:T(8,128)(2,1)S(1)}, bf16[32,2048]{1,0:T(8,128)(2,1)S(1)}, u32[]{:S(2)}, u32[]{:S(2)}) %collective-permute-start.10) | collective-permute-done | bytes 131104 | tf_op jit(solution)/shard_map/ppermute | solution.py:356
  48.7 0.8 collective-permute-start.11
  49.5 2.5 %collective-permute-start.12 = (bf16[32,2048]{1,0:T(8,128)(2,1)S(1)}, bf16[32,2048]{1,0:T(8,128)(2,1)S(1)}, u32[]{:S(2)}, u32[]{:S(2)}) collective-permute-start(bf16[32,2048]{1,0:T(8,128)(2,1)S(1)} %shard_map.107), channel_id=1, source_target_pairs={{0,4},{1,0},{2,12},{3,8},{4,5},{5,1},{6,13},{7,9},{8,6},{9,2},{10,... | collective-permute-start | bytes 393224 | tf_op jit(solution)/shard_map/ppermute | solution.py:442
  52.0 3.0 %collective-permute-start.13 = (bf16[32,2048]{1,0:T(8,128)(2,1)S(1)}, bf16[32,2048]{1,0:T(8,128)(2,1)S(1)}, u32[]{:S(2)}, u32[]{:S(2)}) collective-permute-start(bf16[32,2048]{1,0:T(8,128)(2,1)S(1)} %shard_map.107), channel_id=1, source_target_pairs={{0,8},{1,12},{2,0},{3,4},{4,9},{5,13},{6,1},{7,5},{8,10},{9,14},{1... | collective-permute-start | bytes 393224 | tf_op jit(solution)/shard_map/ppermute | solution.py:442
  55.0 1.6 %collective-permute-start.14 = (bf16[32,2048]{1,0:T(8,128)(2,1)S(1)}, bf16[32,2048]{1,0:T(8,128)(2,1)S(1)}, u32[]{:S(2)}, u32[]{:S(2)}) collective-permute-start(bf16[32,2048]{1,0:T(8,128)(2,1)S(1)} %shard_map.107), channel_id=1, source_target_pairs={{0,12},{1,8},{2,4},{3,0},{4,13},{5,9},{6,5},{7,1},{8,14},{9,10},{1... | collective-permute-start | bytes 393224 | tf_op jit(solution)/shard_map/ppermute | solution.py:442
  56.8 4.2 %collective-permute-done.13.piece_ref = bf16[32,2048]{1,0:T(8,128)(2,1)S(1)} collective-permute-done((bf16[32,2048]{1,0:T(8,128)(2,1)S(1)}, bf16[32,2048]{1,0:T(8,128)(2,1)S(1)}, u32[]{:S(2)}, u32[]{:S(2)}) %collective-permute-start.13) | collective-permute-done | bytes 131104 | tf_op jit(solution)/shard_map/ppermute | solution.py:442
  61.6 1.6 %shard_map.112 = (f32[64,2176]{1,0:T(8,128)S(1)}, bf16[64,2304]{1,0:T(8,128)(2,1)S(1)}, bf16[128,2048]{1,0:T(8,128)(2,1)S(1)}) custom-call(bf16[32,2048]{1,0:T(8,128)(2,1)S(1)} %get-tuple-element.48.refs_0_, bf16[32,2048]{1,0:T(8,128)(2,1)S(1)} %get-tuple-element.49.refs_1_, bf16[32,2048]{1,0:T(8,128)(2,1)S(1)} %get-tuple-element.50.refs_2_, ...), custom_call_target="tpu_custom_call" | custom-call | flops 3000000000 | bytes 31326208 | tf_op jit(solution)/shard_map/pallas_call | solution.py:40
  63.1 2.7 %collective-permute-start.15 = (bf16[64,2304]{1,0:T(8,128)(2,1)S(1)}, bf16[64,2304]{1,0:T(8,128)(2,1)S(1)}, u32[]{:S(2)}, u32[]{:S(2)}) collective-permute-start(bf16[64,2304]{1,0:T(8,128)(2,1)S(1)} %get-tuple-element.57), channel_id=1, source_target_pairs={{0,1},{1,0},{2,3},{3,2},{4,5},{5,4},{6,7},{7,6},{8,9},{9,8},{10,11... | collective-permute-start | bytes 884744 | tf_op jit(solution)/shard_map/ppermute | solution.py:356
  65.8 1.5 %shard_map.115 = (f32[64,2560]{1,0:T(8,128)S(1)}, bf16[64,2560]{1,0:T(8,128)(2,1)S(1)}) custom-call(bf16[128,2048]{1,0:T(8,128)(2,1)S(1)} %get-tuple-element.61.rows_ref, bf16[2048,3584]{1,0:T(8,128)(2,1)S(1)} %bitcast.2, bf16[2048,3584]{1,0:T(8,128)(2,1)S(1)} %bitcast.4), custom_call_target="tpu_custom_call" | custom-call | flops 3000000000 | bytes 30867456 | tf_op jit(solution)/shard_map/pallas_call | solution.py:40
  67.4 1.5 %shard_map.118 = (f32[64,2560]{1,0:T(8,128)S(1)}, bf16[64,2560]{1,0:T(8,128)(2,1)S(1)}) custom-call(bf16[128,2048]{1,0:T(8,128)(2,1)S(1)} %get-tuple-element.61.rows_ref, bf16[2048,3584]{1,0:T(8,128)(2,1)S(1)} %bitcast.2, bf16[2048,3584]{1,0:T(8,128)(2,1)S(1)} %bitcast.4), custom_call_target="tpu_custom_call" | custom-call | flops 3000000000 | bytes 30867456 | tf_op jit(solution)/shard_map/pallas_call | solution.py:40
  69.6 4.5 %collective-permute-start.16 = (bf16[32,2304]{1,0:T(8,128)(2,1)S(1)}, bf16[32,2304]{1,0:T(8,128)(2,1)S(1)}, u32[]{:S(2)}, u32[]{:S(2)}) collective-permute-start(bf16[32,2304]{1,0:T(8,128)(2,1)S(1)} %get-tuple-element.59), channel_id=1, source_target_pairs={{0,2},{2,0},{1,3},{3,1},{4,6},{6,4},{5,7},{7,5},{8,10},{10,8},{9,1... | collective-permute-start | bytes 442376 | tf_op jit(solution)/shard_map/ppermute | solution.py:356
  74.3 2.1 %collective-permute-start.23 = (bf16[32,2560]{1,0:T(8,128)(2,1)S(1)}, bf16[32,2560]{1,0:T(8,128)(2,1)S(1)}, u32[]{:S(2)}, u32[]{:S(2)}) collective-permute-start(bf16[32,2560]{1,0:T(8,128)(2,1)S(1)} %get-tuple-element.69), channel_id=1, source_target_pairs={{0,2},{2,0},{1,3},{3,1},{4,6},{6,4},{5,7},{7,5},{8,10},{10,8},{9,1... | collective-permute-start | bytes 491528 | tf_op jit(solution)/shard_map/ppermute | solution.py:356
  76.3 2.4 %collective-permute-done.16.got_ref = bf16[32,2304]{1,0:T(8,128)(2,1)S(1)} collective-permute-done((bf16[32,2304]{1,0:T(8,128)(2,1)S(1)}, bf16[32,2304]{1,0:T(8,128)(2,1)S(1)}, u32[]{:S(2)}, u32[]{:S(2)}) %collective-permute-start.16) | collective-permute-done | bytes 147488 | tf_op jit(solution)/shard_map/ppermute | solution.py:356
  78.8 2.1 %collective-permute-start.28 = (bf16[32,1024]{1,0:T(8,128)(2,1)S(1)}, bf16[32,1024]{1,0:T(8,128)(2,1)S(1)}, u32[]{:S(2)}, u32[]{:S(2)}) collective-permute-start(bf16[32,1024]{1,0:T(8,128)(2,1)S(1)} %get-tuple-element.70.refs_0_), channel_id=1, source_target_pairs={{0,2},{2,0},{1,3},{3,1},{4,6},{6,4},{5,7},{7,5},{8,10},{10,8},{9,1... | collective-permute-start | bytes 196616 | tf_op jit(solution)/shard_map/ppermute | solution.py:356
  80.9 1.3 %collective-permute-done.18.got_ref = bf16[32,2560]{1,0:T(8,128)(2,1)S(1)} collective-permute-done((bf16[32,2560]{1,0:T(8,128)(2,1)S(1)}, bf16[32,2560]{1,0:T(8,128)(2,1)S(1)}, u32[]{:S(2)}, u32[]{:S(2)}) %collective-permute-start.18) | collective-permute-done | bytes 163872 | tf_op jit(solution)/shard_map/ppermute | solution.py:356
  82.4 2.1 %collective-permute-start.20 = (bf16[32,1280]{1,0:T(8,128)(2,1)S(1)}, bf16[32,1280]{1,0:T(8,128)(2,1)S(1)}, u32[]{:S(2)}, u32[]{:S(2)}) collective-permute-start(bf16[32,1280]{1,0:T(8,128)(2,1)S(1)} %shard_map.117.refs_0_), channel_id=1, source_target_pairs={{0,2},{2,0},{1,3},{3,1},{4,6},{6,4},{5,7},{7,5},{8,10},{10,8},{9,1... | collective-permute-start | bytes 245768 | tf_op jit(solution)/shard_map/ppermute | solution.py:356
  84.4 1.3 %collective-permute-done.23.got_ref = bf16[32,2560]{1,0:T(8,128)(2,1)S(1)} collective-permute-done((bf16[32,2560]{1,0:T(8,128)(2,1)S(1)}, bf16[32,2560]{1,0:T(8,128)(2,1)S(1)}, u32[]{:S(2)}, u32[]{:S(2)}) %collective-permute-start.23) | collective-permute-done | bytes 163872 | tf_op jit(solution)/shard_map/ppermute | solution.py:356
  85.9 2.1 %collective-permute-start.25 = (bf16[32,1280]{1,0:T(8,128)(2,1)S(1)}, bf16[32,1280]{1,0:T(8,128)(2,1)S(1)}, u32[]{:S(2)}, u32[]{:S(2)}) collective-permute-start(bf16[32,1280]{1,0:T(8,128)(2,1)S(1)} %shard_map.120.refs_0_), channel_id=1, source_target_pairs={{0,2},{2,0},{1,3},{3,1},{4,6},{6,4},{5,7},{7,5},{8,10},{10,8},{9,1... | collective-permute-start | bytes 245768 | tf_op jit(solution)/shard_map/ppermute | solution.py:356
  88.5 0.7 collective-permute-done.27.refs_1_
  89.7 0.8 collective-permute-done.25.refs_2_
  90.5 0.7 shard_map.121.refs_5_
  91.8 0.9 shard_map.122.refs_5_
  92.7 0.9 shard_map.123
  93.5 2.6 %collective-permute-start.31 = (bf16[32,2048]{1,0:T(8,128)(2,1)S(1)}, bf16[32,2048]{1,0:T(8,128)(2,1)S(1)}, u32[]{:S(2)}, u32[]{:S(2)}) collective-permute-start(bf16[32,2048]{1,0:T(8,128)(2,1)S(1)} %get-tuple-element.74), channel_id=1, source_target_pairs={{0,4},{4,0},{8,12},{12,8},{1,5},{5,1},{9,13},{13,9},{2,6},{6,2},{1... | collective-permute-start | bytes 393224 | tf_op jit(solution)/shard_map/ppermute | solution.py:360
  96.2 4.3 %collective-permute-done.31.got_ref = bf16[32,2048]{1,0:T(8,128)(2,1)S(1)} collective-permute-done((bf16[32,2048]{1,0:T(8,128)(2,1)S(1)}, bf16[32,2048]{1,0:T(8,128)(2,1)S(1)}, u32[]{:S(2)}, u32[]{:S(2)}) %collective-permute-start.31) | collective-permute-done | bytes 131104 | tf_op jit(solution)/shard_map/ppermute | solution.py:360
  100.5 3.6 %collective-permute-start.32 = (bf16[32,2048]{1,0:T(8,128)(2,1)S(1)}, bf16[32,2048]{1,0:T(8,128)(2,1)S(1)}, u32[]{:S(2)}, u32[]{:S(2)}) collective-permute-start(bf16[32,2048]{1,0:T(8,128)(2,1)S(1)} %shard_map.124), channel_id=1, source_target_pairs={{0,8},{4,12},{8,0},{12,4},{1,9},{5,13},{9,1},{13,5},{2,10},{6,14},... | collective-permute-start | bytes 393224 | tf_op jit(solution)/shard_map/ppermute | solution.py:360
  104.1 5.2 %collective-permute-done.32.refs_1_ = bf16[32,2048]{1,0:T(8,128)(2,1)S(1)} collective-permute-done((bf16[32,2048]{1,0:T(8,128)(2,1)S(1)}, bf16[32,2048]{1,0:T(8,128)(2,1)S(1)}, u32[]{:S(2)}, u32[]{:S(2)}) %collective-permute-start.32) | collective-permute-done | bytes 131104 | tf_op jit(solution)/shard_map/ppermute | solution.py:360
  109.4 0.7 shard_map.125
  (82 shorter events, 5.1 us)
Async XLA Ops:
  0.0 8.9 %collective-permute-start = (bf16[32,2048]{1,0:T(8,128)(2,1)}, bf16[32,2048]{1,0:T(8,128)(2,1)S(1)}, u32[]{:S(2)}, u32[]{:S(2)}) collective-permute-start(bf16[32,2048]{1,0:T(8,128)(2,1)} %q_hbm.1), channel_id=1, source_target_pairs={{0,4},{4,0},{8,12},{12,8},{1,5},{5,1},{9,13},{13,9},{2,6},{6,2},{1... | collective-permute-start | bytes 393224 | tf_op jit(solution)/shard_map/ppermute | solution.py:360
  3.1 9.0 %collective-permute-start.2 = (bf16[32,2048]{1,0:T(8,128)(2,1)}, bf16[32,2048]{1,0:T(8,128)(2,1)S(1)}, u32[]{:S(2)}, u32[]{:S(2)}) collective-permute-start(bf16[32,2048]{1,0:T(8,128)(2,1)} %q_hbm.1), channel_id=1, source_target_pairs={{0,8},{4,12},{8,0},{12,4},{1,9},{5,13},{9,1},{13,5},{2,10},{6,14},... | collective-permute-start | bytes 393224 | tf_op jit(solution)/shard_map/ppermute | solution.py:360
  9.7 30.3 %slice-start.12 = ((s8[8388608]{0:T(1024)(128)(4,1)}), s8[4194304]{0:T(1024)(128)(4,1)S(1)}, s32[]{:S(2)}) async-start(s8[8388608]{0:T(1024)(128)(4,1)} %bitcast.11), calls=%async_computation.12 | async-start | bytes 8388608
  9.7 13.4 %collective-permute-start.1 = (bf16[32,2176]{1,0:T(8,128)(2,1)S(1)}, bf16[32,2176]{1,0:T(8,128)(2,1)S(1)}, u32[]{:S(2)}, u32[]{:S(2)}) collective-permute-start(bf16[32,2176]{1,0:T(8,128)(2,1)S(1)} %shard_map.101), channel_id=1, source_target_pairs={{0,4},{4,0},{8,12},{12,8},{1,5},{5,1},{9,13},{13,9},{2,6},{6,2},{1... | collective-permute-start | bytes 417800 | tf_op jit(solution)/shard_map/ppermute | solution.py:360
  12.1 8.2 %collective-permute-start.4 = (bf16[32,2048]{1,0:T(8,128)(2,1)S(1)}, bf16[32,2048]{1,0:T(8,128)(2,1)S(1)}, u32[]{:S(2)}, u32[]{:S(2)}) collective-permute-start(bf16[32,2048]{1,0:T(8,128)(2,1)S(1)} %collective-permute-done.2.q_ref), channel_id=1, source_target_pairs={{0,4},{4,0},{8,12},{12,8},{1,5},{5,1},{9,13},{13,9},{2,6},{6,2},{1... | collective-permute-start | bytes 393224 | tf_op jit(solution)/shard_map/ppermute | solution.py:360
  13.2 26.8 %slice-start.13 = ((s8[8388608]{0:T(1024)(128)(4,1)}), s8[4194304]{0:T(1024)(128)(4,1)S(1)}, s32[]{:S(2)}) async-start(s8[8388608]{0:T(1024)(128)(4,1)} %bitcast.11), calls=%async_computation.13 | async-start | bytes 8388608
  13.3 9.9 %collective-permute-start.3 = (bf16[32,2176]{1,0:T(8,128)(2,1)S(1)}, bf16[32,2176]{1,0:T(8,128)(2,1)S(1)}, u32[]{:S(2)}, u32[]{:S(2)}) collective-permute-start(bf16[32,2176]{1,0:T(8,128)(2,1)S(1)} %shard_map.102), channel_id=1, source_target_pairs={{0,8},{4,12},{8,0},{12,4},{1,9},{5,13},{9,1},{13,5},{2,10},{6,14},... | collective-permute-start | bytes 417800 | tf_op jit(solution)/shard_map/ppermute | solution.py:360
  21.1 6.9 %collective-permute-start.5 = (bf16[32,2176]{1,0:T(8,128)(2,1)S(1)}, bf16[32,2176]{1,0:T(8,128)(2,1)S(1)}, u32[]{:S(2)}, u32[]{:S(2)}) collective-permute-start(bf16[32,2176]{1,0:T(8,128)(2,1)S(1)} %shard_map.103), channel_id=1, source_target_pairs={{0,12},{4,8},{8,4},{12,0},{1,13},{5,9},{9,5},{13,1},{2,14},{6,10},... | collective-permute-start | bytes 417800 | tf_op jit(solution)/shard_map/ppermute | solution.py:360
  28.5 6.5 %collective-permute-start.7 = (bf16[32,2048]{1,0:T(8,128)(2,1)S(1)}, bf16[32,2048]{1,0:T(8,128)(2,1)S(1)}, u32[]{:S(2)}, u32[]{:S(2)}) collective-permute-start(bf16[32,2048]{1,0:T(8,128)(2,1)S(1)} %shard_map.104.refs_0_), channel_id=1, source_target_pairs={{0,8},{4,12},{8,0},{12,4},{1,9},{5,13},{9,1},{13,5},{2,10},{6,14},... | collective-permute-start | bytes 393224 | tf_op jit(solution)/shard_map/ppermute | solution.py:360
  29.8 7.5 %collective-permute-start.6 = (bf16[32,2048]{1,0:T(8,128)(2,1)S(1)}, bf16[32,2048]{1,0:T(8,128)(2,1)S(1)}, u32[]{:S(2)}, u32[]{:S(2)}) collective-permute-start(bf16[32,2048]{1,0:T(8,128)(2,1)S(1)} %shard_map.104.refs_0_), channel_id=1, source_target_pairs={{0,4},{4,0},{8,12},{12,8},{1,5},{5,1},{9,13},{13,9},{2,6},{6,2},{1... | collective-permute-start | bytes 393224 | tf_op jit(solution)/shard_map/ppermute | solution.py:360
  35.0 5.0 %collective-permute-start.8 = (bf16[32,2048]{1,0:T(8,128)(2,1)S(1)}, bf16[32,2048]{1,0:T(8,128)(2,1)S(1)}, u32[]{:S(2)}, u32[]{:S(2)}) collective-permute-start(bf16[32,2048]{1,0:T(8,128)(2,1)S(1)} %collective-permute-done.7.refs_2_), channel_id=1, source_target_pairs={{0,4},{4,0},{8,12},{12,8},{1,5},{5,1},{9,13},{13,9},{2,6},{6,2},{1... | collective-permute-start | bytes 393224 | tf_op jit(solution)/shard_map/ppermute | solution.py:360
  41.3 7.3 %copy-start.1 = (bf16[32,2048]{1,0:T(8,128)(2,1)S(1)}, bf16[32,2048]{1,0:T(8,128)(2,1)}, u32[]{:S(2)}) copy-start(bf16[32,2048]{1,0:T(8,128)(2,1)} %stream_ref.1) | copy-start | bytes 393220
  41.3 1.6 %collective-permute-start.9 = (bf16[64,2048]{1,0:T(8,128)(2,1)S(1)}, bf16[64,2048]{1,0:T(8,128)(2,1)S(1)}, u32[]{:S(2)}, u32[]{:S(2)}) collective-permute-start(bf16[64,2048]{1,0:T(8,128)(2,1)S(1)} %get-tuple-element.45), channel_id=1, source_target_pairs={{0,1},{1,0},{2,3},{3,2},{4,5},{5,4},{6,7},{7,6},{8,9},{9,8},{10,11... | collective-permute-start | bytes 786440 | tf_op jit(solution)/shard_map/ppermute | solution.py:356
  42.9 18.5 %slice-start = ((s8[14680064]{0:T(1024)(128)(4,1)}), s8[4194304]{0:T(1024)(128)(4,1)S(1)}, s32[]{:S(2)}) async-start(s8[14680064]{0:T(1024)(128)(4,1)} %bitcast.1), calls=%async_computation | async-start | bytes 8388608
  42.9 18.5 %slice-start.1 = ((s8[14680064]{0:T(1024)(128)(4,1)}), s8[4194304]{0:T(1024)(128)(4,1)S(1)}, s32[]{:S(2)}) async-start(s8[14680064]{0:T(1024)(128)(4,1)} %bitcast.1), calls=%async_computation.1 | async-start | bytes 8388608
  42.9 18.5 %slice-start.4 = ((s8[14680064]{0:T(1024)(128)(4,1)}), s8[2097152]{0:T(1024)(128)(4,1)S(1)}, s32[]{:S(2)}) async-start(s8[14680064]{0:T(1024)(128)(4,1)} %bitcast.3), calls=%async_computation.4 | async-start | bytes 4194304
  42.9 18.5 %slice-start.5 = ((s8[14680064]{0:T(1024)(128)(4,1)}), s8[4194304]{0:T(1024)(128)(4,1)S(1)}, s32[]{:S(2)}) async-start(s8[14680064]{0:T(1024)(128)(4,1)} %bitcast.3), calls=%async_computation.5 | async-start | bytes 8388608
  43.0 13.6 %copy-start = (f32[8192]{0:T(1024)S(1)}, f32[8192]{0:T(1024)}, u32[]{:S(2)}) copy-start(f32[8192]{0:T(1024)} %param.16) | copy-start | bytes 98308
  43.0 5.6 %collective-permute-start.10 = (bf16[32,2048]{1,0:T(8,128)(2,1)S(1)}, bf16[32,2048]{1,0:T(8,128)(2,1)S(1)}, u32[]{:S(2)}, u32[]{:S(2)}) collective-permute-start(bf16[32,2048]{1,0:T(8,128)(2,1)S(1)} %get-tuple-element.47), channel_id=1, source_target_pairs={{0,2},{2,0},{1,3},{3,1},{4,6},{6,4},{5,7},{7,5},{8,10},{10,8},{9,1... | collective-permute-start | bytes 393224 | tf_op jit(solution)/shard_map/ppermute | solution.py:356
  48.6 12.9 %slice-start.2 = ((s8[14680064]{0:T(1024)(128)(4,1)}), s8[4194304]{0:T(1024)(128)(4,1)S(1)}, s32[]{:S(2)}) async-start(s8[14680064]{0:T(1024)(128)(4,1)} %bitcast.1), calls=%async_computation.2 | async-start | bytes 8388608
  48.6 12.9 %slice-start.3 = ((s8[14680064]{0:T(1024)(128)(4,1)}), s8[2097152]{0:T(1024)(128)(4,1)S(1)}, s32[]{:S(2)}) async-start(s8[14680064]{0:T(1024)(128)(4,1)} %bitcast.1), calls=%async_computation.3 | async-start | bytes 4194304
  48.6 12.9 %slice-start.6 = ((s8[14680064]{0:T(1024)(128)(4,1)}), s8[4194304]{0:T(1024)(128)(4,1)S(1)}, s32[]{:S(2)}) async-start(s8[14680064]{0:T(1024)(128)(4,1)} %bitcast.3), calls=%async_computation.6 | async-start | bytes 8388608
  48.6 12.9 %slice-start.7 = ((s8[14680064]{0:T(1024)(128)(4,1)}), s8[4194304]{0:T(1024)(128)(4,1)S(1)}, s32[]{:S(2)}) async-start(s8[14680064]{0:T(1024)(128)(4,1)} %bitcast.3), calls=%async_computation.7 | async-start | bytes 8388608
  48.7 7.9 %collective-permute-start.11 = (bf16[32,2048]{1,0:T(8,128)(2,1)S(1)}, bf16[32,2048]{1,0:T(8,128)(2,1)S(1)}, u32[]{:S(2)}, u32[]{:S(2)}) collective-permute-start(bf16[32,2048]{1,0:T(8,128)(2,1)S(1)} %shard_map.107), channel_id=1, source_target_pairs={{0,0},{1,4},{2,8},{3,12},{4,1},{5,5},{6,9},{7,13},{8,2},{9,6},{10,... | collective-permute-start | bytes 393224 | tf_op jit(solution)/shard_map/ppermute | solution.py:442
  49.5 7.2 %collective-permute-start.12 = (bf16[32,2048]{1,0:T(8,128)(2,1)S(1)}, bf16[32,2048]{1,0:T(8,128)(2,1)S(1)}, u32[]{:S(2)}, u32[]{:S(2)}) collective-permute-start(bf16[32,2048]{1,0:T(8,128)(2,1)S(1)} %shard_map.107), channel_id=1, source_target_pairs={{0,4},{1,0},{2,12},{3,8},{4,5},{5,1},{6,13},{7,9},{8,6},{9,2},{10,... | collective-permute-start | bytes 393224 | tf_op jit(solution)/shard_map/ppermute | solution.py:442
  52.0 9.1 %collective-permute-start.13 = (bf16[32,2048]{1,0:T(8,128)(2,1)S(1)}, bf16[32,2048]{1,0:T(8,128)(2,1)S(1)}, u32[]{:S(2)}, u32[]{:S(2)}) collective-permute-start(bf16[32,2048]{1,0:T(8,128)(2,1)S(1)} %shard_map.107), channel_id=1, source_target_pairs={{0,8},{1,12},{2,0},{3,4},{4,9},{5,13},{6,1},{7,5},{8,10},{9,14},{1... | collective-permute-start | bytes 393224 | tf_op jit(solution)/shard_map/ppermute | solution.py:442
  55.0 6.4 %collective-permute-start.14 = (bf16[32,2048]{1,0:T(8,128)(2,1)S(1)}, bf16[32,2048]{1,0:T(8,128)(2,1)S(1)}, u32[]{:S(2)}, u32[]{:S(2)}) collective-permute-start(bf16[32,2048]{1,0:T(8,128)(2,1)S(1)} %shard_map.107), channel_id=1, source_target_pairs={{0,12},{1,8},{2,4},{3,0},{4,13},{5,9},{6,5},{7,1},{8,14},{9,10},{1... | collective-permute-start | bytes 393224 | tf_op jit(solution)/shard_map/ppermute | solution.py:442
  63.1 6.4 %collective-permute-start.15 = (bf16[64,2304]{1,0:T(8,128)(2,1)S(1)}, bf16[64,2304]{1,0:T(8,128)(2,1)S(1)}, u32[]{:S(2)}, u32[]{:S(2)}) collective-permute-start(bf16[64,2304]{1,0:T(8,128)(2,1)S(1)} %get-tuple-element.57), channel_id=1, source_target_pairs={{0,1},{1,0},{2,3},{3,2},{4,5},{5,4},{6,7},{7,6},{8,9},{9,8},{10,11... | collective-permute-start | bytes 884744 | tf_op jit(solution)/shard_map/ppermute | solution.py:356
  67.3 6.7 %collective-permute-start.17 = (bf16[64,2560]{1,0:T(8,128)(2,1)S(1)}, bf16[64,2560]{1,0:T(8,128)(2,1)S(1)}, u32[]{:S(2)}, u32[]{:S(2)}) collective-permute-start(bf16[64,2560]{1,0:T(8,128)(2,1)S(1)} %get-tuple-element.63), channel_id=1, source_target_pairs={{0,1},{1,0},{2,3},{3,2},{4,5},{5,4},{6,7},{7,6},{8,9},{9,8},{10,11... | collective-permute-start | bytes 983048 | tf_op jit(solution)/shard_map/ppermute | solution.py:356
  69.0 5.2 %collective-permute-start.22 = (bf16[64,2560]{1,0:T(8,128)(2,1)S(1)}, bf16[64,2560]{1,0:T(8,128)(2,1)S(1)}, u32[]{:S(2)}, u32[]{:S(2)}) collective-permute-start(bf16[64,2560]{1,0:T(8,128)(2,1)S(1)} %get-tuple-element.67), channel_id=1, source_target_pairs={{0,1},{1,0},{2,3},{3,2},{4,5},{5,4},{6,7},{7,6},{8,9},{9,8},{10,11... | collective-permute-start | bytes 983048 | tf_op jit(solution)/shard_map/ppermute | solution.py:356
  69.6 9.2 %collective-permute-start.16 = (bf16[32,2304]{1,0:T(8,128)(2,1)S(1)}, bf16[32,2304]{1,0:T(8,128)(2,1)S(1)}, u32[]{:S(2)}, u32[]{:S(2)}) collective-permute-start(bf16[32,2304]{1,0:T(8,128)(2,1)S(1)} %get-tuple-element.59), channel_id=1, source_target_pairs={{0,2},{2,0},{1,3},{3,1},{4,6},{6,4},{5,7},{7,5},{8,10},{10,8},{9,1... | collective-permute-start | bytes 442376 | tf_op jit(solution)/shard_map/ppermute | solution.py:356
  74.1 8.1 %collective-permute-start.18 = (bf16[32,2560]{1,0:T(8,128)(2,1)S(1)}, bf16[32,2560]{1,0:T(8,128)(2,1)S(1)}, u32[]{:S(2)}, u32[]{:S(2)}) collective-permute-start(bf16[32,2560]{1,0:T(8,128)(2,1)S(1)} %get-tuple-element.65), channel_id=1, source_target_pairs={{0,2},{2,0},{1,3},{3,1},{4,6},{6,4},{5,7},{7,5},{8,10},{10,8},{9,1... | collective-permute-start | bytes 491528 | tf_op jit(solution)/shard_map/ppermute | solution.py:356
  74.3 11.5 %collective-permute-start.23 = (bf16[32,2560]{1,0:T(8,128)(2,1)S(1)}, bf16[32,2560]{1,0:T(8,128)(2,1)S(1)}, u32[]{:S(2)}, u32[]{:S(2)}) collective-permute-start(bf16[32,2560]{1,0:T(8,128)(2,1)S(1)} %get-tuple-element.69), channel_id=1, source_target_pairs={{0,2},{2,0},{1,3},{3,1},{4,6},{6,4},{5,7},{7,5},{8,10},{10,8},{9,1... | collective-permute-start | bytes 491528 | tf_op jit(solution)/shard_map/ppermute | solution.py:356
  78.7 11.7 %slice-start.8 = ((s8[14680064]{0:T(1024)(128)(4,1)}), s8[4194304]{0:T(1024)(128)(4,1)S(1)}, s32[]{:S(2)}) async-start(s8[14680064]{0:T(1024)(128)(4,1)} %bitcast.5), calls=%async_computation.8 | async-start | bytes 8388608
  78.8 11.7 %slice-start.9 = ((s8[14680064]{0:T(1024)(128)(4,1)}), s8[4194304]{0:T(1024)(128)(4,1)S(1)}, s32[]{:S(2)}) async-start(s8[14680064]{0:T(1024)(128)(4,1)} %bitcast.5), calls=%async_computation.9 | async-start | bytes 8388608
  78.8 9.1 %collective-permute-start.28 = (bf16[32,1024]{1,0:T(8,128)(2,1)S(1)}, bf16[32,1024]{1,0:T(8,128)(2,1)S(1)}, u32[]{:S(2)}, u32[]{:S(2)}) collective-permute-start(bf16[32,1024]{1,0:T(8,128)(2,1)S(1)} %get-tuple-element.70.refs_0_), channel_id=1, source_target_pairs={{0,2},{2,0},{1,3},{3,1},{4,6},{6,4},{5,7},{7,5},{8,10},{10,8},{9,1... | collective-permute-start | bytes 196616 | tf_op jit(solution)/shard_map/ppermute | solution.py:356
  82.3 8.2 %slice-start.10 = ((s8[14680064]{0:T(1024)(128)(4,1)}), s8[4194304]{0:T(1024)(128)(4,1)S(1)}, s32[]{:S(2)}) async-start(s8[14680064]{0:T(1024)(128)(4,1)} %bitcast.5), calls=%async_computation.10 | async-start | bytes 8388608
  82.4 7.0 %collective-permute-start.20 = (bf16[32,1280]{1,0:T(8,128)(2,1)S(1)}, bf16[32,1280]{1,0:T(8,128)(2,1)S(1)}, u32[]{:S(2)}, u32[]{:S(2)}) collective-permute-start(bf16[32,1280]{1,0:T(8,128)(2,1)S(1)} %shard_map.117.refs_0_), channel_id=1, source_target_pairs={{0,2},{2,0},{1,3},{3,1},{4,6},{6,4},{5,7},{7,5},{8,10},{10,8},{9,1... | collective-permute-start | bytes 245768 | tf_op jit(solution)/shard_map/ppermute | solution.py:356
  85.9 4.6 %collective-permute-start.25 = (bf16[32,1280]{1,0:T(8,128)(2,1)S(1)}, bf16[32,1280]{1,0:T(8,128)(2,1)S(1)}, u32[]{:S(2)}, u32[]{:S(2)}) collective-permute-start(bf16[32,1280]{1,0:T(8,128)(2,1)S(1)} %shard_map.120.refs_0_), channel_id=1, source_target_pairs={{0,2},{2,0},{1,3},{3,1},{4,6},{6,4},{5,7},{7,5},{8,10},{10,8},{9,1... | collective-permute-start | bytes 245768 | tf_op jit(solution)/shard_map/ppermute | solution.py:356
  88.0 1.3 %collective-permute-start.27 = (bf16[32,1024]{1,0:T(8,128)(2,1)S(1)}, bf16[32,1024]{1,0:T(8,128)(2,1)S(1)}, u32[]{:S(2)}, u32[]{:S(2)}) collective-permute-start(bf16[32,1024]{1,0:T(8,128)(2,1)S(1)} %get-tuple-element.70.refs_0_), channel_id=1, source_target_pairs={{0,1},{1,0},{2,3},{3,2},{4,5},{5,4},{6,7},{7,6},{8,9},{9,8},{10,11... | collective-permute-start | bytes 196616 | tf_op jit(solution)/shard_map/ppermute | solution.py:356
  88.0 2.5 %collective-permute-start.29 = (bf16[32,1024]{1,0:T(8,128)(2,1)S(1)}, bf16[32,1024]{1,0:T(8,128)(2,1)S(1)}, u32[]{:S(2)}, u32[]{:S(2)}) collective-permute-start(bf16[32,1024]{1,0:T(8,128)(2,1)S(1)} %collective-permute-done.28.refs_2_), channel_id=1, source_target_pairs={{0,1},{1,0},{2,3},{3,2},{4,5},{5,4},{6,7},{7,6},{8,9},{9,8},{10,11... | collective-permute-start | bytes 196616 | tf_op jit(solution)/shard_map/ppermute | solution.py:356
  88.5 4.2 %collective-permute-start.19 = (bf16[32,1280]{1,0:T(8,128)(2,1)S(1)}, bf16[32,1280]{1,0:T(8,128)(2,1)S(1)}, u32[]{:S(2)}, u32[]{:S(2)}) collective-permute-start(bf16[32,1280]{1,0:T(8,128)(2,1)S(1)} %shard_map.117.refs_0_), channel_id=1, source_target_pairs={{0,1},{1,0},{2,3},{3,2},{4,5},{5,4},{6,7},{7,6},{8,9},{9,8},{10,11... | collective-permute-start | bytes 245768 | tf_op jit(solution)/shard_map/ppermute | solution.py:356
  89.2 2.1 %collective-permute-start.24 = (bf16[32,1280]{1,0:T(8,128)(2,1)S(1)}, bf16[32,1280]{1,0:T(8,128)(2,1)S(1)}, u32[]{:S(2)}, u32[]{:S(2)}) collective-permute-start(bf16[32,1280]{1,0:T(8,128)(2,1)S(1)} %shard_map.120.refs_0_), channel_id=1, source_target_pairs={{0,1},{1,0},{2,3},{3,2},{4,5},{5,4},{6,7},{7,6},{8,9},{9,8},{10,11... | collective-permute-start | bytes 245768 | tf_op jit(solution)/shard_map/ppermute | solution.py:356
  89.4 3.3 %collective-permute-start.21 = (bf16[32,1280]{1,0:T(8,128)(2,1)S(1)}, bf16[32,1280]{1,0:T(8,128)(2,1)S(1)}, u32[]{:S(2)}, u32[]{:S(2)}) collective-permute-start(bf16[32,1280]{1,0:T(8,128)(2,1)S(1)} %collective-permute-done.20.refs_2_), channel_id=1, source_target_pairs={{0,1},{1,0},{2,3},{3,2},{4,5},{5,4},{6,7},{7,6},{8,9},{9,8},{10,11... | collective-permute-start | bytes 245768 | tf_op jit(solution)/shard_map/ppermute | solution.py:356
  90.5 1.3 %collective-permute-start.26 = (bf16[32,1280]{1,0:T(8,128)(2,1)S(1)}, bf16[32,1280]{1,0:T(8,128)(2,1)S(1)}, u32[]{:S(2)}, u32[]{:S(2)}) collective-permute-start(bf16[32,1280]{1,0:T(8,128)(2,1)S(1)} %collective-permute-done.25.refs_2_), channel_id=1, source_target_pairs={{0,1},{1,0},{2,3},{3,2},{4,5},{5,4},{6,7},{7,6},{8,9},{9,8},{10,11... | collective-permute-start | bytes 245768 | tf_op jit(solution)/shard_map/ppermute | solution.py:356
  93.5 6.9 %collective-permute-start.31 = (bf16[32,2048]{1,0:T(8,128)(2,1)S(1)}, bf16[32,2048]{1,0:T(8,128)(2,1)S(1)}, u32[]{:S(2)}, u32[]{:S(2)}) collective-permute-start(bf16[32,2048]{1,0:T(8,128)(2,1)S(1)} %get-tuple-element.74), channel_id=1, source_target_pairs={{0,4},{4,0},{8,12},{12,8},{1,5},{5,1},{9,13},{13,9},{2,6},{6,2},{1... | collective-permute-start | bytes 393224 | tf_op jit(solution)/shard_map/ppermute | solution.py:360
  96.1 8.0 %collective-permute-start.30 = (bf16[32,2048]{1,0:T(8,128)(2,1)S(1)}, bf16[32,2048]{1,0:T(8,128)(2,1)S(1)}, u32[]{:S(2)}, u32[]{:S(2)}) collective-permute-start(bf16[32,2048]{1,0:T(8,128)(2,1)S(1)} %get-tuple-element.72), channel_id=1, source_target_pairs={{0,4},{4,0},{8,12},{12,8},{1,5},{5,1},{9,13},{13,9},{2,6},{6,2},{1... | collective-permute-start | bytes 393224 | tf_op jit(solution)/shard_map/ppermute | solution.py:360
  100.5 8.9 %collective-permute-start.32 = (bf16[32,2048]{1,0:T(8,128)(2,1)S(1)}, bf16[32,2048]{1,0:T(8,128)(2,1)S(1)}, u32[]{:S(2)}, u32[]{:S(2)}) collective-permute-start(bf16[32,2048]{1,0:T(8,128)(2,1)S(1)} %shard_map.124), channel_id=1, source_target_pairs={{0,8},{4,12},{8,0},{12,4},{1,9},{5,13},{9,1},{13,5},{2,10},{6,14},... | collective-permute-start | bytes 393224 | tf_op jit(solution)/shard_map/ppermute | solution.py:360
  (2 other events, 5.4 us)

commit v4 on v2

--- a/solution.py
+++ b/solution.py
@@ -161,8 +161,7 @@
 
 
 def blend_kernel(*refs):
-    out_ref = refs[-1]
-    parts = refs[:-1]
+    parts, (out_ref, low_ref, high_ref) = refs[:-3], refs[-3:]
     heads = out_ref.shape[1] // DH
     logs = []
     for part in parts:
@@ -176,10 +175,13 @@
     shares = [share / total for share in shares]
     for head in range(heads):
         span = slice(head * DH, (head + 1) * DH)
-        out_ref[:, span] = functools.reduce(
+        value = functools.reduce(
             jnp.add,
             [share[:, head : head + 1] * part[:, span].astype(F32) for share, part in zip(shares, parts)],
         ).astype(BF16)
+        out_ref[:, span] = value
+        at = head * DH % low_ref.shape[1]
+        (low_ref if head * 2 < heads else high_ref)[:, at : at + DH] = value
 
 
 def place():
@@ -209,8 +211,11 @@
 def project_kernel(tile, *refs):
     pieces, (weight_ref, keep_ref, send_ref, rows_ref) = refs[:-4], refs[-4:]
     rows = pieces[0].shape[0]
-    for n, piece in enumerate(pieces):
-        rows_ref[pl.ds(place_of(n, rows, len(pieces)), rows), :] = piece[...]
+    half = pieces[2].shape[1]
+    for n, parts in enumerate((pieces[:1], pieces[1:2], pieces[2:4], pieces[4:6])):
+        at = pl.ds(place_of(n, rows, 4), rows)
+        for i, part in enumerate(parts):
+            rows_ref[at, i * half : i * half + part.shape[1]] = part[...]
     product(rows_ref, weight_ref, 0, keep_ref, send_ref, 0, weight_ref.shape[1], tile)
 
 
@@ -323,29 +328,39 @@
         out_ref[:, columns] = part
 
 
-def down_kernel(tile, *refs):
-    pieces, (weight_ref, so_far_ref, own_ref) = refs[:4], refs[4:7]
-    sends, rows_ref = refs[7:-1], refs[-1]
+def down_kernel(tile, first, *refs):
+    pieces, (weight_ref, so_far_ref) = refs[:4], refs[4:6]
+    given, (own_ref, *sends, rows_ref) = refs[6:-5], refs[-5:]
+    for ref in given:
+        sends[0][:, :first] = ref[...]
     gather_rows(pieces, rows_ref)
     rows = pieces[0].shape[0]
     depth = rows_ref.shape[1]
     start = weight_ref.shape[0] - depth
-    for at in range(0, weight_ref.shape[1], tile):
-        columns = slice(at, at + tile)
-        part = so_far_ref[:, columns] + jnp.dot(
-            rows_ref[...], weight_ref[start:, columns], preferred_element_type=F32
-        )
-        own_ref[:, columns] = part[:rows]
+    for at in range(0, own_ref.shape[1], tile):
+        source = slice(first + at, first + at + tile)
+        target = slice(at, at + tile)
+        part = so_far_ref[:, source] + jnp.dot(
+            rows_ref[...], weight_ref[start:, source], preferred_element_type=F32
+        )
+        own_ref[:, target] = part[:rows]
         for n, send in enumerate(sends):
-            send[:, columns] = part[(n + 1) * rows : (n + 2) * rows].astype(BF16)
-
-
-def final_kernel(middle_ref, own_ref, *refs):
-    parts, out_ref = refs[:-1], refs[-1]
-    total = own_ref[...]
-    for part in parts:
-        total = total + part[...].astype(F32)
-    out_ref[...] = (middle_ref[...].astype(F32) + total).astype(BF16)
+            place_at = source if send.shape[1] > own_ref.shape[1] else target
+            send[:, place_at] = part[(n + 1) * rows : (n + 2) * rows].astype(send.dtype)
+
+
+def add_kernel(own_ref, got_ref, out_ref):
+    out_ref[...] = (own_ref[...] + got_ref[...].astype(F32)).astype(BF16)
+
+
+def final_kernel(middle_ref, near_ref, *refs):
+    owns, fars, out_ref = refs[:2], refs[2:4], refs[4]
+    start = 0
+    for own, far in zip(owns, fars):
+        columns = slice(start, start + own.shape[1])
+        total = own[...] + near_ref[:, columns].astype(F32) + far[...].astype(F32)
+        out_ref[:, columns] = (middle_ref[:, columns].astype(F32) + total).astype(BF16)
+        start += own.shape[1]
 
 
 def swap(x, axis):
@@ -407,19 +422,24 @@
         )
     back = {m: turn(partial[m], CTX, n_context, m) for m in order}
     back[0] = partial[0]
-    blended = call(
-        blend_kernel, struct((rows, heads_width), BF16), [VM] * 4, tuple(back[m] for m in range(4))
-    )
-
-    attention = {m: turn(blended, CTX, n_context, m) for m in (2, 1)}
-    attention[3] = turn(attention[2], CTX, n_context, 1)
-    attention[0] = blended
+    low = struct((rows, heads_width // 2), BF16)
+    blended, *halves = call(
+        blend_kernel,
+        (struct((rows, heads_width), BF16), low, low),
+        [VM] * 4,
+        tuple(back[m] for m in range(4)),
+    )
+
+    beside = turn(blended, CTX, n_context, 1)
+    across = [turn(h, CTX, n_context, 2) for h in halves]
+    relayed = [turn(h, CTX, n_context, 1) for h in across]
+    attention = (blended, beside, *across, *relayed)
     width = out_weight.shape[1]
     keep, away = call(
         functools.partial(project_kernel, 512),
         (struct((n_head * rows, width), F32), struct((n_head * rows, width), BF16)),
-        [VM] * 5,
-        tuple(attention[m] for m in range(4)) + (in_vmem(out_weight),),
+        [VM] * 7,
+        attention + (in_vmem(out_weight),),
         scratch=[pltpu.VMEM((total, heads_width), BF16)],
         cost=6,
     )
@@ -521,16 +541,31 @@
                 scratch=[pltpu.VMEM((total, chunk), BF16)],
             ),
         )
-    res = call(
-        functools.partial(down_kernel, 512),
-        (struct((rows, out_width), F32),) + (struct((rows, out_width), BF16),) * 3,
+    half = out_width // 2
+    owns, fars = [], []
+    near = ()
+    for n in range(2):
+        own, beside, two, three = call(
+            functools.partial(down_kernel, 512, n * half),
+            tuple(
+                struct((rows, w), t)
+                for w, t in ((half, F32), ((n + 1) * half, BF16), (half, F32), (half, BF16))
+            ),
+            [VM] * (6 + n),
+            hidden[-1] + (down_vmem,) + so_far + near,
+            scratch=[pltpu.VMEM((total, chunks[-1][1]), BF16)],
+        )
+        near = (beside,)
+        pair = call(
+            add_kernel, struct((rows, half), BF16), [VM] * 2, (two, turn(three, CTX, n_context, 1))
+        )
+        owns.append(own)
+        fars.append(turn(pair, CTX, n_context, 2))
+    return call(
+        final_kernel,
+        struct((rows, out_width), BF16),
         [VM] * 6,
-        hidden[-1] + (down_vmem,) + so_far,
-        scratch=[pltpu.VMEM((total, chunks[-1][1]), BF16)],
-    )
-    parts = [turn(res[m], CTX, n_context, m) for m in order]
-    return call(
-        final_kernel, struct((rows, out_width), BF16), [VM] * 5, (all_middle[0], res[0]) + tuple(parts)
+        (all_middle[0], turn(near[0], CTX, n_context, 1), *owns, *fars),
     )
 
 

time: 111 us -> 110 us (level)
  waiting for transfers between devices: 47.8 us -> 42.6 us
  starting transfers between devices: 46.1 us -> 50.7 us
    ppermute x12 -> x16, waiting for transfers between devices: 30.8 us -> 23.7 us  [turn(): return lax.ppermute(x, axis, [(i, i ^ offset) for i in range(n)])]
    ppermute x12 -> x16, starting transfers between devices: 19.3 us -> 25.1 us  [turn(): return lax.ppermute(x, axis, [(i, i ^ offset) for i in range(n)])]
    ppermute x4, waiting for transfers between devices: 4.38 us -> 6.3 us  [direct_body(): lax.ppermute(middle, ALL, [(a * n_context + b, (b ^ m) * n_context + a) f...]
    pallas_call x25 -> x28, Pallas kernels: 15.6 us -> 15.8 us  [call(): pl.pallas_call(kernel, out_shape=out, in_specs=in_specs, out_specs=jax.tr...]
  transfers between devices with their start and end apart: 33 -> 37, of which waited for: 18 -> 18; matrix products, arithmetic and copies ran while one was open for 0% -> 0% of each run, Pallas kernels for 9% -> 10%
where the time goes in v4:
time: 110 us
  starting transfers between devices  50.7 us (46%)
  waiting for transfers between devices  42.6 us (39%)
  Pallas kernels  15.8 us (14%)
    ppermute x16, starting transfers between devices, turn(): return lax.ppermute(x, axis, [(i, i ^ offset) for i in range(n)])  25.1 us
    ppermute x16, waiting for transfers between devices, turn(): return lax.ppermute(x, axis, [(i, i ^ offset) for i in range(n)])  23.7 us
    ppermute x17, starting transfers between devices, swap(): return lax.ppermute(x, axis, [(0, 1), (1, 0)])  18.2 us
    pallas_call x28, Pallas kernels, call(): pl.pallas_call(kernel, out_shape=out, in_specs=in_specs, out_specs=jax.tr...  15.8 us
    ppermute x17, waiting for transfers between devices, swap(): return lax.ppermute(x, axis, [(0, 1), (1, 0)])  12.6 us
    ppermute x4, starting transfers between devices, direct_body(): lax.ppermute(middle, ALL, [(a * n_context + b, (b ^ m) * n_context + a) f...  7.45 us
    ppermute x4, waiting for transfers between devices, direct_body(): lax.ppermute(middle, ALL, [(a * n_context + b, (b ^ m) * n_context + a) f...  6.3 us
  transfers between devices with their start and end apart: 37, of which 18 were waited for; matrix products, arithmetic and copies ran while one was open for 0% of the time, Pallas kernels for 10%

profile of v4, /device:TPU:0, one launch (start us, length us, event | category | flops | bytes accessed | tf_op | source)
XLA Modules:
  0.0 110.3 jit_solution(17337097984843675105)
XLA Ops:
  0.0 3.1 %collective-permute-start = (bf16[32,2048]{1,0:T(8,128)(2,1)}, bf16[32,2048]{1,0:T(8,128)(2,1)S(1)}, u32[]{:S(2)}, u32[]{:S(2)}) collective-permute-start(bf16[32,2048]{1,0:T(8,128)(2,1)} %q_hbm.1), channel_id=1, source_target_pairs={{0,4},{4,0},{8,12},{12,8},{1,5},{5,1},{9,13},{13,9},{2,6},{6,2},{1... | collective-permute-start | bytes 393224 | tf_op jit(solution)/shard_map/ppermute | solution.py:371
  3.1 2.6 %collective-permute-start.2 = (bf16[32,2048]{1,0:T(8,128)(2,1)}, bf16[32,2048]{1,0:T(8,128)(2,1)S(1)}, u32[]{:S(2)}, u32[]{:S(2)}) collective-permute-start(bf16[32,2048]{1,0:T(8,128)(2,1)} %q_hbm.1), channel_id=1, source_target_pairs={{0,8},{4,12},{8,0},{12,4},{1,9},{5,13},{9,1},{13,5},{2,10},{6,14},... | collective-permute-start | bytes 393224 | tf_op jit(solution)/shard_map/ppermute | solution.py:371
  6.3 2.6 %shard_map.100 = (bf16[512,256]{1,0:T(8,128)(2,1)S(1)}, bf16[512,256]{1,0:T(8,128)(2,1)S(1)}, s32[8,128]{1,0:T(8,128)S(1)}, bf16[32,2176]{1,0:T(8,128)(2,1)S(1)}) custom-call(s32[1,8]{1,0:T(1,128)S(1)} %copy-done.2, bf16[32,2048]{1,0:T(8,128)(2,1)} %q_hbm.1, bf16[2048,256]{1,0:T(8,128)(2,1)} %key_hbm.1, bf16[2048,256]{1,0:T(8,128)(2,1)} %value_hbm.1), custom_call_target="tpu_custom_call" | custom-call | flops 3000000000 | bytes 2895904 | tf_op jit(solution)/shard_map/pallas_call | solution.py:40
  8.9 0.8 shard_map.101
  10.2 1.8 %collective-permute-done.2.q_ref = bf16[32,2048]{1,0:T(8,128)(2,1)S(1)} collective-permute-done((bf16[32,2048]{1,0:T(8,128)(2,1)}, bf16[32,2048]{1,0:T(8,128)(2,1)S(1)}, u32[]{:S(2)}, u32[]{:S(2)}) %collective-permute-start.2) | collective-permute-done | bytes 131104 | tf_op jit(solution)/shard_map/ppermute | solution.py:371
  12.4 0.8 shard_map.102
  13.2 2.7 %collective-permute-start.3 = (bf16[32,2176]{1,0:T(8,128)(2,1)S(1)}, bf16[32,2176]{1,0:T(8,128)(2,1)S(1)}, u32[]{:S(2)}, u32[]{:S(2)}) collective-permute-start(bf16[32,2176]{1,0:T(8,128)(2,1)S(1)} %shard_map.102), channel_id=1, source_target_pairs={{0,8},{4,12},{8,0},{12,4},{1,9},{5,13},{9,1},{13,5},{2,10},{6,14},... | collective-permute-start | bytes 417800 | tf_op jit(solution)/shard_map/ppermute | solution.py:371
  15.9 4.4 %collective-permute-done.4.q_ref = bf16[32,2048]{1,0:T(8,128)(2,1)S(1)} collective-permute-done((bf16[32,2048]{1,0:T(8,128)(2,1)S(1)}, bf16[32,2048]{1,0:T(8,128)(2,1)S(1)}, u32[]{:S(2)}, u32[]{:S(2)}) %collective-permute-start.4) | collective-permute-done | bytes 131104 | tf_op jit(solution)/shard_map/ppermute | solution.py:371
  20.3 0.8 shard_map.103
  21.1 1.9 %collective-permute-start.5 = (bf16[32,2176]{1,0:T(8,128)(2,1)S(1)}, bf16[32,2176]{1,0:T(8,128)(2,1)S(1)}, u32[]{:S(2)}, u32[]{:S(2)}) collective-permute-start(bf16[32,2176]{1,0:T(8,128)(2,1)S(1)} %shard_map.103), channel_id=1, source_target_pairs={{0,12},{4,8},{8,4},{12,0},{1,13},{5,9},{9,5},{13,1},{2,14},{6,10},... | collective-permute-start | bytes 417800 | tf_op jit(solution)/shard_map/ppermute | solution.py:371
  23.1 5.0 %collective-permute-done.5.refs_3_ = bf16[32,2176]{1,0:T(8,128)(2,1)S(1)} collective-permute-done((bf16[32,2176]{1,0:T(8,128)(2,1)S(1)}, bf16[32,2176]{1,0:T(8,128)(2,1)S(1)}, u32[]{:S(2)}, u32[]{:S(2)}) %collective-permute-start.5) | collective-permute-done | bytes 139296 | tf_op jit(solution)/shard_map/ppermute | solution.py:371
  28.5 1.2 %collective-permute-start.7 = (bf16[32,1024]{1,0:T(8,128)(2,1)S(1)}, bf16[32,1024]{1,0:T(8,128)(2,1)S(1)}, u32[]{:S(2)}, u32[]{:S(2)}) collective-permute-start(bf16[32,1024]{1,0:T(8,128)(2,1)S(1)} %get-tuple-element.52), channel_id=1, source_target_pairs={{0,8},{4,12},{8,0},{12,4},{1,9},{5,13},{9,1},{13,5},{2,10},{6,14},... | collective-permute-start | bytes 196616 | tf_op jit(solution)/shard_map/ppermute | solution.py:371
  29.8 1.8 %collective-permute-start.8 = (bf16[32,1024]{1,0:T(8,128)(2,1)S(1)}, bf16[32,1024]{1,0:T(8,128)(2,1)S(1)}, u32[]{:S(2)}, u32[]{:S(2)}) collective-permute-start(bf16[32,1024]{1,0:T(8,128)(2,1)S(1)} %get-tuple-element.53), channel_id=1, source_target_pairs={{0,8},{4,12},{8,0},{12,4},{1,9},{5,13},{9,1},{13,5},{2,10},{6,14},... | collective-permute-start | bytes 196616 | tf_op jit(solution)/shard_map/ppermute | solution.py:371
  31.5 2.5 %collective-permute-done.7.refs_2_ = bf16[32,1024]{1,0:T(8,128)(2,1)S(1)} collective-permute-done((bf16[32,1024]{1,0:T(8,128)(2,1)S(1)}, bf16[32,1024]{1,0:T(8,128)(2,1)S(1)}, u32[]{:S(2)}, u32[]{:S(2)}) %collective-permute-start.7) | collective-permute-done | bytes 65568 | tf_op jit(solution)/shard_map/ppermute | solution.py:371
  34.1 0.9 collective-permute-done.8.refs_3_
  35.0 1.4 %collective-permute-start.10 = (bf16[32,1024]{1,0:T(8,128)(2,1)S(1)}, bf16[32,1024]{1,0:T(8,128)(2,1)S(1)}, u32[]{:S(2)}, u32[]{:S(2)}) collective-permute-start(bf16[32,1024]{1,0:T(8,128)(2,1)S(1)} %collective-permute-done.8.refs_3_), channel_id=1, source_target_pairs={{0,4},{4,0},{8,12},{12,8},{1,5},{5,1},{9,13},{13,9},{2,6},{6,2},{1... | collective-permute-start | bytes 196616 | tf_op jit(solution)/shard_map/ppermute | solution.py:371
  36.4 1.8 %collective-permute-done.9.refs_4_ = bf16[32,1024]{1,0:T(8,128)(2,1)S(1)} collective-permute-done((bf16[32,1024]{1,0:T(8,128)(2,1)S(1)}, bf16[32,1024]{1,0:T(8,128)(2,1)S(1)}, u32[]{:S(2)}, u32[]{:S(2)}) %collective-permute-start.9) | collective-permute-done | bytes 65568 | tf_op jit(solution)/shard_map/ppermute | solution.py:371
  38.3 1.0 collective-permute-done.10.refs_5_
  39.3 1.3 %shard_map.105 = (f32[64,2048]{1,0:T(8,128)S(1)}, bf16[64,2048]{1,0:T(8,128)(2,1)S(1)}) custom-call(bf16[32,2048]{1,0:T(8,128)(2,1)S(1)} %get-tuple-element.51.refs_0_, bf16[32,2048]{1,0:T(8,128)(2,1)S(1)} %collective-permute-done.6.refs_1_, bf16[32,1024]{1,0:T(8,128)(2,1)S(1)} %collective-permute-done.7.refs_2_, ...), custom_call_target="tpu_custom_call" | custom-call | flops 6000000000 | bytes 9699328 | tf_op jit(solution)/shard_map/pallas_call | solution.py:40
  40.7 1.5 %collective-permute-done.11.got_ref = bf16[64,2048]{1,0:T(8,128)(2,1)S(1)} collective-permute-done((bf16[64,2048]{1,0:T(8,128)(2,1)S(1)}, bf16[64,2048]{1,0:T(8,128)(2,1)S(1)}, u32[]{:S(2)}, u32[]{:S(2)}) %collective-permute-start.11) | collective-permute-done | bytes 262176 | tf_op jit(solution)/shard_map/ppermute | solution.py:367
  42.3 1.5 %collective-permute-start.12 = (bf16[32,2048]{1,0:T(8,128)(2,1)S(1)}, bf16[32,2048]{1,0:T(8,128)(2,1)S(1)}, u32[]{:S(2)}, u32[]{:S(2)}) collective-permute-start(bf16[32,2048]{1,0:T(8,128)(2,1)S(1)} %get-tuple-element.57), channel_id=1, source_target_pairs={{0,2},{2,0},{1,3},{3,1},{4,6},{6,4},{5,7},{7,5},{8,10},{10,8},{9,1... | collective-permute-start | bytes 393224 | tf_op jit(solution)/shard_map/ppermute | solution.py:367
  43.8 4.0 %collective-permute-done.12.got_ref = bf16[32,2048]{1,0:T(8,128)(2,1)S(1)} collective-permute-done((bf16[32,2048]{1,0:T(8,128)(2,1)S(1)}, bf16[32,2048]{1,0:T(8,128)(2,1)S(1)}, u32[]{:S(2)}, u32[]{:S(2)}) %collective-permute-start.12) | collective-permute-done | bytes 131104 | tf_op jit(solution)/shard_map/ppermute | solution.py:367
  48.0 0.8 collective-permute-start.13
  48.8 3.0 %collective-permute-start.14 = (bf16[32,2048]{1,0:T(8,128)(2,1)S(1)}, bf16[32,2048]{1,0:T(8,128)(2,1)S(1)}, u32[]{:S(2)}, u32[]{:S(2)}) collective-permute-start(bf16[32,2048]{1,0:T(8,128)(2,1)S(1)} %shard_map.107), channel_id=1, source_target_pairs={{0,4},{1,0},{2,12},{3,8},{4,5},{5,1},{6,13},{7,9},{8,6},{9,2},{10,... | collective-permute-start | bytes 393224 | tf_op jit(solution)/shard_map/ppermute | solution.py:458
  51.8 2.5 %collective-permute-start.15 = (bf16[32,2048]{1,0:T(8,128)(2,1)S(1)}, bf16[32,2048]{1,0:T(8,128)(2,1)S(1)}, u32[]{:S(2)}, u32[]{:S(2)}) collective-permute-start(bf16[32,2048]{1,0:T(8,128)(2,1)S(1)} %shard_map.107), channel_id=1, source_target_pairs={{0,8},{1,12},{2,0},{3,4},{4,9},{5,13},{6,1},{7,5},{8,10},{9,14},{1... | collective-permute-start | bytes 393224 | tf_op jit(solution)/shard_map/ppermute | solution.py:458
  54.2 1.2 %collective-permute-start.16 = (bf16[32,2048]{1,0:T(8,128)(2,1)S(1)}, bf16[32,2048]{1,0:T(8,128)(2,1)S(1)}, u32[]{:S(2)}, u32[]{:S(2)}) collective-permute-start(bf16[32,2048]{1,0:T(8,128)(2,1)S(1)} %shard_map.107), channel_id=1, source_target_pairs={{0,12},{1,8},{2,4},{3,0},{4,13},{5,9},{6,5},{7,1},{8,14},{9,10},{1... | collective-permute-start | bytes 393224 | tf_op jit(solution)/shard_map/ppermute | solution.py:458
  55.7 6.3 %collective-permute-done.15.piece_ref = bf16[32,2048]{1,0:T(8,128)(2,1)S(1)} collective-permute-done((bf16[32,2048]{1,0:T(8,128)(2,1)S(1)}, bf16[32,2048]{1,0:T(8,128)(2,1)S(1)}, u32[]{:S(2)}, u32[]{:S(2)}) %collective-permute-start.15) | collective-permute-done | bytes 131104 | tf_op jit(solution)/shard_map/ppermute | solution.py:458
  62.3 1.6 %shard_map.112 = (f32[64,2176]{1,0:T(8,128)S(1)}, bf16[64,2304]{1,0:T(8,128)(2,1)S(1)}, bf16[128,2048]{1,0:T(8,128)(2,1)S(1)}) custom-call(bf16[32,2048]{1,0:T(8,128)(2,1)S(1)} %get-tuple-element.58.refs_0_, bf16[32,2048]{1,0:T(8,128)(2,1)S(1)} %get-tuple-element.59.refs_1_, bf16[32,2048]{1,0:T(8,128)(2,1)S(1)} %get-tuple-element.60.refs_2_, ...), custom_call_target="tpu_custom_call" | custom-call | flops 3000000000 | bytes 31326208 | tf_op jit(solution)/shard_map/pallas_call | solution.py:40
  63.9 0.8 collective-permute-start.17
  64.6 1.5 %shard_map.115 = (f32[64,2560]{1,0:T(8,128)S(1)}, bf16[64,2560]{1,0:T(8,128)(2,1)S(1)}) custom-call(bf16[128,2048]{1,0:T(8,128)(2,1)S(1)} %get-tuple-element.71.rows_ref, bf16[2048,3584]{1,0:T(8,128)(2,1)S(1)} %bitcast.4, bf16[2048,3584]{1,0:T(8,128)(2,1)S(1)} %bitcast.6), custom_call_target="tpu_custom_call" | custom-call | flops 3000000000 | bytes 30867456 | tf_op jit(solution)/shard_map/pallas_call | solution.py:40
  66.3 1.5 %shard_map.118 = (f32[64,2560]{1,0:T(8,128)S(1)}, bf16[64,2560]{1,0:T(8,128)(2,1)S(1)}) custom-call(bf16[128,2048]{1,0:T(8,128)(2,1)S(1)} %get-tuple-element.71.rows_ref, bf16[2048,3584]{1,0:T(8,128)(2,1)S(1)} %bitcast.4, bf16[2048,3584]{1,0:T(8,128)(2,1)S(1)} %bitcast.6), custom_call_target="tpu_custom_call" | custom-call | flops 3000000000 | bytes 30867456 | tf_op jit(solution)/shard_map/pallas_call | solution.py:40
  68.4 5.7 %collective-permute-start.18 = (bf16[32,2304]{1,0:T(8,128)(2,1)S(1)}, bf16[32,2304]{1,0:T(8,128)(2,1)S(1)}, u32[]{:S(2)}, u32[]{:S(2)}) collective-permute-start(bf16[32,2304]{1,0:T(8,128)(2,1)S(1)} %get-tuple-element.69), channel_id=1, source_target_pairs={{0,2},{2,0},{1,3},{3,1},{4,6},{6,4},{5,7},{7,5},{8,10},{10,8},{9,1... | collective-permute-start | bytes 442376 | tf_op jit(solution)/shard_map/ppermute | solution.py:367
  74.3 2.1 %collective-permute-start.25 = (bf16[32,2560]{1,0:T(8,128)(2,1)S(1)}, bf16[32,2560]{1,0:T(8,128)(2,1)S(1)}, u32[]{:S(2)}, u32[]{:S(2)}) collective-permute-start(bf16[32,2560]{1,0:T(8,128)(2,1)S(1)} %get-tuple-element.79), channel_id=1, source_target_pairs={{0,2},{2,0},{1,3},{3,1},{4,6},{6,4},{5,7},{7,5},{8,10},{10,8},{9,1... | collective-permute-start | bytes 491528 | tf_op jit(solution)/shard_map/ppermute | solution.py:367
  76.4 2.4 %collective-permute-done.18.got_ref = bf16[32,2304]{1,0:T(8,128)(2,1)S(1)} collective-permute-done((bf16[32,2304]{1,0:T(8,128)(2,1)S(1)}, bf16[32,2304]{1,0:T(8,128)(2,1)S(1)}, u32[]{:S(2)}, u32[]{:S(2)}) %collective-permute-start.18) | collective-permute-done | bytes 147488 | tf_op jit(solution)/shard_map/ppermute | solution.py:367
  78.9 2.1 %collective-permute-start.30 = (bf16[32,1024]{1,0:T(8,128)(2,1)S(1)}, bf16[32,1024]{1,0:T(8,128)(2,1)S(1)}, u32[]{:S(2)}, u32[]{:S(2)}) collective-permute-start(bf16[32,1024]{1,0:T(8,128)(2,1)S(1)} %get-tuple-element.80.refs_0_), channel_id=1, source_target_pairs={{0,2},{2,0},{1,3},{3,1},{4,6},{6,4},{5,7},{7,5},{8,10},{10,8},{9,1... | collective-permute-start | bytes 196616 | tf_op jit(solution)/shard_map/ppermute | solution.py:367
  81.0 1.3 %collective-permute-done.20.got_ref = bf16[32,2560]{1,0:T(8,128)(2,1)S(1)} collective-permute-done((bf16[32,2560]{1,0:T(8,128)(2,1)S(1)}, bf16[32,2560]{1,0:T(8,128)(2,1)S(1)}, u32[]{:S(2)}, u32[]{:S(2)}) %collective-permute-start.20) | collective-permute-done | bytes 163872 | tf_op jit(solution)/shard_map/ppermute | solution.py:367
  82.4 2.1 %collective-permute-start.22 = (bf16[32,1280]{1,0:T(8,128)(2,1)S(1)}, bf16[32,1280]{1,0:T(8,128)(2,1)S(1)}, u32[]{:S(2)}, u32[]{:S(2)}) collective-permute-start(bf16[32,1280]{1,0:T(8,128)(2,1)S(1)} %shard_map.117.refs_0_), channel_id=1, source_target_pairs={{0,2},{2,0},{1,3},{3,1},{4,6},{6,4},{5,7},{7,5},{8,10},{10,8},{9,1... | collective-permute-start | bytes 245768 | tf_op jit(solution)/shard_map/ppermute | solution.py:367
  84.5 1.3 %collective-permute-done.25.got_ref = bf16[32,2560]{1,0:T(8,128)(2,1)S(1)} collective-permute-done((bf16[32,2560]{1,0:T(8,128)(2,1)S(1)}, bf16[32,2560]{1,0:T(8,128)(2,1)S(1)}, u32[]{:S(2)}, u32[]{:S(2)}) %collective-permute-start.25) | collective-permute-done | bytes 163872 | tf_op jit(solution)/shard_map/ppermute | solution.py:367
  85.9 2.1 %collective-permute-start.27 = (bf16[32,1280]{1,0:T(8,128)(2,1)S(1)}, bf16[32,1280]{1,0:T(8,128)(2,1)S(1)}, u32[]{:S(2)}, u32[]{:S(2)}) collective-permute-start(bf16[32,1280]{1,0:T(8,128)(2,1)S(1)} %shard_map.120.refs_0_), channel_id=1, source_target_pairs={{0,2},{2,0},{1,3},{3,1},{4,6},{6,4},{5,7},{7,5},{8,10},{10,8},{9,1... | collective-permute-start | bytes 245768 | tf_op jit(solution)/shard_map/ppermute | solution.py:367
  88.5 0.7 collective-permute-done.29.refs_1_
  89.8 0.8 collective-permute-done.27.refs_2_
  91.8 0.9 shard_map.122.refs_5_
  93.2 1.7 %collective-permute-start.33 = (bf16[32,1024]{1,0:T(8,128)(2,1)S(1)}, bf16[32,1024]{1,0:T(8,128)(2,1)S(1)}, u32[]{:S(2)}, u32[]{:S(2)}) collective-permute-start(bf16[32,1024]{1,0:T(8,128)(2,1)S(1)} %get-tuple-element.86), channel_id=1, source_target_pairs={{0,4},{4,0},{8,12},{12,8},{1,5},{5,1},{9,13},{13,9},{2,6},{6,2},{1... | collective-permute-start | bytes 196616 | tf_op jit(solution)/shard_map/ppermute | solution.py:371
  95.9 1.6 %collective-permute-start.35 = (bf16[32,1024]{1,0:T(8,128)(2,1)S(1)}, bf16[32,1024]{1,0:T(8,128)(2,1)S(1)}, u32[]{:S(2)}, u32[]{:S(2)}) collective-permute-start(bf16[32,1024]{1,0:T(8,128)(2,1)S(1)} %get-tuple-element.88), channel_id=1, source_target_pairs={{0,4},{4,0},{8,12},{12,8},{1,5},{5,1},{9,13},{13,9},{2,6},{6,2},{1... | collective-permute-start | bytes 196616 | tf_op jit(solution)/shard_map/ppermute | solution.py:371
  97.6 3.3 %collective-permute-start.34 = (bf16[32,1024]{1,0:T(8,128)(2,1)S(1)}, bf16[32,1024]{1,0:T(8,128)(2,1)S(1)}, u32[]{:S(2)}, u32[]{:S(2)}) collective-permute-start(bf16[32,1024]{1,0:T(8,128)(2,1)S(1)} %shard_map.125), channel_id=1, source_target_pairs={{0,8},{4,12},{8,0},{12,4},{1,9},{5,13},{9,1},{13,5},{2,10},{6,14},... | collective-permute-start | bytes 196616 | tf_op jit(solution)/shard_map/ppermute | solution.py:371
  100.9 2.7 %collective-permute-done.35.got_ref = bf16[32,1024]{1,0:T(8,128)(2,1)S(1)} collective-permute-done((bf16[32,1024]{1,0:T(8,128)(2,1)S(1)}, bf16[32,1024]{1,0:T(8,128)(2,1)S(1)}, u32[]{:S(2)}, u32[]{:S(2)}) %collective-permute-start.35) | collective-permute-done | bytes 65568 | tf_op jit(solution)/shard_map/ppermute | solution.py:371
  103.6 2.4 %collective-permute-start.36 = (bf16[32,1024]{1,0:T(8,128)(2,1)S(1)}, bf16[32,1024]{1,0:T(8,128)(2,1)S(1)}, u32[]{:S(2)}, u32[]{:S(2)}) collective-permute-start(bf16[32,1024]{1,0:T(8,128)(2,1)S(1)} %shard_map.126), channel_id=1, source_target_pairs={{0,8},{4,12},{8,0},{12,4},{1,9},{5,13},{9,1},{13,5},{2,10},{6,14},... | collective-permute-start | bytes 196616 | tf_op jit(solution)/shard_map/ppermute | solution.py:371
  106.1 3.5 %collective-permute-done.36.refs_3_ = bf16[32,1024]{1,0:T(8,128)(2,1)S(1)} collective-permute-done((bf16[32,1024]{1,0:T(8,128)(2,1)S(1)}, bf16[32,1024]{1,0:T(8,128)(2,1)S(1)}, u32[]{:S(2)}, u32[]{:S(2)}) %collective-permute-start.36) | collective-permute-done | bytes 65568 | tf_op jit(solution)/shard_map/ppermute | solution.py:371
  (92 shorter events, 8.5 us)
Async XLA Ops:
  0.0 8.9 %collective-permute-start = (bf16[32,2048]{1,0:T(8,128)(2,1)}, bf16[32,2048]{1,0:T(8,128)(2,1)S(1)}, u32[]{:S(2)}, u32[]{:S(2)}) collective-permute-start(bf16[32,2048]{1,0:T(8,128)(2,1)} %q_hbm.1), channel_id=1, source_target_pairs={{0,4},{4,0},{8,12},{12,8},{1,5},{5,1},{9,13},{13,9},{2,6},{6,2},{1... | collective-permute-start | bytes 393224 | tf_op jit(solution)/shard_map/ppermute | solution.py:371
  3.1 9.0 %collective-permute-start.2 = (bf16[32,2048]{1,0:T(8,128)(2,1)}, bf16[32,2048]{1,0:T(8,128)(2,1)S(1)}, u32[]{:S(2)}, u32[]{:S(2)}) collective-permute-start(bf16[32,2048]{1,0:T(8,128)(2,1)} %q_hbm.1), channel_id=1, source_target_pairs={{0,8},{4,12},{8,0},{12,4},{1,9},{5,13},{9,1},{13,5},{2,10},{6,14},... | collective-permute-start | bytes 393224 | tf_op jit(solution)/shard_map/ppermute | solution.py:371
  9.7 29.5 %slice-start.12 = ((s8[8388608]{0:T(1024)(128)(4,1)}), s8[4194304]{0:T(1024)(128)(4,1)S(1)}, s32[]{:S(2)}) async-start(s8[8388608]{0:T(1024)(128)(4,1)} %bitcast.11), calls=%async_computation.12 | async-start | bytes 8388608
  9.7 13.3 %collective-permute-start.1 = (bf16[32,2176]{1,0:T(8,128)(2,1)S(1)}, bf16[32,2176]{1,0:T(8,128)(2,1)S(1)}, u32[]{:S(2)}, u32[]{:S(2)}) collective-permute-start(bf16[32,2176]{1,0:T(8,128)(2,1)S(1)} %shard_map.101), channel_id=1, source_target_pairs={{0,4},{4,0},{8,12},{12,8},{1,5},{5,1},{9,13},{13,9},{2,6},{6,2},{1... | collective-permute-start | bytes 417800 | tf_op jit(solution)/shard_map/ppermute | solution.py:371
  12.1 8.2 %collective-permute-start.4 = (bf16[32,2048]{1,0:T(8,128)(2,1)S(1)}, bf16[32,2048]{1,0:T(8,128)(2,1)S(1)}, u32[]{:S(2)}, u32[]{:S(2)}) collective-permute-start(bf16[32,2048]{1,0:T(8,128)(2,1)S(1)} %collective-permute-done.2.q_ref), channel_id=1, source_target_pairs={{0,4},{4,0},{8,12},{12,8},{1,5},{5,1},{9,13},{13,9},{2,6},{6,2},{1... | collective-permute-start | bytes 393224 | tf_op jit(solution)/shard_map/ppermute | solution.py:371
  13.2 26.0 %slice-start.13 = ((s8[8388608]{0:T(1024)(128)(4,1)}), s8[4194304]{0:T(1024)(128)(4,1)S(1)}, s32[]{:S(2)}) async-start(s8[8388608]{0:T(1024)(128)(4,1)} %bitcast.11), calls=%async_computation.13 | async-start | bytes 8388608
  13.2 9.8 %collective-permute-start.3 = (bf16[32,2176]{1,0:T(8,128)(2,1)S(1)}, bf16[32,2176]{1,0:T(8,128)(2,1)S(1)}, u32[]{:S(2)}, u32[]{:S(2)}) collective-permute-start(bf16[32,2176]{1,0:T(8,128)(2,1)S(1)} %shard_map.102), channel_id=1, source_target_pairs={{0,8},{4,12},{8,0},{12,4},{1,9},{5,13},{9,1},{13,5},{2,10},{6,14},... | collective-permute-start | bytes 417800 | tf_op jit(solution)/shard_map/ppermute | solution.py:371
  21.1 6.9 %collective-permute-start.5 = (bf16[32,2176]{1,0:T(8,128)(2,1)S(1)}, bf16[32,2176]{1,0:T(8,128)(2,1)S(1)}, u32[]{:S(2)}, u32[]{:S(2)}) collective-permute-start(bf16[32,2176]{1,0:T(8,128)(2,1)S(1)} %shard_map.103), channel_id=1, source_target_pairs={{0,12},{4,8},{8,4},{12,0},{1,13},{5,9},{9,5},{13,1},{2,14},{6,10},... | collective-permute-start | bytes 417800 | tf_op jit(solution)/shard_map/ppermute | solution.py:371
  28.5 5.5 %collective-permute-start.7 = (bf16[32,1024]{1,0:T(8,128)(2,1)S(1)}, bf16[32,1024]{1,0:T(8,128)(2,1)S(1)}, u32[]{:S(2)}, u32[]{:S(2)}) collective-permute-start(bf16[32,1024]{1,0:T(8,128)(2,1)S(1)} %get-tuple-element.52), channel_id=1, source_target_pairs={{0,8},{4,12},{8,0},{12,4},{1,9},{5,13},{9,1},{13,5},{2,10},{6,14},... | collective-permute-start | bytes 196616 | tf_op jit(solution)/shard_map/ppermute | solution.py:371
  29.8 5.2 %collective-permute-start.8 = (bf16[32,1024]{1,0:T(8,128)(2,1)S(1)}, bf16[32,1024]{1,0:T(8,128)(2,1)S(1)}, u32[]{:S(2)}, u32[]{:S(2)}) collective-permute-start(bf16[32,1024]{1,0:T(8,128)(2,1)S(1)} %get-tuple-element.53), channel_id=1, source_target_pairs={{0,8},{4,12},{8,0},{12,4},{1,9},{5,13},{9,1},{13,5},{2,10},{6,14},... | collective-permute-start | bytes 196616 | tf_op jit(solution)/shard_map/ppermute | solution.py:371
  31.5 7.7 %collective-permute-start.6 = (bf16[32,2048]{1,0:T(8,128)(2,1)S(1)}, bf16[32,2048]{1,0:T(8,128)(2,1)S(1)}, u32[]{:S(2)}, u32[]{:S(2)}) collective-permute-start(bf16[32,2048]{1,0:T(8,128)(2,1)S(1)} %get-tuple-element.51.refs_0_), channel_id=1, source_target_pairs={{0,4},{4,0},{8,12},{12,8},{1,5},{5,1},{9,13},{13,9},{2,6},{6,2},{1... | collective-permute-start | bytes 393224 | tf_op jit(solution)/shard_map/ppermute | solution.py:371
  34.0 4.3 %collective-permute-start.9 = (bf16[32,1024]{1,0:T(8,128)(2,1)S(1)}, bf16[32,1024]{1,0:T(8,128)(2,1)S(1)}, u32[]{:S(2)}, u32[]{:S(2)}) collective-permute-start(bf16[32,1024]{1,0:T(8,128)(2,1)S(1)} %collective-permute-done.7.refs_2_), channel_id=1, source_target_pairs={{0,4},{4,0},{8,12},{12,8},{1,5},{5,1},{9,13},{13,9},{2,6},{6,2},{1... | collective-permute-start | bytes 196616 | tf_op jit(solution)/shard_map/ppermute | solution.py:371
  35.0 4.3 %collective-permute-start.10 = (bf16[32,1024]{1,0:T(8,128)(2,1)S(1)}, bf16[32,1024]{1,0:T(8,128)(2,1)S(1)}, u32[]{:S(2)}, u32[]{:S(2)}) collective-permute-start(bf16[32,1024]{1,0:T(8,128)(2,1)S(1)} %collective-permute-done.8.refs_3_), channel_id=1, source_target_pairs={{0,4},{4,0},{8,12},{12,8},{1,5},{5,1},{9,13},{13,9},{2,6},{6,2},{1... | collective-permute-start | bytes 196616 | tf_op jit(solution)/shard_map/ppermute | solution.py:371
  40.6 1.6 %collective-permute-start.11 = (bf16[64,2048]{1,0:T(8,128)(2,1)S(1)}, bf16[64,2048]{1,0:T(8,128)(2,1)S(1)}, u32[]{:S(2)}, u32[]{:S(2)}) collective-permute-start(bf16[64,2048]{1,0:T(8,128)(2,1)S(1)} %get-tuple-element.55), channel_id=1, source_target_pairs={{0,1},{1,0},{2,3},{3,2},{4,5},{5,4},{6,7},{7,6},{8,9},{9,8},{10,11... | collective-permute-start | bytes 786440 | tf_op jit(solution)/shard_map/ppermute | solution.py:367
  42.2 20.0 %slice-start.4 = ((s8[14680064]{0:T(1024)(128)(4,1)}), s8[4194304]{0:T(1024)(128)(4,1)S(1)}, s32[]{:S(2)}) async-start(s8[14680064]{0:T(1024)(128)(4,1)} %bitcast.3), calls=%async_computation.4 | async-start | bytes 8388608
  42.2 20.0 %slice-start.5 = ((s8[14680064]{0:T(1024)(128)(4,1)}), s8[4194304]{0:T(1024)(128)(4,1)S(1)}, s32[]{:S(2)}) async-start(s8[14680064]{0:T(1024)(128)(4,1)} %bitcast.3), calls=%async_computation.5 | async-start | bytes 8388608
  42.2 20.0 %slice-start.8 = ((s8[14680064]{0:T(1024)(128)(4,1)}), s8[2097152]{0:T(1024)(128)(4,1)S(1)}, s32[]{:S(2)}) async-start(s8[14680064]{0:T(1024)(128)(4,1)} %bitcast.5), calls=%async_computation.8 | async-start | bytes 4194304
  42.2 20.0 %slice-start.9 = ((s8[14680064]{0:T(1024)(128)(4,1)}), s8[4194304]{0:T(1024)(128)(4,1)S(1)}, s32[]{:S(2)}) async-start(s8[14680064]{0:T(1024)(128)(4,1)} %bitcast.5), calls=%async_computation.9 | async-start | bytes 8388608
  42.3 13.2 %copy-start = (f32[8192]{0:T(1024)S(1)}, f32[8192]{0:T(1024)}, u32[]{:S(2)}) copy-start(f32[8192]{0:T(1024)} %param.16) | copy-start | bytes 98308
  42.3 5.6 %collective-permute-start.12 = (bf16[32,2048]{1,0:T(8,128)(2,1)S(1)}, bf16[32,2048]{1,0:T(8,128)(2,1)S(1)}, u32[]{:S(2)}, u32[]{:S(2)}) collective-permute-start(bf16[32,2048]{1,0:T(8,128)(2,1)S(1)} %get-tuple-element.57), channel_id=1, source_target_pairs={{0,2},{2,0},{1,3},{3,1},{4,6},{6,4},{5,7},{7,5},{8,10},{10,8},{9,1... | collective-permute-start | bytes 393224 | tf_op jit(solution)/shard_map/ppermute | solution.py:367
  47.9 14.4 %slice-start.6 = ((s8[14680064]{0:T(1024)(128)(4,1)}), s8[4194304]{0:T(1024)(128)(4,1)S(1)}, s32[]{:S(2)}) async-start(s8[14680064]{0:T(1024)(128)(4,1)} %bitcast.3), calls=%async_computation.6 | async-start | bytes 8388608
  47.9 14.4 %slice-start.7 = ((s8[14680064]{0:T(1024)(128)(4,1)}), s8[2097152]{0:T(1024)(128)(4,1)S(1)}, s32[]{:S(2)}) async-start(s8[14680064]{0:T(1024)(128)(4,1)} %bitcast.3), calls=%async_computation.7 | async-start | bytes 4194304
  47.9 14.4 %slice-start.10 = ((s8[14680064]{0:T(1024)(128)(4,1)}), s8[4194304]{0:T(1024)(128)(4,1)S(1)}, s32[]{:S(2)}) async-start(s8[14680064]{0:T(1024)(128)(4,1)} %bitcast.5), calls=%async_computation.10 | async-start | bytes 8388608
  47.9 14.4 %slice-start.11 = ((s8[14680064]{0:T(1024)(128)(4,1)}), s8[4194304]{0:T(1024)(128)(4,1)S(1)}, s32[]{:S(2)}) async-start(s8[14680064]{0:T(1024)(128)(4,1)} %bitcast.5), calls=%async_computation.11 | async-start | bytes 8388608
  48.0 7.5 %collective-permute-start.13 = (bf16[32,2048]{1,0:T(8,128)(2,1)S(1)}, bf16[32,2048]{1,0:T(8,128)(2,1)S(1)}, u32[]{:S(2)}, u32[]{:S(2)}) collective-permute-start(bf16[32,2048]{1,0:T(8,128)(2,1)S(1)} %shard_map.107), channel_id=1, source_target_pairs={{0,0},{1,4},{2,8},{3,12},{4,1},{5,5},{6,9},{7,13},{8,2},{9,6},{10,... | collective-permute-start | bytes 393224 | tf_op jit(solution)/shard_map/ppermute | solution.py:458
  48.8 6.8 %collective-permute-start.14 = (bf16[32,2048]{1,0:T(8,128)(2,1)S(1)}, bf16[32,2048]{1,0:T(8,128)(2,1)S(1)}, u32[]{:S(2)}, u32[]{:S(2)}) collective-permute-start(bf16[32,2048]{1,0:T(8,128)(2,1)S(1)} %shard_map.107), channel_id=1, source_target_pairs={{0,4},{1,0},{2,12},{3,8},{4,5},{5,1},{6,13},{7,9},{8,6},{9,2},{10,... | collective-permute-start | bytes 393224 | tf_op jit(solution)/shard_map/ppermute | solution.py:458
  51.8 10.2 %collective-permute-start.15 = (bf16[32,2048]{1,0:T(8,128)(2,1)S(1)}, bf16[32,2048]{1,0:T(8,128)(2,1)S(1)}, u32[]{:S(2)}, u32[]{:S(2)}) collective-permute-start(bf16[32,2048]{1,0:T(8,128)(2,1)S(1)} %shard_map.107), channel_id=1, source_target_pairs={{0,8},{1,12},{2,0},{3,4},{4,9},{5,13},{6,1},{7,5},{8,10},{9,14},{1... | collective-permute-start | bytes 393224 | tf_op jit(solution)/shard_map/ppermute | solution.py:458
  54.2 7.9 %collective-permute-start.16 = (bf16[32,2048]{1,0:T(8,128)(2,1)S(1)}, bf16[32,2048]{1,0:T(8,128)(2,1)S(1)}, u32[]{:S(2)}, u32[]{:S(2)}) collective-permute-start(bf16[32,2048]{1,0:T(8,128)(2,1)S(1)} %shard_map.107), channel_id=1, source_target_pairs={{0,12},{1,8},{2,4},{3,0},{4,13},{5,9},{6,5},{7,1},{8,14},{9,10},{1... | collective-permute-start | bytes 393224 | tf_op jit(solution)/shard_map/ppermute | solution.py:458
  63.9 4.5 %collective-permute-start.17 = (bf16[64,2304]{1,0:T(8,128)(2,1)S(1)}, bf16[64,2304]{1,0:T(8,128)(2,1)S(1)}, u32[]{:S(2)}, u32[]{:S(2)}) collective-permute-start(bf16[64,2304]{1,0:T(8,128)(2,1)S(1)} %get-tuple-element.67), channel_id=1, source_target_pairs={{0,1},{1,0},{2,3},{3,2},{4,5},{5,4},{6,7},{7,6},{8,9},{9,8},{10,11... | collective-permute-start | bytes 884744 | tf_op jit(solution)/shard_map/ppermute | solution.py:367
  66.2 7.9 %collective-permute-start.19 = (bf16[64,2560]{1,0:T(8,128)(2,1)S(1)}, bf16[64,2560]{1,0:T(8,128)(2,1)S(1)}, u32[]{:S(2)}, u32[]{:S(2)}) collective-permute-start(bf16[64,2560]{1,0:T(8,128)(2,1)S(1)} %get-tuple-element.73), channel_id=1, source_target_pairs={{0,1},{1,0},{2,3},{3,2},{4,5},{5,4},{6,7},{7,6},{8,9},{9,8},{10,11... | collective-permute-start | bytes 983048 | tf_op jit(solution)/shard_map/ppermute | solution.py:367
  67.8 6.5 %collective-permute-start.24 = (bf16[64,2560]{1,0:T(8,128)(2,1)S(1)}, bf16[64,2560]{1,0:T(8,128)(2,1)S(1)}, u32[]{:S(2)}, u32[]{:S(2)}) collective-permute-start(bf16[64,2560]{1,0:T(8,128)(2,1)S(1)} %get-tuple-element.77), channel_id=1, source_target_pairs={{0,1},{1,0},{2,3},{3,2},{4,5},{5,4},{6,7},{7,6},{8,9},{9,8},{10,11... | collective-permute-start | bytes 983048 | tf_op jit(solution)/shard_map/ppermute | solution.py:367
  68.4 10.4 %collective-permute-start.18 = (bf16[32,2304]{1,0:T(8,128)(2,1)S(1)}, bf16[32,2304]{1,0:T(8,128)(2,1)S(1)}, u32[]{:S(2)}, u32[]{:S(2)}) collective-permute-start(bf16[32,2304]{1,0:T(8,128)(2,1)S(1)} %get-tuple-element.69), channel_id=1, source_target_pairs={{0,2},{2,0},{1,3},{3,1},{4,6},{6,4},{5,7},{7,5},{8,10},{10,8},{9,1... | collective-permute-start | bytes 442376 | tf_op jit(solution)/shard_map/ppermute | solution.py:367
  74.2 8.1 %collective-permute-start.20 = (bf16[32,2560]{1,0:T(8,128)(2,1)S(1)}, bf16[32,2560]{1,0:T(8,128)(2,1)S(1)}, u32[]{:S(2)}, u32[]{:S(2)}) collective-permute-start(bf16[32,2560]{1,0:T(8,128)(2,1)S(1)} %get-tuple-element.75), channel_id=1, source_target_pairs={{0,2},{2,0},{1,3},{3,1},{4,6},{6,4},{5,7},{7,5},{8,10},{10,8},{9,1... | collective-permute-start | bytes 491528 | tf_op jit(solution)/shard_map/ppermute | solution.py:367
  74.3 11.5 %collective-permute-start.25 = (bf16[32,2560]{1,0:T(8,128)(2,1)S(1)}, bf16[32,2560]{1,0:T(8,128)(2,1)S(1)}, u32[]{:S(2)}, u32[]{:S(2)}) collective-permute-start(bf16[32,2560]{1,0:T(8,128)(2,1)S(1)} %get-tuple-element.79), channel_id=1, source_target_pairs={{0,2},{2,0},{1,3},{3,1},{4,6},{6,4},{5,7},{7,5},{8,10},{10,8},{9,1... | collective-permute-start | bytes 491528 | tf_op jit(solution)/shard_map/ppermute | solution.py:367
  78.9 9.1 %collective-permute-start.30 = (bf16[32,1024]{1,0:T(8,128)(2,1)S(1)}, bf16[32,1024]{1,0:T(8,128)(2,1)S(1)}, u32[]{:S(2)}, u32[]{:S(2)}) collective-permute-start(bf16[32,1024]{1,0:T(8,128)(2,1)S(1)} %get-tuple-element.80.refs_0_), channel_id=1, source_target_pairs={{0,2},{2,0},{1,3},{3,1},{4,6},{6,4},{5,7},{7,5},{8,10},{10,8},{9,1... | collective-permute-start | bytes 196616 | tf_op jit(solution)/shard_map/ppermute | solution.py:367
  82.4 7.0 %collective-permute-start.22 = (bf16[32,1280]{1,0:T(8,128)(2,1)S(1)}, bf16[32,1280]{1,0:T(8,128)(2,1)S(1)}, u32[]{:S(2)}, u32[]{:S(2)}) collective-permute-start(bf16[32,1280]{1,0:T(8,128)(2,1)S(1)} %shard_map.117.refs_0_), channel_id=1, source_target_pairs={{0,2},{2,0},{1,3},{3,1},{4,6},{6,4},{5,7},{7,5},{8,10},{10,8},{9,1... | collective-permute-start | bytes 245768 | tf_op jit(solution)/shard_map/ppermute | solution.py:367
  85.9 4.6 %collective-permute-start.27 = (bf16[32,1280]{1,0:T(8,128)(2,1)S(1)}, bf16[32,1280]{1,0:T(8,128)(2,1)S(1)}, u32[]{:S(2)}, u32[]{:S(2)}) collective-permute-start(bf16[32,1280]{1,0:T(8,128)(2,1)S(1)} %shard_map.120.refs_0_), channel_id=1, source_target_pairs={{0,2},{2,0},{1,3},{3,1},{4,6},{6,4},{5,7},{7,5},{8,10},{10,8},{9,1... | collective-permute-start | bytes 245768 | tf_op jit(solution)/shard_map/ppermute | solution.py:367
  88.0 1.3 %collective-permute-start.29 = (bf16[32,1024]{1,0:T(8,128)(2,1)S(1)}, bf16[32,1024]{1,0:T(8,128)(2,1)S(1)}, u32[]{:S(2)}, u32[]{:S(2)}) collective-permute-start(bf16[32,1024]{1,0:T(8,128)(2,1)S(1)} %get-tuple-element.80.refs_0_), channel_id=1, source_target_pairs={{0,1},{1,0},{2,3},{3,2},{4,5},{5,4},{6,7},{7,6},{8,9},{9,8},{10,11... | collective-permute-start | bytes 196616 | tf_op jit(solution)/shard_map/ppermute | solution.py:367
  88.0 2.5 %collective-permute-start.31 = (bf16[32,1024]{1,0:T(8,128)(2,1)S(1)}, bf16[32,1024]{1,0:T(8,128)(2,1)S(1)}, u32[]{:S(2)}, u32[]{:S(2)}) collective-permute-start(bf16[32,1024]{1,0:T(8,128)(2,1)S(1)} %collective-permute-done.30.refs_2_), channel_id=1, source_target_pairs={{0,1},{1,0},{2,3},{3,2},{4,5},{5,4},{6,7},{7,6},{8,9},{9,8},{10,11... | collective-permute-start | bytes 196616 | tf_op jit(solution)/shard_map/ppermute | solution.py:367
  88.5 4.2 %collective-permute-start.21 = (bf16[32,1280]{1,0:T(8,128)(2,1)S(1)}, bf16[32,1280]{1,0:T(8,128)(2,1)S(1)}, u32[]{:S(2)}, u32[]{:S(2)}) collective-permute-start(bf16[32,1280]{1,0:T(8,128)(2,1)S(1)} %shard_map.117.refs_0_), channel_id=1, source_target_pairs={{0,1},{1,0},{2,3},{3,2},{4,5},{5,4},{6,7},{7,6},{8,9},{9,8},{10,11... | collective-permute-start | bytes 245768 | tf_op jit(solution)/shard_map/ppermute | solution.py:367
  89.3 2.1 %collective-permute-start.26 = (bf16[32,1280]{1,0:T(8,128)(2,1)S(1)}, bf16[32,1280]{1,0:T(8,128)(2,1)S(1)}, u32[]{:S(2)}, u32[]{:S(2)}) collective-permute-start(bf16[32,1280]{1,0:T(8,128)(2,1)S(1)} %shard_map.120.refs_0_), channel_id=1, source_target_pairs={{0,1},{1,0},{2,3},{3,2},{4,5},{5,4},{6,7},{7,6},{8,9},{9,8},{10,11... | collective-permute-start | bytes 245768 | tf_op jit(solution)/shard_map/ppermute | solution.py:367
  89.4 3.3 %collective-permute-start.23 = (bf16[32,1280]{1,0:T(8,128)(2,1)S(1)}, bf16[32,1280]{1,0:T(8,128)(2,1)S(1)}, u32[]{:S(2)}, u32[]{:S(2)}) collective-permute-start(bf16[32,1280]{1,0:T(8,128)(2,1)S(1)} %collective-permute-done.22.refs_2_), channel_id=1, source_target_pairs={{0,1},{1,0},{2,3},{3,2},{4,5},{5,4},{6,7},{7,6},{8,9},{9,8},{10,11... | collective-permute-start | bytes 245768 | tf_op jit(solution)/shard_map/ppermute | solution.py:367
  90.5 1.3 %collective-permute-start.28 = (bf16[32,1280]{1,0:T(8,128)(2,1)S(1)}, bf16[32,1280]{1,0:T(8,128)(2,1)S(1)}, u32[]{:S(2)}, u32[]{:S(2)}) collective-permute-start(bf16[32,1280]{1,0:T(8,128)(2,1)S(1)} %collective-permute-done.27.refs_2_), channel_id=1, source_target_pairs={{0,1},{1,0},{2,3},{3,2},{4,5},{5,4},{6,7},{7,6},{8,9},{9,8},{10,11... | collective-permute-start | bytes 245768 | tf_op jit(solution)/shard_map/ppermute | solution.py:367
  93.2 4.3 %collective-permute-start.33 = (bf16[32,1024]{1,0:T(8,128)(2,1)S(1)}, bf16[32,1024]{1,0:T(8,128)(2,1)S(1)}, u32[]{:S(2)}, u32[]{:S(2)}) collective-permute-start(bf16[32,1024]{1,0:T(8,128)(2,1)S(1)} %get-tuple-element.86), channel_id=1, source_target_pairs={{0,4},{4,0},{8,12},{12,8},{1,5},{5,1},{9,13},{13,9},{2,6},{6,2},{1... | collective-permute-start | bytes 196616 | tf_op jit(solution)/shard_map/ppermute | solution.py:371
  95.5 10.6 %collective-permute-start.32 = (bf16[32,2048]{1,0:T(8,128)(2,1)S(1)}, bf16[32,2048]{1,0:T(8,128)(2,1)S(1)}, u32[]{:S(2)}, u32[]{:S(2)}) collective-permute-start(bf16[32,2048]{1,0:T(8,128)(2,1)S(1)} %get-tuple-element.82), channel_id=1, source_target_pairs={{0,4},{4,0},{8,12},{12,8},{1,5},{5,1},{9,13},{13,9},{2,6},{6,2},{1... | collective-permute-start | bytes 393224 | tf_op jit(solution)/shard_map/ppermute | solution.py:371
  95.9 7.7 %collective-permute-start.35 = (bf16[32,1024]{1,0:T(8,128)(2,1)S(1)}, bf16[32,1024]{1,0:T(8,128)(2,1)S(1)}, u32[]{:S(2)}, u32[]{:S(2)}) collective-permute-start(bf16[32,1024]{1,0:T(8,128)(2,1)S(1)} %get-tuple-element.88), channel_id=1, source_target_pairs={{0,4},{4,0},{8,12},{12,8},{1,5},{5,1},{9,13},{13,9},{2,6},{6,2},{1... | collective-permute-start | bytes 196616 | tf_op jit(solution)/shard_map/ppermute | solution.py:371
  97.6 8.5 %collective-permute-start.34 = (bf16[32,1024]{1,0:T(8,128)(2,1)S(1)}, bf16[32,1024]{1,0:T(8,128)(2,1)S(1)}, u32[]{:S(2)}, u32[]{:S(2)}) collective-permute-start(bf16[32,1024]{1,0:T(8,128)(2,1)S(1)} %shard_map.125), channel_id=1, source_target_pairs={{0,8},{4,12},{8,0},{12,4},{1,9},{5,13},{9,1},{13,5},{2,10},{6,14},... | collective-permute-start | bytes 196616 | tf_op jit(solution)/shard_map/ppermute | solution.py:371
  103.6 5.9 %collective-permute-start.36 = (bf16[32,1024]{1,0:T(8,128)(2,1)S(1)}, bf16[32,1024]{1,0:T(8,128)(2,1)S(1)}, u32[]{:S(2)}, u32[]{:S(2)}) collective-permute-start(bf16[32,1024]{1,0:T(8,128)(2,1)S(1)} %shard_map.126), channel_id=1, source_target_pairs={{0,8},{4,12},{8,0},{12,4},{1,9},{5,13},{9,1},{13,5},{2,10},{6,14},... | collective-permute-start | bytes 196616 | tf_op jit(solution)/shard_map/ppermute | solution.py:371
  (6 other events, 44.4 us)

commit v5 on v4

--- a/solution.py
+++ b/solution.py
@@ -329,10 +329,8 @@
 
 
 def down_kernel(tile, first, *refs):
-    pieces, (weight_ref, so_far_ref) = refs[:4], refs[4:6]
-    given, (own_ref, *sends, rows_ref) = refs[6:-5], refs[-5:]
-    for ref in given:
-        sends[0][:, :first] = ref[...]
+    pieces, (weight_ref, so_far_ref, own_ref) = refs[:4], refs[4:7]
+    sends, rows_ref = refs[7:-1], refs[-1]
     gather_rows(pieces, rows_ref)
     rows = pieces[0].shape[0]
     depth = rows_ref.shape[1]
@@ -345,22 +343,21 @@
         )
         own_ref[:, target] = part[:rows]
         for n, send in enumerate(sends):
-            place_at = source if send.shape[1] > own_ref.shape[1] else target
-            send[:, place_at] = part[(n + 1) * rows : (n + 2) * rows].astype(send.dtype)
+            send[:, target] = part[(n + 1) * rows : (n + 2) * rows].astype(send.dtype)
 
 
 def add_kernel(own_ref, got_ref, out_ref):
     out_ref[...] = (own_ref[...] + got_ref[...].astype(F32)).astype(BF16)
 
 
-def final_kernel(middle_ref, near_ref, *refs):
-    owns, fars, out_ref = refs[:2], refs[2:4], refs[4]
-    start = 0
-    for own, far in zip(owns, fars):
-        columns = slice(start, start + own.shape[1])
-        total = own[...] + near_ref[:, columns].astype(F32) + far[...].astype(F32)
+def final_kernel(middle_ref, *refs):
+    parts, out_ref = refs[:-1], refs[-1]
+    width = out_ref.shape[1] * 3 // len(parts)
+    for n in range(0, len(parts), 3):
+        columns = slice(n // 3 * width, (n // 3 + 1) * width)
+        own, near, far = parts[n : n + 3]
+        total = own[...] + near[...].astype(F32) + far[...].astype(F32)
         out_ref[:, columns] = (middle_ref[:, columns].astype(F32) + total).astype(BF16)
-        start += own.shape[1]
 
 
 def swap(x, axis):
@@ -542,30 +539,21 @@
             ),
         )
     half = out_width // 2
-    owns, fars = [], []
-    near = ()
+    results = []
     for n in range(2):
-        own, beside, two, three = call(
+        own, near, two, three = call(
             functools.partial(down_kernel, 512, n * half),
-            tuple(
-                struct((rows, w), t)
-                for w, t in ((half, F32), ((n + 1) * half, BF16), (half, F32), (half, BF16))
-            ),
-            [VM] * (6 + n),
-            hidden[-1] + (down_vmem,) + so_far + near,
+            tuple(struct((rows, half), t) for t in (F32, BF16, F32, BF16)),
+            [VM] * 6,
+            hidden[-1] + (down_vmem,) + so_far,
             scratch=[pltpu.VMEM((total, chunks[-1][1]), BF16)],
         )
-        near = (beside,)
-        pair = call(
-            add_kernel, struct((rows, half), BF16), [VM] * 2, (two, turn(three, CTX, n_context, 1))
-        )
-        owns.append(own)
-        fars.append(turn(pair, CTX, n_context, 2))
+        beside = turn(three, CTX, n_context, 1)
+        pair = call(add_kernel, struct((rows, half), BF16), [VM] * 2, (two, beside))
+        far = turn(pair, CTX, n_context, 2)
+        results += [own, turn(near, CTX, n_context, 1), far]
     return call(
-        final_kernel,
-        struct((rows, out_width), BF16),
-        [VM] * 6,
-        (all_middle[0], turn(near[0], CTX, n_context, 1), *owns, *fars),
+        final_kernel, struct((rows, out_width), BF16), [VM] * 7, (all_middle[0],) + tuple(results)
     )
 
 

time: 110 us -> 109 us (level)
  waiting for transfers between devices: 42.6 us -> 40.9 us
    ppermute x16 -> x17, waiting for transfers between devices: 23.7 us -> 21.9 us  [turn(): return lax.ppermute(x, axis, [(i, i ^ offset) for i in range(n)])]
    ppermute x16 -> x17, starting transfers between devices: 25.1 us -> 25.7 us  [turn(): return lax.ppermute(x, axis, [(i, i ^ offset) for i in range(n)])]
  transfers between devices with their start and end apart: 37 -> 38, of which waited for: 18 -> 19; matrix products, arithmetic and copies ran while one was open for 0% -> 0% of each run, Pallas kernels for 10% -> 10%
where the time goes in v5:
time: 109 us
  starting transfers between devices  51.3 us (47%)
  waiting for transfers between devices  40.9 us (38%)
  Pallas kernels  15.8 us (14%)
    ppermute x17, starting transfers between devices, turn(): return lax.ppermute(x, axis, [(i, i ^ offset) for i in range(n)])  25.7 us
    ppermute x17, waiting for transfers between devices, turn(): return lax.ppermute(x, axis, [(i, i ^ offset) for i in range(n)])  21.9 us
    ppermute x17, starting transfers between devices, swap(): return lax.ppermute(x, axis, [(0, 1), (1, 0)])  18.2 us
    pallas_call x28, Pallas kernels, call(): pl.pallas_call(kernel, out_shape=out, in_specs=in_specs, out_specs=jax.tr...  15.8 us
    ppermute x17, waiting for transfers between devices, swap(): return lax.ppermute(x, axis, [(0, 1), (1, 0)])  12.6 us
    ppermute x4, starting transfers between devices, direct_body(): lax.ppermute(middle, ALL, [(a * n_context + b, (b ^ m) * n_context + a) f...  7.45 us
    ppermute x4, waiting for transfers between devices, direct_body(): lax.ppermute(middle, ALL, [(a * n_context + b, (b ^ m) * n_context + a) f...  6.3 us
  transfers between devices with their start and end apart: 38, of which 19 were waited for; matrix products, arithmetic and copies ran while one was open for 0% of the time, Pallas kernels for 10%

profile of v5, /device:TPU:0, one launch (start us, length us, event | category | flops | bytes accessed | tf_op | source)
XLA Modules:
  0.0 109.1 jit_solution(3242550887041133411)
XLA Ops:
  0.0 3.1 %collective-permute-start = (bf16[32,2048]{1,0:T(8,128)(2,1)}, bf16[32,2048]{1,0:T(8,128)(2,1)S(1)}, u32[]{:S(2)}, u32[]{:S(2)}) collective-permute-start(bf16[32,2048]{1,0:T(8,128)(2,1)} %q_hbm.1), channel_id=1, source_target_pairs={{0,4},{4,0},{8,12},{12,8},{1,5},{5,1},{9,13},{13,9},{2,6},{6,2},{1... | collective-permute-start | bytes 393224 | tf_op jit(solution)/shard_map/ppermute | solution.py:368
  3.1 2.6 %collective-permute-start.2 = (bf16[32,2048]{1,0:T(8,128)(2,1)}, bf16[32,2048]{1,0:T(8,128)(2,1)S(1)}, u32[]{:S(2)}, u32[]{:S(2)}) collective-permute-start(bf16[32,2048]{1,0:T(8,128)(2,1)} %q_hbm.1), channel_id=1, source_target_pairs={{0,8},{4,12},{8,0},{12,4},{1,9},{5,13},{9,1},{13,5},{2,10},{6,14},... | collective-permute-start | bytes 393224 | tf_op jit(solution)/shard_map/ppermute | solution.py:368
  6.3 2.6 %shard_map.100 = (bf16[512,256]{1,0:T(8,128)(2,1)S(1)}, bf16[512,256]{1,0:T(8,128)(2,1)S(1)}, s32[8,128]{1,0:T(8,128)S(1)}, bf16[32,2176]{1,0:T(8,128)(2,1)S(1)}) custom-call(s32[1,8]{1,0:T(1,128)S(1)} %copy-done.2, bf16[32,2048]{1,0:T(8,128)(2,1)} %q_hbm.1, bf16[2048,256]{1,0:T(8,128)(2,1)} %key_hbm.1, bf16[2048,256]{1,0:T(8,128)(2,1)} %value_hbm.1), custom_call_target="tpu_custom_call" | custom-call | flops 3000000000 | bytes 2895904 | tf_op jit(solution)/shard_map/pallas_call | solution.py:40
  8.9 0.8 shard_map.101
  10.2 1.8 %collective-permute-done.2.q_ref = bf16[32,2048]{1,0:T(8,128)(2,1)S(1)} collective-permute-done((bf16[32,2048]{1,0:T(8,128)(2,1)}, bf16[32,2048]{1,0:T(8,128)(2,1)S(1)}, u32[]{:S(2)}, u32[]{:S(2)}) %collective-permute-start.2) | collective-permute-done | bytes 131104 | tf_op jit(solution)/shard_map/ppermute | solution.py:368
  12.4 0.8 shard_map.102
  13.2 2.7 %collective-permute-start.3 = (bf16[32,2176]{1,0:T(8,128)(2,1)S(1)}, bf16[32,2176]{1,0:T(8,128)(2,1)S(1)}, u32[]{:S(2)}, u32[]{:S(2)}) collective-permute-start(bf16[32,2176]{1,0:T(8,128)(2,1)S(1)} %shard_map.102), channel_id=1, source_target_pairs={{0,8},{4,12},{8,0},{12,4},{1,9},{5,13},{9,1},{13,5},{2,10},{6,14},... | collective-permute-start | bytes 417800 | tf_op jit(solution)/shard_map/ppermute | solution.py:368
  15.9 4.4 %collective-permute-done.4.q_ref = bf16[32,2048]{1,0:T(8,128)(2,1)S(1)} collective-permute-done((bf16[32,2048]{1,0:T(8,128)(2,1)S(1)}, bf16[32,2048]{1,0:T(8,128)(2,1)S(1)}, u32[]{:S(2)}, u32[]{:S(2)}) %collective-permute-start.4) | collective-permute-done | bytes 131104 | tf_op jit(solution)/shard_map/ppermute | solution.py:368
  20.3 0.8 shard_map.103
  21.1 1.9 %collective-permute-start.5 = (bf16[32,2176]{1,0:T(8,128)(2,1)S(1)}, bf16[32,2176]{1,0:T(8,128)(2,1)S(1)}, u32[]{:S(2)}, u32[]{:S(2)}) collective-permute-start(bf16[32,2176]{1,0:T(8,128)(2,1)S(1)} %shard_map.103), channel_id=1, source_target_pairs={{0,12},{4,8},{8,4},{12,0},{1,13},{5,9},{9,5},{13,1},{2,14},{6,10},... | collective-permute-start | bytes 417800 | tf_op jit(solution)/shard_map/ppermute | solution.py:368
  23.1 5.0 %collective-permute-done.5.refs_3_ = bf16[32,2176]{1,0:T(8,128)(2,1)S(1)} collective-permute-done((bf16[32,2176]{1,0:T(8,128)(2,1)S(1)}, bf16[32,2176]{1,0:T(8,128)(2,1)S(1)}, u32[]{:S(2)}, u32[]{:S(2)}) %collective-permute-start.5) | collective-permute-done | bytes 139296 | tf_op jit(solution)/shard_map/ppermute | solution.py:368
  28.5 1.2 %collective-permute-start.7 = (bf16[32,1024]{1,0:T(8,128)(2,1)S(1)}, bf16[32,1024]{1,0:T(8,128)(2,1)S(1)}, u32[]{:S(2)}, u32[]{:S(2)}) collective-permute-start(bf16[32,1024]{1,0:T(8,128)(2,1)S(1)} %get-tuple-element.52), channel_id=1, source_target_pairs={{0,8},{4,12},{8,0},{12,4},{1,9},{5,13},{9,1},{13,5},{2,10},{6,14},... | collective-permute-start | bytes 196616 | tf_op jit(solution)/shard_map/ppermute | solution.py:368
  29.8 1.8 %collective-permute-start.8 = (bf16[32,1024]{1,0:T(8,128)(2,1)S(1)}, bf16[32,1024]{1,0:T(8,128)(2,1)S(1)}, u32[]{:S(2)}, u32[]{:S(2)}) collective-permute-start(bf16[32,1024]{1,0:T(8,128)(2,1)S(1)} %get-tuple-element.53), channel_id=1, source_target_pairs={{0,8},{4,12},{8,0},{12,4},{1,9},{5,13},{9,1},{13,5},{2,10},{6,14},... | collective-permute-start | bytes 196616 | tf_op jit(solution)/shard_map/ppermute | solution.py:368
  31.5 2.5 %collective-permute-done.7.refs_2_ = bf16[32,1024]{1,0:T(8,128)(2,1)S(1)} collective-permute-done((bf16[32,1024]{1,0:T(8,128)(2,1)S(1)}, bf16[32,1024]{1,0:T(8,128)(2,1)S(1)}, u32[]{:S(2)}, u32[]{:S(2)}) %collective-permute-start.7) | collective-permute-done | bytes 65568 | tf_op jit(solution)/shard_map/ppermute | solution.py:368
  34.1 0.9 collective-permute-done.8.refs_3_
  35.0 1.4 %collective-permute-start.10 = (bf16[32,1024]{1,0:T(8,128)(2,1)S(1)}, bf16[32,1024]{1,0:T(8,128)(2,1)S(1)}, u32[]{:S(2)}, u32[]{:S(2)}) collective-permute-start(bf16[32,1024]{1,0:T(8,128)(2,1)S(1)} %collective-permute-done.8.refs_3_), channel_id=1, source_target_pairs={{0,4},{4,0},{8,12},{12,8},{1,5},{5,1},{9,13},{13,9},{2,6},{6,2},{1... | collective-permute-start | bytes 196616 | tf_op jit(solution)/shard_map/ppermute | solution.py:368
  36.4 1.8 %collective-permute-done.9.refs_4_ = bf16[32,1024]{1,0:T(8,128)(2,1)S(1)} collective-permute-done((bf16[32,1024]{1,0:T(8,128)(2,1)S(1)}, bf16[32,1024]{1,0:T(8,128)(2,1)S(1)}, u32[]{:S(2)}, u32[]{:S(2)}) %collective-permute-start.9) | collective-permute-done | bytes 65568 | tf_op jit(solution)/shard_map/ppermute | solution.py:368
  38.3 1.0 collective-permute-done.10.refs_5_
  39.3 1.3 %shard_map.105 = (f32[64,2048]{1,0:T(8,128)S(1)}, bf16[64,2048]{1,0:T(8,128)(2,1)S(1)}) custom-call(bf16[32,2048]{1,0:T(8,128)(2,1)S(1)} %get-tuple-element.51.refs_0_, bf16[32,2048]{1,0:T(8,128)(2,1)S(1)} %collective-permute-done.6.refs_1_, bf16[32,1024]{1,0:T(8,128)(2,1)S(1)} %collective-permute-done.7.refs_2_, ...), custom_call_target="tpu_custom_call" | custom-call | flops 6000000000 | bytes 9699328 | tf_op jit(solution)/shard_map/pallas_call | solution.py:40
  40.7 1.5 %collective-permute-done.11.got_ref = bf16[64,2048]{1,0:T(8,128)(2,1)S(1)} collective-permute-done((bf16[64,2048]{1,0:T(8,128)(2,1)S(1)}, bf16[64,2048]{1,0:T(8,128)(2,1)S(1)}, u32[]{:S(2)}, u32[]{:S(2)}) %collective-permute-start.11) | collective-permute-done | bytes 262176 | tf_op jit(solution)/shard_map/ppermute | solution.py:364
  42.3 1.5 %collective-permute-start.12 = (bf16[32,2048]{1,0:T(8,128)(2,1)S(1)}, bf16[32,2048]{1,0:T(8,128)(2,1)S(1)}, u32[]{:S(2)}, u32[]{:S(2)}) collective-permute-start(bf16[32,2048]{1,0:T(8,128)(2,1)S(1)} %get-tuple-element.57), channel_id=1, source_target_pairs={{0,2},{2,0},{1,3},{3,1},{4,6},{6,4},{5,7},{7,5},{8,10},{10,8},{9,1... | collective-permute-start | bytes 393224 | tf_op jit(solution)/shard_map/ppermute | solution.py:364
  43.8 4.0 %collective-permute-done.12.got_ref = bf16[32,2048]{1,0:T(8,128)(2,1)S(1)} collective-permute-done((bf16[32,2048]{1,0:T(8,128)(2,1)S(1)}, bf16[32,2048]{1,0:T(8,128)(2,1)S(1)}, u32[]{:S(2)}, u32[]{:S(2)}) %collective-permute-start.12) | collective-permute-done | bytes 131104 | tf_op jit(solution)/shard_map/ppermute | solution.py:364
  48.0 0.8 collective-permute-start.13
  48.8 3.0 %collective-permute-start.14 = (bf16[32,2048]{1,0:T(8,128)(2,1)S(1)}, bf16[32,2048]{1,0:T(8,128)(2,1)S(1)}, u32[]{:S(2)}, u32[]{:S(2)}) collective-permute-start(bf16[32,2048]{1,0:T(8,128)(2,1)S(1)} %shard_map.107), channel_id=1, source_target_pairs={{0,4},{1,0},{2,12},{3,8},{4,5},{5,1},{6,13},{7,9},{8,6},{9,2},{10,... | collective-permute-start | bytes 393224 | tf_op jit(solution)/shard_map/ppermute | solution.py:455
  51.8 2.5 %collective-permute-start.15 = (bf16[32,2048]{1,0:T(8,128)(2,1)S(1)}, bf16[32,2048]{1,0:T(8,128)(2,1)S(1)}, u32[]{:S(2)}, u32[]{:S(2)}) collective-permute-start(bf16[32,2048]{1,0:T(8,128)(2,1)S(1)} %shard_map.107), channel_id=1, source_target_pairs={{0,8},{1,12},{2,0},{3,4},{4,9},{5,13},{6,1},{7,5},{8,10},{9,14},{1... | collective-permute-start | bytes 393224 | tf_op jit(solution)/shard_map/ppermute | solution.py:455
  54.2 1.2 %collective-permute-start.16 = (bf16[32,2048]{1,0:T(8,128)(2,1)S(1)}, bf16[32,2048]{1,0:T(8,128)(2,1)S(1)}, u32[]{:S(2)}, u32[]{:S(2)}) collective-permute-start(bf16[32,2048]{1,0:T(8,128)(2,1)S(1)} %shard_map.107), channel_id=1, source_target_pairs={{0,12},{1,8},{2,4},{3,0},{4,13},{5,9},{6,5},{7,1},{8,14},{9,10},{1... | collective-permute-start | bytes 393224 | tf_op jit(solution)/shard_map/ppermute | solution.py:455
  55.7 6.3 %collective-permute-done.15.piece_ref = bf16[32,2048]{1,0:T(8,128)(2,1)S(1)} collective-permute-done((bf16[32,2048]{1,0:T(8,128)(2,1)S(1)}, bf16[32,2048]{1,0:T(8,128)(2,1)S(1)}, u32[]{:S(2)}, u32[]{:S(2)}) %collective-permute-start.15) | collective-permute-done | bytes 131104 | tf_op jit(solution)/shard_map/ppermute | solution.py:455
  62.3 1.6 %shard_map.112 = (f32[64,2176]{1,0:T(8,128)S(1)}, bf16[64,2304]{1,0:T(8,128)(2,1)S(1)}, bf16[128,2048]{1,0:T(8,128)(2,1)S(1)}) custom-call(bf16[32,2048]{1,0:T(8,128)(2,1)S(1)} %get-tuple-element.58.refs_0_, bf16[32,2048]{1,0:T(8,128)(2,1)S(1)} %get-tuple-element.59.refs_1_, bf16[32,2048]{1,0:T(8,128)(2,1)S(1)} %get-tuple-element.60.refs_2_, ...), custom_call_target="tpu_custom_call" | custom-call | flops 3000000000 | bytes 31326208 | tf_op jit(solution)/shard_map/pallas_call | solution.py:40
  63.9 0.8 collective-permute-start.17
  64.6 1.5 %shard_map.115 = (f32[64,2560]{1,0:T(8,128)S(1)}, bf16[64,2560]{1,0:T(8,128)(2,1)S(1)}) custom-call(bf16[128,2048]{1,0:T(8,128)(2,1)S(1)} %get-tuple-element.71.rows_ref, bf16[2048,3584]{1,0:T(8,128)(2,1)S(1)} %bitcast.4, bf16[2048,3584]{1,0:T(8,128)(2,1)S(1)} %bitcast.6), custom_call_target="tpu_custom_call" | custom-call | flops 3000000000 | bytes 30867456 | tf_op jit(solution)/shard_map/pallas_call | solution.py:40
  66.3 1.5 %shard_map.118 = (f32[64,2560]{1,0:T(8,128)S(1)}, bf16[64,2560]{1,0:T(8,128)(2,1)S(1)}) custom-call(bf16[128,2048]{1,0:T(8,128)(2,1)S(1)} %get-tuple-element.71.rows_ref, bf16[2048,3584]{1,0:T(8,128)(2,1)S(1)} %bitcast.4, bf16[2048,3584]{1,0:T(8,128)(2,1)S(1)} %bitcast.6), custom_call_target="tpu_custom_call" | custom-call | flops 3000000000 | bytes 30867456 | tf_op jit(solution)/shard_map/pallas_call | solution.py:40
  68.4 5.7 %collective-permute-start.18 = (bf16[32,2304]{1,0:T(8,128)(2,1)S(1)}, bf16[32,2304]{1,0:T(8,128)(2,1)S(1)}, u32[]{:S(2)}, u32[]{:S(2)}) collective-permute-start(bf16[32,2304]{1,0:T(8,128)(2,1)S(1)} %get-tuple-element.69), channel_id=1, source_target_pairs={{0,2},{2,0},{1,3},{3,1},{4,6},{6,4},{5,7},{7,5},{8,10},{10,8},{9,1... | collective-permute-start | bytes 442376 | tf_op jit(solution)/shard_map/ppermute | solution.py:364
  74.3 2.1 %collective-permute-start.25 = (bf16[32,2560]{1,0:T(8,128)(2,1)S(1)}, bf16[32,2560]{1,0:T(8,128)(2,1)S(1)}, u32[]{:S(2)}, u32[]{:S(2)}) collective-permute-start(bf16[32,2560]{1,0:T(8,128)(2,1)S(1)} %get-tuple-element.79), channel_id=1, source_target_pairs={{0,2},{2,0},{1,3},{3,1},{4,6},{6,4},{5,7},{7,5},{8,10},{10,8},{9,1... | collective-permute-start | bytes 491528 | tf_op jit(solution)/shard_map/ppermute | solution.py:364
  76.4 2.4 %collective-permute-done.18.got_ref = bf16[32,2304]{1,0:T(8,128)(2,1)S(1)} collective-permute-done((bf16[32,2304]{1,0:T(8,128)(2,1)S(1)}, bf16[32,2304]{1,0:T(8,128)(2,1)S(1)}, u32[]{:S(2)}, u32[]{:S(2)}) %collective-permute-start.18) | collective-permute-done | bytes 147488 | tf_op jit(solution)/shard_map/ppermute | solution.py:364
  78.9 2.1 %collective-permute-start.30 = (bf16[32,1024]{1,0:T(8,128)(2,1)S(1)}, bf16[32,1024]{1,0:T(8,128)(2,1)S(1)}, u32[]{:S(2)}, u32[]{:S(2)}) collective-permute-start(bf16[32,1024]{1,0:T(8,128)(2,1)S(1)} %get-tuple-element.80.refs_0_), channel_id=1, source_target_pairs={{0,2},{2,0},{1,3},{3,1},{4,6},{6,4},{5,7},{7,5},{8,10},{10,8},{9,1... | collective-permute-start | bytes 196616 | tf_op jit(solution)/shard_map/ppermute | solution.py:364
  81.0 1.3 %collective-permute-done.20.got_ref = bf16[32,2560]{1,0:T(8,128)(2,1)S(1)} collective-permute-done((bf16[32,2560]{1,0:T(8,128)(2,1)S(1)}, bf16[32,2560]{1,0:T(8,128)(2,1)S(1)}, u32[]{:S(2)}, u32[]{:S(2)}) %collective-permute-start.20) | collective-permute-done | bytes 163872 | tf_op jit(solution)/shard_map/ppermute | solution.py:364
  82.4 2.1 %collective-permute-start.22 = (bf16[32,1280]{1,0:T(8,128)(2,1)S(1)}, bf16[32,1280]{1,0:T(8,128)(2,1)S(1)}, u32[]{:S(2)}, u32[]{:S(2)}) collective-permute-start(bf16[32,1280]{1,0:T(8,128)(2,1)S(1)} %shard_map.117.refs_0_), channel_id=1, source_target_pairs={{0,2},{2,0},{1,3},{3,1},{4,6},{6,4},{5,7},{7,5},{8,10},{10,8},{9,1... | collective-permute-start | bytes 245768 | tf_op jit(solution)/shard_map/ppermute | solution.py:364
  84.5 1.3 %collective-permute-done.25.got_ref = bf16[32,2560]{1,0:T(8,128)(2,1)S(1)} collective-permute-done((bf16[32,2560]{1,0:T(8,128)(2,1)S(1)}, bf16[32,2560]{1,0:T(8,128)(2,1)S(1)}, u32[]{:S(2)}, u32[]{:S(2)}) %collective-permute-start.25) | collective-permute-done | bytes 163872 | tf_op jit(solution)/shard_map/ppermute | solution.py:364
  85.9 2.1 %collective-permute-start.27 = (bf16[32,1280]{1,0:T(8,128)(2,1)S(1)}, bf16[32,1280]{1,0:T(8,128)(2,1)S(1)}, u32[]{:S(2)}, u32[]{:S(2)}) collective-permute-start(bf16[32,1280]{1,0:T(8,128)(2,1)S(1)} %shard_map.120.refs_0_), channel_id=1, source_target_pairs={{0,2},{2,0},{1,3},{3,1},{4,6},{6,4},{5,7},{7,5},{8,10},{10,8},{9,1... | collective-permute-start | bytes 245768 | tf_op jit(solution)/shard_map/ppermute | solution.py:364
  89.8 0.8 collective-permute-done.27.refs_2_
  91.8 0.9 shard_map.122.refs_5_
  93.2 1.7 %collective-permute-start.32 = (bf16[32,1024]{1,0:T(8,128)(2,1)S(1)}, bf16[32,1024]{1,0:T(8,128)(2,1)S(1)}, u32[]{:S(2)}, u32[]{:S(2)}) collective-permute-start(bf16[32,1024]{1,0:T(8,128)(2,1)S(1)} %get-tuple-element.82), channel_id=1, source_target_pairs={{0,4},{4,0},{8,12},{12,8},{1,5},{5,1},{9,13},{13,9},{2,6},{6,2},{1... | collective-permute-start | bytes 196616 | tf_op jit(solution)/shard_map/ppermute | solution.py:368
  95.9 1.7 %collective-permute-start.35 = (bf16[32,1024]{1,0:T(8,128)(2,1)S(1)}, bf16[32,1024]{1,0:T(8,128)(2,1)S(1)}, u32[]{:S(2)}, u32[]{:S(2)}) collective-permute-start(bf16[32,1024]{1,0:T(8,128)(2,1)S(1)} %get-tuple-element.86), channel_id=1, source_target_pairs={{0,4},{4,0},{8,12},{12,8},{1,5},{5,1},{9,13},{13,9},{2,6},{6,2},{1... | collective-permute-start | bytes 196616 | tf_op jit(solution)/shard_map/ppermute | solution.py:368
  98.0 1.9 %collective-permute-done.33.got_ref = bf16[32,1024]{1,0:T(8,128)(2,1)S(1)} collective-permute-done((bf16[32,1024]{1,0:T(8,128)(2,1)S(1)}, bf16[32,1024]{1,0:T(8,128)(2,1)S(1)}, u32[]{:S(2)}, u32[]{:S(2)}) %collective-permute-start.33) | collective-permute-done | bytes 65568 | tf_op jit(solution)/shard_map/ppermute | solution.py:368
  99.9 3.2 %collective-permute-start.34 = (bf16[32,1024]{1,0:T(8,128)(2,1)S(1)}, bf16[32,1024]{1,0:T(8,128)(2,1)S(1)}, u32[]{:S(2)}, u32[]{:S(2)}) collective-permute-start(bf16[32,1024]{1,0:T(8,128)(2,1)S(1)} %shard_map.124), channel_id=1, source_target_pairs={{0,8},{4,12},{8,0},{12,4},{1,9},{5,13},{9,1},{13,5},{2,10},{6,14},... | collective-permute-start | bytes 196616 | tf_op jit(solution)/shard_map/ppermute | solution.py:368
  103.1 2.7 %collective-permute-start.37 = (bf16[32,1024]{1,0:T(8,128)(2,1)S(1)}, bf16[32,1024]{1,0:T(8,128)(2,1)S(1)}, u32[]{:S(2)}, u32[]{:S(2)}) collective-permute-start(bf16[32,1024]{1,0:T(8,128)(2,1)S(1)} %shard_map.126), channel_id=1, source_target_pairs={{0,8},{4,12},{8,0},{12,4},{1,9},{5,13},{9,1},{13,5},{2,10},{6,14},... | collective-permute-start | bytes 196616 | tf_op jit(solution)/shard_map/ppermute | solution.py:368
  105.8 1.4 %collective-permute-done.34.refs_2_ = bf16[32,1024]{1,0:T(8,128)(2,1)S(1)} collective-permute-done((bf16[32,1024]{1,0:T(8,128)(2,1)S(1)}, bf16[32,1024]{1,0:T(8,128)(2,1)S(1)}, u32[]{:S(2)}, u32[]{:S(2)}) %collective-permute-start.34) | collective-permute-done | bytes 65568 | tf_op jit(solution)/shard_map/ppermute | solution.py:368
  107.2 1.2 %collective-permute-done.37.refs_5_ = bf16[32,1024]{1,0:T(8,128)(2,1)S(1)} collective-permute-done((bf16[32,1024]{1,0:T(8,128)(2,1)S(1)}, bf16[32,1024]{1,0:T(8,128)(2,1)S(1)}, u32[]{:S(2)}, u32[]{:S(2)}) %collective-permute-start.37) | collective-permute-done | bytes 65568 | tf_op jit(solution)/shard_map/ppermute | solution.py:368
  (94 shorter events, 9.6 us)
Async XLA Ops:
  0.0 8.9 %collective-permute-start = (bf16[32,2048]{1,0:T(8,128)(2,1)}, bf16[32,2048]{1,0:T(8,128)(2,1)S(1)}, u32[]{:S(2)}, u32[]{:S(2)}) collective-permute-start(bf16[32,2048]{1,0:T(8,128)(2,1)} %q_hbm.1), channel_id=1, source_target_pairs={{0,4},{4,0},{8,12},{12,8},{1,5},{5,1},{9,13},{13,9},{2,6},{6,2},{1... | collective-permute-start | bytes 393224 | tf_op jit(solution)/shard_map/ppermute | solution.py:368
  3.1 9.0 %collective-permute-start.2 = (bf16[32,2048]{1,0:T(8,128)(2,1)}, bf16[32,2048]{1,0:T(8,128)(2,1)S(1)}, u32[]{:S(2)}, u32[]{:S(2)}) collective-permute-start(bf16[32,2048]{1,0:T(8,128)(2,1)} %q_hbm.1), channel_id=1, source_target_pairs={{0,8},{4,12},{8,0},{12,4},{1,9},{5,13},{9,1},{13,5},{2,10},{6,14},... | collective-permute-start | bytes 393224 | tf_op jit(solution)/shard_map/ppermute | solution.py:368
  9.7 29.5 %slice-start.12 = ((s8[8388608]{0:T(1024)(128)(4,1)}), s8[4194304]{0:T(1024)(128)(4,1)S(1)}, s32[]{:S(2)}) async-start(s8[8388608]{0:T(1024)(128)(4,1)} %bitcast.11), calls=%async_computation.12 | async-start | bytes 8388608
  9.7 13.3 %collective-permute-start.1 = (bf16[32,2176]{1,0:T(8,128)(2,1)S(1)}, bf16[32,2176]{1,0:T(8,128)(2,1)S(1)}, u32[]{:S(2)}, u32[]{:S(2)}) collective-permute-start(bf16[32,2176]{1,0:T(8,128)(2,1)S(1)} %shard_map.101), channel_id=1, source_target_pairs={{0,4},{4,0},{8,12},{12,8},{1,5},{5,1},{9,13},{13,9},{2,6},{6,2},{1... | collective-permute-start | bytes 417800 | tf_op jit(solution)/shard_map/ppermute | solution.py:368
  12.1 8.2 %collective-permute-start.4 = (bf16[32,2048]{1,0:T(8,128)(2,1)S(1)}, bf16[32,2048]{1,0:T(8,128)(2,1)S(1)}, u32[]{:S(2)}, u32[]{:S(2)}) collective-permute-start(bf16[32,2048]{1,0:T(8,128)(2,1)S(1)} %collective-permute-done.2.q_ref), channel_id=1, source_target_pairs={{0,4},{4,0},{8,12},{12,8},{1,5},{5,1},{9,13},{13,9},{2,6},{6,2},{1... | collective-permute-start | bytes 393224 | tf_op jit(solution)/shard_map/ppermute | solution.py:368
  13.2 26.0 %slice-start.13 = ((s8[8388608]{0:T(1024)(128)(4,1)}), s8[4194304]{0:T(1024)(128)(4,1)S(1)}, s32[]{:S(2)}) async-start(s8[8388608]{0:T(1024)(128)(4,1)} %bitcast.11), calls=%async_computation.13 | async-start | bytes 8388608
  13.2 9.8 %collective-permute-start.3 = (bf16[32,2176]{1,0:T(8,128)(2,1)S(1)}, bf16[32,2176]{1,0:T(8,128)(2,1)S(1)}, u32[]{:S(2)}, u32[]{:S(2)}) collective-permute-start(bf16[32,2176]{1,0:T(8,128)(2,1)S(1)} %shard_map.102), channel_id=1, source_target_pairs={{0,8},{4,12},{8,0},{12,4},{1,9},{5,13},{9,1},{13,5},{2,10},{6,14},... | collective-permute-start | bytes 417800 | tf_op jit(solution)/shard_map/ppermute | solution.py:368
  21.1 6.9 %collective-permute-start.5 = (bf16[32,2176]{1,0:T(8,128)(2,1)S(1)}, bf16[32,2176]{1,0:T(8,128)(2,1)S(1)}, u32[]{:S(2)}, u32[]{:S(2)}) collective-permute-start(bf16[32,2176]{1,0:T(8,128)(2,1)S(1)} %shard_map.103), channel_id=1, source_target_pairs={{0,12},{4,8},{8,4},{12,0},{1,13},{5,9},{9,5},{13,1},{2,14},{6,10},... | collective-permute-start | bytes 417800 | tf_op jit(solution)/shard_map/ppermute | solution.py:368
  28.5 5.5 %collective-permute-start.7 = (bf16[32,1024]{1,0:T(8,128)(2,1)S(1)}, bf16[32,1024]{1,0:T(8,128)(2,1)S(1)}, u32[]{:S(2)}, u32[]{:S(2)}) collective-permute-start(bf16[32,1024]{1,0:T(8,128)(2,1)S(1)} %get-tuple-element.52), channel_id=1, source_target_pairs={{0,8},{4,12},{8,0},{12,4},{1,9},{5,13},{9,1},{13,5},{2,10},{6,14},... | collective-permute-start | bytes 196616 | tf_op jit(solution)/shard_map/ppermute | solution.py:368
  29.8 5.2 %collective-permute-start.8 = (bf16[32,1024]{1,0:T(8,128)(2,1)S(1)}, bf16[32,1024]{1,0:T(8,128)(2,1)S(1)}, u32[]{:S(2)}, u32[]{:S(2)}) collective-permute-start(bf16[32,1024]{1,0:T(8,128)(2,1)S(1)} %get-tuple-element.53), channel_id=1, source_target_pairs={{0,8},{4,12},{8,0},{12,4},{1,9},{5,13},{9,1},{13,5},{2,10},{6,14},... | collective-permute-start | bytes 196616 | tf_op jit(solution)/shard_map/ppermute | solution.py:368
  31.5 7.7 %collective-permute-start.6 = (bf16[32,2048]{1,0:T(8,128)(2,1)S(1)}, bf16[32,2048]{1,0:T(8,128)(2,1)S(1)}, u32[]{:S(2)}, u32[]{:S(2)}) collective-permute-start(bf16[32,2048]{1,0:T(8,128)(2,1)S(1)} %get-tuple-element.51.refs_0_), channel_id=1, source_target_pairs={{0,4},{4,0},{8,12},{12,8},{1,5},{5,1},{9,13},{13,9},{2,6},{6,2},{1... | collective-permute-start | bytes 393224 | tf_op jit(solution)/shard_map/ppermute | solution.py:368
  34.0 4.3 %collective-permute-start.9 = (bf16[32,1024]{1,0:T(8,128)(2,1)S(1)}, bf16[32,1024]{1,0:T(8,128)(2,1)S(1)}, u32[]{:S(2)}, u32[]{:S(2)}) collective-permute-start(bf16[32,1024]{1,0:T(8,128)(2,1)S(1)} %collective-permute-done.7.refs_2_), channel_id=1, source_target_pairs={{0,4},{4,0},{8,12},{12,8},{1,5},{5,1},{9,13},{13,9},{2,6},{6,2},{1... | collective-permute-start | bytes 196616 | tf_op jit(solution)/shard_map/ppermute | solution.py:368
  35.0 4.3 %collective-permute-start.10 = (bf16[32,1024]{1,0:T(8,128)(2,1)S(1)}, bf16[32,1024]{1,0:T(8,128)(2,1)S(1)}, u32[]{:S(2)}, u32[]{:S(2)}) collective-permute-start(bf16[32,1024]{1,0:T(8,128)(2,1)S(1)} %collective-permute-done.8.refs_3_), channel_id=1, source_target_pairs={{0,4},{4,0},{8,12},{12,8},{1,5},{5,1},{9,13},{13,9},{2,6},{6,2},{1... | collective-permute-start | bytes 196616 | tf_op jit(solution)/shard_map/ppermute | solution.py:368
  40.6 1.6 %collective-permute-start.11 = (bf16[64,2048]{1,0:T(8,128)(2,1)S(1)}, bf16[64,2048]{1,0:T(8,128)(2,1)S(1)}, u32[]{:S(2)}, u32[]{:S(2)}) collective-permute-start(bf16[64,2048]{1,0:T(8,128)(2,1)S(1)} %get-tuple-element.55), channel_id=1, source_target_pairs={{0,1},{1,0},{2,3},{3,2},{4,5},{5,4},{6,7},{7,6},{8,9},{9,8},{10,11... | collective-permute-start | bytes 786440 | tf_op jit(solution)/shard_map/ppermute | solution.py:364
  42.2 20.0 %slice-start.4 = ((s8[14680064]{0:T(1024)(128)(4,1)}), s8[4194304]{0:T(1024)(128)(4,1)S(1)}, s32[]{:S(2)}) async-start(s8[14680064]{0:T(1024)(128)(4,1)} %bitcast.3), calls=%async_computation.4 | async-start | bytes 8388608
  42.2 20.0 %slice-start.5 = ((s8[14680064]{0:T(1024)(128)(4,1)}), s8[4194304]{0:T(1024)(128)(4,1)S(1)}, s32[]{:S(2)}) async-start(s8[14680064]{0:T(1024)(128)(4,1)} %bitcast.3), calls=%async_computation.5 | async-start | bytes 8388608
  42.2 20.0 %slice-start.8 = ((s8[14680064]{0:T(1024)(128)(4,1)}), s8[2097152]{0:T(1024)(128)(4,1)S(1)}, s32[]{:S(2)}) async-start(s8[14680064]{0:T(1024)(128)(4,1)} %bitcast.5), calls=%async_computation.8 | async-start | bytes 4194304
  42.2 20.0 %slice-start.9 = ((s8[14680064]{0:T(1024)(128)(4,1)}), s8[4194304]{0:T(1024)(128)(4,1)S(1)}, s32[]{:S(2)}) async-start(s8[14680064]{0:T(1024)(128)(4,1)} %bitcast.5), calls=%async_computation.9 | async-start | bytes 8388608
  42.3 5.6 %collective-permute-start.12 = (bf16[32,2048]{1,0:T(8,128)(2,1)S(1)}, bf16[32,2048]{1,0:T(8,128)(2,1)S(1)}, u32[]{:S(2)}, u32[]{:S(2)}) collective-permute-start(bf16[32,2048]{1,0:T(8,128)(2,1)S(1)} %get-tuple-element.57), channel_id=1, source_target_pairs={{0,2},{2,0},{1,3},{3,1},{4,6},{6,4},{5,7},{7,5},{8,10},{10,8},{9,1... | collective-permute-start | bytes 393224 | tf_op jit(solution)/shard_map/ppermute | solution.py:364
  47.9 14.4 %slice-start.6 = ((s8[14680064]{0:T(1024)(128)(4,1)}), s8[4194304]{0:T(1024)(128)(4,1)S(1)}, s32[]{:S(2)}) async-start(s8[14680064]{0:T(1024)(128)(4,1)} %bitcast.3), calls=%async_computation.6 | async-start | bytes 8388608
  47.9 14.4 %slice-start.7 = ((s8[14680064]{0:T(1024)(128)(4,1)}), s8[2097152]{0:T(1024)(128)(4,1)S(1)}, s32[]{:S(2)}) async-start(s8[14680064]{0:T(1024)(128)(4,1)} %bitcast.3), calls=%async_computation.7 | async-start | bytes 4194304
  47.9 14.4 %slice-start.10 = ((s8[14680064]{0:T(1024)(128)(4,1)}), s8[4194304]{0:T(1024)(128)(4,1)S(1)}, s32[]{:S(2)}) async-start(s8[14680064]{0:T(1024)(128)(4,1)} %bitcast.5), calls=%async_computation.10 | async-start | bytes 8388608
  47.9 14.4 %slice-start.11 = ((s8[14680064]{0:T(1024)(128)(4,1)}), s8[4194304]{0:T(1024)(128)(4,1)S(1)}, s32[]{:S(2)}) async-start(s8[14680064]{0:T(1024)(128)(4,1)} %bitcast.5), calls=%async_computation.11 | async-start | bytes 8388608
  48.0 7.5 %collective-permute-start.13 = (bf16[32,2048]{1,0:T(8,128)(2,1)S(1)}, bf16[32,2048]{1,0:T(8,128)(2,1)S(1)}, u32[]{:S(2)}, u32[]{:S(2)}) collective-permute-start(bf16[32,2048]{1,0:T(8,128)(2,1)S(1)} %shard_map.107), channel_id=1, source_target_pairs={{0,0},{1,4},{2,8},{3,12},{4,1},{5,5},{6,9},{7,13},{8,2},{9,6},{10,... | collective-permute-start | bytes 393224 | tf_op jit(solution)/shard_map/ppermute | solution.py:455
  48.8 6.8 %collective-permute-start.14 = (bf16[32,2048]{1,0:T(8,128)(2,1)S(1)}, bf16[32,2048]{1,0:T(8,128)(2,1)S(1)}, u32[]{:S(2)}, u32[]{:S(2)}) collective-permute-start(bf16[32,2048]{1,0:T(8,128)(2,1)S(1)} %shard_map.107), channel_id=1, source_target_pairs={{0,4},{1,0},{2,12},{3,8},{4,5},{5,1},{6,13},{7,9},{8,6},{9,2},{10,... | collective-permute-start | bytes 393224 | tf_op jit(solution)/shard_map/ppermute | solution.py:455
  51.8 10.2 %collective-permute-start.15 = (bf16[32,2048]{1,0:T(8,128)(2,1)S(1)}, bf16[32,2048]{1,0:T(8,128)(2,1)S(1)}, u32[]{:S(2)}, u32[]{:S(2)}) collective-permute-start(bf16[32,2048]{1,0:T(8,128)(2,1)S(1)} %shard_map.107), channel_id=1, source_target_pairs={{0,8},{1,12},{2,0},{3,4},{4,9},{5,13},{6,1},{7,5},{8,10},{9,14},{1... | collective-permute-start | bytes 393224 | tf_op jit(solution)/shard_map/ppermute | solution.py:455
  54.2 7.9 %collective-permute-start.16 = (bf16[32,2048]{1,0:T(8,128)(2,1)S(1)}, bf16[32,2048]{1,0:T(8,128)(2,1)S(1)}, u32[]{:S(2)}, u32[]{:S(2)}) collective-permute-start(bf16[32,2048]{1,0:T(8,128)(2,1)S(1)} %shard_map.107), channel_id=1, source_target_pairs={{0,12},{1,8},{2,4},{3,0},{4,13},{5,9},{6,5},{7,1},{8,14},{9,10},{1... | collective-permute-start | bytes 393224 | tf_op jit(solution)/shard_map/ppermute | solution.py:455
  63.9 4.5 %collective-permute-start.17 = (bf16[64,2304]{1,0:T(8,128)(2,1)S(1)}, bf16[64,2304]{1,0:T(8,128)(2,1)S(1)}, u32[]{:S(2)}, u32[]{:S(2)}) collective-permute-start(bf16[64,2304]{1,0:T(8,128)(2,1)S(1)} %get-tuple-element.67), channel_id=1, source_target_pairs={{0,1},{1,0},{2,3},{3,2},{4,5},{5,4},{6,7},{7,6},{8,9},{9,8},{10,11... | collective-permute-start | bytes 884744 | tf_op jit(solution)/shard_map/ppermute | solution.py:364
  66.2 7.9 %collective-permute-start.19 = (bf16[64,2560]{1,0:T(8,128)(2,1)S(1)}, bf16[64,2560]{1,0:T(8,128)(2,1)S(1)}, u32[]{:S(2)}, u32[]{:S(2)}) collective-permute-start(bf16[64,2560]{1,0:T(8,128)(2,1)S(1)} %get-tuple-element.73), channel_id=1, source_target_pairs={{0,1},{1,0},{2,3},{3,2},{4,5},{5,4},{6,7},{7,6},{8,9},{9,8},{10,11... | collective-permute-start | bytes 983048 | tf_op jit(solution)/shard_map/ppermute | solution.py:364
  67.8 6.5 %collective-permute-start.24 = (bf16[64,2560]{1,0:T(8,128)(2,1)S(1)}, bf16[64,2560]{1,0:T(8,128)(2,1)S(1)}, u32[]{:S(2)}, u32[]{:S(2)}) collective-permute-start(bf16[64,2560]{1,0:T(8,128)(2,1)S(1)} %get-tuple-element.77), channel_id=1, source_target_pairs={{0,1},{1,0},{2,3},{3,2},{4,5},{5,4},{6,7},{7,6},{8,9},{9,8},{10,11... | collective-permute-start | bytes 983048 | tf_op jit(solution)/shard_map/ppermute | solution.py:364
  68.4 10.4 %collective-permute-start.18 = (bf16[32,2304]{1,0:T(8,128)(2,1)S(1)}, bf16[32,2304]{1,0:T(8,128)(2,1)S(1)}, u32[]{:S(2)}, u32[]{:S(2)}) collective-permute-start(bf16[32,2304]{1,0:T(8,128)(2,1)S(1)} %get-tuple-element.69), channel_id=1, source_target_pairs={{0,2},{2,0},{1,3},{3,1},{4,6},{6,4},{5,7},{7,5},{8,10},{10,8},{9,1... | collective-permute-start | bytes 442376 | tf_op jit(solution)/shard_map/ppermute | solution.py:364
  74.2 8.1 %collective-permute-start.20 = (bf16[32,2560]{1,0:T(8,128)(2,1)S(1)}, bf16[32,2560]{1,0:T(8,128)(2,1)S(1)}, u32[]{:S(2)}, u32[]{:S(2)}) collective-permute-start(bf16[32,2560]{1,0:T(8,128)(2,1)S(1)} %get-tuple-element.75), channel_id=1, source_target_pairs={{0,2},{2,0},{1,3},{3,1},{4,6},{6,4},{5,7},{7,5},{8,10},{10,8},{9,1... | collective-permute-start | bytes 491528 | tf_op jit(solution)/shard_map/ppermute | solution.py:364
  74.3 11.5 %collective-permute-start.25 = (bf16[32,2560]{1,0:T(8,128)(2,1)S(1)}, bf16[32,2560]{1,0:T(8,128)(2,1)S(1)}, u32[]{:S(2)}, u32[]{:S(2)}) collective-permute-start(bf16[32,2560]{1,0:T(8,128)(2,1)S(1)} %get-tuple-element.79), channel_id=1, source_target_pairs={{0,2},{2,0},{1,3},{3,1},{4,6},{6,4},{5,7},{7,5},{8,10},{10,8},{9,1... | collective-permute-start | bytes 491528 | tf_op jit(solution)/shard_map/ppermute | solution.py:364
  78.9 9.1 %collective-permute-start.30 = (bf16[32,1024]{1,0:T(8,128)(2,1)S(1)}, bf16[32,1024]{1,0:T(8,128)(2,1)S(1)}, u32[]{:S(2)}, u32[]{:S(2)}) collective-permute-start(bf16[32,1024]{1,0:T(8,128)(2,1)S(1)} %get-tuple-element.80.refs_0_), channel_id=1, source_target_pairs={{0,2},{2,0},{1,3},{3,1},{4,6},{6,4},{5,7},{7,5},{8,10},{10,8},{9,1... | collective-permute-start | bytes 196616 | tf_op jit(solution)/shard_map/ppermute | solution.py:364
  82.4 7.0 %collective-permute-start.22 = (bf16[32,1280]{1,0:T(8,128)(2,1)S(1)}, bf16[32,1280]{1,0:T(8,128)(2,1)S(1)}, u32[]{:S(2)}, u32[]{:S(2)}) collective-permute-start(bf16[32,1280]{1,0:T(8,128)(2,1)S(1)} %shard_map.117.refs_0_), channel_id=1, source_target_pairs={{0,2},{2,0},{1,3},{3,1},{4,6},{6,4},{5,7},{7,5},{8,10},{10,8},{9,1... | collective-permute-start | bytes 245768 | tf_op jit(solution)/shard_map/ppermute | solution.py:364
  85.9 4.6 %collective-permute-start.27 = (bf16[32,1280]{1,0:T(8,128)(2,1)S(1)}, bf16[32,1280]{1,0:T(8,128)(2,1)S(1)}, u32[]{:S(2)}, u32[]{:S(2)}) collective-permute-start(bf16[32,1280]{1,0:T(8,128)(2,1)S(1)} %shard_map.120.refs_0_), channel_id=1, source_target_pairs={{0,2},{2,0},{1,3},{3,1},{4,6},{6,4},{5,7},{7,5},{8,10},{10,8},{9,1... | collective-permute-start | bytes 245768 | tf_op jit(solution)/shard_map/ppermute | solution.py:364
  88.0 1.3 %collective-permute-start.29 = (bf16[32,1024]{1,0:T(8,128)(2,1)S(1)}, bf16[32,1024]{1,0:T(8,128)(2,1)S(1)}, u32[]{:S(2)}, u32[]{:S(2)}) collective-permute-start(bf16[32,1024]{1,0:T(8,128)(2,1)S(1)} %get-tuple-element.80.refs_0_), channel_id=1, source_target_pairs={{0,1},{1,0},{2,3},{3,2},{4,5},{5,4},{6,7},{7,6},{8,9},{9,8},{10,11... | collective-permute-start | bytes 196616 | tf_op jit(solution)/shard_map/ppermute | solution.py:364
  88.0 2.5 %collective-permute-start.31 = (bf16[32,1024]{1,0:T(8,128)(2,1)S(1)}, bf16[32,1024]{1,0:T(8,128)(2,1)S(1)}, u32[]{:S(2)}, u32[]{:S(2)}) collective-permute-start(bf16[32,1024]{1,0:T(8,128)(2,1)S(1)} %collective-permute-done.30.refs_2_), channel_id=1, source_target_pairs={{0,1},{1,0},{2,3},{3,2},{4,5},{5,4},{6,7},{7,6},{8,9},{9,8},{10,11... | collective-permute-start | bytes 196616 | tf_op jit(solution)/shard_map/ppermute | solution.py:364
  88.5 4.2 %collective-permute-start.21 = (bf16[32,1280]{1,0:T(8,128)(2,1)S(1)}, bf16[32,1280]{1,0:T(8,128)(2,1)S(1)}, u32[]{:S(2)}, u32[]{:S(2)}) collective-permute-start(bf16[32,1280]{1,0:T(8,128)(2,1)S(1)} %shard_map.117.refs_0_), channel_id=1, source_target_pairs={{0,1},{1,0},{2,3},{3,2},{4,5},{5,4},{6,7},{7,6},{8,9},{9,8},{10,11... | collective-permute-start | bytes 245768 | tf_op jit(solution)/shard_map/ppermute | solution.py:364
  89.3 2.1 %collective-permute-start.26 = (bf16[32,1280]{1,0:T(8,128)(2,1)S(1)}, bf16[32,1280]{1,0:T(8,128)(2,1)S(1)}, u32[]{:S(2)}, u32[]{:S(2)}) collective-permute-start(bf16[32,1280]{1,0:T(8,128)(2,1)S(1)} %shard_map.120.refs_0_), channel_id=1, source_target_pairs={{0,1},{1,0},{2,3},{3,2},{4,5},{5,4},{6,7},{7,6},{8,9},{9,8},{10,11... | collective-permute-start | bytes 245768 | tf_op jit(solution)/shard_map/ppermute | solution.py:364
  89.4 3.3 %collective-permute-start.23 = (bf16[32,1280]{1,0:T(8,128)(2,1)S(1)}, bf16[32,1280]{1,0:T(8,128)(2,1)S(1)}, u32[]{:S(2)}, u32[]{:S(2)}) collective-permute-start(bf16[32,1280]{1,0:T(8,128)(2,1)S(1)} %collective-permute-done.22.refs_2_), channel_id=1, source_target_pairs={{0,1},{1,0},{2,3},{3,2},{4,5},{5,4},{6,7},{7,6},{8,9},{9,8},{10,11... | collective-permute-start | bytes 245768 | tf_op jit(solution)/shard_map/ppermute | solution.py:364
  90.5 1.3 %collective-permute-start.28 = (bf16[32,1280]{1,0:T(8,128)(2,1)S(1)}, bf16[32,1280]{1,0:T(8,128)(2,1)S(1)}, u32[]{:S(2)}, u32[]{:S(2)}) collective-permute-start(bf16[32,1280]{1,0:T(8,128)(2,1)S(1)} %collective-permute-done.27.refs_2_), channel_id=1, source_target_pairs={{0,1},{1,0},{2,3},{3,2},{4,5},{5,4},{6,7},{7,6},{8,9},{9,8},{10,11... | collective-permute-start | bytes 245768 | tf_op jit(solution)/shard_map/ppermute | solution.py:364
  93.2 12.6 %collective-permute-start.32 = (bf16[32,1024]{1,0:T(8,128)(2,1)S(1)}, bf16[32,1024]{1,0:T(8,128)(2,1)S(1)}, u32[]{:S(2)}, u32[]{:S(2)}) collective-permute-start(bf16[32,1024]{1,0:T(8,128)(2,1)S(1)} %get-tuple-element.82), channel_id=1, source_target_pairs={{0,4},{4,0},{8,12},{12,8},{1,5},{5,1},{9,13},{13,9},{2,6},{6,2},{1... | collective-permute-start | bytes 196616 | tf_op jit(solution)/shard_map/ppermute | solution.py:368
  94.9 4.9 %collective-permute-start.33 = (bf16[32,1024]{1,0:T(8,128)(2,1)S(1)}, bf16[32,1024]{1,0:T(8,128)(2,1)S(1)}, u32[]{:S(2)}, u32[]{:S(2)}) collective-permute-start(bf16[32,1024]{1,0:T(8,128)(2,1)S(1)} %get-tuple-element.84), channel_id=1, source_target_pairs={{0,4},{4,0},{8,12},{12,8},{1,5},{5,1},{9,13},{13,9},{2,6},{6,2},{1... | collective-permute-start | bytes 196616 | tf_op jit(solution)/shard_map/ppermute | solution.py:368
  95.9 10.0 %collective-permute-start.35 = (bf16[32,1024]{1,0:T(8,128)(2,1)S(1)}, bf16[32,1024]{1,0:T(8,128)(2,1)S(1)}, u32[]{:S(2)}, u32[]{:S(2)}) collective-permute-start(bf16[32,1024]{1,0:T(8,128)(2,1)S(1)} %get-tuple-element.86), channel_id=1, source_target_pairs={{0,4},{4,0},{8,12},{12,8},{1,5},{5,1},{9,13},{13,9},{2,6},{6,2},{1... | collective-permute-start | bytes 196616 | tf_op jit(solution)/shard_map/ppermute | solution.py:368
  97.6 5.5 %collective-permute-start.36 = (bf16[32,1024]{1,0:T(8,128)(2,1)S(1)}, bf16[32,1024]{1,0:T(8,128)(2,1)S(1)}, u32[]{:S(2)}, u32[]{:S(2)}) collective-permute-start(bf16[32,1024]{1,0:T(8,128)(2,1)S(1)} %get-tuple-element.88), channel_id=1, source_target_pairs={{0,4},{4,0},{8,12},{12,8},{1,5},{5,1},{9,13},{13,9},{2,6},{6,2},{1... | collective-permute-start | bytes 196616 | tf_op jit(solution)/shard_map/ppermute | solution.py:368
  99.9 7.3 %collective-permute-start.34 = (bf16[32,1024]{1,0:T(8,128)(2,1)S(1)}, bf16[32,1024]{1,0:T(8,128)(2,1)S(1)}, u32[]{:S(2)}, u32[]{:S(2)}) collective-permute-start(bf16[32,1024]{1,0:T(8,128)(2,1)S(1)} %shard_map.124), channel_id=1, source_target_pairs={{0,8},{4,12},{8,0},{12,4},{1,9},{5,13},{9,1},{13,5},{2,10},{6,14},... | collective-permute-start | bytes 196616 | tf_op jit(solution)/shard_map/ppermute | solution.py:368
  103.1 5.3 %collective-permute-start.37 = (bf16[32,1024]{1,0:T(8,128)(2,1)S(1)}, bf16[32,1024]{1,0:T(8,128)(2,1)S(1)}, u32[]{:S(2)}, u32[]{:S(2)}) collective-permute-start(bf16[32,1024]{1,0:T(8,128)(2,1)S(1)} %shard_map.126), channel_id=1, source_target_pairs={{0,8},{4,12},{8,0},{12,4},{1,9},{5,13},{9,1},{13,5},{2,10},{6,14},... | collective-permute-start | bytes 196616 | tf_op jit(solution)/shard_map/ppermute | solution.py:368
  (7 other events, 57.6 us)

commit v6 on v5

--- a/solution.py
+++ b/solution.py
@@ -161,7 +161,8 @@
 
 
 def blend_kernel(*refs):
-    parts, (out_ref, low_ref, high_ref) = refs[:-3], refs[-3:]
+    out_ref = refs[-1]
+    parts = refs[:-1]
     heads = out_ref.shape[1] // DH
     logs = []
     for part in parts:
@@ -175,13 +176,10 @@
     shares = [share / total for share in shares]
     for head in range(heads):
         span = slice(head * DH, (head + 1) * DH)
-        value = functools.reduce(
+        out_ref[:, span] = functools.reduce(
             jnp.add,
             [share[:, head : head + 1] * part[:, span].astype(F32) for share, part in zip(shares, parts)],
         ).astype(BF16)
-        out_ref[:, span] = value
-        at = head * DH % low_ref.shape[1]
-        (low_ref if head * 2 < heads else high_ref)[:, at : at + DH] = value
 
 
 def place():
@@ -211,11 +209,8 @@
 def project_kernel(tile, *refs):
     pieces, (weight_ref, keep_ref, send_ref, rows_ref) = refs[:-4], refs[-4:]
     rows = pieces[0].shape[0]
-    half = pieces[2].shape[1]
-    for n, parts in enumerate((pieces[:1], pieces[1:2], pieces[2:4], pieces[4:6])):
-        at = pl.ds(place_of(n, rows, 4), rows)
-        for i, part in enumerate(parts):
-            rows_ref[at, i * half : i * half + part.shape[1]] = part[...]
+    for n, piece in enumerate(pieces):
+        rows_ref[pl.ds(place_of(n, rows, len(pieces)), rows), :] = piece[...]
     product(rows_ref, weight_ref, 0, keep_ref, send_ref, 0, weight_ref.shape[1], tile)
 
 
@@ -419,24 +414,19 @@
         )
     back = {m: turn(partial[m], CTX, n_context, m) for m in order}
     back[0] = partial[0]
-    low = struct((rows, heads_width // 2), BF16)
-    blended, *halves = call(
-        blend_kernel,
-        (struct((rows, heads_width), BF16), low, low),
-        [VM] * 4,
-        tuple(back[m] for m in range(4)),
-    )
-
-    beside = turn(blended, CTX, n_context, 1)
-    across = [turn(h, CTX, n_context, 2) for h in halves]
-    relayed = [turn(h, CTX, n_context, 1) for h in across]
-    attention = (blended, beside, *across, *relayed)
+    blended = call(
+        blend_kernel, struct((rows, heads_width), BF16), [VM] * 4, tuple(back[m] for m in range(4))
+    )
+
+    attention = {m: turn(blended, CTX, n_context, m) for m in (2, 1)}
+    attention[3] = turn(attention[2], CTX, n_context, 1)
+    attention[0] = blended
     width = out_weight.shape[1]
     keep, away = call(
         functools.partial(project_kernel, 512),
         (struct((n_head * rows, width), F32), struct((n_head * rows, width), BF16)),
-        [VM] * 7,
-        attention + (in_vmem(out_weight),),
+        [VM] * 5,
+        tuple(attention[m] for m in range(4)) + (in_vmem(out_weight),),
         scratch=[pltpu.VMEM((total, heads_width), BF16)],
         cost=6,
     )
@@ -495,6 +485,7 @@
                 tuple(p[0] for p in prepared)
                 + tuple(p[1] for p in prepared)
                 + (gate_vmem, up_vmem),
+                cost=0,
             )
         else:
             keep, away = call(
@@ -502,6 +493,7 @@
                 out,
                 [VM] * 3,
                 (all_rows, gate_vmem, up_vmem),
+                cost=0,
             )
         keep, away = call(
             functools.partial(fold_kernel, 2 * chunk),
@@ -511,6 +503,7 @@
             ),
             [VM, VM],
             (keep, swap(away, SEC)),
+            cost=3 if start + chunk == hidden_width else 0,
         )
         got = swap(away, HEAD)
         if c == 0:

time: 109 us -> 110 us (level)
    ppermute x17 -> x15, waiting for transfers between devices: 21.9 us -> 24.5 us  [turn(): return lax.ppermute(x, axis, [(i, i ^ offset) for i in range(n)])]
    ppermute x4, waiting for transfers between devices: 6.3 us -> 4.38 us  [direct_body(): lax.ppermute(middle, ALL, [(a * n_context + b, (b ^ m) * n_context + a) f...]
    ppermute x17 -> x15, starting transfers between devices: 25.7 us -> 24.6 us  [turn(): return lax.ppermute(x, axis, [(i, i ^ offset) for i in range(n)])]
  transfers between devices with their start and end apart: 38 -> 36, of which waited for: 19 -> 19; matrix products, arithmetic and copies ran while one was open for 0% -> 0% of each run, Pallas kernels for 10% -> 9%
where the time goes in v6:
time: 110 us
  starting transfers between devices  51.4 us (47%)
  waiting for transfers between devices  41.5 us (38%)
  Pallas kernels  15.8 us (14%)
    ppermute x15, starting transfers between devices, turn(): return lax.ppermute(x, axis, [(i, i ^ offset) for i in range(n)])  24.6 us
    ppermute x15, waiting for transfers between devices, turn(): return lax.ppermute(x, axis, [(i, i ^ offset) for i in range(n)])  24.5 us
    ppermute x17, starting transfers between devices, swap(): return lax.ppermute(x, axis, [(0, 1), (1, 0)])  18.8 us
    pallas_call x28, Pallas kernels, call(): pl.pallas_call(kernel, out_shape=out, in_specs=in_specs, out_specs=jax.tr...  15.8 us
    ppermute x17, waiting for transfers between devices, swap(): return lax.ppermute(x, axis, [(0, 1), (1, 0)])  12.6 us
    ppermute x4, starting transfers between devices, direct_body(): lax.ppermute(middle, ALL, [(a * n_context + b, (b ^ m) * n_context + a) f...  7.87 us
    ppermute x4, waiting for transfers between devices, direct_body(): lax.ppermute(middle, ALL, [(a * n_context + b, (b ^ m) * n_context + a) f...  4.38 us
  transfers between devices with their start and end apart: 36, of which 19 were waited for; matrix products, arithmetic and copies ran while one was open for 0% of the time, Pallas kernels for 9%

profile of v6, /device:TPU:0, one launch (start us, length us, event | category | flops | bytes accessed | tf_op | source)
XLA Modules:
  0.0 109.8 jit_solution(15670563731354447754)
XLA Ops:
  0.0 3.1 %collective-permute-start = (bf16[32,2048]{1,0:T(8,128)(2,1)}, bf16[32,2048]{1,0:T(8,128)(2,1)S(1)}, u32[]{:S(2)}, u32[]{:S(2)}) collective-permute-start(bf16[32,2048]{1,0:T(8,128)(2,1)} %q_hbm.1), channel_id=1, source_target_pairs={{0,4},{4,0},{8,12},{12,8},{1,5},{5,1},{9,13},{13,9},{2,6},{6,2},{1... | collective-permute-start | bytes 393224 | tf_op jit(solution)/shard_map/ppermute | solution.py:363
  3.1 2.6 %collective-permute-start.2 = (bf16[32,2048]{1,0:T(8,128)(2,1)}, bf16[32,2048]{1,0:T(8,128)(2,1)S(1)}, u32[]{:S(2)}, u32[]{:S(2)}) collective-permute-start(bf16[32,2048]{1,0:T(8,128)(2,1)} %q_hbm.1), channel_id=1, source_target_pairs={{0,8},{4,12},{8,0},{12,4},{1,9},{5,13},{9,1},{13,5},{2,10},{6,14},... | collective-permute-start | bytes 393224 | tf_op jit(solution)/shard_map/ppermute | solution.py:363
  6.3 2.6 %shard_map.100 = (bf16[512,256]{1,0:T(8,128)(2,1)S(1)}, bf16[512,256]{1,0:T(8,128)(2,1)S(1)}, s32[8,128]{1,0:T(8,128)S(1)}, bf16[32,2176]{1,0:T(8,128)(2,1)S(1)}) custom-call(s32[1,8]{1,0:T(1,128)S(1)} %copy-done.2, bf16[32,2048]{1,0:T(8,128)(2,1)} %q_hbm.1, bf16[2048,256]{1,0:T(8,128)(2,1)} %key_hbm.1, bf16[2048,256]{1,0:T(8,128)(2,1)} %value_hbm.1), custom_call_target="tpu_custom_call" | custom-call | flops 3000000000 | bytes 2895904 | tf_op jit(solution)/shard_map/pallas_call | solution.py:40
  8.9 0.8 shard_map.101
  10.3 1.8 %collective-permute-done.2.q_ref = bf16[32,2048]{1,0:T(8,128)(2,1)S(1)} collective-permute-done((bf16[32,2048]{1,0:T(8,128)(2,1)}, bf16[32,2048]{1,0:T(8,128)(2,1)S(1)}, u32[]{:S(2)}, u32[]{:S(2)}) %collective-permute-start.2) | collective-permute-done | bytes 131104 | tf_op jit(solution)/shard_map/ppermute | solution.py:363
  12.4 0.8 shard_map.102
  13.3 2.7 %collective-permute-start.3 = (bf16[32,2176]{1,0:T(8,128)(2,1)S(1)}, bf16[32,2176]{1,0:T(8,128)(2,1)S(1)}, u32[]{:S(2)}, u32[]{:S(2)}) collective-permute-start(bf16[32,2176]{1,0:T(8,128)(2,1)S(1)} %shard_map.102), channel_id=1, source_target_pairs={{0,8},{4,12},{8,0},{12,4},{1,9},{5,13},{9,1},{13,5},{2,10},{6,14},... | collective-permute-start | bytes 417800 | tf_op jit(solution)/shard_map/ppermute | solution.py:363
  15.9 4.4 %collective-permute-done.4.q_ref = bf16[32,2048]{1,0:T(8,128)(2,1)S(1)} collective-permute-done((bf16[32,2048]{1,0:T(8,128)(2,1)S(1)}, bf16[32,2048]{1,0:T(8,128)(2,1)S(1)}, u32[]{:S(2)}, u32[]{:S(2)}) %collective-permute-start.4) | collective-permute-done | bytes 131104 | tf_op jit(solution)/shard_map/ppermute | solution.py:363
  20.3 0.8 shard_map.103
  21.1 2.0 %collective-permute-start.5 = (bf16[32,2176]{1,0:T(8,128)(2,1)S(1)}, bf16[32,2176]{1,0:T(8,128)(2,1)S(1)}, u32[]{:S(2)}, u32[]{:S(2)}) collective-permute-start(bf16[32,2176]{1,0:T(8,128)(2,1)S(1)} %shard_map.103), channel_id=1, source_target_pairs={{0,12},{4,8},{8,4},{12,0},{1,13},{5,9},{9,5},{13,1},{2,14},{6,10},... | collective-permute-start | bytes 417800 | tf_op jit(solution)/shard_map/ppermute | solution.py:363
  23.1 5.0 %collective-permute-done.5.refs_3_ = bf16[32,2176]{1,0:T(8,128)(2,1)S(1)} collective-permute-done((bf16[32,2176]{1,0:T(8,128)(2,1)S(1)}, bf16[32,2176]{1,0:T(8,128)(2,1)S(1)}, u32[]{:S(2)}, u32[]{:S(2)}) %collective-permute-start.5) | collective-permute-done | bytes 139296 | tf_op jit(solution)/shard_map/ppermute | solution.py:363
  28.5 1.2 %collective-permute-start.7 = (bf16[32,2048]{1,0:T(8,128)(2,1)S(1)}, bf16[32,2048]{1,0:T(8,128)(2,1)S(1)}, u32[]{:S(2)}, u32[]{:S(2)}) collective-permute-start(bf16[32,2048]{1,0:T(8,128)(2,1)S(1)} %shard_map.104.refs_0_), channel_id=1, source_target_pairs={{0,8},{4,12},{8,0},{12,4},{1,9},{5,13},{9,1},{13,5},{2,10},{6,14},... | collective-permute-start | bytes 393224 | tf_op jit(solution)/shard_map/ppermute | solution.py:363
  29.8 1.4 %collective-permute-start.6 = (bf16[32,2048]{1,0:T(8,128)(2,1)S(1)}, bf16[32,2048]{1,0:T(8,128)(2,1)S(1)}, u32[]{:S(2)}, u32[]{:S(2)}) collective-permute-start(bf16[32,2048]{1,0:T(8,128)(2,1)S(1)} %shard_map.104.refs_0_), channel_id=1, source_target_pairs={{0,4},{4,0},{8,12},{12,8},{1,5},{5,1},{9,13},{13,9},{2,6},{6,2},{1... | collective-permute-start | bytes 393224 | tf_op jit(solution)/shard_map/ppermute | solution.py:363
  31.2 3.9 %collective-permute-done.7.refs_2_ = bf16[32,2048]{1,0:T(8,128)(2,1)S(1)} collective-permute-done((bf16[32,2048]{1,0:T(8,128)(2,1)S(1)}, bf16[32,2048]{1,0:T(8,128)(2,1)S(1)}, u32[]{:S(2)}, u32[]{:S(2)}) %collective-permute-start.7) | collective-permute-done | bytes 131104 | tf_op jit(solution)/shard_map/ppermute | solution.py:363
  35.1 2.1 %collective-permute-done.6.refs_1_ = bf16[32,2048]{1,0:T(8,128)(2,1)S(1)} collective-permute-done((bf16[32,2048]{1,0:T(8,128)(2,1)S(1)}, bf16[32,2048]{1,0:T(8,128)(2,1)S(1)}, u32[]{:S(2)}, u32[]{:S(2)}) %collective-permute-start.6) | collective-permute-done | bytes 131104 | tf_op jit(solution)/shard_map/ppermute | solution.py:363
  37.2 2.8 %collective-permute-done.8.refs_3_ = bf16[32,2048]{1,0:T(8,128)(2,1)S(1)} collective-permute-done((bf16[32,2048]{1,0:T(8,128)(2,1)S(1)}, bf16[32,2048]{1,0:T(8,128)(2,1)S(1)}, u32[]{:S(2)}, u32[]{:S(2)}) %collective-permute-start.8) | collective-permute-done | bytes 131104 | tf_op jit(solution)/shard_map/ppermute | solution.py:363
  40.0 1.3 %shard_map.105 = (f32[64,2048]{1,0:T(8,128)S(1)}, bf16[64,2048]{1,0:T(8,128)(2,1)S(1)}) custom-call(bf16[32,2048]{1,0:T(8,128)(2,1)S(1)} %shard_map.104.refs_0_, bf16[32,2048]{1,0:T(8,128)(2,1)S(1)} %collective-permute-done.6.refs_1_, bf16[32,2048]{1,0:T(8,128)(2,1)S(1)} %collective-permute-done.7.refs_2_, ...), custom_call_target="tpu_custom_call" | custom-call | flops 6000000000 | bytes 9699328 | tf_op jit(solution)/shard_map/pallas_call | solution.py:40
  41.4 1.5 %collective-permute-done.9.got_ref = bf16[64,2048]{1,0:T(8,128)(2,1)S(1)} collective-permute-done((bf16[64,2048]{1,0:T(8,128)(2,1)S(1)}, bf16[64,2048]{1,0:T(8,128)(2,1)S(1)}, u32[]{:S(2)}, u32[]{:S(2)}) %collective-permute-start.9) | collective-permute-done | bytes 262176 | tf_op jit(solution)/shard_map/ppermute | solution.py:359
  43.0 1.6 %collective-permute-start.10 = (bf16[32,2048]{1,0:T(8,128)(2,1)S(1)}, bf16[32,2048]{1,0:T(8,128)(2,1)S(1)}, u32[]{:S(2)}, u32[]{:S(2)}) collective-permute-start(bf16[32,2048]{1,0:T(8,128)(2,1)S(1)} %get-tuple-element.51), channel_id=1, source_target_pairs={{0,2},{2,0},{1,3},{3,1},{4,6},{6,4},{5,7},{7,5},{8,10},{10,8},{9,1... | collective-permute-start | bytes 393224 | tf_op jit(solution)/shard_map/ppermute | solution.py:359
  44.6 4.0 %collective-permute-done.10.got_ref = bf16[32,2048]{1,0:T(8,128)(2,1)S(1)} collective-permute-done((bf16[32,2048]{1,0:T(8,128)(2,1)S(1)}, bf16[32,2048]{1,0:T(8,128)(2,1)S(1)}, u32[]{:S(2)}, u32[]{:S(2)}) %collective-permute-start.10) | collective-permute-done | bytes 131104 | tf_op jit(solution)/shard_map/ppermute | solution.py:359
  48.7 0.8 collective-permute-start.11
  49.5 2.5 %collective-permute-start.12 = (bf16[32,2048]{1,0:T(8,128)(2,1)S(1)}, bf16[32,2048]{1,0:T(8,128)(2,1)S(1)}, u32[]{:S(2)}, u32[]{:S(2)}) collective-permute-start(bf16[32,2048]{1,0:T(8,128)(2,1)S(1)} %shard_map.107), channel_id=1, source_target_pairs={{0,4},{1,0},{2,12},{3,8},{4,5},{5,1},{6,13},{7,9},{8,6},{9,2},{10,... | collective-permute-start | bytes 393224 | tf_op jit(solution)/shard_map/ppermute | solution.py:445
  52.0 3.0 %collective-permute-start.13 = (bf16[32,2048]{1,0:T(8,128)(2,1)S(1)}, bf16[32,2048]{1,0:T(8,128)(2,1)S(1)}, u32[]{:S(2)}, u32[]{:S(2)}) collective-permute-start(bf16[32,2048]{1,0:T(8,128)(2,1)S(1)} %shard_map.107), channel_id=1, source_target_pairs={{0,8},{1,12},{2,0},{3,4},{4,9},{5,13},{6,1},{7,5},{8,10},{9,14},{1... | collective-permute-start | bytes 393224 | tf_op jit(solution)/shard_map/ppermute | solution.py:445
  55.0 1.6 %collective-permute-start.14 = (bf16[32,2048]{1,0:T(8,128)(2,1)S(1)}, bf16[32,2048]{1,0:T(8,128)(2,1)S(1)}, u32[]{:S(2)}, u32[]{:S(2)}) collective-permute-start(bf16[32,2048]{1,0:T(8,128)(2,1)S(1)} %shard_map.107), channel_id=1, source_target_pairs={{0,12},{1,8},{2,4},{3,0},{4,13},{5,9},{6,5},{7,1},{8,14},{9,10},{1... | collective-permute-start | bytes 393224 | tf_op jit(solution)/shard_map/ppermute | solution.py:445
  56.8 4.2 %collective-permute-done.13.piece_ref = bf16[32,2048]{1,0:T(8,128)(2,1)S(1)} collective-permute-done((bf16[32,2048]{1,0:T(8,128)(2,1)S(1)}, bf16[32,2048]{1,0:T(8,128)(2,1)S(1)}, u32[]{:S(2)}, u32[]{:S(2)}) %collective-permute-start.13) | collective-permute-done | bytes 131104 | tf_op jit(solution)/shard_map/ppermute | solution.py:445
  61.6 1.6 %shard_map.112 = (f32[64,2176]{1,0:T(8,128)S(1)}, bf16[64,2304]{1,0:T(8,128)(2,1)S(1)}, bf16[128,2048]{1,0:T(8,128)(2,1)S(1)}) custom-call(bf16[32,2048]{1,0:T(8,128)(2,1)S(1)} %get-tuple-element.52.refs_0_, bf16[32,2048]{1,0:T(8,128)(2,1)S(1)} %get-tuple-element.53.refs_1_, bf16[32,2048]{1,0:T(8,128)(2,1)S(1)} %get-tuple-element.54.refs_2_, ...), custom_call_target="tpu_custom_call" | custom-call | bytes 31326208 | tf_op jit(solution)/shard_map/pallas_call | solution.py:40
  63.1 1.5 %shard_map.115 = (f32[64,2560]{1,0:T(8,128)S(1)}, bf16[64,2560]{1,0:T(8,128)(2,1)S(1)}) custom-call(bf16[128,2048]{1,0:T(8,128)(2,1)S(1)} %get-tuple-element.65.rows_ref, bf16[2048,3584]{1,0:T(8,128)(2,1)S(1)} %bitcast.4, bf16[2048,3584]{1,0:T(8,128)(2,1)S(1)} %bitcast.6), custom_call_target="tpu_custom_call" | custom-call | bytes 30867456 | tf_op jit(solution)/shard_map/pallas_call | solution.py:40
  64.7 2.7 %collective-permute-start.17 = (bf16[64,2560]{1,0:T(8,128)(2,1)S(1)}, bf16[64,2560]{1,0:T(8,128)(2,1)S(1)}, u32[]{:S(2)}, u32[]{:S(2)}) collective-permute-start(bf16[64,2560]{1,0:T(8,128)(2,1)S(1)} %get-tuple-element.67), channel_id=1, source_target_pairs={{0,1},{1,0},{2,3},{3,2},{4,5},{5,4},{6,7},{7,6},{8,9},{9,8},{10,11... | collective-permute-start | bytes 983048 | tf_op jit(solution)/shard_map/ppermute | solution.py:359
  67.4 1.5 %shard_map.118 = (f32[64,2560]{1,0:T(8,128)S(1)}, bf16[64,2560]{1,0:T(8,128)(2,1)S(1)}) custom-call(bf16[128,2048]{1,0:T(8,128)(2,1)S(1)} %get-tuple-element.65.rows_ref, bf16[2048,3584]{1,0:T(8,128)(2,1)S(1)} %bitcast.4, bf16[2048,3584]{1,0:T(8,128)(2,1)S(1)} %bitcast.6), custom_call_target="tpu_custom_call" | custom-call | bytes 30867456 | tf_op jit(solution)/shard_map/pallas_call | solution.py:40
  69.5 4.5 %collective-permute-start.16 = (bf16[32,2304]{1,0:T(8,128)(2,1)S(1)}, bf16[32,2304]{1,0:T(8,128)(2,1)S(1)}, u32[]{:S(2)}, u32[]{:S(2)}) collective-permute-start(bf16[32,2304]{1,0:T(8,128)(2,1)S(1)} %get-tuple-element.63), channel_id=1, source_target_pairs={{0,2},{2,0},{1,3},{3,1},{4,6},{6,4},{5,7},{7,5},{8,10},{10,8},{9,1... | collective-permute-start | bytes 442376 | tf_op jit(solution)/shard_map/ppermute | solution.py:359
  74.3 2.1 %collective-permute-start.23 = (bf16[32,2560]{1,0:T(8,128)(2,1)S(1)}, bf16[32,2560]{1,0:T(8,128)(2,1)S(1)}, u32[]{:S(2)}, u32[]{:S(2)}) collective-permute-start(bf16[32,2560]{1,0:T(8,128)(2,1)S(1)} %get-tuple-element.73), channel_id=1, source_target_pairs={{0,2},{2,0},{1,3},{3,1},{4,6},{6,4},{5,7},{7,5},{8,10},{10,8},{9,1... | collective-permute-start | bytes 491528 | tf_op jit(solution)/shard_map/ppermute | solution.py:359
  76.3 2.4 %collective-permute-done.16.got_ref = bf16[32,2304]{1,0:T(8,128)(2,1)S(1)} collective-permute-done((bf16[32,2304]{1,0:T(8,128)(2,1)S(1)}, bf16[32,2304]{1,0:T(8,128)(2,1)S(1)}, u32[]{:S(2)}, u32[]{:S(2)}) %collective-permute-start.16) | collective-permute-done | bytes 147488 | tf_op jit(solution)/shard_map/ppermute | solution.py:359
  78.8 2.1 %collective-permute-start.28 = (bf16[32,1024]{1,0:T(8,128)(2,1)S(1)}, bf16[32,1024]{1,0:T(8,128)(2,1)S(1)}, u32[]{:S(2)}, u32[]{:S(2)}) collective-permute-start(bf16[32,1024]{1,0:T(8,128)(2,1)S(1)} %get-tuple-element.74.refs_0_), channel_id=1, source_target_pairs={{0,2},{2,0},{1,3},{3,1},{4,6},{6,4},{5,7},{7,5},{8,10},{10,8},{9,1... | collective-permute-start | bytes 196616 | tf_op jit(solution)/shard_map/ppermute | solution.py:359
  80.9 1.3 %collective-permute-done.18.got_ref = bf16[32,2560]{1,0:T(8,128)(2,1)S(1)} collective-permute-done((bf16[32,2560]{1,0:T(8,128)(2,1)S(1)}, bf16[32,2560]{1,0:T(8,128)(2,1)S(1)}, u32[]{:S(2)}, u32[]{:S(2)}) %collective-permute-start.18) | collective-permute-done | bytes 163872 | tf_op jit(solution)/shard_map/ppermute | solution.py:359
  82.3 2.1 %collective-permute-start.20 = (bf16[32,1280]{1,0:T(8,128)(2,1)S(1)}, bf16[32,1280]{1,0:T(8,128)(2,1)S(1)}, u32[]{:S(2)}, u32[]{:S(2)}) collective-permute-start(bf16[32,1280]{1,0:T(8,128)(2,1)S(1)} %shard_map.117.refs_0_), channel_id=1, source_target_pairs={{0,2},{2,0},{1,3},{3,1},{4,6},{6,4},{5,7},{7,5},{8,10},{10,8},{9,1... | collective-permute-start | bytes 245768 | tf_op jit(solution)/shard_map/ppermute | solution.py:359
  84.4 1.3 %collective-permute-done.23.got_ref = bf16[32,2560]{1,0:T(8,128)(2,1)S(1)} collective-permute-done((bf16[32,2560]{1,0:T(8,128)(2,1)S(1)}, bf16[32,2560]{1,0:T(8,128)(2,1)S(1)}, u32[]{:S(2)}, u32[]{:S(2)}) %collective-permute-start.23) | collective-permute-done | bytes 163872 | tf_op jit(solution)/shard_map/ppermute | solution.py:359
  85.8 2.1 %collective-permute-start.25 = (bf16[32,1280]{1,0:T(8,128)(2,1)S(1)}, bf16[32,1280]{1,0:T(8,128)(2,1)S(1)}, u32[]{:S(2)}, u32[]{:S(2)}) collective-permute-start(bf16[32,1280]{1,0:T(8,128)(2,1)S(1)} %shard_map.120.refs_0_), channel_id=1, source_target_pairs={{0,2},{2,0},{1,3},{3,1},{4,6},{6,4},{5,7},{7,5},{8,10},{10,8},{9,1... | collective-permute-start | bytes 245768 | tf_op jit(solution)/shard_map/ppermute | solution.py:359
  88.5 0.7 collective-permute-done.27.refs_1_
  90.5 0.7 shard_map.121.refs_5_
  91.7 0.9 shard_map.122.refs_5_
  93.1 2.6 %collective-permute-start.30 = (bf16[32,1024]{1,0:T(8,128)(2,1)S(1)}, bf16[32,1024]{1,0:T(8,128)(2,1)S(1)}, u32[]{:S(2)}, u32[]{:S(2)}) collective-permute-start(bf16[32,1024]{1,0:T(8,128)(2,1)S(1)} %get-tuple-element.76), channel_id=1, source_target_pairs={{0,4},{4,0},{8,12},{12,8},{1,5},{5,1},{9,13},{13,9},{2,6},{6,2},{1... | collective-permute-start | bytes 196616 | tf_op jit(solution)/shard_map/ppermute | solution.py:363
  96.3 2.0 %collective-permute-start.33 = (bf16[32,1024]{1,0:T(8,128)(2,1)S(1)}, bf16[32,1024]{1,0:T(8,128)(2,1)S(1)}, u32[]{:S(2)}, u32[]{:S(2)}) collective-permute-start(bf16[32,1024]{1,0:T(8,128)(2,1)S(1)} %get-tuple-element.80), channel_id=1, source_target_pairs={{0,4},{4,0},{8,12},{12,8},{1,5},{5,1},{9,13},{13,9},{2,6},{6,2},{1... | collective-permute-start | bytes 196616 | tf_op jit(solution)/shard_map/ppermute | solution.py:363
  98.4 1.9 %collective-permute-done.31.got_ref = bf16[32,1024]{1,0:T(8,128)(2,1)S(1)} collective-permute-done((bf16[32,1024]{1,0:T(8,128)(2,1)S(1)}, bf16[32,1024]{1,0:T(8,128)(2,1)S(1)}, u32[]{:S(2)}, u32[]{:S(2)}) %collective-permute-start.31) | collective-permute-done | bytes 65568 | tf_op jit(solution)/shard_map/ppermute | solution.py:363
  100.3 3.3 %collective-permute-start.32 = (bf16[32,1024]{1,0:T(8,128)(2,1)S(1)}, bf16[32,1024]{1,0:T(8,128)(2,1)S(1)}, u32[]{:S(2)}, u32[]{:S(2)}) collective-permute-start(bf16[32,1024]{1,0:T(8,128)(2,1)S(1)} %shard_map.124), channel_id=1, source_target_pairs={{0,8},{4,12},{8,0},{12,4},{1,9},{5,13},{9,1},{13,5},{2,10},{6,14},... | collective-permute-start | bytes 196616 | tf_op jit(solution)/shard_map/ppermute | solution.py:363
  103.7 2.8 %collective-permute-start.35 = (bf16[32,1024]{1,0:T(8,128)(2,1)S(1)}, bf16[32,1024]{1,0:T(8,128)(2,1)S(1)}, u32[]{:S(2)}, u32[]{:S(2)}) collective-permute-start(bf16[32,1024]{1,0:T(8,128)(2,1)S(1)} %shard_map.126), channel_id=1, source_target_pairs={{0,8},{4,12},{8,0},{12,4},{1,9},{5,13},{9,1},{13,5},{2,10},{6,14},... | collective-permute-start | bytes 196616 | tf_op jit(solution)/shard_map/ppermute | solution.py:363
  106.5 1.4 %collective-permute-done.32.refs_2_ = bf16[32,1024]{1,0:T(8,128)(2,1)S(1)} collective-permute-done((bf16[32,1024]{1,0:T(8,128)(2,1)S(1)}, bf16[32,1024]{1,0:T(8,128)(2,1)S(1)}, u32[]{:S(2)}, u32[]{:S(2)}) %collective-permute-start.32) | collective-permute-done | bytes 65568 | tf_op jit(solution)/shard_map/ppermute | solution.py:363
  107.9 1.1 %collective-permute-done.35.refs_5_ = bf16[32,1024]{1,0:T(8,128)(2,1)S(1)} collective-permute-done((bf16[32,1024]{1,0:T(8,128)(2,1)S(1)}, bf16[32,1024]{1,0:T(8,128)(2,1)S(1)}, u32[]{:S(2)}, u32[]{:S(2)}) %collective-permute-start.35) | collective-permute-done | bytes 65568 | tf_op jit(solution)/shard_map/ppermute | solution.py:363
  109.1 0.7 shard_map.127
  (90 shorter events, 7.5 us)
Async XLA Ops:
  0.0 8.9 %collective-permute-start = (bf16[32,2048]{1,0:T(8,128)(2,1)}, bf16[32,2048]{1,0:T(8,128)(2,1)S(1)}, u32[]{:S(2)}, u32[]{:S(2)}) collective-permute-start(bf16[32,2048]{1,0:T(8,128)(2,1)} %q_hbm.1), channel_id=1, source_target_pairs={{0,4},{4,0},{8,12},{12,8},{1,5},{5,1},{9,13},{13,9},{2,6},{6,2},{1... | collective-permute-start | bytes 393224 | tf_op jit(solution)/shard_map/ppermute | solution.py:363
  3.1 9.0 %collective-permute-start.2 = (bf16[32,2048]{1,0:T(8,128)(2,1)}, bf16[32,2048]{1,0:T(8,128)(2,1)S(1)}, u32[]{:S(2)}, u32[]{:S(2)}) collective-permute-start(bf16[32,2048]{1,0:T(8,128)(2,1)} %q_hbm.1), channel_id=1, source_target_pairs={{0,8},{4,12},{8,0},{12,4},{1,9},{5,13},{9,1},{13,5},{2,10},{6,14},... | collective-permute-start | bytes 393224 | tf_op jit(solution)/shard_map/ppermute | solution.py:363
  9.7 30.3 %slice-start.12 = ((s8[8388608]{0:T(1024)(128)(4,1)}), s8[4194304]{0:T(1024)(128)(4,1)S(1)}, s32[]{:S(2)}) async-start(s8[8388608]{0:T(1024)(128)(4,1)} %bitcast.11), calls=%async_computation.12 | async-start | bytes 8388608
  9.7 13.4 %collective-permute-start.1 = (bf16[32,2176]{1,0:T(8,128)(2,1)S(1)}, bf16[32,2176]{1,0:T(8,128)(2,1)S(1)}, u32[]{:S(2)}, u32[]{:S(2)}) collective-permute-start(bf16[32,2176]{1,0:T(8,128)(2,1)S(1)} %shard_map.101), channel_id=1, source_target_pairs={{0,4},{4,0},{8,12},{12,8},{1,5},{5,1},{9,13},{13,9},{2,6},{6,2},{1... | collective-permute-start | bytes 417800 | tf_op jit(solution)/shard_map/ppermute | solution.py:363
  12.1 8.2 %collective-permute-start.4 = (bf16[32,2048]{1,0:T(8,128)(2,1)S(1)}, bf16[32,2048]{1,0:T(8,128)(2,1)S(1)}, u32[]{:S(2)}, u32[]{:S(2)}) collective-permute-start(bf16[32,2048]{1,0:T(8,128)(2,1)S(1)} %collective-permute-done.2.q_ref), channel_id=1, source_target_pairs={{0,4},{4,0},{8,12},{12,8},{1,5},{5,1},{9,13},{13,9},{2,6},{6,2},{1... | collective-permute-start | bytes 393224 | tf_op jit(solution)/shard_map/ppermute | solution.py:363
  13.2 26.8 %slice-start.13 = ((s8[8388608]{0:T(1024)(128)(4,1)}), s8[4194304]{0:T(1024)(128)(4,1)S(1)}, s32[]{:S(2)}) async-start(s8[8388608]{0:T(1024)(128)(4,1)} %bitcast.11), calls=%async_computation.13 | async-start | bytes 8388608
  13.3 9.9 %collective-permute-start.3 = (bf16[32,2176]{1,0:T(8,128)(2,1)S(1)}, bf16[32,2176]{1,0:T(8,128)(2,1)S(1)}, u32[]{:S(2)}, u32[]{:S(2)}) collective-permute-start(bf16[32,2176]{1,0:T(8,128)(2,1)S(1)} %shard_map.102), channel_id=1, source_target_pairs={{0,8},{4,12},{8,0},{12,4},{1,9},{5,13},{9,1},{13,5},{2,10},{6,14},... | collective-permute-start | bytes 417800 | tf_op jit(solution)/shard_map/ppermute | solution.py:363
  21.1 6.9 %collective-permute-start.5 = (bf16[32,2176]{1,0:T(8,128)(2,1)S(1)}, bf16[32,2176]{1,0:T(8,128)(2,1)S(1)}, u32[]{:S(2)}, u32[]{:S(2)}) collective-permute-start(bf16[32,2176]{1,0:T(8,128)(2,1)S(1)} %shard_map.103), channel_id=1, source_target_pairs={{0,12},{4,8},{8,4},{12,0},{1,13},{5,9},{9,5},{13,1},{2,14},{6,10},... | collective-permute-start | bytes 417800 | tf_op jit(solution)/shard_map/ppermute | solution.py:363
  28.5 6.5 %collective-permute-start.7 = (bf16[32,2048]{1,0:T(8,128)(2,1)S(1)}, bf16[32,2048]{1,0:T(8,128)(2,1)S(1)}, u32[]{:S(2)}, u32[]{:S(2)}) collective-permute-start(bf16[32,2048]{1,0:T(8,128)(2,1)S(1)} %shard_map.104.refs_0_), channel_id=1, source_target_pairs={{0,8},{4,12},{8,0},{12,4},{1,9},{5,13},{9,1},{13,5},{2,10},{6,14},... | collective-permute-start | bytes 393224 | tf_op jit(solution)/shard_map/ppermute | solution.py:363
  29.8 7.5 %collective-permute-start.6 = (bf16[32,2048]{1,0:T(8,128)(2,1)S(1)}, bf16[32,2048]{1,0:T(8,128)(2,1)S(1)}, u32[]{:S(2)}, u32[]{:S(2)}) collective-permute-start(bf16[32,2048]{1,0:T(8,128)(2,1)S(1)} %shard_map.104.refs_0_), channel_id=1, source_target_pairs={{0,4},{4,0},{8,12},{12,8},{1,5},{5,1},{9,13},{13,9},{2,6},{6,2},{1... | collective-permute-start | bytes 393224 | tf_op jit(solution)/shard_map/ppermute | solution.py:363
  35.0 5.0 %collective-permute-start.8 = (bf16[32,2048]{1,0:T(8,128)(2,1)S(1)}, bf16[32,2048]{1,0:T(8,128)(2,1)S(1)}, u32[]{:S(2)}, u32[]{:S(2)}) collective-permute-start(bf16[32,2048]{1,0:T(8,128)(2,1)S(1)} %collective-permute-done.7.refs_2_), channel_id=1, source_target_pairs={{0,4},{4,0},{8,12},{12,8},{1,5},{5,1},{9,13},{13,9},{2,6},{6,2},{1... | collective-permute-start | bytes 393224 | tf_op jit(solution)/shard_map/ppermute | solution.py:363
  41.3 1.6 %collective-permute-start.9 = (bf16[64,2048]{1,0:T(8,128)(2,1)S(1)}, bf16[64,2048]{1,0:T(8,128)(2,1)S(1)}, u32[]{:S(2)}, u32[]{:S(2)}) collective-permute-start(bf16[64,2048]{1,0:T(8,128)(2,1)S(1)} %get-tuple-element.49), channel_id=1, source_target_pairs={{0,1},{1,0},{2,3},{3,2},{4,5},{5,4},{6,7},{7,6},{8,9},{9,8},{10,11... | collective-permute-start | bytes 786440 | tf_op jit(solution)/shard_map/ppermute | solution.py:359
  42.9 18.5 %slice-start.4 = ((s8[14680064]{0:T(1024)(128)(4,1)}), s8[4194304]{0:T(1024)(128)(4,1)S(1)}, s32[]{:S(2)}) async-start(s8[14680064]{0:T(1024)(128)(4,1)} %bitcast.3), calls=%async_computation.4 | async-start | bytes 8388608
  42.9 18.5 %slice-start.5 = ((s8[14680064]{0:T(1024)(128)(4,1)}), s8[4194304]{0:T(1024)(128)(4,1)S(1)}, s32[]{:S(2)}) async-start(s8[14680064]{0:T(1024)(128)(4,1)} %bitcast.3), calls=%async_computation.5 | async-start | bytes 8388608
  42.9 18.5 %slice-start.8 = ((s8[14680064]{0:T(1024)(128)(4,1)}), s8[2097152]{0:T(1024)(128)(4,1)S(1)}, s32[]{:S(2)}) async-start(s8[14680064]{0:T(1024)(128)(4,1)} %bitcast.5), calls=%async_computation.8 | async-start | bytes 4194304
  42.9 18.5 %slice-start.9 = ((s8[14680064]{0:T(1024)(128)(4,1)}), s8[4194304]{0:T(1024)(128)(4,1)S(1)}, s32[]{:S(2)}) async-start(s8[14680064]{0:T(1024)(128)(4,1)} %bitcast.5), calls=%async_computation.9 | async-start | bytes 8388608
  43.0 13.6 %copy-start = (f32[8192]{0:T(1024)S(1)}, f32[8192]{0:T(1024)}, u32[]{:S(2)}) copy-start(f32[8192]{0:T(1024)} %param.16) | copy-start | bytes 98308
  43.0 5.6 %collective-permute-start.10 = (bf16[32,2048]{1,0:T(8,128)(2,1)S(1)}, bf16[32,2048]{1,0:T(8,128)(2,1)S(1)}, u32[]{:S(2)}, u32[]{:S(2)}) collective-permute-start(bf16[32,2048]{1,0:T(8,128)(2,1)S(1)} %get-tuple-element.51), channel_id=1, source_target_pairs={{0,2},{2,0},{1,3},{3,1},{4,6},{6,4},{5,7},{7,5},{8,10},{10,8},{9,1... | collective-permute-start | bytes 393224 | tf_op jit(solution)/shard_map/ppermute | solution.py:359
  48.6 12.9 %slice-start.6 = ((s8[14680064]{0:T(1024)(128)(4,1)}), s8[4194304]{0:T(1024)(128)(4,1)S(1)}, s32[]{:S(2)}) async-start(s8[14680064]{0:T(1024)(128)(4,1)} %bitcast.3), calls=%async_computation.6 | async-start | bytes 8388608
  48.6 12.9 %slice-start.7 = ((s8[14680064]{0:T(1024)(128)(4,1)}), s8[2097152]{0:T(1024)(128)(4,1)S(1)}, s32[]{:S(2)}) async-start(s8[14680064]{0:T(1024)(128)(4,1)} %bitcast.3), calls=%async_computation.7 | async-start | bytes 4194304
  48.6 12.9 %slice-start.10 = ((s8[14680064]{0:T(1024)(128)(4,1)}), s8[4194304]{0:T(1024)(128)(4,1)S(1)}, s32[]{:S(2)}) async-start(s8[14680064]{0:T(1024)(128)(4,1)} %bitcast.5), calls=%async_computation.10 | async-start | bytes 8388608
  48.6 12.9 %slice-start.11 = ((s8[14680064]{0:T(1024)(128)(4,1)}), s8[4194304]{0:T(1024)(128)(4,1)S(1)}, s32[]{:S(2)}) async-start(s8[14680064]{0:T(1024)(128)(4,1)} %bitcast.5), calls=%async_computation.11 | async-start | bytes 8388608
  48.7 7.9 %collective-permute-start.11 = (bf16[32,2048]{1,0:T(8,128)(2,1)S(1)}, bf16[32,2048]{1,0:T(8,128)(2,1)S(1)}, u32[]{:S(2)}, u32[]{:S(2)}) collective-permute-start(bf16[32,2048]{1,0:T(8,128)(2,1)S(1)} %shard_map.107), channel_id=1, source_target_pairs={{0,0},{1,4},{2,8},{3,12},{4,1},{5,5},{6,9},{7,13},{8,2},{9,6},{10,... | collective-permute-start | bytes 393224 | tf_op jit(solution)/shard_map/ppermute | solution.py:445
  49.5 7.2 %collective-permute-start.12 = (bf16[32,2048]{1,0:T(8,128)(2,1)S(1)}, bf16[32,2048]{1,0:T(8,128)(2,1)S(1)}, u32[]{:S(2)}, u32[]{:S(2)}) collective-permute-start(bf16[32,2048]{1,0:T(8,128)(2,1)S(1)} %shard_map.107), channel_id=1, source_target_pairs={{0,4},{1,0},{2,12},{3,8},{4,5},{5,1},{6,13},{7,9},{8,6},{9,2},{10,... | collective-permute-start | bytes 393224 | tf_op jit(solution)/shard_map/ppermute | solution.py:445
  52.0 9.1 %collective-permute-start.13 = (bf16[32,2048]{1,0:T(8,128)(2,1)S(1)}, bf16[32,2048]{1,0:T(8,128)(2,1)S(1)}, u32[]{:S(2)}, u32[]{:S(2)}) collective-permute-start(bf16[32,2048]{1,0:T(8,128)(2,1)S(1)} %shard_map.107), channel_id=1, source_target_pairs={{0,8},{1,12},{2,0},{3,4},{4,9},{5,13},{6,1},{7,5},{8,10},{9,14},{1... | collective-permute-start | bytes 393224 | tf_op jit(solution)/shard_map/ppermute | solution.py:445
  55.0 6.4 %collective-permute-start.14 = (bf16[32,2048]{1,0:T(8,128)(2,1)S(1)}, bf16[32,2048]{1,0:T(8,128)(2,1)S(1)}, u32[]{:S(2)}, u32[]{:S(2)}) collective-permute-start(bf16[32,2048]{1,0:T(8,128)(2,1)S(1)} %shard_map.107), channel_id=1, source_target_pairs={{0,12},{1,8},{2,4},{3,0},{4,13},{5,9},{6,5},{7,1},{8,14},{9,10},{1... | collective-permute-start | bytes 393224 | tf_op jit(solution)/shard_map/ppermute | solution.py:445
  64.7 9.4 %collective-permute-start.17 = (bf16[64,2560]{1,0:T(8,128)(2,1)S(1)}, bf16[64,2560]{1,0:T(8,128)(2,1)S(1)}, u32[]{:S(2)}, u32[]{:S(2)}) collective-permute-start(bf16[64,2560]{1,0:T(8,128)(2,1)S(1)} %get-tuple-element.67), channel_id=1, source_target_pairs={{0,1},{1,0},{2,3},{3,2},{4,5},{5,4},{6,7},{7,6},{8,9},{9,8},{10,11... | collective-permute-start | bytes 983048 | tf_op jit(solution)/shard_map/ppermute | solution.py:359
  67.3 2.1 %collective-permute-start.15 = (bf16[64,2304]{1,0:T(8,128)(2,1)S(1)}, bf16[64,2304]{1,0:T(8,128)(2,1)S(1)}, u32[]{:S(2)}, u32[]{:S(2)}) collective-permute-start(bf16[64,2304]{1,0:T(8,128)(2,1)S(1)} %get-tuple-element.61), channel_id=1, source_target_pairs={{0,1},{1,0},{2,3},{3,2},{4,5},{5,4},{6,7},{7,6},{8,9},{9,8},{10,11... | collective-permute-start | bytes 884744 | tf_op jit(solution)/shard_map/ppermute | solution.py:359
  69.0 5.2 %collective-permute-start.22 = (bf16[64,2560]{1,0:T(8,128)(2,1)S(1)}, bf16[64,2560]{1,0:T(8,128)(2,1)S(1)}, u32[]{:S(2)}, u32[]{:S(2)}) collective-permute-start(bf16[64,2560]{1,0:T(8,128)(2,1)S(1)} %get-tuple-element.71), channel_id=1, source_target_pairs={{0,1},{1,0},{2,3},{3,2},{4,5},{5,4},{6,7},{7,6},{8,9},{9,8},{10,11... | collective-permute-start | bytes 983048 | tf_op jit(solution)/shard_map/ppermute | solution.py:359
  69.5 9.2 %collective-permute-start.16 = (bf16[32,2304]{1,0:T(8,128)(2,1)S(1)}, bf16[32,2304]{1,0:T(8,128)(2,1)S(1)}, u32[]{:S(2)}, u32[]{:S(2)}) collective-permute-start(bf16[32,2304]{1,0:T(8,128)(2,1)S(1)} %get-tuple-element.63), channel_id=1, source_target_pairs={{0,2},{2,0},{1,3},{3,1},{4,6},{6,4},{5,7},{7,5},{8,10},{10,8},{9,1... | collective-permute-start | bytes 442376 | tf_op jit(solution)/shard_map/ppermute | solution.py:359
  74.1 8.1 %collective-permute-start.18 = (bf16[32,2560]{1,0:T(8,128)(2,1)S(1)}, bf16[32,2560]{1,0:T(8,128)(2,1)S(1)}, u32[]{:S(2)}, u32[]{:S(2)}) collective-permute-start(bf16[32,2560]{1,0:T(8,128)(2,1)S(1)} %get-tuple-element.69), channel_id=1, source_target_pairs={{0,2},{2,0},{1,3},{3,1},{4,6},{6,4},{5,7},{7,5},{8,10},{10,8},{9,1... | collective-permute-start | bytes 491528 | tf_op jit(solution)/shard_map/ppermute | solution.py:359
  74.3 11.5 %collective-permute-start.23 = (bf16[32,2560]{1,0:T(8,128)(2,1)S(1)}, bf16[32,2560]{1,0:T(8,128)(2,1)S(1)}, u32[]{:S(2)}, u32[]{:S(2)}) collective-permute-start(bf16[32,2560]{1,0:T(8,128)(2,1)S(1)} %get-tuple-element.73), channel_id=1, source_target_pairs={{0,2},{2,0},{1,3},{3,1},{4,6},{6,4},{5,7},{7,5},{8,10},{10,8},{9,1... | collective-permute-start | bytes 491528 | tf_op jit(solution)/shard_map/ppermute | solution.py:359
  78.7 11.7 %slice-start.1 = ((s8[14680064]{0:T(1024)(128)(4,1)}), s8[4194304]{0:T(1024)(128)(4,1)S(1)}, s32[]{:S(2)}) async-start(s8[14680064]{0:T(1024)(128)(4,1)} %bitcast.1), calls=%async_computation.1 | async-start | bytes 8388608
  78.8 9.1 %collective-permute-start.28 = (bf16[32,1024]{1,0:T(8,128)(2,1)S(1)}, bf16[32,1024]{1,0:T(8,128)(2,1)S(1)}, u32[]{:S(2)}, u32[]{:S(2)}) collective-permute-start(bf16[32,1024]{1,0:T(8,128)(2,1)S(1)} %get-tuple-element.74.refs_0_), channel_id=1, source_target_pairs={{0,2},{2,0},{1,3},{3,1},{4,6},{6,4},{5,7},{7,5},{8,10},{10,8},{9,1... | collective-permute-start | bytes 196616 | tf_op jit(solution)/shard_map/ppermute | solution.py:359
  82.3 7.0 %collective-permute-start.20 = (bf16[32,1280]{1,0:T(8,128)(2,1)S(1)}, bf16[32,1280]{1,0:T(8,128)(2,1)S(1)}, u32[]{:S(2)}, u32[]{:S(2)}) collective-permute-start(bf16[32,1280]{1,0:T(8,128)(2,1)S(1)} %shard_map.117.refs_0_), channel_id=1, source_target_pairs={{0,2},{2,0},{1,3},{3,1},{4,6},{6,4},{5,7},{7,5},{8,10},{10,8},{9,1... | collective-permute-start | bytes 245768 | tf_op jit(solution)/shard_map/ppermute | solution.py:359
  85.8 4.6 %collective-permute-start.25 = (bf16[32,1280]{1,0:T(8,128)(2,1)S(1)}, bf16[32,1280]{1,0:T(8,128)(2,1)S(1)}, u32[]{:S(2)}, u32[]{:S(2)}) collective-permute-start(bf16[32,1280]{1,0:T(8,128)(2,1)S(1)} %shard_map.120.refs_0_), channel_id=1, source_target_pairs={{0,2},{2,0},{1,3},{3,1},{4,6},{6,4},{5,7},{7,5},{8,10},{10,8},{9,1... | collective-permute-start | bytes 245768 | tf_op jit(solution)/shard_map/ppermute | solution.py:359
  87.9 1.3 %collective-permute-start.27 = (bf16[32,1024]{1,0:T(8,128)(2,1)S(1)}, bf16[32,1024]{1,0:T(8,128)(2,1)S(1)}, u32[]{:S(2)}, u32[]{:S(2)}) collective-permute-start(bf16[32,1024]{1,0:T(8,128)(2,1)S(1)} %get-tuple-element.74.refs_0_), channel_id=1, source_target_pairs={{0,1},{1,0},{2,3},{3,2},{4,5},{5,4},{6,7},{7,6},{8,9},{9,8},{10,11... | collective-permute-start | bytes 196616 | tf_op jit(solution)/shard_map/ppermute | solution.py:359
  87.9 2.5 %collective-permute-start.29 = (bf16[32,1024]{1,0:T(8,128)(2,1)S(1)}, bf16[32,1024]{1,0:T(8,128)(2,1)S(1)}, u32[]{:S(2)}, u32[]{:S(2)}) collective-permute-start(bf16[32,1024]{1,0:T(8,128)(2,1)S(1)} %collective-permute-done.28.refs_2_), channel_id=1, source_target_pairs={{0,1},{1,0},{2,3},{3,2},{4,5},{5,4},{6,7},{7,6},{8,9},{9,8},{10,11... | collective-permute-start | bytes 196616 | tf_op jit(solution)/shard_map/ppermute | solution.py:359
  88.4 4.1 %collective-permute-start.19 = (bf16[32,1280]{1,0:T(8,128)(2,1)S(1)}, bf16[32,1280]{1,0:T(8,128)(2,1)S(1)}, u32[]{:S(2)}, u32[]{:S(2)}) collective-permute-start(bf16[32,1280]{1,0:T(8,128)(2,1)S(1)} %shard_map.117.refs_0_), channel_id=1, source_target_pairs={{0,1},{1,0},{2,3},{3,2},{4,5},{5,4},{6,7},{7,6},{8,9},{9,8},{10,11... | collective-permute-start | bytes 245768 | tf_op jit(solution)/shard_map/ppermute | solution.py:359
  89.2 2.0 %collective-permute-start.24 = (bf16[32,1280]{1,0:T(8,128)(2,1)S(1)}, bf16[32,1280]{1,0:T(8,128)(2,1)S(1)}, u32[]{:S(2)}, u32[]{:S(2)}) collective-permute-start(bf16[32,1280]{1,0:T(8,128)(2,1)S(1)} %shard_map.120.refs_0_), channel_id=1, source_target_pairs={{0,1},{1,0},{2,3},{3,2},{4,5},{5,4},{6,7},{7,6},{8,9},{9,8},{10,11... | collective-permute-start | bytes 245768 | tf_op jit(solution)/shard_map/ppermute | solution.py:359
  89.4 3.2 %collective-permute-start.21 = (bf16[32,1280]{1,0:T(8,128)(2,1)S(1)}, bf16[32,1280]{1,0:T(8,128)(2,1)S(1)}, u32[]{:S(2)}, u32[]{:S(2)}) collective-permute-start(bf16[32,1280]{1,0:T(8,128)(2,1)S(1)} %collective-permute-done.20.refs_2_), channel_id=1, source_target_pairs={{0,1},{1,0},{2,3},{3,2},{4,5},{5,4},{6,7},{7,6},{8,9},{9,8},{10,11... | collective-permute-start | bytes 245768 | tf_op jit(solution)/shard_map/ppermute | solution.py:359
  90.4 1.3 %collective-permute-start.26 = (bf16[32,1280]{1,0:T(8,128)(2,1)S(1)}, bf16[32,1280]{1,0:T(8,128)(2,1)S(1)}, u32[]{:S(2)}, u32[]{:S(2)}) collective-permute-start(bf16[32,1280]{1,0:T(8,128)(2,1)S(1)} %collective-permute-done.25.refs_2_), channel_id=1, source_target_pairs={{0,1},{1,0},{2,3},{3,2},{4,5},{5,4},{6,7},{7,6},{8,9},{9,8},{10,11... | collective-permute-start | bytes 245768 | tf_op jit(solution)/shard_map/ppermute | solution.py:359
  93.1 13.4 %collective-permute-start.30 = (bf16[32,1024]{1,0:T(8,128)(2,1)S(1)}, bf16[32,1024]{1,0:T(8,128)(2,1)S(1)}, u32[]{:S(2)}, u32[]{:S(2)}) collective-permute-start(bf16[32,1024]{1,0:T(8,128)(2,1)S(1)} %get-tuple-element.76), channel_id=1, source_target_pairs={{0,4},{4,0},{8,12},{12,8},{1,5},{5,1},{9,13},{13,9},{2,6},{6,2},{1... | collective-permute-start | bytes 196616 | tf_op jit(solution)/shard_map/ppermute | solution.py:363
  95.7 4.6 %collective-permute-start.31 = (bf16[32,1024]{1,0:T(8,128)(2,1)S(1)}, bf16[32,1024]{1,0:T(8,128)(2,1)S(1)}, u32[]{:S(2)}, u32[]{:S(2)}) collective-permute-start(bf16[32,1024]{1,0:T(8,128)(2,1)S(1)} %get-tuple-element.78), channel_id=1, source_target_pairs={{0,4},{4,0},{8,12},{12,8},{1,5},{5,1},{9,13},{13,9},{2,6},{6,2},{1... | collective-permute-start | bytes 196616 | tf_op jit(solution)/shard_map/ppermute | solution.py:363
  96.3 10.1 %collective-permute-start.33 = (bf16[32,1024]{1,0:T(8,128)(2,1)S(1)}, bf16[32,1024]{1,0:T(8,128)(2,1)S(1)}, u32[]{:S(2)}, u32[]{:S(2)}) collective-permute-start(bf16[32,1024]{1,0:T(8,128)(2,1)S(1)} %get-tuple-element.80), channel_id=1, source_target_pairs={{0,4},{4,0},{8,12},{12,8},{1,5},{5,1},{9,13},{13,9},{2,6},{6,2},{1... | collective-permute-start | bytes 196616 | tf_op jit(solution)/shard_map/ppermute | solution.py:363
  98.3 5.3 %collective-permute-start.34 = (bf16[32,1024]{1,0:T(8,128)(2,1)S(1)}, bf16[32,1024]{1,0:T(8,128)(2,1)S(1)}, u32[]{:S(2)}, u32[]{:S(2)}) collective-permute-start(bf16[32,1024]{1,0:T(8,128)(2,1)S(1)} %get-tuple-element.82), channel_id=1, source_target_pairs={{0,4},{4,0},{8,12},{12,8},{1,5},{5,1},{9,13},{13,9},{2,6},{6,2},{1... | collective-permute-start | bytes 196616 | tf_op jit(solution)/shard_map/ppermute | solution.py:363
  100.3 7.6 %collective-permute-start.32 = (bf16[32,1024]{1,0:T(8,128)(2,1)S(1)}, bf16[32,1024]{1,0:T(8,128)(2,1)S(1)}, u32[]{:S(2)}, u32[]{:S(2)}) collective-permute-start(bf16[32,1024]{1,0:T(8,128)(2,1)S(1)} %shard_map.124), channel_id=1, source_target_pairs={{0,8},{4,12},{8,0},{12,4},{1,9},{5,13},{9,1},{13,5},{2,10},{6,14},... | collective-permute-start | bytes 196616 | tf_op jit(solution)/shard_map/ppermute | solution.py:363
  103.7 5.4 %collective-permute-start.35 = (bf16[32,1024]{1,0:T(8,128)(2,1)S(1)}, bf16[32,1024]{1,0:T(8,128)(2,1)S(1)}, u32[]{:S(2)}, u32[]{:S(2)}) collective-permute-start(bf16[32,1024]{1,0:T(8,128)(2,1)S(1)} %shard_map.126), channel_id=1, source_target_pairs={{0,8},{4,12},{8,0},{12,4},{1,9},{5,13},{9,1},{13,5},{2,10},{6,14},... | collective-permute-start | bytes 196616 | tf_op jit(solution)/shard_map/ppermute | solution.py:363
  (5 other events, 32.5 us)
